TPU v7x, 32 devices: a whole 2x2x4 slice. The times are simulated.
32 devices in a mesh: seg: 8 (over z, core), sec: 4 (over y, x).
Axes of the slice: x: 2, y: 2, z: 4, core: 2. Of those that a mesh axis runs over, the one named last changes fastest.
Arguments:
- left_env: bfloat16 [8, 4, 16, 256, 256], P('seg', 'sec'), as said below
- right_env: bfloat16 [8, 4, 16, 256, 256], P('seg', 'sec'), as said below
- left_piece: bfloat16 [8, 4, 256, 256], P('seg', 'sec'), may hold values from -0.375 to 0.375
- right_piece: bfloat16 [8, 4, 256, 256], P('seg', 'sec'), may hold values from -0.375 to 0.375
- guess: bfloat16 [8, 4, 256, 256], P('seg', 'sec'), may hold values from -0.375 to 0.375
- inverse_values: float32 [8, 4, 256], P('seg', 'sec'), may hold values from 0.5 to 4
- precond: bfloat16 [8, 4, 256, 256], P('seg', 'sec'), may hold values from 0.25 to 2
- sector_rows: int32 [8, 4], P('seg', 'sec'), may hold values from 64 to 256, as said below
Outputs:
- polar_factor: float32 [8, 4, 256, 256], P('seg', 'sec')
- next_left: bfloat16 [8, 4, 256, 256], P('seg', 'sec')
- energies: float32 [8], P('seg')
Inputs may be any that keep to these rules, and one draw needn't show every extreme that they name: `sector_rows`: some block has 256 live states and some has 64. `left_env`: each channel's block is symmetric. `right_env`: each channel's block is symmetric.
All inputs are finite; a program needn't handle non-finite values.
Results may differ from a plain program's by a relative error of at most 0.006.
Values may be sent and summed in bfloat16 or wider, within the bound.
No kernel may reach another device: no remote copies, remote signals or barrier semaphores. Data moves between devices by JAX's collectives and lax.ppermute only.
A program may use at most 64 MiB of HBM per device.

v0:
```python
import jax
import jax.numpy as jnp
from jax import lax
from jax.sharding import PartitionSpec as P

WD = 2
ITERS = 2
NS_STEPS = 3


def from_behind(value, axis, steps):
    count = lax.axis_size(axis)
    first, last = (max(0, -steps), min(count, count - steps))
    return lax.ppermute(value, axis, [(source, source + steps) for source in range(first, last)])


def shards(
    left_env, right_env, left_piece, right_piece, guess, inverse_values, precond, sector_rows
):
    f32 = jnp.float32
    bf16 = jnp.bfloat16
    lenv = left_env[0, 0]
    renv = right_env[0, 0]
    size = lenv.shape[-1]
    count = sector_rows[0, 0]
    idx_r = lax.broadcasted_iota(jnp.int32, (size, size), 0)
    idx_c = lax.broadcasted_iota(jnp.int32, (size, size), 1)
    mask = ((idx_r < count) & (idx_c < count)).astype(f32)
    lraise = lenv[WD:]
    rraise = renv[WD:]

    def lowering(vbf):
        inner = jnp.einsum("wji,jk->wik", lraise, vbf, preferred_element_type=f32).astype(bf16)
        return jnp.einsum("wik,wlk->il", inner, rraise, preferred_element_type=f32).astype(bf16)

    def raising(vbf):
        inner = jnp.einsum("wij,jk->wik", lraise, vbf, preferred_element_type=f32).astype(bf16)
        return jnp.einsum("wik,wkl->il", inner, rraise, preferred_element_type=f32)

    def apply_op(vec):
        vbf = vec.astype(bf16)
        from_below = from_behind(vbf, "sec", 1)
        down = lowering(vbf)
        from_above = from_behind(down, "sec", -1)
        inner = jnp.einsum("wij,jk->wik", lenv[:WD], vbf, preferred_element_type=f32).astype(bf16)
        diag = jnp.einsum("wik,wkl->il", inner, renv[:WD], preferred_element_type=f32)
        return mask * (diag + raising(from_below) + from_above.astype(f32))

    bnext = from_behind(right_piece[0, 0], "seg", -1)
    scaled = (left_piece[0, 0].astype(f32) * inverse_values[0, 0][None, :]).astype(bf16)
    start = mask * (jnp.dot(scaled, bnext, preferred_element_type=f32) + guess[0, 0].astype(f32))
    norm_start = lax.psum(jnp.sum(start * start), "sec")
    x = start / jnp.sqrt(norm_start)
    g = apply_op(x)
    prec = precond[0, 0].astype(f32)
    lam = jnp.float32(0.0)
    for step in range(ITERS):
        pg = prec * g
        px = prec * x
        moments = lax.psum(
            (
                jnp.sum(x * g),
                jnp.sum(x * pg),
                jnp.sum(x * px),
                jnp.sum(pg * pg),
                jnp.sum(pg * px),
                jnp.sum(px * px),
                jnp.sum(x * x),
            ),
            "sec",
        )
        a, xpg, xpx, pgpg, pgpx, pxpx, xx = moments
        p = pg - a * px
        s = xpg - a * xpx
        q = p - s * x
        pp = pgpg - 2.0 * a * pgpx + a * a * pxpx
        qq = pp - 2.0 * s * s + s * s * xx
        t = q / jnp.sqrt(qq)
        h = apply_op(t)
        b, c = lax.psum((jnp.sum(x * h), jnp.sum(t * h)), "sec")
        lam = 0.5 * (a + c) - jnp.sqrt((0.5 * (a - c)) ** 2 + b * b)
        coeff_x = c - lam
        coeff_t = -b
        nrm = jnp.sqrt(coeff_x * coeff_x + coeff_t * coeff_t)
        x = (coeff_x * x + coeff_t * t) / nrm
        g = (coeff_x * g + coeff_t * h) / nrm
    highest = lax.Precision.HIGHEST
    frob = jnp.sum(x * x)
    polar = x * lax.rsqrt(frob + 1e-06)
    for step in range(NS_STEPS):
        gram = jnp.dot(polar, polar.T, precision=highest, preferred_element_type=f32)
        polar = 1.5 * polar - 0.5 * jnp.dot(
            gram, polar, precision=highest, preferred_element_type=f32
        )
    weight = jnp.dot(polar.T, x, precision=highest, preferred_element_type=f32).astype(bf16)
    handed = from_behind(weight, "seg", 1)
    return (polar[None, None], handed[None, None], jnp.reshape(lam, (1,)))


def solution(mesh):
    placed = (
        P("seg", "sec", None, None, None),
        P("seg", "sec", None, None, None),
        P("seg", "sec", None, None),
        P("seg", "sec", None, None),
        P("seg", "sec", None, None),
        P("seg", "sec", None),
        P("seg", "sec", None, None),
        P("seg", "sec"),
    )
    return jax.shard_map(
        shards,
        mesh=mesh,
        in_specs=placed,
        out_specs=(P("seg", "sec", None, None), P("seg", "sec", None, None), P("seg")),
        check_vma=False,
    )
```

profile of v0, /device:TPU:1, one launch (start us, length us, event | category | flops | bytes accessed | tf_op | source)
XLA Modules:
  0.0 149.4 jit_solution(15739701416612282570)
XLA Ops:
  0.6 1.9 %collective-permute-start = (bf16[256,256]{1,0:T(8,128)(2,1)}, bf16[256,256]{1,0:T(8,128)(2,1)S(1)}, u32[]{:S(2)}, u32[]{:S(2)}) collective-permute-start(bf16[256,256]{1,0:T(8,128)(2,1)} %bitcast.372), channel_id=1, source_target_pairs={{4,0},{8,4},{12,8},{16,12},{20,16},{24,20},{28,24},{5,1},{9,5},{13... | collective-permute-start | bytes 393224 | tf_op jit(solution)/shard_map/ppermute | solution.py:14
  3.2 4.8 %collective-permute-done = bf16[256,256]{1,0:T(8,128)(2,1)S(1)} collective-permute-done((bf16[256,256]{1,0:T(8,128)(2,1)}, bf16[256,256]{1,0:T(8,128)(2,1)S(1)}, u32[]{:S(2)}, u32[]{:S(2)}) %collective-permute-start) | collective-permute-done | bytes 131104 | tf_op jit(solution)/shard_map/ppermute | solution.py:14
  8.1 1.8 %multiply_reduce_fusion.19 = (f32[]{:T(128)}, f32[256,256]{1,0:T(8,128)S(1)}) fusion(bf16[1,1,256,256]{3,2,1,0:T(8,128)(2,1)} %param.12, bf16[256,256]{1,0:T(8,128)(2,1)S(1)} %collective-permute-done, bf16[1,1,256,256]{3,2,1,0:T(8,128)(2,1)} %param.10, f32[256]{0:T(256)} %bitcast.373, pred[256]{0:T(512)(128)(4,1)S(1)} %iota_compare_fusion), kind=kOutput, calls=%fused_computation.123 | convolution fusion | flops 34144256 | bytes 656644 | tf_op jit(solution)/shard_map/dot_general | solution.py:51
  9.9 8.5 %psum.133 = f32[]{:T(128)} all-reduce(f32[]{:T(128)} %get-tuple-element.53), channel_id=1, replica_groups=mesh['seg'=8,'sec'=4] {'sec'}, use_global_device_ids=true, to_apply=%region_1.0 | all-reduce | flops 1 | bytes 8 | tf_op jit(solution)/shard_map/psum | solution.py:52
  19.1 1.4 collective-permute-start.1
  20.6 3.7 %fusion.192 = bf16[256,256]{1,0:T(8,128)(2,1)S(1)} fusion(bf16[1,1,16,256,256]{4,3,2,1,0:T(8,128)(2,1)} %param.9, bf16[1,1,16,256,256]{4,3,2,1,0:T(8,128)(2,1)} %param.8, bf16[256,256]{1,0:T(8,128)(2,1)S(1)} %fusion.262), kind=kOutput, calls=%fused_computation.74 | convolution fusion | flops 940507136 | bytes 3932160 | tf_op jit(solution)/shard_map/wik,wlk->il/dot_general | solution.py:34
  24.3 1.3 collective-permute-start.2
  25.6 1.4 fusion.62
  27.0 5.3 %collective-permute-done.2 = bf16[256,256]{1,0:T(8,128)(2,1)S(1)} collective-permute-done((bf16[256,256]{1,0:T(8,128)(2,1)S(1)}, bf16[256,256]{1,0:T(8,128)(2,1)S(1)}, u32[]{:S(2)}, u32[]{:S(2)}) %collective-permute-start.2) | collective-permute-done | bytes 131104 | tf_op jit(solution)/shard_map/ppermute | solution.py:14
  32.3 4.0 %multiply_reduce_fusion.16 = (f32[]{:T(128)}, f32[]{:T(128)}, f32[]{:T(128)}, f32[]{:T(128)}, f32[]{:T(128)}, /*index=5*/f32[]{:T(128)}, f32[]{:T(128)}, f32[256,256]{1,0:T(8,128)S(1)}) fusion(bf16[1,1,256,256]{3,2,1,0:T(8,128)(2,1)S(1)} %copy-done, f32[256,256]{1,0:T(8,128)S(1)} %get-tuple-element.54, f32[]{:T(128)S(6)} %sqrt.21, ...), kind=kOutput, calls=%fused_computation.120 | convolution fusion | flops 941948928 | bytes 4850720 | tf_op jit(solution)/shard_map/wik,wkl->il/dot_general | solution.py:38
  36.3 8.5 %all-reduce.3 = (f32[]{:T(128)}, f32[]{:T(128)}, f32[]{:T(128)}, f32[]{:T(128)}, f32[]{:T(128)}, /*index=5*/f32[]{:T(128)}, f32[]{:T(128)}) all-reduce(f32[]{:T(128)} %get-tuple-element.20, f32[]{:T(128)} %get-tuple-element.17, f32[]{:T(128)} %get-tuple-element.18, f32[]{:T(128)} %get-tuple-element.16, ...), channel_id=1, replica_groups=mesh['seg'=8,'sec'=4] {'sec'}, use_global_device_ids=true, to_apply=%region_9.0 | all-reduce | flops 7 | bytes 56 | tf_op jit(solution)/shard_map/psum | solution.py:60
  51.1 0.7 fusion.264
  51.8 3.2 %fusion.185 = bf16[256,256]{1,0:T(8,128)(2,1)S(1)} fusion(bf16[1,1,16,256,256]{4,3,2,1,0:T(8,128)(2,1)S(1)} %copy-done.2, bf16[1,1,16,256,256]{4,3,2,1,0:T(8,128)(2,1)} %param.8, bf16[256,256]{1,0:T(8,128)(2,1)S(1)} %get-tuple-element.51), kind=kOutput, calls=%fused_computation.73 | convolution fusion | flops 940507136 | bytes 3932160 | tf_op jit(solution)/shard_map/wik,wlk->il/dot_general | solution.py:34
  55.0 1.7 %collective-permute-start.3 = (bf16[256,256]{1,0:T(8,128)(2,1)S(1)}, bf16[256,256]{1,0:T(8,128)(2,1)S(1)}, u32[]{:S(2)}, u32[]{:S(2)}) collective-permute-start(bf16[256,256]{1,0:T(8,128)(2,1)S(1)} %get-tuple-element.51), channel_id=1, source_target_pairs={{0,1},{1,2},{2,3},{4,5},{5,6},{6,7},{8,9},{9,10},{10,11},{12,13},{... | collective-permute-start | bytes 393224 | tf_op jit(solution)/shard_map/ppermute | solution.py:14
  56.6 1.3 collective-permute-start.4
  57.9 2.1 %fusion.65 = f32[256,256]{1,0:T(8,128)} fusion(bf16[1,1,16,256,256]{4,3,2,1,0:T(8,128)(2,1)S(1)} %copy-done.2, bf16[1,1,16,256,256]{4,3,2,1,0:T(8,128)(2,1)} %param.8, bf16[256,256]{1,0:T(8,128)(2,1)S(1)} %get-tuple-element.51), kind=kOutput, calls=%fused_computation.44 | convolution fusion | flops 134348800 | bytes 917504 | tf_op jit(solution)/shard_map/wik,wkl->il/dot_general | solution.py:46
  60.0 3.7 %collective-permute-done.4 = bf16[256,256]{1,0:T(8,128)(2,1)S(1)} collective-permute-done((bf16[256,256]{1,0:T(8,128)(2,1)S(1)}, bf16[256,256]{1,0:T(8,128)(2,1)S(1)}, u32[]{:S(2)}, u32[]{:S(2)}) %collective-permute-start.4) | collective-permute-done | bytes 131104 | tf_op jit(solution)/shard_map/ppermute | solution.py:14
  63.7 4.4 %multiply_reduce_fusion.10 = (f32[]{:T(128)}, f32[]{:T(128)}, f32[256,256]{1,0:T(8,128)S(1)}) fusion(f32[256,256]{1,0:T(8,128)S(1)} %get-tuple-element.54, f32[]{:T(128)S(6)} %sqrt.21, f32[256,256]{1,0:T(8,128)S(1)} %get-tuple-element.52, bf16[256,256]{1,0:T(8,128)(2,1)S(1)} %collective-permute-done.4, f32[256,256]{1,0:T(8,128)} %fusion.65, ...), kind=kOutput, calls=%fused_computation.113 | convolution fusion | flops 941096960 | bytes 4981772 | tf_op jit(solution)/shard_map/wik,wkl->il/dot_general | solution.py:38
  68.0 8.5 %all-reduce.2 = (f32[]{:T(128)}, f32[]{:T(128)}) all-reduce(f32[]{:T(128)} %get-tuple-element.25, f32[]{:T(128)} %get-tuple-element.24), channel_id=1, replica_groups=mesh['seg'=8,'sec'=4] {'sec'}, use_global_device_ids=true, to_apply=%region_17.0 | all-reduce | flops 2 | bytes 16 | tf_op jit(solution)/shard_map/psum | solution.py:80
  81.7 1.0 multiply_reduce_fusion.7
  82.7 6.4 %all-reduce.1 = (f32[]{:T(128)}, f32[]{:T(128)}, f32[]{:T(128)}, f32[]{:T(128)}, f32[]{:T(128)}, /*index=5*/f32[]{:T(128)}, f32[]{:T(128)}) all-reduce(f32[]{:T(128)} %get-tuple-element.14, f32[]{:T(128)} %get-tuple-element.11, f32[]{:T(128)} %get-tuple-element.12, f32[]{:T(128)} %get-tuple-element.10, ...), channel_id=1, replica_groups=mesh['seg'=8,'sec'=4] {'sec'}, use_global_device_ids=true, to_apply=%region_27.0 | all-reduce | flops 7 | bytes 56 | tf_op jit(solution)/shard_map/psum | solution.py:60
  95.5 0.7 fusion.263
  96.3 3.9 %fusion.178 = bf16[256,256]{1,0:T(8,128)(2,1)S(1)} fusion(bf16[1,1,16,256,256]{4,3,2,1,0:T(8,128)(2,1)} %param.9, bf16[1,1,16,256,256]{4,3,2,1,0:T(8,128)(2,1)} %param.8, bf16[256,256]{1,0:T(8,128)(2,1)S(1)} %get-tuple-element.47), kind=kOutput, calls=%fused_computation.72 | convolution fusion | flops 940507136 | bytes 3932160 | tf_op jit(solution)/shard_map/wik,wlk->il/dot_general | solution.py:34
  100.2 3.4 %collective-permute-start.5 = (bf16[256,256]{1,0:T(8,128)(2,1)S(1)}, bf16[256,256]{1,0:T(8,128)(2,1)S(1)}, u32[]{:S(2)}, u32[]{:S(2)}) collective-permute-start(bf16[256,256]{1,0:T(8,128)(2,1)S(1)} %get-tuple-element.47), channel_id=1, source_target_pairs={{0,1},{1,2},{2,3},{4,5},{5,6},{6,7},{8,9},{9,10},{10,11},{12,13},{... | collective-permute-start | bytes 393224 | tf_op jit(solution)/shard_map/ppermute | solution.py:14
  103.5 1.3 collective-permute-start.6
  104.9 1.4 fusion.68
  106.2 3.0 %collective-permute-done.6 = bf16[256,256]{1,0:T(8,128)(2,1)S(1)} collective-permute-done((bf16[256,256]{1,0:T(8,128)(2,1)S(1)}, bf16[256,256]{1,0:T(8,128)(2,1)S(1)}, u32[]{:S(2)}, u32[]{:S(2)}) %collective-permute-start.6) | collective-permute-done | bytes 131104 | tf_op jit(solution)/shard_map/ppermute | solution.py:14
  109.3 3.8 %multiply_reduce_fusion.1 = (f32[]{:T(128)}, f32[]{:T(128)}) fusion(f32[256,256]{1,0:T(8,128)S(1)} %get-tuple-element.50, f32[256,256]{1,0:T(8,128)S(1)} %get-tuple-element.48, bf16[256,256]{1,0:T(8,128)(2,1)S(1)} %collective-permute-done.6, f32[256,256]{1,0:T(8,128)S(1)} %fusion.68, bf16[1,1,16,256,256]{4,3,2,1,0:T(8,128)(2,1)S(1)} %copy-done.3, ...), kind=kOutput, calls=%fused_computation.101 | convolution fusion | flops 941031424 | bytes 4719624 | tf_op jit(solution)/shard_map/wik,wkl->il/dot_general | solution.py:38
  113.1 8.3 %all-reduce = (f32[]{:T(128)}, f32[]{:T(128)}) all-reduce(f32[]{:T(128)} %get-tuple-element.22, f32[]{:T(128)} %get-tuple-element.21), channel_id=1, replica_groups=mesh['seg'=8,'sec'=4] {'sec'}, use_global_device_ids=true, to_apply=%region_35.0 | all-reduce | flops 2 | bytes 16 | tf_op jit(solution)/shard_map/psum | solution.py:80
  126.6 0.7 multiply_reduce_fusion
  131.0 14.7 %collective-permute-start.7 = (bf16[256,256]{1,0:T(8,128)(2,1)S(1)}, bf16[256,256]{1,0:T(8,128)(2,1)S(1)}, u32[]{:S(2)}, u32[]{:S(2)}) collective-permute-start(bf16[256,256]{1,0:T(8,128)(2,1)S(1)} %convolution_convert_fusion.3), channel_id=1, source_target_pairs={{0,4},{4,8},{8,12},{12,16},{16,20},{20,24},{24,28},{1,5},{5,9},{9,... | collective-permute-start | bytes 393224 | tf_op jit(solution)/shard_map/ppermute | solution.py:14
  145.7 1.9 %collective-permute-done.7 = bf16[256,256]{1,0:T(8,128)(2,1)S(1)} collective-permute-done((bf16[256,256]{1,0:T(8,128)(2,1)S(1)}, bf16[256,256]{1,0:T(8,128)(2,1)S(1)}, u32[]{:S(2)}, u32[]{:S(2)}) %collective-permute-start.7) | collective-permute-done | bytes 131104 | tf_op jit(solution)/shard_map/ppermute | solution.py:14
  (21 shorter events, 3.7 us)
Async XLA Ops:
  0.6 7.4 %collective-permute-start = (bf16[256,256]{1,0:T(8,128)(2,1)}, bf16[256,256]{1,0:T(8,128)(2,1)S(1)}, u32[]{:S(2)}, u32[]{:S(2)}) collective-permute-start(bf16[256,256]{1,0:T(8,128)(2,1)} %bitcast.372), channel_id=1, source_target_pairs={{4,0},{8,4},{12,8},{16,12},{20,16},{24,20},{28,24},{5,1},{9,5},{13... | collective-permute-start | bytes 393224 | tf_op jit(solution)/shard_map/ppermute | solution.py:14
  19.1 6.5 %copy-start.2 = (bf16[1,1,16,256,256]{4,3,2,1,0:T(8,128)(2,1)S(1)}, bf16[1,1,16,256,256]{4,3,2,1,0:T(8,128)(2,1)}, u32[]{:S(2)}) copy-start(bf16[1,1,16,256,256]{4,3,2,1,0:T(8,128)(2,1)} %param.9) | copy-start | bytes 6291460
  19.1 13.2 %copy-start = (bf16[1,1,256,256]{3,2,1,0:T(8,128)(2,1)S(1)}, bf16[1,1,256,256]{3,2,1,0:T(8,128)(2,1)}, u32[]{:S(2)}) copy-start(bf16[1,1,256,256]{3,2,1,0:T(8,128)(2,1)} %param.14) | copy-start | bytes 393220
  19.1 13.2 %collective-permute-start.1 = (bf16[256,256]{1,0:T(8,128)(2,1)S(1)}, bf16[256,256]{1,0:T(8,128)(2,1)S(1)}, u32[]{:S(2)}, u32[]{:S(2)}) collective-permute-start(bf16[256,256]{1,0:T(8,128)(2,1)S(1)} %fusion.262), channel_id=1, source_target_pairs={{0,1},{1,2},{2,3},{4,5},{5,6},{6,7},{8,9},{9,10},{10,11},{12,13},{... | collective-permute-start | bytes 393224 | tf_op jit(solution)/shard_map/ppermute | solution.py:14
  24.3 8.0 %collective-permute-start.2 = (bf16[256,256]{1,0:T(8,128)(2,1)S(1)}, bf16[256,256]{1,0:T(8,128)(2,1)S(1)}, u32[]{:S(2)}, u32[]{:S(2)}) collective-permute-start(bf16[256,256]{1,0:T(8,128)(2,1)S(1)} %fusion.192), channel_id=1, source_target_pairs={{1,0},{2,1},{3,2},{5,4},{6,5},{7,6},{9,8},{10,9},{11,10},{13,12},{... | collective-permute-start | bytes 393224 | tf_op jit(solution)/shard_map/ppermute | solution.py:14
  55.0 8.7 %collective-permute-start.3 = (bf16[256,256]{1,0:T(8,128)(2,1)S(1)}, bf16[256,256]{1,0:T(8,128)(2,1)S(1)}, u32[]{:S(2)}, u32[]{:S(2)}) collective-permute-start(bf16[256,256]{1,0:T(8,128)(2,1)S(1)} %get-tuple-element.51), channel_id=1, source_target_pairs={{0,1},{1,2},{2,3},{4,5},{5,6},{6,7},{8,9},{9,10},{10,11},{12,13},{... | collective-permute-start | bytes 393224 | tf_op jit(solution)/shard_map/ppermute | solution.py:14
  56.6 7.0 %collective-permute-start.4 = (bf16[256,256]{1,0:T(8,128)(2,1)S(1)}, bf16[256,256]{1,0:T(8,128)(2,1)S(1)}, u32[]{:S(2)}, u32[]{:S(2)}) collective-permute-start(bf16[256,256]{1,0:T(8,128)(2,1)S(1)} %fusion.185), channel_id=1, source_target_pairs={{1,0},{2,1},{3,2},{5,4},{6,5},{7,6},{9,8},{10,9},{11,10},{13,12},{... | collective-permute-start | bytes 393224 | tf_op jit(solution)/shard_map/ppermute | solution.py:14
  96.3 8.6 %copy-start.3 = (bf16[1,1,16,256,256]{4,3,2,1,0:T(8,128)(2,1)S(1)}, bf16[1,1,16,256,256]{4,3,2,1,0:T(8,128)(2,1)}, u32[]{:S(2)}) copy-start(bf16[1,1,16,256,256]{4,3,2,1,0:T(8,128)(2,1)} %param.9) | copy-start | bytes 6291460
  100.2 9.1 %collective-permute-start.5 = (bf16[256,256]{1,0:T(8,128)(2,1)S(1)}, bf16[256,256]{1,0:T(8,128)(2,1)S(1)}, u32[]{:S(2)}, u32[]{:S(2)}) collective-permute-start(bf16[256,256]{1,0:T(8,128)(2,1)S(1)} %get-tuple-element.47), channel_id=1, source_target_pairs={{0,1},{1,2},{2,3},{4,5},{5,6},{6,7},{8,9},{9,10},{10,11},{12,13},{... | collective-permute-start | bytes 393224 | tf_op jit(solution)/shard_map/ppermute | solution.py:14
  103.5 5.7 %collective-permute-start.6 = (bf16[256,256]{1,0:T(8,128)(2,1)S(1)}, bf16[256,256]{1,0:T(8,128)(2,1)S(1)}, u32[]{:S(2)}, u32[]{:S(2)}) collective-permute-start(bf16[256,256]{1,0:T(8,128)(2,1)S(1)} %fusion.178), channel_id=1, source_target_pairs={{1,0},{2,1},{3,2},{5,4},{6,5},{7,6},{9,8},{10,9},{11,10},{13,12},{... | collective-permute-start | bytes 393224 | tf_op jit(solution)/shard_map/ppermute | solution.py:14
  130.4 17.9 %copy-start.1 = (f32[256,256]{1,0:T(8,128)}, f32[256,256]{1,0:T(8,128)S(1)}, u32[]{:S(2)}) copy-start(f32[256,256]{1,0:T(8,128)S(1)} %fusion.69) | copy-start | bytes 786436
  131.0 16.6 %collective-permute-start.7 = (bf16[256,256]{1,0:T(8,128)(2,1)S(1)}, bf16[256,256]{1,0:T(8,128)(2,1)S(1)}, u32[]{:S(2)}, u32[]{:S(2)}) collective-permute-start(bf16[256,256]{1,0:T(8,128)(2,1)S(1)} %convolution_convert_fusion.3), channel_id=1, source_target_pairs={{0,4},{4,8},{8,12},{12,16},{16,20},{20,24},{24,28},{1,5},{5,9},{9,... | collective-permute-start | bytes 393224 | tf_op jit(solution)/shard_map/ppermute | solution.py:14
where the time goes:
time: 150 us; the launch traced here: 149 us
  blocking collectives  40.3 us (27%)
  matrix products  32.5 us (22%)
  between operations  27.1 us (18%)
  starting transfers between devices  26.9 us (18%)
  waiting for transfers between devices  18.8 us (13%)
  other arithmetic  3.09 us (2%)
    ppermute x8, starting transfers between devices, from_behind(): lax.ppermute(value, axis, [(source, source + steps) for source in range(f...  26.9 us
    ppermute x8, waiting for transfers between devices, from_behind(): lax.ppermute(value, axis, [(source, source + steps) for source in range(f...  18.8 us
    psum x2, blocking collectives, shards(): b, c = lax.psum((jnp.sum(x * h), jnp.sum(t * h)), 'sec')  16.8 us
    psum x2, blocking collectives, shards(): lax.psum((jnp.sum(x * g), jnp.sum(x * pg), jnp.sum(x * px), jnp.sum(pg *...  15 us
    dot_general x3, matrix products, raising(): return jnp.einsum('wik,wkl->il', inner, rraise, preferred_element_type=f32)  12.1 us
    dot_general x3, matrix products, lowering(): jnp.einsum('wik,wlk->il', inner, rraise, preferred_element_type=f32)  10.8 us
    psum x1, blocking collectives, shards(): norm_start = lax.psum(jnp.sum(start * start), 'sec')  8.5 us
    dot_general x3, matrix products, apply_op(): jnp.einsum('wik,wkl->il', inner, renv[:WD], preferred_element_type=f32)  4.86 us
  transfers between devices with their start and end apart: 8, of which 5 were waited for; matrix products, arithmetic and copies ran while one was open for 6% of the time, Pallas kernels for 0%

commit v1 on v0

v1 whole, which is shorter than its diff:
```python
import functools

import jax
import jax.numpy as jnp
from jax import lax
from jax.experimental import pallas as pl
from jax.experimental.pallas import tpu as pltpu
from jax.sharding import PartitionSpec as P

WD = 2
NS_STEPS = 3
ROWS = 8
LANES = 128
F32 = jnp.float32
BF16 = jnp.bfloat16
VMEM = pl.BlockSpec(memory_space=pltpu.VMEM)
SMEM = pl.BlockSpec(memory_space=pltpu.SMEM)


def shift(value, axis, steps):
    count = lax.axis_size(axis)
    first, last = max(0, -steps), min(count, count - steps)
    return lax.ppermute(value, axis, [(source, source + steps) for source in range(first, last)])


def exchange(value, axis):
    count = lax.axis_size(axis)
    if count & (count - 1):
        return [lax.psum(value, axis)]
    parts, done = [value], 1
    while done < count:
        if len(parts) > 1:
            parts = [total(parts)]
        radix = 4 if count // done >= 4 else 2
        for digit in range(1, radix):
            pairs = [(source, source ^ (digit * done)) for source in range(count)]
            parts.append(lax.ppermute(parts[0], axis, pairs))
        done *= radix
    return parts


def total(parts):
    while len(parts) > 1:
        parts = [parts[i] + parts[i + 1] for i in range(0, len(parts), 2)]
    return parts[0]


def fold(product):
    row = jnp.sum(product, axis=0, keepdims=True)
    width = row.shape[-1]
    out = row[:, :LANES]
    for start in range(LANES, width, LANES):
        out = out + row[:, start : start + LANES]
    return out


def scalars(refs, count):
    sums = jnp.sum(total([ref[...] for ref in refs]), axis=1, keepdims=True)
    return [sums[i : i + 1] for i in range(count)]


def sandwich(left, right, value, inner, first, last):
    size = value.shape[-1]
    for w in range(first, last):
        product = jnp.dot(left[w], value, preferred_element_type=F32)
        inner[:, w * size : (w + 1) * size] = product.astype(BF16)
    stacked = right[first:last].reshape((last - first) * size, size)
    return jnp.dot(inner[:, first * size : last * size], stacked, preferred_element_type=F32)


def start_kernel(scaled, behind, guess, mask, y_ref, yb_ref):
    size = mask.shape[-1]
    start = jnp.dot(scaled[...], behind[...], preferred_element_type=F32) + guess[...].astype(F32)
    y = mask[...] * start * (1.0 / (1 << (size - 1).bit_length()))
    y_ref[...] = y
    yb_ref[...] = y.astype(BF16)


def lower_kernel(pairs, sends, left, right, vector_b, *refs):
    ops, outs = refs[: len(refs) - 4 - sends], refs[len(refs) - 4 - sends :]
    inner = outs[-1]
    low_ref, diag_ref, stat_ref = outs[:3]
    channels = left.shape[0]
    value = vector_b[...]
    low = sandwich(left, right, value, inner, WD, channels)
    low_ref[...] = low
    if sends:
        outs[3][...] = low.astype(BF16)
    diag = sandwich(left, right, value, inner, 0, WD)
    diag_ref[...] = diag
    stat_ref[...] = jnp.zeros(stat_ref.shape, F32)
    for row, (one, two) in enumerate(pairs):
        other = diag if two is None else ops[two][...]
        stat_ref[row : row + 1] = fold(ops[one][...] * other)


def cross_kernel(row, below, low, stat, out):
    out[...] = stat[...]
    out[row : row + 1] = stat[row : row + 1] + 2.0 * fold(below[...].astype(F32) * low[...])


def raise_kernel(left, right, below, after, up_ref, inner):
    up_ref[...] = sandwich(left, right, below[...], inner, WD, left.shape[0])


def first_kernel(parts, *refs):
    y_ref, diag, up, above, mask, prec = refs[parts : parts + 6]
    g_ref, p_ref, pb_ref = refs[parts + 6 :]
    yy, yhy = scalars(refs[:parts], 2)
    g = mask[...] * (diag[...] + up[...] + above[...].astype(F32))
    g_ref[...] = g
    p = prec[...].astype(F32) * (g - (yhy / yy) * y_ref[...])
    p_ref[...] = p
    pb_ref[...] = p.astype(BF16)


def ritz(a, b, c):
    lam = 0.5 * (a + c) - jnp.sqrt((0.5 * (a - c)) ** 2 + b * b)
    u, w = c - lam, -b
    n = jnp.sqrt(u * u + w * w)
    return lam, u / n, w / n


def second_kernel(parts, *refs):
    y_ref, g_ref, p_ref, diag, up, above, mask, prec = refs[parts : parts + 8]
    x_out, g_out, p_out, pb_out, lam_out = refs[parts + 8 :]
    yy, yg, yp, pp, pg, php = scalars(refs[:parts], 6)
    a = yg / yy
    s = yp / yy
    qq = pp - 2.0 * s * yp + s * s * yy
    b = (pg - s * yg) / jnp.sqrt(qq * yy)
    c = (php - 2.0 * s * pg + s * s * yg) / qq
    lam, u, w = ritz(a, b, c)
    along_p = w / jnp.sqrt(qq)
    along_y = u / jnp.sqrt(yy) - along_p * s
    hp = mask[...] * (diag[...] + up[...] + above[...].astype(F32))
    x = along_y * y_ref[...] + along_p * p_ref[...]
    g = along_y * g_ref[...] + along_p * hp
    p = prec[...].astype(F32) * (g - lam * x)
    x_out[...] = x
    g_out[...] = g
    p_out[...] = p
    pb_out[...] = p.astype(BF16)
    lam_out[...] = jnp.broadcast_to(lam, lam_out.shape)


def split(value):
    high = value.astype(BF16)
    return high, (value - high.astype(F32)).astype(BF16)


def product(one, two, over):
    dims = ((over[:1], over[1:]), ((), ()))
    dot = functools.partial(lax.dot_general, dimension_numbers=dims, preferred_element_type=F32)
    (one_high, one_low), (two_high, two_low) = one, two
    return dot(one_high, two_high) + (dot(one_high, two_low) + dot(one_low, two_high))


def last_kernel(parts, *refs):
    x_ref, p_ref, lam_ref = refs[parts : parts + 3]
    polar_out, weight_out, lam_out = refs[parts + 3 :]
    xp, pp, pg, php = scalars(refs[:parts], 4)
    a = lam_ref[0:1, 0:1]
    qq = pp - xp * xp
    b = (pg - xp * a) / jnp.sqrt(qq)
    c = (php - 2.0 * xp * pg + xp * xp * a) / qq
    lam, u, w = ritz(a, b, c)
    along_p = w / jnp.sqrt(qq)
    along_x = u - along_p * xp
    lam_out[0] = lam[0, 0]
    x = along_x * x_ref[...] + along_p * p_ref[...]
    frob = jnp.sum(jnp.sum(x * x, axis=0, keepdims=True), axis=1, keepdims=True)
    polar = x * lax.rsqrt(frob + 1e-06)
    for _ in range(NS_STEPS):
        halves = split(polar)
        gram = product(halves, halves, (1, 1))
        polar = 1.5 * polar - 0.5 * product(split(gram), halves, (1, 0))
    polar_out[0, 0] = polar
    weight_out[0, 0] = product(split(polar), split(x), (0, 0)).astype(BF16)


def shards(
    left_env, right_env, left_piece, right_piece, guess, inverse_values, precond, sector_rows
):
    left, right = left_env[0, 0], right_env[0, 0]
    channels, size = left.shape[0], left.shape[-1]
    count = sector_rows[0, 0]
    matrix = jax.ShapeDtypeStruct((size, size), F32)
    narrow = jax.ShapeDtypeStruct((size, size), BF16)
    stats = jax.ShapeDtypeStruct((ROWS, LANES), F32)
    inner = pltpu.VMEM((size, channels * size), BF16)

    def call(kernel, name, outs, *operands, scratch=(), out_specs=None):
        return pl.pallas_call(
            kernel,
            name=name,
            out_shape=outs,
            in_specs=[VMEM] * len(operands),
            out_specs=out_specs or [VMEM] * len(outs),
            scratch_shapes=list(scratch),
            compiler_params=pltpu.CompilerParams(vmem_limit_bytes=16 << 20),
        )(*operands)

    behind = shift(right_piece[0, 0], "seg", -1)
    idx_r = lax.broadcasted_iota(jnp.int32, (size, size), 0)
    idx_c = lax.broadcasted_iota(jnp.int32, (size, size), 1)
    mask = ((idx_r < count) & (idx_c < count)).astype(F32)
    scaled = (left_piece[0, 0].astype(F32) * inverse_values[0, 0][None, :]).astype(BF16)
    prec = precond[0, 0]

    y, yb = call(start_kernel, "start", [matrix, narrow], scaled, behind, guess[0, 0], mask)

    def half(name, vector_b, pairs, operands, row, sends):
        below = shift(vector_b, "sec", 1)
        outs = [matrix, matrix, stats] + [narrow] * sends
        kernel = functools.partial(lower_kernel, pairs, sends)
        low, diag, stat, *sent = call(
            kernel, name + "_lower", outs, left, right, vector_b, *operands, scratch=[inner]
        )
        above = shift(sent[0], "sec", -1) if sends else None
        (stat,) = call(functools.partial(cross_kernel, row), name + "_cross", [stats], below, low, stat)
        return below, diag, above, stat

    def raised(name, below, stat):
        return call(raise_kernel, name, [matrix], left, right, below, stat, scratch=[inner])[0]

    below, diag, above, stat = half("one", yb, [(0, 0), (0, None)], [y], 1, 1)
    parts = exchange(stat, "sec")
    up = raised("one_raise", below, stat)
    kernel = functools.partial(first_kernel, len(parts))
    g, p, pb = call(
        kernel, "first", [matrix, matrix, narrow], *parts, y, diag, up, above, mask, prec
    )

    pairs = [(0, 0), (0, 1), (0, 2), (2, 2), (2, 1), (2, None)]
    below, diag, above, stat = half("two", pb, pairs, [y, g, p], 5, 1)
    parts = exchange(stat, "sec")
    up = raised("two_raise", below, stat)
    kernel = functools.partial(second_kernel, len(parts))
    x, g, p, pb, lam = call(
        kernel,
        "second",
        [matrix, matrix, matrix, narrow, stats],
        *parts, y, g, p, diag, up, above, mask, prec,
    )

    pairs = [(0, 2), (2, 2), (2, 1), (2, None)]
    below, diag, above, stat = half("three", pb, pairs, [x, g, p], 3, 0)
    parts = exchange(stat, "sec")
    kernel = functools.partial(last_kernel, len(parts))
    block = (1, 1, size, size)
    polar, weight, energy = call(
        kernel,
        "last",
        [
            jax.ShapeDtypeStruct(block, F32),
            jax.ShapeDtypeStruct(block, BF16),
            jax.ShapeDtypeStruct((1,), F32),
        ],
        *parts, x, p, lam,
        out_specs=[VMEM, VMEM, SMEM],
    )
    return polar, shift(weight, "seg", 1), energy


def solution(mesh):
    placed = (
        P("seg", "sec", None, None, None),
        P("seg", "sec", None, None, None),
        P("seg", "sec", None, None),
        P("seg", "sec", None, None),
        P("seg", "sec", None, None),
        P("seg", "sec", None),
        P("seg", "sec", None, None),
        P("seg", "sec"),
    )
    return jax.shard_map(
        shards,
        mesh=mesh,
        in_specs=placed,
        out_specs=(P("seg", "sec", None, None), P("seg", "sec", None, None), P("seg")),
        check_vma=False,
    )
```

time: 150 us -> 62.4 us (0.42)
  the two profiles are of different devices: /device:TPU:1 before, /device:TPU:28 now
where the time goes in v1:
time: 62.4 us; the launch traced here: 62.1 us
  starting transfers between devices  31.9 us (51%)
  waiting for transfers between devices  12.2 us (20%)
  Pallas kernels  10.7 us (17%)
  local copies, waits for them, and re-layouts  4.75 us (8%)
  between operations  1.47 us (2%)
  other arithmetic  1.04 us (2%)
    ppermute x7, starting transfers between devices, shift(): lax.ppermute(value, axis, [(source, source + steps) for source in range(f...  21.3 us
    pallas_call x12, Pallas kernels, call(): pl.pallas_call(kernel, name=name, out_shape=outs, in_specs=[VMEM] * len(o...  10.7 us
    ppermute x9, starting transfers between devices, exchange(): parts.append(lax.ppermute(parts[0], axis, pairs))  10.6 us
    ppermute x7, waiting for transfers between devices, shift(): lax.ppermute(value, axis, [(source, source + steps) for source in range(f...  8.16 us
    unnamed x13, local copies, waits for them, and re-layouts  4.75 us
    ppermute x9, waiting for transfers between devices, exchange(): parts.append(lax.ppermute(parts[0], axis, pairs))  4 us
  transfers between devices with their start and end apart: 16, of which 8 were waited for; matrix products, arithmetic and copies ran while one was open for 2% of the time, Pallas kernels for 11%

profile of v1, /device:TPU:28, one launch (start us, length us, event | category | flops | bytes accessed | tf_op | source)
XLA Modules:
  0.0 62.1 jit_solution(10106142042044044735)
XLA Ops:
  0.6 1.9 %collective-permute-start = (bf16[256,256]{1,0:T(8,128)(2,1)}, bf16[256,256]{1,0:T(8,128)(2,1)S(1)}, u32[]{:S(2)}, u32[]{:S(2)}) collective-permute-start(bf16[256,256]{1,0:T(8,128)(2,1)} %bitcast.25), channel_id=1, source_target_pairs={{4,0},{8,4},{12,8},{16,12},{20,16},{24,20},{28,24},{5,1},{9,5},{13... | collective-permute-start | bytes 393224 | tf_op jit(solution)/shard_map/ppermute | solution.py:23
  3.3 0.9 %fusion.scaled = bf16[256,256]{1,0:T(8,128)(2,1)S(1)} fusion(bf16[1,1,256,256]{3,2,1,0:T(8,128)(2,1)} %param.10, f32[256]{0:T(256)} %bitcast.24), kind=kLoop, calls=%fused_computation.1 | loop fusion | flops 196608 | bytes 263168 | tf_op jit(solution)/shard_map/convert_element_type | solution.py:208
  4.3 1.1 %collective-permute-done.behind = bf16[256,256]{1,0:T(8,128)(2,1)S(1)} collective-permute-done((bf16[256,256]{1,0:T(8,128)(2,1)}, bf16[256,256]{1,0:T(8,128)(2,1)S(1)}, u32[]{:S(2)}, u32[]{:S(2)}) %collective-permute-start) | collective-permute-done | bytes 131104 | tf_op jit(solution)/shard_map/ppermute | solution.py:23
  5.4 0.9 %copy-done.5 = bf16[1,1,256,256]{3,2,1,0:T(8,128)(2,1)S(1)} copy-done((bf16[1,1,256,256]{3,2,1,0:T(8,128)(2,1)S(1)}, bf16[1,1,256,256]{3,2,1,0:T(8,128)(2,1)}, u32[]{:S(2)}) %copy-start.5) | copy-done | bytes 131096
  6.5 3.4 %collective-permute-start.1 = (bf16[256,256]{1,0:T(8,128)(2,1)S(1)}, bf16[256,256]{1,0:T(8,128)(2,1)S(1)}, u32[]{:S(2)}, u32[]{:S(2)}) collective-permute-start(bf16[256,256]{1,0:T(8,128)(2,1)S(1)} %get-tuple-element.26.vector_b), channel_id=1, source_target_pairs={{0,1},{1,2},{2,3},{4,5},{5,6},{6,7},{8,9},{9,10},{10,11},{12,13},{... | collective-permute-start | bytes 393224 | tf_op jit(solution)/shard_map/ppermute | solution.py:23
  9.9 1.6 %copy-done = bf16[1,1,16,256,256]{4,3,2,1,0:T(8,128)(2,1)S(1)} copy-done((bf16[1,1,16,256,256]{4,3,2,1,0:T(8,128)(2,1)S(1)}, bf16[1,1,16,256,256]{4,3,2,1,0:T(8,128)(2,1)}, u32[]{:S(2)}) %copy-start) | copy-done | bytes 2097176
  11.5 1.6 %copy-done.2 = bf16[1,1,16,256,256]{4,3,2,1,0:T(8,128)(2,1)S(1)} copy-done((bf16[1,1,16,256,256]{4,3,2,1,0:T(8,128)(2,1)S(1)}, bf16[1,1,16,256,256]{4,3,2,1,0:T(8,128)(2,1)}, u32[]{:S(2)}) %copy-start.2) | copy-done | bytes 2097176
  13.1 1.3 %one_lower.1 = (f32[256,256]{1,0:T(8,128)S(1)}, f32[256,256]{1,0:T(8,128)S(1)}, f32[8,128]{1,0:T(8,128)S(1)}, bf16[256,256]{1,0:T(8,128)(2,1)S(1)}) custom-call(bf16[16,256,256]{2,1,0:T(8,128)(2,1)S(1)} %bitcast.11, bf16[16,256,256]{2,1,0:T(8,128)(2,1)S(1)} %bitcast.16, bf16[256,256]{1,0:T(8,128)(2,1)S(1)} %get-tuple-element.26.vector_b, ...), custom_call_target="tpu_custom_call" | custom-call | tf_op jit(solution)/shard_map/one_lower/pallas_call | solution.py:194
  14.4 3.3 %collective-permute-start.5 = (bf16[256,256]{1,0:T(8,128)(2,1)S(1)}, bf16[256,256]{1,0:T(8,128)(2,1)S(1)}, u32[]{:S(2)}, u32[]{:S(2)}) collective-permute-start(bf16[256,256]{1,0:T(8,128)(2,1)S(1)} %get-tuple-element.31), channel_id=1, source_target_pairs={{1,0},{2,1},{3,2},{5,4},{6,5},{7,6},{9,8},{10,9},{11,10},{13,12},{... | collective-permute-start | bytes 393224 | tf_op jit(solution)/shard_map/ppermute | solution.py:23
  18.4 1.5 %collective-permute-start.3 = (f32[8,128]{1,0:T(8,128)S(1)}, f32[8,128]{1,0:T(8,128)S(1)}, u32[]{:S(2)}, u32[]{:S(2)}) collective-permute-start(f32[8,128]{1,0:T(8,128)S(1)} %one_cross.1.after.refs_0_), channel_id=1, source_target_pairs={{0,2},{1,3},{2,0},{3,1},{4,6},{5,7},{6,4},{7,5},{8,10},{9,11},{10,... | collective-permute-start | bytes 12296 | tf_op jit(solution)/shard_map/ppermute | solution.py:37
  19.9 1.4 %collective-permute-start.2 = (f32[8,128]{1,0:T(8,128)S(1)}, f32[8,128]{1,0:T(8,128)S(1)}, u32[]{:S(2)}, u32[]{:S(2)}) collective-permute-start(f32[8,128]{1,0:T(8,128)S(1)} %one_cross.1.after.refs_0_), channel_id=1, source_target_pairs={{0,1},{1,0},{2,3},{3,2},{4,5},{5,4},{6,7},{7,6},{8,9},{9,8},{10,11... | collective-permute-start | bytes 12296 | tf_op jit(solution)/shard_map/ppermute | solution.py:37
  21.3 1.2 %one_raise.1.refs_6_ = f32[256,256]{1,0:T(8,128)S(1)} custom-call(bf16[16,256,256]{2,1,0:T(8,128)(2,1)S(1)} %bitcast.12, bf16[16,256,256]{2,1,0:T(8,128)(2,1)S(1)} %bitcast.17, bf16[256,256]{1,0:T(8,128)(2,1)S(1)} %collective-permute-done.1.below, f32[8,128]{1,0:T(8,128)S(1)} %one_cross.1.after.refs_0_), custom_call_target="tpu_custom_call" | custom-call | tf_op jit(solution)/shard_map/one_raise/pallas_call | solution.py:194
  22.6 0.9 %collective-permute-done.2.refs_1_ = f32[8,128]{1,0:T(8,128)S(1)} collective-permute-done((f32[8,128]{1,0:T(8,128)S(1)}, f32[8,128]{1,0:T(8,128)S(1)}, u32[]{:S(2)}, u32[]{:S(2)}) %collective-permute-start.2) | collective-permute-done | bytes 4128 | tf_op jit(solution)/shard_map/ppermute | solution.py:37
  23.7 3.3 %collective-permute-start.6 = (bf16[256,256]{1,0:T(8,128)(2,1)S(1)}, bf16[256,256]{1,0:T(8,128)(2,1)S(1)}, u32[]{:S(2)}, u32[]{:S(2)}) collective-permute-start(bf16[256,256]{1,0:T(8,128)(2,1)S(1)} %get-tuple-element.32.vector_b), channel_id=1, source_target_pairs={{0,1},{1,2},{2,3},{4,5},{5,6},{6,7},{8,9},{9,10},{10,11},{12,13},{... | collective-permute-start | bytes 393224 | tf_op jit(solution)/shard_map/ppermute | solution.py:23
  27.0 1.3 %two_lower.1 = (f32[256,256]{1,0:T(8,128)S(1)}, f32[256,256]{1,0:T(8,128)S(1)}, f32[8,128]{1,0:T(8,128)S(1)}, bf16[256,256]{1,0:T(8,128)(2,1)S(1)}) custom-call(bf16[16,256,256]{2,1,0:T(8,128)(2,1)S(1)} %bitcast.13, bf16[16,256,256]{2,1,0:T(8,128)(2,1)S(1)} %bitcast.18, bf16[256,256]{1,0:T(8,128)(2,1)S(1)} %get-tuple-element.32.vector_b, ...), custom_call_target="tpu_custom_call" | custom-call | tf_op jit(solution)/shard_map/two_lower/pallas_call | solution.py:194
  28.4 3.4 %collective-permute-start.10 = (bf16[256,256]{1,0:T(8,128)(2,1)S(1)}, bf16[256,256]{1,0:T(8,128)(2,1)S(1)}, u32[]{:S(2)}, u32[]{:S(2)}) collective-permute-start(bf16[256,256]{1,0:T(8,128)(2,1)S(1)} %get-tuple-element.38), channel_id=1, source_target_pairs={{1,0},{2,1},{3,2},{5,4},{6,5},{7,6},{9,8},{10,9},{11,10},{13,12},{... | collective-permute-start | bytes 393224 | tf_op jit(solution)/shard_map/ppermute | solution.py:23
  31.8 0.9 %collective-permute-done.6.below = bf16[256,256]{1,0:T(8,128)(2,1)S(1)} collective-permute-done((bf16[256,256]{1,0:T(8,128)(2,1)S(1)}, bf16[256,256]{1,0:T(8,128)(2,1)S(1)}, u32[]{:S(2)}, u32[]{:S(2)}) %collective-permute-start.6) | collective-permute-done | bytes 131104 | tf_op jit(solution)/shard_map/ppermute | solution.py:23
  32.8 1.2 %collective-permute-start.8 = (f32[8,128]{1,0:T(8,128)S(1)}, f32[8,128]{1,0:T(8,128)S(1)}, u32[]{:S(2)}, u32[]{:S(2)}) collective-permute-start(f32[8,128]{1,0:T(8,128)S(1)} %two_cross.1.after.refs_0_), channel_id=1, source_target_pairs={{0,2},{1,3},{2,0},{3,1},{4,6},{5,7},{6,4},{7,5},{8,10},{9,11},{10,... | collective-permute-start | bytes 12296 | tf_op jit(solution)/shard_map/ppermute | solution.py:37
  34.0 2.2 %collective-permute-start.7 = (f32[8,128]{1,0:T(8,128)S(1)}, f32[8,128]{1,0:T(8,128)S(1)}, u32[]{:S(2)}, u32[]{:S(2)}) collective-permute-start(f32[8,128]{1,0:T(8,128)S(1)} %two_cross.1.after.refs_0_), channel_id=1, source_target_pairs={{0,1},{1,0},{2,3},{3,2},{4,5},{5,4},{6,7},{7,6},{8,9},{9,8},{10,11... | collective-permute-start | bytes 12296 | tf_op jit(solution)/shard_map/ppermute | solution.py:37
  36.2 1.2 %two_raise.1.refs_8_ = f32[256,256]{1,0:T(8,128)S(1)} custom-call(bf16[16,256,256]{2,1,0:T(8,128)(2,1)S(1)} %bitcast.14, bf16[16,256,256]{2,1,0:T(8,128)(2,1)S(1)} %bitcast.19, bf16[256,256]{1,0:T(8,128)(2,1)S(1)} %collective-permute-done.6.below, f32[8,128]{1,0:T(8,128)S(1)} %two_cross.1.after.refs_0_), custom_call_target="tpu_custom_call" | custom-call | tf_op jit(solution)/shard_map/two_raise/pallas_call | solution.py:194
  38.2 4.0 %collective-permute-start.11 = (bf16[256,256]{1,0:T(8,128)(2,1)S(1)}, bf16[256,256]{1,0:T(8,128)(2,1)S(1)}, u32[]{:S(2)}, u32[]{:S(2)}) collective-permute-start(bf16[256,256]{1,0:T(8,128)(2,1)S(1)} %get-tuple-element.39.vector_b), channel_id=1, source_target_pairs={{0,1},{1,2},{2,3},{4,5},{5,6},{6,7},{8,9},{9,10},{10,11},{12,13},{... | collective-permute-start | bytes 393224 | tf_op jit(solution)/shard_map/ppermute | solution.py:23
  42.2 2.0 %three_lower.1 = (f32[256,256]{1,0:T(8,128)S(1)}, f32[256,256]{1,0:T(8,128)}, f32[8,128]{1,0:T(8,128)S(1)}) custom-call(bf16[16,256,256]{2,1,0:T(8,128)(2,1)S(1)} %bitcast.15, bf16[16,256,256]{2,1,0:T(8,128)(2,1)S(1)} %bitcast.20, bf16[256,256]{1,0:T(8,128)(2,1)S(1)} %get-tuple-element.39.vector_b, f32[256,256]{1,0:T(8,128)S(1)} %get-tuple-element.40.refs_0_.refs_4_, ...), custom_call_target="tpu_custom_call" | custom-call | tf_op jit(solution)/shard_map/three_lower/pallas_call | solution.py:194
  44.2 1.8 %collective-permute-done.11.below = bf16[256,256]{1,0:T(8,128)(2,1)S(1)} collective-permute-done((bf16[256,256]{1,0:T(8,128)(2,1)S(1)}, bf16[256,256]{1,0:T(8,128)(2,1)S(1)}, u32[]{:S(2)}, u32[]{:S(2)}) %collective-permute-start.11) | collective-permute-done | bytes 131104 | tf_op jit(solution)/shard_map/ppermute | solution.py:23
  46.0 0.7 %collective-permute-start.14 = (f32[8,128]{1,0:T(8,128)S(1)}, f32[8,128]{1,0:T(8,128)S(1)}, u32[]{:S(2)}, u32[]{:S(2)}) collective-permute-start(f32[8,128]{1,0:T(8,128)S(1)} %three_cross.1.refs_0_), channel_id=1, source_target_pairs={{0,3},{1,2},{2,1},{3,0},{4,7},{5,6},{6,5},{7,4},{8,11},{9,10},{10,... | collective-permute-start | bytes 12296 | tf_op jit(solution)/shard_map/ppermute | solution.py:37
  46.7 2.0 %collective-permute-start.13 = (f32[8,128]{1,0:T(8,128)S(1)}, f32[8,128]{1,0:T(8,128)S(1)}, u32[]{:S(2)}, u32[]{:S(2)}) collective-permute-start(f32[8,128]{1,0:T(8,128)S(1)} %three_cross.1.refs_0_), channel_id=1, source_target_pairs={{0,2},{1,3},{2,0},{3,1},{4,6},{5,7},{6,4},{7,5},{8,10},{9,11},{10,... | collective-permute-start | bytes 12296 | tf_op jit(solution)/shard_map/ppermute | solution.py:37
  48.7 0.9 %collective-permute-start.12 = (f32[8,128]{1,0:T(8,128)S(1)}, f32[8,128]{1,0:T(8,128)S(1)}, u32[]{:S(2)}, u32[]{:S(2)}) collective-permute-start(f32[8,128]{1,0:T(8,128)S(1)} %three_cross.1.refs_0_), channel_id=1, source_target_pairs={{0,1},{1,0},{2,3},{3,2},{4,5},{5,4},{6,7},{7,6},{8,9},{9,8},{10,11... | collective-permute-start | bytes 12296 | tf_op jit(solution)/shard_map/ppermute | solution.py:37
  49.6 1.0 %collective-permute-done.14.refs_3_ = f32[8,128]{1,0:T(8,128)S(1)} collective-permute-done((f32[8,128]{1,0:T(8,128)S(1)}, f32[8,128]{1,0:T(8,128)S(1)}, u32[]{:S(2)}, u32[]{:S(2)}) %collective-permute-start.14) | collective-permute-done | bytes 4128 | tf_op jit(solution)/shard_map/ppermute | solution.py:37
  50.6 1.7 %collective-permute-done.12.refs_1_ = f32[8,128]{1,0:T(8,128)S(1)} collective-permute-done((f32[8,128]{1,0:T(8,128)S(1)}, f32[8,128]{1,0:T(8,128)S(1)}, u32[]{:S(2)}, u32[]{:S(2)}) %collective-permute-start.12) | collective-permute-done | bytes 4128 | tf_op jit(solution)/shard_map/ppermute | solution.py:37
  52.3 2.8 %last.1 = (f32[1,1,256,256]{3,2,1,0:T(8,128)}, bf16[1,1,256,256]{3,2,1,0:T(8,128)(2,1)S(1)}, f32[1]{0:T(128)}) custom-call(f32[8,128]{1,0:T(8,128)S(1)} %three_cross.1.refs_0_, f32[8,128]{1,0:T(8,128)S(1)} %collective-permute-done.12.refs_1_, f32[8,128]{1,0:T(8,128)S(1)} %collective-permute-done.13.refs_2_, f32[8,128]{1,0:T(8,128)S(1)} %collective-permute-done.14.refs_3_, ...), custom_call_target="tpu_custom_call" | custom-call | tf_op jit(solution)/shard_map/last/pallas_call | solution.py:194
  55.1 1.9 %collective-permute-start.15 = (bf16[1,1,256,256]{3,2,1,0:T(8,128)(2,1)S(1)}, bf16[1,1,256,256]{3,2,1,0:T(8,128)(2,1)S(1)}, u32[]{:S(2)}, u32[]{:S(2)}) collective-permute-start(bf16[1,1,256,256]{3,2,1,0:T(8,128)(2,1)S(1)} %get-tuple-element.47), channel_id=1, source_target_pairs={{0,4},{4,8},{8,12},{12,16},{16,20},{20,24},{24,28},{1,5},{5,9},{9,... | collective-permute-start | bytes 393224 | tf_op jit(solution)/shard_map/ppermute | solution.py:23
  57.0 4.4 %collective-permute-done.15 = bf16[1,1,256,256]{3,2,1,0:T(8,128)(2,1)S(1)} collective-permute-done((bf16[1,1,256,256]{3,2,1,0:T(8,128)(2,1)S(1)}, bf16[1,1,256,256]{3,2,1,0:T(8,128)(2,1)S(1)}, u32[]{:S(2)}, u32[]{:S(2)}) %collective-permute-start.15) | collective-permute-done | bytes 131104 | tf_op jit(solution)/shard_map/ppermute | solution.py:23
  61.4 0.7 %copy.13 = bf16[1,1,256,256]{3,2,1,0:T(8,128)(2,1)} copy(bf16[1,1,256,256]{3,2,1,0:T(8,128)(2,1)S(1)} %collective-permute-done.15) | data formatting | bytes 262144
  (28 shorter events, 2.1 us)
Async XLA Ops:
  0.6 4.7 %collective-permute-start = (bf16[256,256]{1,0:T(8,128)(2,1)}, bf16[256,256]{1,0:T(8,128)(2,1)S(1)}, u32[]{:S(2)}, u32[]{:S(2)}) collective-permute-start(bf16[256,256]{1,0:T(8,128)(2,1)} %bitcast.25), channel_id=1, source_target_pairs={{4,0},{8,4},{12,8},{16,12},{20,16},{24,20},{28,24},{5,1},{9,5},{13... | collective-permute-start | bytes 393224 | tf_op jit(solution)/shard_map/ppermute | solution.py:23
  5.4 0.9 %copy-start.5 = (bf16[1,1,256,256]{3,2,1,0:T(8,128)(2,1)S(1)}, bf16[1,1,256,256]{3,2,1,0:T(8,128)(2,1)}, u32[]{:S(2)}) copy-start(bf16[1,1,256,256]{3,2,1,0:T(8,128)(2,1)} %param.12) | copy-start | bytes 393220
  6.5 11.2 %collective-permute-start.1 = (bf16[256,256]{1,0:T(8,128)(2,1)S(1)}, bf16[256,256]{1,0:T(8,128)(2,1)S(1)}, u32[]{:S(2)}, u32[]{:S(2)}) collective-permute-start(bf16[256,256]{1,0:T(8,128)(2,1)S(1)} %get-tuple-element.26.vector_b), channel_id=1, source_target_pairs={{0,1},{1,2},{2,3},{4,5},{5,6},{6,7},{8,9},{9,10},{10,11},{12,13},{... | collective-permute-start | bytes 393224 | tf_op jit(solution)/shard_map/ppermute | solution.py:23
  9.9 1.6 %copy-start = (bf16[1,1,16,256,256]{4,3,2,1,0:T(8,128)(2,1)S(1)}, bf16[1,1,16,256,256]{4,3,2,1,0:T(8,128)(2,1)}, u32[]{:S(2)}) copy-start(bf16[1,1,16,256,256]{4,3,2,1,0:T(8,128)(2,1)} %param.8) | copy-start | bytes 6291460
  11.5 1.6 %copy-start.2 = (bf16[1,1,16,256,256]{4,3,2,1,0:T(8,128)(2,1)S(1)}, bf16[1,1,16,256,256]{4,3,2,1,0:T(8,128)(2,1)}, u32[]{:S(2)}) copy-start(bf16[1,1,16,256,256]{4,3,2,1,0:T(8,128)(2,1)} %param.9) | copy-start | bytes 6291460
  13.1 8.3 %copy-start.1 = (bf16[1,1,16,256,256]{4,3,2,1,0:T(8,128)(2,1)S(1)}, bf16[1,1,16,256,256]{4,3,2,1,0:T(8,128)(2,1)}, u32[]{:S(2)}) copy-start(bf16[1,1,16,256,256]{4,3,2,1,0:T(8,128)(2,1)} %param.8) | copy-start | bytes 6291460
  13.1 8.3 %copy-start.3 = (bf16[1,1,16,256,256]{4,3,2,1,0:T(8,128)(2,1)S(1)}, bf16[1,1,16,256,256]{4,3,2,1,0:T(8,128)(2,1)}, u32[]{:S(2)}) copy-start(bf16[1,1,16,256,256]{4,3,2,1,0:T(8,128)(2,1)} %param.9) | copy-start | bytes 6291460
  14.4 8.2 %collective-permute-start.5 = (bf16[256,256]{1,0:T(8,128)(2,1)S(1)}, bf16[256,256]{1,0:T(8,128)(2,1)S(1)}, u32[]{:S(2)}, u32[]{:S(2)}) collective-permute-start(bf16[256,256]{1,0:T(8,128)(2,1)S(1)} %get-tuple-element.31), channel_id=1, source_target_pairs={{1,0},{2,1},{3,2},{5,4},{6,5},{7,6},{9,8},{10,9},{11,10},{13,12},{... | collective-permute-start | bytes 393224 | tf_op jit(solution)/shard_map/ppermute | solution.py:23
  17.8 5.7 %copy-start.4 = (bf16[1,1,256,256]{3,2,1,0:T(8,128)(2,1)S(1)}, bf16[1,1,256,256]{3,2,1,0:T(8,128)(2,1)}, u32[]{:S(2)}) copy-start(bf16[1,1,256,256]{3,2,1,0:T(8,128)(2,1)} %param.14) | copy-start | bytes 393220
  17.8 4.8 %collective-permute-start.4 = (f32[8,128]{1,0:T(8,128)S(1)}, f32[8,128]{1,0:T(8,128)S(1)}, u32[]{:S(2)}, u32[]{:S(2)}) collective-permute-start(f32[8,128]{1,0:T(8,128)S(1)} %one_cross.1.after.refs_0_), channel_id=1, source_target_pairs={{0,3},{1,2},{2,1},{3,0},{4,7},{5,6},{6,5},{7,4},{8,11},{9,10},{10,... | collective-permute-start | bytes 12296 | tf_op jit(solution)/shard_map/ppermute | solution.py:37
  18.4 4.2 %collective-permute-start.3 = (f32[8,128]{1,0:T(8,128)S(1)}, f32[8,128]{1,0:T(8,128)S(1)}, u32[]{:S(2)}, u32[]{:S(2)}) collective-permute-start(f32[8,128]{1,0:T(8,128)S(1)} %one_cross.1.after.refs_0_), channel_id=1, source_target_pairs={{0,2},{1,3},{2,0},{3,1},{4,6},{5,7},{6,4},{7,5},{8,10},{9,11},{10,... | collective-permute-start | bytes 12296 | tf_op jit(solution)/shard_map/ppermute | solution.py:37
  19.9 3.6 %collective-permute-start.2 = (f32[8,128]{1,0:T(8,128)S(1)}, f32[8,128]{1,0:T(8,128)S(1)}, u32[]{:S(2)}, u32[]{:S(2)}) collective-permute-start(f32[8,128]{1,0:T(8,128)S(1)} %one_cross.1.after.refs_0_), channel_id=1, source_target_pairs={{0,1},{1,0},{2,3},{3,2},{4,5},{5,4},{6,7},{7,6},{8,9},{9,8},{10,11... | collective-permute-start | bytes 12296 | tf_op jit(solution)/shard_map/ppermute | solution.py:37
  23.7 9.0 %collective-permute-start.6 = (bf16[256,256]{1,0:T(8,128)(2,1)S(1)}, bf16[256,256]{1,0:T(8,128)(2,1)S(1)}, u32[]{:S(2)}, u32[]{:S(2)}) collective-permute-start(bf16[256,256]{1,0:T(8,128)(2,1)S(1)} %get-tuple-element.32.vector_b), channel_id=1, source_target_pairs={{0,1},{1,2},{2,3},{4,5},{5,6},{6,7},{8,9},{9,10},{10,11},{12,13},{... | collective-permute-start | bytes 393224 | tf_op jit(solution)/shard_map/ppermute | solution.py:23
  28.4 9.1 %collective-permute-start.10 = (bf16[256,256]{1,0:T(8,128)(2,1)S(1)}, bf16[256,256]{1,0:T(8,128)(2,1)S(1)}, u32[]{:S(2)}, u32[]{:S(2)}) collective-permute-start(bf16[256,256]{1,0:T(8,128)(2,1)S(1)} %get-tuple-element.38), channel_id=1, source_target_pairs={{1,0},{2,1},{3,2},{5,4},{6,5},{7,6},{9,8},{10,9},{11,10},{13,12},{... | collective-permute-start | bytes 393224 | tf_op jit(solution)/shard_map/ppermute | solution.py:23
  32.7 4.8 %collective-permute-start.9 = (f32[8,128]{1,0:T(8,128)S(1)}, f32[8,128]{1,0:T(8,128)S(1)}, u32[]{:S(2)}, u32[]{:S(2)}) collective-permute-start(f32[8,128]{1,0:T(8,128)S(1)} %two_cross.1.after.refs_0_), channel_id=1, source_target_pairs={{0,3},{1,2},{2,1},{3,0},{4,7},{5,6},{6,5},{7,4},{8,11},{9,10},{10,... | collective-permute-start | bytes 12296 | tf_op jit(solution)/shard_map/ppermute | solution.py:37
  32.8 4.7 %collective-permute-start.8 = (f32[8,128]{1,0:T(8,128)S(1)}, f32[8,128]{1,0:T(8,128)S(1)}, u32[]{:S(2)}, u32[]{:S(2)}) collective-permute-start(f32[8,128]{1,0:T(8,128)S(1)} %two_cross.1.after.refs_0_), channel_id=1, source_target_pairs={{0,2},{1,3},{2,0},{3,1},{4,6},{5,7},{6,4},{7,5},{8,10},{9,11},{10,... | collective-permute-start | bytes 12296 | tf_op jit(solution)/shard_map/ppermute | solution.py:37
  34.0 3.8 %collective-permute-start.7 = (f32[8,128]{1,0:T(8,128)S(1)}, f32[8,128]{1,0:T(8,128)S(1)}, u32[]{:S(2)}, u32[]{:S(2)}) collective-permute-start(f32[8,128]{1,0:T(8,128)S(1)} %two_cross.1.after.refs_0_), channel_id=1, source_target_pairs={{0,1},{1,0},{2,3},{3,2},{4,5},{5,4},{6,7},{7,6},{8,9},{9,8},{10,11... | collective-permute-start | bytes 12296 | tf_op jit(solution)/shard_map/ppermute | solution.py:37
  38.2 7.8 %collective-permute-start.11 = (bf16[256,256]{1,0:T(8,128)(2,1)S(1)}, bf16[256,256]{1,0:T(8,128)(2,1)S(1)}, u32[]{:S(2)}, u32[]{:S(2)}) collective-permute-start(bf16[256,256]{1,0:T(8,128)(2,1)S(1)} %get-tuple-element.39.vector_b), channel_id=1, source_target_pairs={{0,1},{1,2},{2,3},{4,5},{5,6},{6,7},{8,9},{9,10},{10,11},{12,13},{... | collective-permute-start | bytes 393224 | tf_op jit(solution)/shard_map/ppermute | solution.py:23
  46.0 4.6 %collective-permute-start.14 = (f32[8,128]{1,0:T(8,128)S(1)}, f32[8,128]{1,0:T(8,128)S(1)}, u32[]{:S(2)}, u32[]{:S(2)}) collective-permute-start(f32[8,128]{1,0:T(8,128)S(1)} %three_cross.1.refs_0_), channel_id=1, source_target_pairs={{0,3},{1,2},{2,1},{3,0},{4,7},{5,6},{6,5},{7,4},{8,11},{9,10},{10,... | collective-permute-start | bytes 12296 | tf_op jit(solution)/shard_map/ppermute | solution.py:37
  46.7 3.9 %collective-permute-start.13 = (f32[8,128]{1,0:T(8,128)S(1)}, f32[8,128]{1,0:T(8,128)S(1)}, u32[]{:S(2)}, u32[]{:S(2)}) collective-permute-start(f32[8,128]{1,0:T(8,128)S(1)} %three_cross.1.refs_0_), channel_id=1, source_target_pairs={{0,2},{1,3},{2,0},{3,1},{4,6},{5,7},{6,4},{7,5},{8,10},{9,11},{10,... | collective-permute-start | bytes 12296 | tf_op jit(solution)/shard_map/ppermute | solution.py:37
  48.7 3.6 %collective-permute-start.12 = (f32[8,128]{1,0:T(8,128)S(1)}, f32[8,128]{1,0:T(8,128)S(1)}, u32[]{:S(2)}, u32[]{:S(2)}) collective-permute-start(f32[8,128]{1,0:T(8,128)S(1)} %three_cross.1.refs_0_), channel_id=1, source_target_pairs={{0,1},{1,0},{2,3},{3,2},{4,5},{5,4},{6,7},{7,6},{8,9},{9,8},{10,11... | collective-permute-start | bytes 12296 | tf_op jit(solution)/shard_map/ppermute | solution.py:37
  55.1 6.3 %collective-permute-start.15 = (bf16[1,1,256,256]{3,2,1,0:T(8,128)(2,1)S(1)}, bf16[1,1,256,256]{3,2,1,0:T(8,128)(2,1)S(1)}, u32[]{:S(2)}, u32[]{:S(2)}) collective-permute-start(bf16[1,1,256,256]{3,2,1,0:T(8,128)(2,1)S(1)} %get-tuple-element.47), channel_id=1, source_target_pairs={{0,4},{4,8},{8,12},{12,16},{16,20},{20,24},{24,28},{1,5},{5,9},{9,... | collective-permute-start | bytes 393224 | tf_op jit(solution)/shard_map/ppermute | solution.py:23

commit v2 on v1

--- a/solution.py
+++ b/solution.py
@@ -15,12 +15,27 @@
 BF16 = jnp.bfloat16
 VMEM = pl.BlockSpec(memory_space=pltpu.VMEM)
 SMEM = pl.BlockSpec(memory_space=pltpu.SMEM)
+COVER = pl.CostEstimate(flops=10**10, bytes_accessed=1 << 24, transcendentals=0)
 
 
 def shift(value, axis, steps):
     count = lax.axis_size(axis)
     first, last = max(0, -steps), min(count, count - steps)
     return lax.ppermute(value, axis, [(source, source + steps) for source in range(first, last)])
+
+
+def rotate(value, axis, steps):
+    count = lax.axis_size(axis)
+    return lax.ppermute(value, axis, [(source, (source + steps) % count) for source in range(count)])
+
+
+def from_below(value):
+    return jnp.where(lax.axis_index("sec") > 0, value, jnp.zeros_like(value))
+
+
+def from_above(value):
+    last = lax.axis_size("sec") - 1
+    return jnp.where(lax.axis_index("sec") < last, value, jnp.zeros_like(value))
 
 
 def exchange(value, axis):
@@ -66,6 +81,14 @@
         inner[:, w * size : (w + 1) * size] = product.astype(BF16)
     stacked = right[first:last].reshape((last - first) * size, size)
     return jnp.dot(inner[:, first * size : last * size], stacked, preferred_element_type=F32)
+
+
+def mask_kernel(rows, mask_out):
+    count = rows[0]
+    shape = mask_out.shape
+    idx_r = lax.broadcasted_iota(jnp.int32, shape, 0)
+    idx_c = lax.broadcasted_iota(jnp.int32, shape, 1)
+    mask_out[...] = jnp.where((idx_r < count) & (idx_c < count), 1.0, 0.0)
 
 
 def start_kernel(scaled, behind, guess, mask, y_ref, yb_ref):
@@ -96,18 +119,19 @@
 
 def cross_kernel(row, below, low, stat, out):
     out[...] = stat[...]
-    out[row : row + 1] = stat[row : row + 1] + 2.0 * fold(below[...].astype(F32) * low[...])
+    crossed = fold(from_below(below[...]).astype(F32) * low[...])
+    out[row : row + 1] = stat[row : row + 1] + 2.0 * crossed
 
 
 def raise_kernel(left, right, below, after, up_ref, inner):
-    up_ref[...] = sandwich(left, right, below[...], inner, WD, left.shape[0])
+    up_ref[...] = from_below(sandwich(left, right, below[...], inner, WD, left.shape[0]))
 
 
 def first_kernel(parts, *refs):
     y_ref, diag, up, above, mask, prec = refs[parts : parts + 6]
     g_ref, p_ref, pb_ref = refs[parts + 6 :]
     yy, yhy = scalars(refs[:parts], 2)
-    g = mask[...] * (diag[...] + up[...] + above[...].astype(F32))
+    g = mask[...] * (diag[...] + up[...] + from_above(above[...].astype(F32)))
     g_ref[...] = g
     p = prec[...].astype(F32) * (g - (yhy / yy) * y_ref[...])
     p_ref[...] = p
@@ -133,7 +157,7 @@
     lam, u, w = ritz(a, b, c)
     along_p = w / jnp.sqrt(qq)
     along_y = u / jnp.sqrt(yy) - along_p * s
-    hp = mask[...] * (diag[...] + up[...] + above[...].astype(F32))
+    hp = mask[...] * (diag[...] + up[...] + from_above(above[...].astype(F32)))
     x = along_y * y_ref[...] + along_p * p_ref[...]
     g = along_y * g_ref[...] + along_p * hp
     p = prec[...].astype(F32) * (g - lam * x)
@@ -144,16 +168,21 @@
     lam_out[...] = jnp.broadcast_to(lam, lam_out.shape)
 
 
+def dot(one, two, over):
+    dims = ((over[:1], over[1:]), ((), ()))
+    return lax.dot_general(one, two, dims, preferred_element_type=F32)
+
+
 def split(value):
     high = value.astype(BF16)
     return high, (value - high.astype(F32)).astype(BF16)
 
 
 def product(one, two, over):
-    dims = ((over[:1], over[1:]), ((), ()))
-    dot = functools.partial(lax.dot_general, dimension_numbers=dims, preferred_element_type=F32)
-    (one_high, one_low), (two_high, two_low) = one, two
-    return dot(one_high, two_high) + (dot(one_high, two_low) + dot(one_low, two_high))
+    (one_high, one_low), (two_high, two_low) = split(one), split(two)
+    return dot(one_high, two_high, over) + (
+        dot(one_high, two_low, over) + dot(one_low, two_high, over)
+    )
 
 
 def last_kernel(parts, *refs):
@@ -172,52 +201,51 @@
     frob = jnp.sum(jnp.sum(x * x, axis=0, keepdims=True), axis=1, keepdims=True)
     polar = x * lax.rsqrt(frob + 1e-06)
     for _ in range(NS_STEPS):
-        halves = split(polar)
-        gram = product(halves, halves, (1, 1))
-        polar = 1.5 * polar - 0.5 * product(split(gram), halves, (1, 0))
+        narrow = polar.astype(BF16)
+        gram = dot(narrow, narrow, (1, 1)).astype(BF16)
+        polar = 1.5 * polar - 0.5 * dot(gram, narrow, (1, 0))
     polar_out[0, 0] = polar
-    weight_out[0, 0] = product(split(polar), split(x), (0, 0)).astype(BF16)
+    weight_out[0, 0] = product(polar, x, (0, 0)).astype(BF16)
 
 
 def shards(
     left_env, right_env, left_piece, right_piece, guess, inverse_values, precond, sector_rows
 ):
-    left, right = left_env[0, 0], right_env[0, 0]
+    left, right, prec = left_env[0, 0], right_env[0, 0], precond[0, 0]
     channels, size = left.shape[0], left.shape[-1]
-    count = sector_rows[0, 0]
     matrix = jax.ShapeDtypeStruct((size, size), F32)
     narrow = jax.ShapeDtypeStruct((size, size), BF16)
     stats = jax.ShapeDtypeStruct((ROWS, LANES), F32)
     inner = pltpu.VMEM((size, channels * size), BF16)
 
-    def call(kernel, name, outs, *operands, scratch=(), out_specs=None):
+    def call(kernel, name, outs, *operands, scratch=(), in_specs=None, out_specs=None, cost=None, limit=16 << 20):
         return pl.pallas_call(
             kernel,
             name=name,
             out_shape=outs,
-            in_specs=[VMEM] * len(operands),
+            in_specs=in_specs or [VMEM] * len(operands),
             out_specs=out_specs or [VMEM] * len(outs),
             scratch_shapes=list(scratch),
-            compiler_params=pltpu.CompilerParams(vmem_limit_bytes=16 << 20),
+            cost_estimate=cost,
+            compiler_params=pltpu.CompilerParams(vmem_limit_bytes=limit),
         )(*operands)
 
     behind = shift(right_piece[0, 0], "seg", -1)
-    idx_r = lax.broadcasted_iota(jnp.int32, (size, size), 0)
-    idx_c = lax.broadcasted_iota(jnp.int32, (size, size), 1)
-    mask = ((idx_r < count) & (idx_c < count)).astype(F32)
-    scaled = (left_piece[0, 0].astype(F32) * inverse_values[0, 0][None, :]).astype(BF16)
-    prec = precond[0, 0]
+    (mask,) = call(
+        mask_kernel, "mask", [matrix], sector_rows[0], in_specs=[SMEM], cost=COVER
+    )
+    scaled = (left_piece[0, 0].astype(F32) * inverse_values[0]).astype(BF16)
 
     y, yb = call(start_kernel, "start", [matrix, narrow], scaled, behind, guess[0, 0], mask)
 
     def half(name, vector_b, pairs, operands, row, sends):
-        below = shift(vector_b, "sec", 1)
+        below = rotate(vector_b, "sec", 1)
         outs = [matrix, matrix, stats] + [narrow] * sends
         kernel = functools.partial(lower_kernel, pairs, sends)
         low, diag, stat, *sent = call(
             kernel, name + "_lower", outs, left, right, vector_b, *operands, scratch=[inner]
         )
-        above = shift(sent[0], "sec", -1) if sends else None
+        above = rotate(sent[0], "sec", -1) if sends else None
         (stat,) = call(functools.partial(cross_kernel, row), name + "_cross", [stats], below, low, stat)
         return below, diag, above, stat
 

time: 62.4 us -> 52.3 us (0.84)
  the two profiles are of different devices: /device:TPU:28 before, /device:TPU:1 now
where the time goes in v2:
time: 52.3 us; the launch traced here: 51.9 us
  starting transfers between devices  25.7 us (49%)
  waiting for transfers between devices  13.2 us (25%)
  Pallas kernels  9.95 us (19%)
  local copies, waits for them, and re-layouts  1.5 us (3%)
  between operations  1.45 us (3%)
    ppermute x2, starting transfers between devices, shift(): lax.ppermute(value, axis, [(source, source + steps) for source in range(f...  11.2 us
    pallas_call x13, Pallas kernels, call(): pl.pallas_call(kernel, name=name, out_shape=outs, in_specs=in_specs or [V...  9.95 us
    ppermute x9, starting transfers between devices, exchange(): parts.append(lax.ppermute(parts[0], axis, pairs))  8.71 us
    ppermute x2, waiting for transfers between devices, shift(): lax.ppermute(value, axis, [(source, source + steps) for source in range(f...  5.85 us
    ppermute x5, starting transfers between devices, rotate(): lax.ppermute(value, axis, [(source, (source + steps) % count) for source...  5.76 us
    ppermute x5, waiting for transfers between devices, rotate(): lax.ppermute(value, axis, [(source, (source + steps) % count) for source...  5.76 us
    ppermute x9, waiting for transfers between devices, exchange(): parts.append(lax.ppermute(parts[0], axis, pairs))  1.61 us
    unnamed x13, local copies, waits for them, and re-layouts  1.5 us
  transfers between devices with their start and end apart: 16, of which 11 were waited for; matrix products, arithmetic and copies ran while one was open for 0% of the time, Pallas kernels for 14%

profile of v2, /device:TPU:1, one launch (start us, length us, event | category | flops | bytes accessed | tf_op | source)
XLA Modules:
  0.0 51.9 jit_solution(11110831088808413765)
XLA Ops:
  0.6 1.9 %collective-permute-start = (bf16[256,256]{1,0:T(8,128)(2,1)}, bf16[256,256]{1,0:T(8,128)(2,1)S(1)}, u32[]{:S(2)}, u32[]{:S(2)}) collective-permute-start(bf16[256,256]{1,0:T(8,128)(2,1)} %bitcast.25), channel_id=1, source_target_pairs={{4,0},{8,4},{12,8},{16,12},{20,16},{24,20},{28,24},{5,1},{9,5},{13... | collective-permute-start | bytes 393224 | tf_op jit(solution)/shard_map/ppermute | solution.py:24
  3.3 0.8 %copy-done.4 = bf16[1,1,256,256]{3,2,1,0:T(8,128)(2,1)S(1)} copy-done((bf16[1,1,256,256]{3,2,1,0:T(8,128)(2,1)S(1)}, bf16[1,1,256,256]{3,2,1,0:T(8,128)(2,1)}, u32[]{:S(2)}) %copy-start.4) | copy-done | bytes 131096
  4.1 3.9 %collective-permute-done.behind = bf16[256,256]{1,0:T(8,128)(2,1)S(1)} collective-permute-done((bf16[256,256]{1,0:T(8,128)(2,1)}, bf16[256,256]{1,0:T(8,128)(2,1)S(1)}, u32[]{:S(2)}, u32[]{:S(2)}) %collective-permute-start) | collective-permute-done | bytes 131104 | tf_op jit(solution)/shard_map/ppermute | solution.py:24
  8.3 1.3 %collective-permute-start.1 = (bf16[256,256]{1,0:T(8,128)(2,1)S(1)}, bf16[256,256]{1,0:T(8,128)(2,1)S(1)}, u32[]{:S(2)}, u32[]{:S(2)}) collective-permute-start(bf16[256,256]{1,0:T(8,128)(2,1)S(1)} %get-tuple-element.26.vector_b), channel_id=1, source_target_pairs={{0,1},{1,2},{2,3},{3,0},{4,5},{5,6},{6,7},{7,4},{8,9},{9,10},{10,1... | collective-permute-start | bytes 393224 | tf_op jit(solution)/shard_map/ppermute | solution.py:29
  9.5 1.3 %one_lower.1 = (f32[256,256]{1,0:T(8,128)S(1)}, f32[256,256]{1,0:T(8,128)S(1)}, f32[8,128]{1,0:T(8,128)S(1)}, bf16[256,256]{1,0:T(8,128)(2,1)S(1)}) custom-call(bf16[16,256,256]{2,1,0:T(8,128)(2,1)S(1)} %bitcast.11, bf16[16,256,256]{2,1,0:T(8,128)(2,1)S(1)} %bitcast.16, bf16[256,256]{1,0:T(8,128)(2,1)S(1)} %get-tuple-element.26.vector_b, ...), custom_call_target="tpu_custom_call" | custom-call | tf_op jit(solution)/shard_map/one_lower/pallas_call | solution.py:222
  10.8 1.2 %collective-permute-start.5 = (bf16[256,256]{1,0:T(8,128)(2,1)S(1)}, bf16[256,256]{1,0:T(8,128)(2,1)S(1)}, u32[]{:S(2)}, u32[]{:S(2)}) collective-permute-start(bf16[256,256]{1,0:T(8,128)(2,1)S(1)} %get-tuple-element.31), channel_id=1, source_target_pairs={{0,3},{1,0},{2,1},{3,2},{4,7},{5,4},{6,5},{7,6},{8,11},{9,8},{10,9... | collective-permute-start | bytes 393224 | tf_op jit(solution)/shard_map/ppermute | solution.py:29
  12.0 1.6 %collective-permute-done.1.below = bf16[256,256]{1,0:T(8,128)(2,1)S(1)} collective-permute-done((bf16[256,256]{1,0:T(8,128)(2,1)S(1)}, bf16[256,256]{1,0:T(8,128)(2,1)S(1)}, u32[]{:S(2)}, u32[]{:S(2)}) %collective-permute-start.1) | collective-permute-done | bytes 131104 | tf_op jit(solution)/shard_map/ppermute | solution.py:29
  13.7 1.7 %collective-permute-start.4 = (f32[8,128]{1,0:T(8,128)S(1)}, f32[8,128]{1,0:T(8,128)S(1)}, u32[]{:S(2)}, u32[]{:S(2)}) collective-permute-start(f32[8,128]{1,0:T(8,128)S(1)} %one_cross.1.after.refs_0_), channel_id=1, source_target_pairs={{0,3},{1,2},{2,1},{3,0},{4,7},{5,6},{6,5},{7,4},{8,11},{9,10},{10,... | collective-permute-start | bytes 12296 | tf_op jit(solution)/shard_map/ppermute | solution.py:52
  15.4 0.3 collective-permute-start.3
  15.7 1.1 %collective-permute-start.2 = (f32[8,128]{1,0:T(8,128)S(1)}, f32[8,128]{1,0:T(8,128)S(1)}, u32[]{:S(2)}, u32[]{:S(2)}) collective-permute-start(f32[8,128]{1,0:T(8,128)S(1)} %one_cross.1.after.refs_0_), channel_id=1, source_target_pairs={{0,1},{1,0},{2,3},{3,2},{4,5},{5,4},{6,7},{7,6},{8,9},{9,8},{10,11... | collective-permute-start | bytes 12296 | tf_op jit(solution)/shard_map/ppermute | solution.py:52
  16.8 1.2 %one_raise.1.refs_6_ = f32[256,256]{1,0:T(8,128)S(1)} custom-call(bf16[16,256,256]{2,1,0:T(8,128)(2,1)S(1)} %bitcast.12, bf16[16,256,256]{2,1,0:T(8,128)(2,1)S(1)} %bitcast.17, bf16[256,256]{1,0:T(8,128)(2,1)S(1)} %collective-permute-done.1.below, f32[8,128]{1,0:T(8,128)S(1)} %one_cross.1.after.refs_0_), custom_call_target="tpu_custom_call" | custom-call | tf_op jit(solution)/shard_map/one_raise/pallas_call | solution.py:222
  18.4 1.2 %collective-permute-start.6 = (bf16[256,256]{1,0:T(8,128)(2,1)S(1)}, bf16[256,256]{1,0:T(8,128)(2,1)S(1)}, u32[]{:S(2)}, u32[]{:S(2)}) collective-permute-start(bf16[256,256]{1,0:T(8,128)(2,1)S(1)} %get-tuple-element.32.vector_b), channel_id=1, source_target_pairs={{0,1},{1,2},{2,3},{3,0},{4,5},{5,6},{6,7},{7,4},{8,9},{9,10},{10,1... | collective-permute-start | bytes 393224 | tf_op jit(solution)/shard_map/ppermute | solution.py:29
  19.5 1.3 %two_lower.1 = (f32[256,256]{1,0:T(8,128)S(1)}, f32[256,256]{1,0:T(8,128)S(1)}, f32[8,128]{1,0:T(8,128)S(1)}, bf16[256,256]{1,0:T(8,128)(2,1)S(1)}) custom-call(bf16[16,256,256]{2,1,0:T(8,128)(2,1)S(1)} %bitcast.13, bf16[16,256,256]{2,1,0:T(8,128)(2,1)S(1)} %bitcast.18, bf16[256,256]{1,0:T(8,128)(2,1)S(1)} %get-tuple-element.32.vector_b, ...), custom_call_target="tpu_custom_call" | custom-call | tf_op jit(solution)/shard_map/two_lower/pallas_call | solution.py:222
  20.9 1.3 %collective-permute-start.10 = (bf16[256,256]{1,0:T(8,128)(2,1)S(1)}, bf16[256,256]{1,0:T(8,128)(2,1)S(1)}, u32[]{:S(2)}, u32[]{:S(2)}) collective-permute-start(bf16[256,256]{1,0:T(8,128)(2,1)S(1)} %get-tuple-element.38), channel_id=1, source_target_pairs={{0,3},{1,0},{2,1},{3,2},{4,7},{5,4},{6,5},{7,6},{8,11},{9,8},{10,9... | collective-permute-start | bytes 393224 | tf_op jit(solution)/shard_map/ppermute | solution.py:29
  22.2 2.2 %collective-permute-done.6.below = bf16[256,256]{1,0:T(8,128)(2,1)S(1)} collective-permute-done((bf16[256,256]{1,0:T(8,128)(2,1)S(1)}, bf16[256,256]{1,0:T(8,128)(2,1)S(1)}, u32[]{:S(2)}, u32[]{:S(2)}) %collective-permute-start.6) | collective-permute-done | bytes 131104 | tf_op jit(solution)/shard_map/ppermute | solution.py:29
  24.4 1.5 %collective-permute-start.9 = (f32[8,128]{1,0:T(8,128)S(1)}, f32[8,128]{1,0:T(8,128)S(1)}, u32[]{:S(2)}, u32[]{:S(2)}) collective-permute-start(f32[8,128]{1,0:T(8,128)S(1)} %two_cross.1.after.refs_0_), channel_id=1, source_target_pairs={{0,3},{1,2},{2,1},{3,0},{4,7},{5,6},{6,5},{7,4},{8,11},{9,10},{10,... | collective-permute-start | bytes 12296 | tf_op jit(solution)/shard_map/ppermute | solution.py:52
  26.1 1.1 %collective-permute-start.7 = (f32[8,128]{1,0:T(8,128)S(1)}, f32[8,128]{1,0:T(8,128)S(1)}, u32[]{:S(2)}, u32[]{:S(2)}) collective-permute-start(f32[8,128]{1,0:T(8,128)S(1)} %two_cross.1.after.refs_0_), channel_id=1, source_target_pairs={{0,1},{1,0},{2,3},{3,2},{4,5},{5,4},{6,7},{7,6},{8,9},{9,8},{10,11... | collective-permute-start | bytes 12296 | tf_op jit(solution)/shard_map/ppermute | solution.py:52
  27.2 1.2 %two_raise.1.refs_8_ = f32[256,256]{1,0:T(8,128)S(1)} custom-call(bf16[16,256,256]{2,1,0:T(8,128)(2,1)S(1)} %bitcast.14, bf16[16,256,256]{2,1,0:T(8,128)(2,1)S(1)} %bitcast.19, bf16[256,256]{1,0:T(8,128)(2,1)S(1)} %collective-permute-done.6.below, f32[8,128]{1,0:T(8,128)S(1)} %two_cross.1.after.refs_0_), custom_call_target="tpu_custom_call" | custom-call | tf_op jit(solution)/shard_map/two_raise/pallas_call | solution.py:222
  28.7 0.2 collective-permute-done.7.refs_1_
  28.9 0.4 second.1
  29.3 0.8 %collective-permute-start.11 = (bf16[256,256]{1,0:T(8,128)(2,1)S(1)}, bf16[256,256]{1,0:T(8,128)(2,1)S(1)}, u32[]{:S(2)}, u32[]{:S(2)}) collective-permute-start(bf16[256,256]{1,0:T(8,128)(2,1)S(1)} %get-tuple-element.39.vector_b), channel_id=1, source_target_pairs={{0,1},{1,2},{2,3},{3,0},{4,5},{5,6},{6,7},{7,4},{8,9},{9,10},{10,1... | collective-permute-start | bytes 393224 | tf_op jit(solution)/shard_map/ppermute | solution.py:29
  30.2 2.0 %three_lower.1 = (f32[256,256]{1,0:T(8,128)S(1)}, f32[256,256]{1,0:T(8,128)}, f32[8,128]{1,0:T(8,128)S(1)}) custom-call(bf16[16,256,256]{2,1,0:T(8,128)(2,1)S(1)} %bitcast.15, bf16[16,256,256]{2,1,0:T(8,128)(2,1)S(1)} %bitcast.20, bf16[256,256]{1,0:T(8,128)(2,1)S(1)} %get-tuple-element.39.vector_b, f32[256,256]{1,0:T(8,128)S(1)} %get-tuple-element.40.refs_0_.refs_4_, ...), custom_call_target="tpu_custom_call" | custom-call | tf_op jit(solution)/shard_map/three_lower/pallas_call | solution.py:222
  32.1 2.0 %collective-permute-done.11.below = bf16[256,256]{1,0:T(8,128)(2,1)S(1)} collective-permute-done((bf16[256,256]{1,0:T(8,128)(2,1)S(1)}, bf16[256,256]{1,0:T(8,128)(2,1)S(1)}, u32[]{:S(2)}, u32[]{:S(2)}) %collective-permute-start.11) | collective-permute-done | bytes 131104 | tf_op jit(solution)/shard_map/ppermute | solution.py:29
  34.1 1.1 %collective-permute-start.14 = (f32[8,128]{1,0:T(8,128)S(1)}, f32[8,128]{1,0:T(8,128)S(1)}, u32[]{:S(2)}, u32[]{:S(2)}) collective-permute-start(f32[8,128]{1,0:T(8,128)S(1)} %three_cross.1.refs_0_), channel_id=1, source_target_pairs={{0,3},{1,2},{2,1},{3,0},{4,7},{5,6},{6,5},{7,4},{8,11},{9,10},{10,... | collective-permute-start | bytes 12296 | tf_op jit(solution)/shard_map/ppermute | solution.py:52
  35.3 0.2 collective-permute-start.13
  35.5 1.4 %collective-permute-start.12 = (f32[8,128]{1,0:T(8,128)S(1)}, f32[8,128]{1,0:T(8,128)S(1)}, u32[]{:S(2)}, u32[]{:S(2)}) collective-permute-start(f32[8,128]{1,0:T(8,128)S(1)} %three_cross.1.refs_0_), channel_id=1, source_target_pairs={{0,1},{1,0},{2,3},{3,2},{4,5},{5,4},{6,7},{7,6},{8,9},{9,8},{10,11... | collective-permute-start | bytes 12296 | tf_op jit(solution)/shard_map/ppermute | solution.py:52
  36.9 0.7 %collective-permute-done.14.refs_3_ = f32[8,128]{1,0:T(8,128)S(1)} collective-permute-done((f32[8,128]{1,0:T(8,128)S(1)}, f32[8,128]{1,0:T(8,128)S(1)}, u32[]{:S(2)}, u32[]{:S(2)}) %collective-permute-start.14) | collective-permute-done | bytes 4128 | tf_op jit(solution)/shard_map/ppermute | solution.py:52
  37.7 0.2 collective-permute-done.12.refs_1_
  37.9 2.0 %last.1 = (f32[1,1,256,256]{3,2,1,0:T(8,128)}, bf16[1,1,256,256]{3,2,1,0:T(8,128)(2,1)S(1)}, f32[1]{0:T(128)}) custom-call(f32[8,128]{1,0:T(8,128)S(1)} %three_cross.1.refs_0_, f32[8,128]{1,0:T(8,128)S(1)} %collective-permute-done.12.refs_1_, f32[8,128]{1,0:T(8,128)S(1)} %collective-permute-done.13.refs_2_, f32[8,128]{1,0:T(8,128)S(1)} %collective-permute-done.14.refs_3_, ...), custom_call_target="tpu_custom_call" | custom-call | tf_op jit(solution)/shard_map/last/pallas_call | solution.py:222
  40.0 9.3 %collective-permute-start.15 = (bf16[1,1,256,256]{3,2,1,0:T(8,128)(2,1)S(1)}, bf16[1,1,256,256]{3,2,1,0:T(8,128)(2,1)S(1)}, u32[]{:S(2)}, u32[]{:S(2)}) collective-permute-start(bf16[1,1,256,256]{3,2,1,0:T(8,128)(2,1)S(1)} %get-tuple-element.47), channel_id=1, source_target_pairs={{0,4},{4,8},{8,12},{12,16},{16,20},{20,24},{24,28},{1,5},{5,9},{9,... | collective-permute-start | bytes 393224 | tf_op jit(solution)/shard_map/ppermute | solution.py:24
  49.3 1.9 %collective-permute-done.15 = bf16[1,1,256,256]{3,2,1,0:T(8,128)(2,1)S(1)} collective-permute-done((bf16[1,1,256,256]{3,2,1,0:T(8,128)(2,1)S(1)}, bf16[1,1,256,256]{3,2,1,0:T(8,128)(2,1)S(1)}, u32[]{:S(2)}, u32[]{:S(2)}) %collective-permute-start.15) | collective-permute-done | bytes 131104 | tf_op jit(solution)/shard_map/ppermute | solution.py:24
  51.2 0.7 %copy.13 = bf16[1,1,256,256]{3,2,1,0:T(8,128)(2,1)} copy(bf16[1,1,256,256]{3,2,1,0:T(8,128)(2,1)S(1)} %collective-permute-done.15) | data formatting | bytes 262144
  (27 shorter events, 1.3 us)
Async XLA Ops:
  0.6 7.4 %collective-permute-start = (bf16[256,256]{1,0:T(8,128)(2,1)}, bf16[256,256]{1,0:T(8,128)(2,1)S(1)}, u32[]{:S(2)}, u32[]{:S(2)}) collective-permute-start(bf16[256,256]{1,0:T(8,128)(2,1)} %bitcast.25), channel_id=1, source_target_pairs={{4,0},{8,4},{12,8},{16,12},{20,16},{24,20},{28,24},{5,1},{9,5},{13... | collective-permute-start | bytes 393224 | tf_op jit(solution)/shard_map/ppermute | solution.py:24
  3.2 0.9 %copy-start.4 = (bf16[1,1,256,256]{3,2,1,0:T(8,128)(2,1)S(1)}, bf16[1,1,256,256]{3,2,1,0:T(8,128)(2,1)}, u32[]{:S(2)}) copy-start(bf16[1,1,256,256]{3,2,1,0:T(8,128)(2,1)} %param.10) | copy-start | bytes 393220
  3.2 0.9 %copy-start.5 = (f32[1,1,256]{2,1,0:T(1,128)S(1)}, f32[1,1,256]{2,1,0:T(1,128)}, u32[]{:S(2)}) copy-start(f32[1,1,256]{2,1,0:T(1,128)} %param.13) | copy-start | bytes 3076
  3.2 4.8 %copy-start.3 = (bf16[1,1,256,256]{3,2,1,0:T(8,128)(2,1)S(1)}, bf16[1,1,256,256]{3,2,1,0:T(8,128)(2,1)}, u32[]{:S(2)}) copy-start(bf16[1,1,256,256]{3,2,1,0:T(8,128)(2,1)} %param.12) | copy-start | bytes 393220
  3.2 6.3 %copy-start = (bf16[1,1,16,256,256]{4,3,2,1,0:T(8,128)(2,1)S(1)}, bf16[1,1,16,256,256]{4,3,2,1,0:T(8,128)(2,1)}, u32[]{:S(2)}) copy-start(bf16[1,1,16,256,256]{4,3,2,1,0:T(8,128)(2,1)} %param.8) | copy-start | bytes 6291460
  3.2 6.3 %copy-start.1 = (bf16[1,1,16,256,256]{4,3,2,1,0:T(8,128)(2,1)S(1)}, bf16[1,1,16,256,256]{4,3,2,1,0:T(8,128)(2,1)}, u32[]{:S(2)}) copy-start(bf16[1,1,16,256,256]{4,3,2,1,0:T(8,128)(2,1)} %param.9) | copy-start | bytes 6291460
  8.3 5.3 %collective-permute-start.1 = (bf16[256,256]{1,0:T(8,128)(2,1)S(1)}, bf16[256,256]{1,0:T(8,128)(2,1)S(1)}, u32[]{:S(2)}, u32[]{:S(2)}) collective-permute-start(bf16[256,256]{1,0:T(8,128)(2,1)S(1)} %get-tuple-element.26.vector_b), channel_id=1, source_target_pairs={{0,1},{1,2},{2,3},{3,0},{4,5},{5,6},{6,7},{7,4},{8,9},{9,10},{10,1... | collective-permute-start | bytes 393224 | tf_op jit(solution)/shard_map/ppermute | solution.py:29
  10.8 7.2 %collective-permute-start.5 = (bf16[256,256]{1,0:T(8,128)(2,1)S(1)}, bf16[256,256]{1,0:T(8,128)(2,1)S(1)}, u32[]{:S(2)}, u32[]{:S(2)}) collective-permute-start(bf16[256,256]{1,0:T(8,128)(2,1)S(1)} %get-tuple-element.31), channel_id=1, source_target_pairs={{0,3},{1,0},{2,1},{3,2},{4,7},{5,4},{6,5},{7,6},{8,11},{9,8},{10,9... | collective-permute-start | bytes 393224 | tf_op jit(solution)/shard_map/ppermute | solution.py:29
  13.7 4.5 %copy-start.2 = (bf16[1,1,256,256]{3,2,1,0:T(8,128)(2,1)S(1)}, bf16[1,1,256,256]{3,2,1,0:T(8,128)(2,1)}, u32[]{:S(2)}) copy-start(bf16[1,1,256,256]{3,2,1,0:T(8,128)(2,1)} %param.14) | copy-start | bytes 393220
  13.7 4.4 %collective-permute-start.4 = (f32[8,128]{1,0:T(8,128)S(1)}, f32[8,128]{1,0:T(8,128)S(1)}, u32[]{:S(2)}, u32[]{:S(2)}) collective-permute-start(f32[8,128]{1,0:T(8,128)S(1)} %one_cross.1.after.refs_0_), channel_id=1, source_target_pairs={{0,3},{1,2},{2,1},{3,0},{4,7},{5,6},{6,5},{7,4},{8,11},{9,10},{10,... | collective-permute-start | bytes 12296 | tf_op jit(solution)/shard_map/ppermute | solution.py:52
  15.4 2.7 %collective-permute-start.3 = (f32[8,128]{1,0:T(8,128)S(1)}, f32[8,128]{1,0:T(8,128)S(1)}, u32[]{:S(2)}, u32[]{:S(2)}) collective-permute-start(f32[8,128]{1,0:T(8,128)S(1)} %one_cross.1.after.refs_0_), channel_id=1, source_target_pairs={{0,2},{1,3},{2,0},{3,1},{4,6},{5,7},{6,4},{7,5},{8,10},{9,11},{10,... | collective-permute-start | bytes 12296 | tf_op jit(solution)/shard_map/ppermute | solution.py:52
  15.7 2.5 %collective-permute-start.2 = (f32[8,128]{1,0:T(8,128)S(1)}, f32[8,128]{1,0:T(8,128)S(1)}, u32[]{:S(2)}, u32[]{:S(2)}) collective-permute-start(f32[8,128]{1,0:T(8,128)S(1)} %one_cross.1.after.refs_0_), channel_id=1, source_target_pairs={{0,1},{1,0},{2,3},{3,2},{4,5},{5,4},{6,7},{7,6},{8,9},{9,8},{10,11... | collective-permute-start | bytes 12296 | tf_op jit(solution)/shard_map/ppermute | solution.py:52
  18.4 6.0 %collective-permute-start.6 = (bf16[256,256]{1,0:T(8,128)(2,1)S(1)}, bf16[256,256]{1,0:T(8,128)(2,1)S(1)}, u32[]{:S(2)}, u32[]{:S(2)}) collective-permute-start(bf16[256,256]{1,0:T(8,128)(2,1)S(1)} %get-tuple-element.32.vector_b), channel_id=1, source_target_pairs={{0,1},{1,2},{2,3},{3,0},{4,5},{5,6},{6,7},{7,4},{8,9},{9,10},{10,1... | collective-permute-start | bytes 393224 | tf_op jit(solution)/shard_map/ppermute | solution.py:29
  20.9 7.6 %collective-permute-start.10 = (bf16[256,256]{1,0:T(8,128)(2,1)S(1)}, bf16[256,256]{1,0:T(8,128)(2,1)S(1)}, u32[]{:S(2)}, u32[]{:S(2)}) collective-permute-start(bf16[256,256]{1,0:T(8,128)(2,1)S(1)} %get-tuple-element.38), channel_id=1, source_target_pairs={{0,3},{1,0},{2,1},{3,2},{4,7},{5,4},{6,5},{7,6},{8,11},{9,8},{10,9... | collective-permute-start | bytes 393224 | tf_op jit(solution)/shard_map/ppermute | solution.py:29
  24.4 4.1 %collective-permute-start.9 = (f32[8,128]{1,0:T(8,128)S(1)}, f32[8,128]{1,0:T(8,128)S(1)}, u32[]{:S(2)}, u32[]{:S(2)}) collective-permute-start(f32[8,128]{1,0:T(8,128)S(1)} %two_cross.1.after.refs_0_), channel_id=1, source_target_pairs={{0,3},{1,2},{2,1},{3,0},{4,7},{5,6},{6,5},{7,4},{8,11},{9,10},{10,... | collective-permute-start | bytes 12296 | tf_op jit(solution)/shard_map/ppermute | solution.py:52
  25.9 2.8 %collective-permute-start.8 = (f32[8,128]{1,0:T(8,128)S(1)}, f32[8,128]{1,0:T(8,128)S(1)}, u32[]{:S(2)}, u32[]{:S(2)}) collective-permute-start(f32[8,128]{1,0:T(8,128)S(1)} %two_cross.1.after.refs_0_), channel_id=1, source_target_pairs={{0,2},{1,3},{2,0},{3,1},{4,6},{5,7},{6,4},{7,5},{8,10},{9,11},{10,... | collective-permute-start | bytes 12296 | tf_op jit(solution)/shard_map/ppermute | solution.py:52
  26.1 2.8 %collective-permute-start.7 = (f32[8,128]{1,0:T(8,128)S(1)}, f32[8,128]{1,0:T(8,128)S(1)}, u32[]{:S(2)}, u32[]{:S(2)}) collective-permute-start(f32[8,128]{1,0:T(8,128)S(1)} %two_cross.1.after.refs_0_), channel_id=1, source_target_pairs={{0,1},{1,0},{2,3},{3,2},{4,5},{5,4},{6,7},{7,6},{8,9},{9,8},{10,11... | collective-permute-start | bytes 12296 | tf_op jit(solution)/shard_map/ppermute | solution.py:52
  29.3 4.8 %collective-permute-start.11 = (bf16[256,256]{1,0:T(8,128)(2,1)S(1)}, bf16[256,256]{1,0:T(8,128)(2,1)S(1)}, u32[]{:S(2)}, u32[]{:S(2)}) collective-permute-start(bf16[256,256]{1,0:T(8,128)(2,1)S(1)} %get-tuple-element.39.vector_b), channel_id=1, source_target_pairs={{0,1},{1,2},{2,3},{3,0},{4,5},{5,6},{6,7},{7,4},{8,9},{9,10},{10,1... | collective-permute-start | bytes 393224 | tf_op jit(solution)/shard_map/ppermute | solution.py:29
  34.1 3.4 %collective-permute-start.14 = (f32[8,128]{1,0:T(8,128)S(1)}, f32[8,128]{1,0:T(8,128)S(1)}, u32[]{:S(2)}, u32[]{:S(2)}) collective-permute-start(f32[8,128]{1,0:T(8,128)S(1)} %three_cross.1.refs_0_), channel_id=1, source_target_pairs={{0,3},{1,2},{2,1},{3,0},{4,7},{5,6},{6,5},{7,4},{8,11},{9,10},{10,... | collective-permute-start | bytes 12296 | tf_op jit(solution)/shard_map/ppermute | solution.py:52
  35.3 2.5 %collective-permute-start.13 = (f32[8,128]{1,0:T(8,128)S(1)}, f32[8,128]{1,0:T(8,128)S(1)}, u32[]{:S(2)}, u32[]{:S(2)}) collective-permute-start(f32[8,128]{1,0:T(8,128)S(1)} %three_cross.1.refs_0_), channel_id=1, source_target_pairs={{0,2},{1,3},{2,0},{3,1},{4,6},{5,7},{6,4},{7,5},{8,10},{9,11},{10,... | collective-permute-start | bytes 12296 | tf_op jit(solution)/shard_map/ppermute | solution.py:52
  35.5 2.5 %collective-permute-start.12 = (f32[8,128]{1,0:T(8,128)S(1)}, f32[8,128]{1,0:T(8,128)S(1)}, u32[]{:S(2)}, u32[]{:S(2)}) collective-permute-start(f32[8,128]{1,0:T(8,128)S(1)} %three_cross.1.refs_0_), channel_id=1, source_target_pairs={{0,1},{1,0},{2,3},{3,2},{4,5},{5,4},{6,7},{7,6},{8,9},{9,8},{10,11... | collective-permute-start | bytes 12296 | tf_op jit(solution)/shard_map/ppermute | solution.py:52
  40.0 11.2 %collective-permute-start.15 = (bf16[1,1,256,256]{3,2,1,0:T(8,128)(2,1)S(1)}, bf16[1,1,256,256]{3,2,1,0:T(8,128)(2,1)S(1)}, u32[]{:S(2)}, u32[]{:S(2)}) collective-permute-start(bf16[1,1,256,256]{3,2,1,0:T(8,128)(2,1)S(1)} %get-tuple-element.47), channel_id=1, source_target_pairs={{0,4},{4,8},{8,12},{12,16},{16,20},{20,24},{24,28},{1,5},{5,9},{9,... | collective-permute-start | bytes 393224 | tf_op jit(solution)/shard_map/ppermute | solution.py:24

commit v3 on v2

--- a/solution.py
+++ b/solution.py
@@ -117,10 +117,34 @@
         stat_ref[row : row + 1] = fold(ops[one][...] * other)
 
 
-def cross_kernel(row, below, low, stat, out):
+def add_cross(row, below, low, stat, out):
     out[...] = stat[...]
-    crossed = fold(from_below(below[...]).astype(F32) * low[...])
-    out[row : row + 1] = stat[row : row + 1] + 2.0 * crossed
+    out[row : row + 1] = stat[row : row + 1] + 2.0 * fold(from_below(below) * low[...])
+
+
+def cross_kernel(below, low, stat, out):
+    add_cross(1, below[...].astype(F32), low, stat, out)
+
+
+def first_cross_kernel(parts, *refs):
+    y, g, prec, low, stat, out, p_out = refs[parts:]
+    yy, yhy = scalars(refs[:parts], 2)
+    p = prec[...].astype(F32) * (g[...].astype(F32) - (yhy / yy) * y[...].astype(F32))
+    p_out[...] = p.astype(BF16)
+    add_cross(5, p, low, stat, out)
+
+
+def second_cross_kernel(y, g, p, hp, prec, coefficients, low, stat, out):
+    along_y, along_p, lam = [coefficients[i : i + 1, 0:1] for i in range(3)]
+    x = along_y * y[...].astype(F32) + along_p * p[...].astype(F32)
+    hx = along_y * g[...].astype(F32) + along_p * hp[...].astype(F32)
+    add_cross(3, prec[...].astype(F32) * (hx - lam * x), low, stat, out)
+
+
+def join_kernel(diag, up, above, mask, out, out_b):
+    joined = mask[...] * (diag[...] + up[...] + from_above(above[...].astype(F32)))
+    out[...] = joined
+    out_b[...] = joined.astype(BF16)
 
 
 def raise_kernel(left, right, below, after, up_ref, inner):
@@ -128,12 +152,9 @@
 
 
 def first_kernel(parts, *refs):
-    y_ref, diag, up, above, mask, prec = refs[parts : parts + 6]
-    g_ref, p_ref, pb_ref = refs[parts + 6 :]
+    y_ref, g_ref, prec, p_ref, pb_ref = refs[parts:]
     yy, yhy = scalars(refs[:parts], 2)
-    g = mask[...] * (diag[...] + up[...] + from_above(above[...].astype(F32)))
-    g_ref[...] = g
-    p = prec[...].astype(F32) * (g - (yhy / yy) * y_ref[...])
+    p = prec[...].astype(F32) * (g_ref[...] - (yhy / yy) * y_ref[...])
     p_ref[...] = p
     pb_ref[...] = p.astype(BF16)
 
@@ -146,8 +167,8 @@
 
 
 def second_kernel(parts, *refs):
-    y_ref, g_ref, p_ref, diag, up, above, mask, prec = refs[parts : parts + 8]
-    x_out, g_out, p_out, pb_out, lam_out = refs[parts + 8 :]
+    y_ref, g_ref, p_ref, hp_ref, prec = refs[parts : parts + 5]
+    x_out, g_out, p_out, pb_out, coefficients = refs[parts + 5 :]
     yy, yg, yp, pp, pg, php = scalars(refs[:parts], 6)
     a = yg / yy
     s = yp / yy
@@ -157,15 +178,15 @@
     lam, u, w = ritz(a, b, c)
     along_p = w / jnp.sqrt(qq)
     along_y = u / jnp.sqrt(yy) - along_p * s
-    hp = mask[...] * (diag[...] + up[...] + from_above(above[...].astype(F32)))
     x = along_y * y_ref[...] + along_p * p_ref[...]
-    g = along_y * g_ref[...] + along_p * hp
+    g = along_y * g_ref[...] + along_p * hp_ref[...]
     p = prec[...].astype(F32) * (g - lam * x)
     x_out[...] = x
     g_out[...] = g
     p_out[...] = p
     pb_out[...] = p.astype(BF16)
-    lam_out[...] = jnp.broadcast_to(lam, lam_out.shape)
+    for i, value in enumerate([along_y, along_p, lam]):
+        coefficients[i : i + 1] = jnp.broadcast_to(value, (1, LANES))
 
 
 def dot(one, two, over):
@@ -186,10 +207,10 @@
 
 
 def last_kernel(parts, *refs):
-    x_ref, p_ref, lam_ref = refs[parts : parts + 3]
+    x_ref, p_ref, coefficients = refs[parts : parts + 3]
     polar_out, weight_out, lam_out = refs[parts + 3 :]
     xp, pp, pg, php = scalars(refs[:parts], 4)
-    a = lam_ref[0:1, 0:1]
+    a = coefficients[2:3, 0:1]
     qq = pp - xp * xp
     b = (pg - xp * a) / jnp.sqrt(qq)
     c = (php - 2.0 * xp * pg + xp * xp * a) / qq
@@ -238,42 +259,52 @@
 
     y, yb = call(start_kernel, "start", [matrix, narrow], scaled, behind, guess[0, 0], mask)
 
-    def half(name, vector_b, pairs, operands, row, sends):
-        below = rotate(vector_b, "sec", 1)
+    def half(name, vector_b, pairs, operands, sends):
         outs = [matrix, matrix, stats] + [narrow] * sends
         kernel = functools.partial(lower_kernel, pairs, sends)
         low, diag, stat, *sent = call(
-            kernel, name + "_lower", outs, left, right, vector_b, *operands, scratch=[inner]
+            kernel, name, outs, left, right, vector_b, *operands, scratch=[inner]
         )
-        above = rotate(sent[0], "sec", -1) if sends else None
-        (stat,) = call(functools.partial(cross_kernel, row), name + "_cross", [stats], below, low, stat)
-        return below, diag, above, stat
-
-    def raised(name, below, stat):
-        return call(raise_kernel, name, [matrix], left, right, below, stat, scratch=[inner])[0]
-
-    below, diag, above, stat = half("one", yb, [(0, 0), (0, None)], [y], 1, 1)
+        return low, diag, stat, rotate(sent[0], "sec", -1) if sends else None
+
+    def joined(name, below, after, diag, above):
+        (up,) = call(
+            raise_kernel, name + "_raise", [matrix], left, right, below, after, scratch=[inner]
+        )
+        return call(join_kernel, name + "_join", [matrix, narrow], diag, up, above, mask)
+
+    y_below = rotate(yb, "sec", 1)
+    low, diag, stat, above = half("one_lower", yb, [(0, 0), (0, None)], [y], 1)
+    prec_below = rotate(prec, "sec", 1)
+    (stat,) = call(cross_kernel, "one_cross", [stats], y_below, low, stat)
     parts = exchange(stat, "sec")
-    up = raised("one_raise", below, stat)
+    g, gb = joined("one", y_below, stat, diag, above)
+    g_below = rotate(gb, "sec", 1)
     kernel = functools.partial(first_kernel, len(parts))
-    g, p, pb = call(
-        kernel, "first", [matrix, matrix, narrow], *parts, y, diag, up, above, mask, prec
-    )
+    p, pb = call(kernel, "first", [matrix, narrow], *parts, y, g, prec)
 
     pairs = [(0, 0), (0, 1), (0, 2), (2, 2), (2, 1), (2, None)]
-    below, diag, above, stat = half("two", pb, pairs, [y, g, p], 5, 1)
+    low, diag, stat, above = half("two_lower", pb, pairs, [y, g, p], 1)
+    kernel = functools.partial(first_cross_kernel, len(parts))
+    stat, p_below = call(
+        kernel, "two_cross", [stats, narrow], *parts, y_below, g_below, prec_below, low, stat
+    )
     parts = exchange(stat, "sec")
-    up = raised("two_raise", below, stat)
+    hp, hpb = joined("two", p_below, stat, diag, above)
+    hp_below = rotate(hpb, "sec", 1)
     kernel = functools.partial(second_kernel, len(parts))
-    x, g, p, pb, lam = call(
-        kernel,
-        "second",
-        [matrix, matrix, matrix, narrow, stats],
-        *parts, y, g, p, diag, up, above, mask, prec,
+    x, g, p, pb, coefficients = call(
+        kernel, "second", [matrix, matrix, matrix, narrow, stats], *parts, y, g, p, hp, prec
     )
 
     pairs = [(0, 2), (2, 2), (2, 1), (2, None)]
-    below, diag, above, stat = half("three", pb, pairs, [x, g, p], 3, 0)
+    low, diag, stat, _ = half("three_lower", pb, pairs, [x, g, p], 0)
+    (stat,) = call(
+        second_cross_kernel,
+        "three_cross",
+        [stats],
+        y_below, g_below, p_below, hp_below, prec_below, coefficients, low, stat,
+    )
     parts = exchange(stat, "sec")
     kernel = functools.partial(last_kernel, len(parts))
     block = (1, 1, size, size)
@@ -285,7 +316,7 @@
             jax.ShapeDtypeStruct(block, BF16),
             jax.ShapeDtypeStruct((1,), F32),
         ],
-        *parts, x, p, lam,
+        *parts, x, p, coefficients,
         out_specs=[VMEM, VMEM, SMEM],
     )
     return polar, shift(weight, "seg", 1), energy

time: 52.3 us -> 53.8 us (1.029); the launches traced: 51.9 us -> 52.7 us
  waiting for transfers between devices: 13.2 us -> 14.9 us
  starting transfers between devices: 25.7 us -> 24.4 us
    ppermute x9, waiting for transfers between devices: 1.61 us -> 3.85 us  [exchange(): parts.append(lax.ppermute(parts[0], axis, pairs))]
    ppermute x2, starting transfers between devices: 11.2 us -> 9.97 us  [shift(): lax.ppermute(value, axis, [(source, source + steps) for source in range(f...]
    ppermute x5 -> x6, waiting for transfers between devices: 5.76 us -> 5.18 us  [rotate(): lax.ppermute(value, axis, [(source, (source + steps) % count) for source...]
    pallas_call x13 -> x15, Pallas kernels: 9.95 us -> 10.4 us  [call(): pl.pallas_call(kernel, name=name, out_shape=outs, in_specs=in_specs or [V...]
    ppermute x5 -> x6, starting transfers between devices: 5.76 us -> 5.91 us  [rotate(): lax.ppermute(value, axis, [(source, (source + steps) % count) for source...]
  transfers between devices with their start and end apart: 16 -> 17, of which waited for: 11 -> 8; matrix products, arithmetic and copies ran while one was open for 0% -> 0% of each run, Pallas kernels for 14% -> 15%
where the time goes in v3:
time: 53.8 us; the launch traced here: 52.7 us
  starting transfers between devices  24.4 us (45%)
  waiting for transfers between devices  14.9 us (28%)
  Pallas kernels  10.4 us (19%)
  local copies, waits for them, and re-layouts  1.5 us (3%)
  between operations  1.43 us (3%)
    pallas_call x15, Pallas kernels, call(): pl.pallas_call(kernel, name=name, out_shape=outs, in_specs=in_specs or [V...  10.4 us
    ppermute x2, starting transfers between devices, shift(): lax.ppermute(value, axis, [(source, source + steps) for source in range(f...  9.97 us
    ppermute x9, starting transfers between devices, exchange(): parts.append(lax.ppermute(parts[0], axis, pairs))  8.55 us
    ppermute x6, starting transfers between devices, rotate(): lax.ppermute(value, axis, [(source, (source + steps) % count) for source...  5.91 us
    ppermute x2, waiting for transfers between devices, shift(): lax.ppermute(value, axis, [(source, source + steps) for source in range(f...  5.85 us
    ppermute x6, waiting for transfers between devices, rotate(): lax.ppermute(value, axis, [(source, (source + steps) % count) for source...  5.18 us
    ppermute x9, waiting for transfers between devices, exchange(): parts.append(lax.ppermute(parts[0], axis, pairs))  3.85 us
    unnamed x13, local copies, waits for them, and re-layouts  1.5 us
  transfers between devices with their start and end apart: 17, of which 8 were waited for; matrix products, arithmetic and copies ran while one was open for 0% of the time, Pallas kernels for 15%

profile of v3, /device:TPU:1, one launch (start us, length us, event | category | flops | bytes accessed | tf_op | source)
XLA Modules:
  0.0 52.7 jit_solution(902892810202546675)
XLA Ops:
  0.6 1.9 %collective-permute-start = (bf16[256,256]{1,0:T(8,128)(2,1)}, bf16[256,256]{1,0:T(8,128)(2,1)S(1)}, u32[]{:S(2)}, u32[]{:S(2)}) collective-permute-start(bf16[256,256]{1,0:T(8,128)(2,1)} %bitcast.26), channel_id=1, source_target_pairs={{4,0},{8,4},{12,8},{16,12},{20,16},{24,20},{28,24},{5,1},{9,5},{13... | collective-permute-start | bytes 393224 | tf_op jit(solution)/shard_map/ppermute | solution.py:24
  3.3 0.8 %copy-done.4 = bf16[1,1,256,256]{3,2,1,0:T(8,128)(2,1)S(1)} copy-done((bf16[1,1,256,256]{3,2,1,0:T(8,128)(2,1)S(1)}, bf16[1,1,256,256]{3,2,1,0:T(8,128)(2,1)}, u32[]{:S(2)}) %copy-start.4) | copy-done | bytes 131096
  4.1 3.9 %collective-permute-done.behind = bf16[256,256]{1,0:T(8,128)(2,1)S(1)} collective-permute-done((bf16[256,256]{1,0:T(8,128)(2,1)}, bf16[256,256]{1,0:T(8,128)(2,1)S(1)}, u32[]{:S(2)}, u32[]{:S(2)}) %collective-permute-start) | collective-permute-done | bytes 131104 | tf_op jit(solution)/shard_map/ppermute | solution.py:24
  8.3 1.3 %collective-permute-start.1 = (bf16[256,256]{1,0:T(8,128)(2,1)S(1)}, bf16[256,256]{1,0:T(8,128)(2,1)S(1)}, u32[]{:S(2)}, u32[]{:S(2)}) collective-permute-start(bf16[256,256]{1,0:T(8,128)(2,1)S(1)} %get-tuple-element.31.vector_b), channel_id=1, source_target_pairs={{0,1},{1,2},{2,3},{3,0},{4,5},{5,6},{6,7},{7,4},{8,9},{9,10},{10,1... | collective-permute-start | bytes 393224 | tf_op jit(solution)/shard_map/ppermute | solution.py:29
  9.5 1.3 %one_lower.1 = (f32[256,256]{1,0:T(8,128)S(1)}, f32[256,256]{1,0:T(8,128)S(1)}, f32[8,128]{1,0:T(8,128)S(1)}, bf16[256,256]{1,0:T(8,128)(2,1)S(1)}) custom-call(bf16[16,256,256]{2,1,0:T(8,128)(2,1)S(1)} %bitcast.11, bf16[16,256,256]{2,1,0:T(8,128)(2,1)S(1)} %bitcast.16, bf16[256,256]{1,0:T(8,128)(2,1)S(1)} %get-tuple-element.31.vector_b, ...), custom_call_target="tpu_custom_call" | custom-call | tf_op jit(solution)/shard_map/one_lower/pallas_call | solution.py:243
  10.8 1.2 %collective-permute-start.2 = (bf16[256,256]{1,0:T(8,128)(2,1)S(1)}, bf16[256,256]{1,0:T(8,128)(2,1)S(1)}, u32[]{:S(2)}, u32[]{:S(2)}) collective-permute-start(bf16[256,256]{1,0:T(8,128)(2,1)S(1)} %get-tuple-element.36), channel_id=1, source_target_pairs={{0,3},{1,0},{2,1},{3,2},{4,7},{5,4},{6,5},{7,6},{8,11},{9,8},{10,9... | collective-permute-start | bytes 393224 | tf_op jit(solution)/shard_map/ppermute | solution.py:29
  12.0 1.6 %collective-permute-done.1.below.refs_4_.y = bf16[256,256]{1,0:T(8,128)(2,1)S(1)} collective-permute-done((bf16[256,256]{1,0:T(8,128)(2,1)S(1)}, bf16[256,256]{1,0:T(8,128)(2,1)S(1)}, u32[]{:S(2)}, u32[]{:S(2)}) %collective-permute-start.1) | collective-permute-done | bytes 131104 | tf_op jit(solution)/shard_map/ppermute | solution.py:29
  13.6 1.7 %collective-permute-start.6 = (f32[8,128]{1,0:T(8,128)S(1)}, f32[8,128]{1,0:T(8,128)S(1)}, u32[]{:S(2)}, u32[]{:S(2)}) collective-permute-start(f32[8,128]{1,0:T(8,128)S(1)} %one_cross.1.after.refs_0_), channel_id=1, source_target_pairs={{0,3},{1,2},{2,1},{3,0},{4,7},{5,6},{6,5},{7,4},{8,11},{9,10},{10,... | collective-permute-start | bytes 12296 | tf_op jit(solution)/shard_map/ppermute | solution.py:52
  15.4 0.3 collective-permute-start.5
  15.7 1.1 %collective-permute-start.4 = (f32[8,128]{1,0:T(8,128)S(1)}, f32[8,128]{1,0:T(8,128)S(1)}, u32[]{:S(2)}, u32[]{:S(2)}) collective-permute-start(f32[8,128]{1,0:T(8,128)S(1)} %one_cross.1.after.refs_0_), channel_id=1, source_target_pairs={{0,1},{1,0},{2,3},{3,2},{4,5},{5,4},{6,7},{7,6},{8,9},{9,8},{10,11... | collective-permute-start | bytes 12296 | tf_op jit(solution)/shard_map/ppermute | solution.py:52
  16.8 0.4 collective-permute-start.7
  17.2 1.2 %one_raise.1.up = f32[256,256]{1,0:T(8,128)S(1)} custom-call(bf16[16,256,256]{2,1,0:T(8,128)(2,1)S(1)} %bitcast.12, bf16[16,256,256]{2,1,0:T(8,128)(2,1)S(1)} %bitcast.17, bf16[256,256]{1,0:T(8,128)(2,1)S(1)} %collective-permute-done.1.below.refs_4_.y, f32[8,128]{1,0:T(8,128)S(1)} %one_cross.1.after.refs_0_), custom_call_target="tpu_custom_call" | custom-call | tf_op jit(solution)/shard_map/one_raise/pallas_call | solution.py:243
  18.5 2.3 %collective-permute-start.3 = (bf16[256,256]{1,0:T(8,128)(2,1)S(1)}, bf16[256,256]{1,0:T(8,128)(2,1)S(1)}, u32[]{:S(2)}, u32[]{:S(2)}) collective-permute-start(bf16[256,256]{1,0:T(8,128)(2,1)S(1)} %get-tuple-element.37), channel_id=1, source_target_pairs={{0,1},{1,2},{2,3},{3,0},{4,5},{5,6},{6,7},{7,4},{8,9},{9,10},{10,1... | collective-permute-start | bytes 393224 | tf_op jit(solution)/shard_map/ppermute | solution.py:29
  21.1 1.3 %two_lower.1 = (f32[256,256]{1,0:T(8,128)S(1)}, f32[256,256]{1,0:T(8,128)S(1)}, f32[8,128]{1,0:T(8,128)S(1)}, bf16[256,256]{1,0:T(8,128)(2,1)S(1)}) custom-call(bf16[16,256,256]{2,1,0:T(8,128)(2,1)S(1)} %bitcast.13, bf16[16,256,256]{2,1,0:T(8,128)(2,1)S(1)} %bitcast.18, bf16[256,256]{1,0:T(8,128)(2,1)S(1)} %get-tuple-element.39.vector_b, ...), custom_call_target="tpu_custom_call" | custom-call | tf_op jit(solution)/shard_map/two_lower/pallas_call | solution.py:243
  22.5 2.4 %collective-permute-done.3.refs_5_.g = bf16[256,256]{1,0:T(8,128)(2,1)S(1)} collective-permute-done((bf16[256,256]{1,0:T(8,128)(2,1)S(1)}, bf16[256,256]{1,0:T(8,128)(2,1)S(1)}, u32[]{:S(2)}, u32[]{:S(2)}) %collective-permute-start.3) | collective-permute-done | bytes 131104 | tf_op jit(solution)/shard_map/ppermute | solution.py:29
  25.1 1.2 %two_raise.1.up = f32[256,256]{1,0:T(8,128)S(1)} custom-call(bf16[16,256,256]{2,1,0:T(8,128)(2,1)S(1)} %bitcast.14, bf16[16,256,256]{2,1,0:T(8,128)(2,1)S(1)} %bitcast.19, bf16[256,256]{1,0:T(8,128)(2,1)S(1)} %get-tuple-element.43.below.p, f32[8,128]{1,0:T(8,128)S(1)} %get-tuple-element.45.after.refs_0_), custom_call_target="tpu_custom_call" | custom-call | tf_op jit(solution)/shard_map/two_raise/pallas_call | solution.py:243
  26.3 1.2 %collective-permute-done.8.above = bf16[256,256]{1,0:T(8,128)(2,1)S(1)} collective-permute-done((bf16[256,256]{1,0:T(8,128)(2,1)S(1)}, bf16[256,256]{1,0:T(8,128)(2,1)S(1)}, u32[]{:S(2)}, u32[]{:S(2)}) %collective-permute-start.8) | collective-permute-done | bytes 131104 | tf_op jit(solution)/shard_map/ppermute | solution.py:29
  27.6 0.6 %collective-permute-start.9 = (bf16[256,256]{1,0:T(8,128)(2,1)S(1)}, bf16[256,256]{1,0:T(8,128)(2,1)S(1)}, u32[]{:S(2)}, u32[]{:S(2)}) collective-permute-start(bf16[256,256]{1,0:T(8,128)(2,1)S(1)} %get-tuple-element.47), channel_id=1, source_target_pairs={{0,1},{1,2},{2,3},{3,0},{4,5},{5,6},{6,7},{7,4},{8,9},{9,10},{10,1... | collective-permute-start | bytes 393224 | tf_op jit(solution)/shard_map/ppermute | solution.py:29
  28.3 1.8 %collective-permute-start.12 = (f32[8,128]{1,0:T(8,128)S(1)}, f32[8,128]{1,0:T(8,128)S(1)}, u32[]{:S(2)}, u32[]{:S(2)}) collective-permute-start(f32[8,128]{1,0:T(8,128)S(1)} %get-tuple-element.45.after.refs_0_), channel_id=1, source_target_pairs={{0,3},{1,2},{2,1},{3,0},{4,7},{5,6},{6,5},{7,4},{8,11},{9,10},{10,... | collective-permute-start | bytes 12296 | tf_op jit(solution)/shard_map/ppermute | solution.py:52
  30.1 0.5 collective-permute-start.11
  30.6 0.4 collective-permute-start.10
  30.9 2.8 %collective-permute-done.12.refs_3_ = f32[8,128]{1,0:T(8,128)S(1)} collective-permute-done((f32[8,128]{1,0:T(8,128)S(1)}, f32[8,128]{1,0:T(8,128)S(1)}, u32[]{:S(2)}, u32[]{:S(2)}) %collective-permute-start.12) | collective-permute-done | bytes 4128 | tf_op jit(solution)/shard_map/ppermute | solution.py:52
  33.7 0.4 second.1
  34.1 2.0 %three_lower.1 = (f32[256,256]{1,0:T(8,128)S(1)}, f32[256,256]{1,0:T(8,128)}, f32[8,128]{1,0:T(8,128)S(1)}) custom-call(bf16[16,256,256]{2,1,0:T(8,128)(2,1)S(1)} %bitcast.15, bf16[16,256,256]{2,1,0:T(8,128)(2,1)S(1)} %bitcast.20, bf16[256,256]{1,0:T(8,128)(2,1)S(1)} %get-tuple-element.50.vector_b, f32[256,256]{1,0:T(8,128)S(1)} %get-tuple-element.51.refs_0_.refs_4_, ...), custom_call_target="tpu_custom_call" | custom-call | tf_op jit(solution)/shard_map/three_lower/pallas_call | solution.py:243
  36.3 0.7 %collective-permute-start.15 = (f32[8,128]{1,0:T(8,128)S(1)}, f32[8,128]{1,0:T(8,128)S(1)}, u32[]{:S(2)}, u32[]{:S(2)}) collective-permute-start(f32[8,128]{1,0:T(8,128)S(1)} %three_cross.1.refs_0_), channel_id=1, source_target_pairs={{0,3},{1,2},{2,1},{3,0},{4,7},{5,6},{6,5},{7,4},{8,11},{9,10},{10,... | collective-permute-start | bytes 12296 | tf_op jit(solution)/shard_map/ppermute | solution.py:52
  37.0 0.6 %collective-permute-start.14 = (f32[8,128]{1,0:T(8,128)S(1)}, f32[8,128]{1,0:T(8,128)S(1)}, u32[]{:S(2)}, u32[]{:S(2)}) collective-permute-start(f32[8,128]{1,0:T(8,128)S(1)} %three_cross.1.refs_0_), channel_id=1, source_target_pairs={{0,2},{1,3},{2,0},{3,1},{4,6},{5,7},{6,4},{7,5},{8,10},{9,11},{10,... | collective-permute-start | bytes 12296 | tf_op jit(solution)/shard_map/ppermute | solution.py:52
  37.6 1.4 %collective-permute-start.13 = (f32[8,128]{1,0:T(8,128)S(1)}, f32[8,128]{1,0:T(8,128)S(1)}, u32[]{:S(2)}, u32[]{:S(2)}) collective-permute-start(f32[8,128]{1,0:T(8,128)S(1)} %three_cross.1.refs_0_), channel_id=1, source_target_pairs={{0,1},{1,0},{2,3},{3,2},{4,5},{5,4},{6,7},{7,6},{8,9},{9,8},{10,11... | collective-permute-start | bytes 12296 | tf_op jit(solution)/shard_map/ppermute | solution.py:52
  39.0 0.7 %collective-permute-done.15.refs_3_ = f32[8,128]{1,0:T(8,128)S(1)} collective-permute-done((f32[8,128]{1,0:T(8,128)S(1)}, f32[8,128]{1,0:T(8,128)S(1)}, u32[]{:S(2)}, u32[]{:S(2)}) %collective-permute-start.15) | collective-permute-done | bytes 4128 | tf_op jit(solution)/shard_map/ppermute | solution.py:52
  40.1 2.0 %last.1 = (f32[1,1,256,256]{3,2,1,0:T(8,128)}, bf16[1,1,256,256]{3,2,1,0:T(8,128)(2,1)S(1)}, f32[1]{0:T(128)}) custom-call(f32[8,128]{1,0:T(8,128)S(1)} %three_cross.1.refs_0_, f32[8,128]{1,0:T(8,128)S(1)} %collective-permute-done.13.refs_1_, f32[8,128]{1,0:T(8,128)S(1)} %collective-permute-done.14.refs_2_, f32[8,128]{1,0:T(8,128)S(1)} %collective-permute-done.15.refs_3_, ...), custom_call_target="tpu_custom_call" | custom-call | tf_op jit(solution)/shard_map/last/pallas_call | solution.py:243
  42.1 8.0 %collective-permute-start.16 = (bf16[1,1,256,256]{3,2,1,0:T(8,128)(2,1)S(1)}, bf16[1,1,256,256]{3,2,1,0:T(8,128)(2,1)S(1)}, u32[]{:S(2)}, u32[]{:S(2)}) collective-permute-start(bf16[1,1,256,256]{3,2,1,0:T(8,128)(2,1)S(1)} %get-tuple-element.57), channel_id=1, source_target_pairs={{0,4},{4,8},{8,12},{12,16},{16,20},{20,24},{24,28},{1,5},{5,9},{9,... | collective-permute-start | bytes 393224 | tf_op jit(solution)/shard_map/ppermute | solution.py:24
  50.1 1.9 %collective-permute-done.16 = bf16[1,1,256,256]{3,2,1,0:T(8,128)(2,1)S(1)} collective-permute-done((bf16[1,1,256,256]{3,2,1,0:T(8,128)(2,1)S(1)}, bf16[1,1,256,256]{3,2,1,0:T(8,128)(2,1)S(1)}, u32[]{:S(2)}, u32[]{:S(2)}) %collective-permute-start.16) | collective-permute-done | bytes 131104 | tf_op jit(solution)/shard_map/ppermute | solution.py:24
  52.1 0.7 %copy.13 = bf16[1,1,256,256]{3,2,1,0:T(8,128)(2,1)} copy(bf16[1,1,256,256]{3,2,1,0:T(8,128)(2,1)S(1)} %collective-permute-done.16) | data formatting | bytes 262144
  (31 shorter events, 1.6 us)
Async XLA Ops:
  0.6 7.4 %collective-permute-start = (bf16[256,256]{1,0:T(8,128)(2,1)}, bf16[256,256]{1,0:T(8,128)(2,1)S(1)}, u32[]{:S(2)}, u32[]{:S(2)}) collective-permute-start(bf16[256,256]{1,0:T(8,128)(2,1)} %bitcast.26), channel_id=1, source_target_pairs={{4,0},{8,4},{12,8},{16,12},{20,16},{24,20},{28,24},{5,1},{9,5},{13... | collective-permute-start | bytes 393224 | tf_op jit(solution)/shard_map/ppermute | solution.py:24
  3.2 0.9 %copy-start.4 = (bf16[1,1,256,256]{3,2,1,0:T(8,128)(2,1)S(1)}, bf16[1,1,256,256]{3,2,1,0:T(8,128)(2,1)}, u32[]{:S(2)}) copy-start(bf16[1,1,256,256]{3,2,1,0:T(8,128)(2,1)} %param.10) | copy-start | bytes 393220
  3.2 0.9 %copy-start.5 = (f32[1,1,256]{2,1,0:T(1,128)S(1)}, f32[1,1,256]{2,1,0:T(1,128)}, u32[]{:S(2)}) copy-start(f32[1,1,256]{2,1,0:T(1,128)} %param.13) | copy-start | bytes 3076
  3.2 4.8 %copy-start.3 = (bf16[1,1,256,256]{3,2,1,0:T(8,128)(2,1)S(1)}, bf16[1,1,256,256]{3,2,1,0:T(8,128)(2,1)}, u32[]{:S(2)}) copy-start(bf16[1,1,256,256]{3,2,1,0:T(8,128)(2,1)} %param.12) | copy-start | bytes 393220
  3.2 6.3 %copy-start = (bf16[1,1,16,256,256]{4,3,2,1,0:T(8,128)(2,1)S(1)}, bf16[1,1,16,256,256]{4,3,2,1,0:T(8,128)(2,1)}, u32[]{:S(2)}) copy-start(bf16[1,1,16,256,256]{4,3,2,1,0:T(8,128)(2,1)} %param.8) | copy-start | bytes 6291460
  3.2 6.3 %copy-start.1 = (bf16[1,1,16,256,256]{4,3,2,1,0:T(8,128)(2,1)S(1)}, bf16[1,1,16,256,256]{4,3,2,1,0:T(8,128)(2,1)}, u32[]{:S(2)}) copy-start(bf16[1,1,16,256,256]{4,3,2,1,0:T(8,128)(2,1)} %param.9) | copy-start | bytes 6291460
  8.3 5.3 %collective-permute-start.1 = (bf16[256,256]{1,0:T(8,128)(2,1)S(1)}, bf16[256,256]{1,0:T(8,128)(2,1)S(1)}, u32[]{:S(2)}, u32[]{:S(2)}) collective-permute-start(bf16[256,256]{1,0:T(8,128)(2,1)S(1)} %get-tuple-element.31.vector_b), channel_id=1, source_target_pairs={{0,1},{1,2},{2,3},{3,0},{4,5},{5,6},{6,7},{7,4},{8,9},{9,10},{10,1... | collective-permute-start | bytes 393224 | tf_op jit(solution)/shard_map/ppermute | solution.py:29
  9.5 7.3 %copy-start.2 = (bf16[1,1,256,256]{3,2,1,0:T(8,128)(2,1)S(1)}, bf16[1,1,256,256]{3,2,1,0:T(8,128)(2,1)}, u32[]{:S(2)}) copy-start(bf16[1,1,256,256]{3,2,1,0:T(8,128)(2,1)} %param.14) | copy-start | bytes 393220
  10.8 7.6 %collective-permute-start.2 = (bf16[256,256]{1,0:T(8,128)(2,1)S(1)}, bf16[256,256]{1,0:T(8,128)(2,1)S(1)}, u32[]{:S(2)}, u32[]{:S(2)}) collective-permute-start(bf16[256,256]{1,0:T(8,128)(2,1)S(1)} %get-tuple-element.36), channel_id=1, source_target_pairs={{0,3},{1,0},{2,1},{3,2},{4,7},{5,4},{6,5},{7,6},{8,11},{9,8},{10,9... | collective-permute-start | bytes 393224 | tf_op jit(solution)/shard_map/ppermute | solution.py:29
  13.6 7.2 %collective-permute-start.6 = (f32[8,128]{1,0:T(8,128)S(1)}, f32[8,128]{1,0:T(8,128)S(1)}, u32[]{:S(2)}, u32[]{:S(2)}) collective-permute-start(f32[8,128]{1,0:T(8,128)S(1)} %one_cross.1.after.refs_0_), channel_id=1, source_target_pairs={{0,3},{1,2},{2,1},{3,0},{4,7},{5,6},{6,5},{7,4},{8,11},{9,10},{10,... | collective-permute-start | bytes 12296 | tf_op jit(solution)/shard_map/ppermute | solution.py:52
  15.4 5.5 %collective-permute-start.5 = (f32[8,128]{1,0:T(8,128)S(1)}, f32[8,128]{1,0:T(8,128)S(1)}, u32[]{:S(2)}, u32[]{:S(2)}) collective-permute-start(f32[8,128]{1,0:T(8,128)S(1)} %one_cross.1.after.refs_0_), channel_id=1, source_target_pairs={{0,2},{1,3},{2,0},{3,1},{4,6},{5,7},{6,4},{7,5},{8,10},{9,11},{10,... | collective-permute-start | bytes 12296 | tf_op jit(solution)/shard_map/ppermute | solution.py:52
  15.7 5.1 %collective-permute-start.4 = (f32[8,128]{1,0:T(8,128)S(1)}, f32[8,128]{1,0:T(8,128)S(1)}, u32[]{:S(2)}, u32[]{:S(2)}) collective-permute-start(f32[8,128]{1,0:T(8,128)S(1)} %one_cross.1.after.refs_0_), channel_id=1, source_target_pairs={{0,1},{1,0},{2,3},{3,2},{4,5},{5,4},{6,7},{7,6},{8,9},{9,8},{10,11... | collective-permute-start | bytes 12296 | tf_op jit(solution)/shard_map/ppermute | solution.py:52
  16.8 5.7 %collective-permute-start.7 = (bf16[256,256]{1,0:T(8,128)(2,1)S(1)}, bf16[256,256]{1,0:T(8,128)(2,1)S(1)}, u32[]{:S(2)}, u32[]{:S(2)}) collective-permute-start(bf16[256,256]{1,0:T(8,128)(2,1)S(1)} %bitcast.21), channel_id=1, source_target_pairs={{0,1},{1,2},{2,3},{3,0},{4,5},{5,6},{6,7},{7,4},{8,9},{9,10},{10,1... | collective-permute-start | bytes 393224 | tf_op jit(solution)/shard_map/ppermute | solution.py:29
  18.5 6.4 %collective-permute-start.3 = (bf16[256,256]{1,0:T(8,128)(2,1)S(1)}, bf16[256,256]{1,0:T(8,128)(2,1)S(1)}, u32[]{:S(2)}, u32[]{:S(2)}) collective-permute-start(bf16[256,256]{1,0:T(8,128)(2,1)S(1)} %get-tuple-element.37), channel_id=1, source_target_pairs={{0,1},{1,2},{2,3},{3,0},{4,5},{5,6},{6,7},{7,4},{8,9},{9,10},{10,1... | collective-permute-start | bytes 393224 | tf_op jit(solution)/shard_map/ppermute | solution.py:29
  22.4 5.2 %collective-permute-start.8 = (bf16[256,256]{1,0:T(8,128)(2,1)S(1)}, bf16[256,256]{1,0:T(8,128)(2,1)S(1)}, u32[]{:S(2)}, u32[]{:S(2)}) collective-permute-start(bf16[256,256]{1,0:T(8,128)(2,1)S(1)} %get-tuple-element.46), channel_id=1, source_target_pairs={{0,3},{1,0},{2,1},{3,2},{4,7},{5,4},{6,5},{7,6},{8,11},{9,8},{10,9... | collective-permute-start | bytes 393224 | tf_op jit(solution)/shard_map/ppermute | solution.py:29
  27.6 8.4 %collective-permute-start.9 = (bf16[256,256]{1,0:T(8,128)(2,1)S(1)}, bf16[256,256]{1,0:T(8,128)(2,1)S(1)}, u32[]{:S(2)}, u32[]{:S(2)}) collective-permute-start(bf16[256,256]{1,0:T(8,128)(2,1)S(1)} %get-tuple-element.47), channel_id=1, source_target_pairs={{0,1},{1,2},{2,3},{3,0},{4,5},{5,6},{6,7},{7,4},{8,9},{9,10},{10,1... | collective-permute-start | bytes 393224 | tf_op jit(solution)/shard_map/ppermute | solution.py:29
  28.3 5.5 %collective-permute-start.12 = (f32[8,128]{1,0:T(8,128)S(1)}, f32[8,128]{1,0:T(8,128)S(1)}, u32[]{:S(2)}, u32[]{:S(2)}) collective-permute-start(f32[8,128]{1,0:T(8,128)S(1)} %get-tuple-element.45.after.refs_0_), channel_id=1, source_target_pairs={{0,3},{1,2},{2,1},{3,0},{4,7},{5,6},{6,5},{7,4},{8,11},{9,10},{10,... | collective-permute-start | bytes 12296 | tf_op jit(solution)/shard_map/ppermute | solution.py:52
  30.1 3.6 %collective-permute-start.11 = (f32[8,128]{1,0:T(8,128)S(1)}, f32[8,128]{1,0:T(8,128)S(1)}, u32[]{:S(2)}, u32[]{:S(2)}) collective-permute-start(f32[8,128]{1,0:T(8,128)S(1)} %get-tuple-element.45.after.refs_0_), channel_id=1, source_target_pairs={{0,2},{1,3},{2,0},{3,1},{4,6},{5,7},{6,4},{7,5},{8,10},{9,11},{10,... | collective-permute-start | bytes 12296 | tf_op jit(solution)/shard_map/ppermute | solution.py:52
  30.6 3.2 %collective-permute-start.10 = (f32[8,128]{1,0:T(8,128)S(1)}, f32[8,128]{1,0:T(8,128)S(1)}, u32[]{:S(2)}, u32[]{:S(2)}) collective-permute-start(f32[8,128]{1,0:T(8,128)S(1)} %get-tuple-element.45.after.refs_0_), channel_id=1, source_target_pairs={{0,1},{1,0},{2,3},{3,2},{4,5},{5,4},{6,7},{7,6},{8,9},{9,8},{10,11... | collective-permute-start | bytes 12296 | tf_op jit(solution)/shard_map/ppermute | solution.py:52
  36.3 3.4 %collective-permute-start.15 = (f32[8,128]{1,0:T(8,128)S(1)}, f32[8,128]{1,0:T(8,128)S(1)}, u32[]{:S(2)}, u32[]{:S(2)}) collective-permute-start(f32[8,128]{1,0:T(8,128)S(1)} %three_cross.1.refs_0_), channel_id=1, source_target_pairs={{0,3},{1,2},{2,1},{3,0},{4,7},{5,6},{6,5},{7,4},{8,11},{9,10},{10,... | collective-permute-start | bytes 12296 | tf_op jit(solution)/shard_map/ppermute | solution.py:52
  37.0 2.7 %collective-permute-start.14 = (f32[8,128]{1,0:T(8,128)S(1)}, f32[8,128]{1,0:T(8,128)S(1)}, u32[]{:S(2)}, u32[]{:S(2)}) collective-permute-start(f32[8,128]{1,0:T(8,128)S(1)} %three_cross.1.refs_0_), channel_id=1, source_target_pairs={{0,2},{1,3},{2,0},{3,1},{4,6},{5,7},{6,4},{7,5},{8,10},{9,11},{10,... | collective-permute-start | bytes 12296 | tf_op jit(solution)/shard_map/ppermute | solution.py:52
  37.6 2.5 %collective-permute-start.13 = (f32[8,128]{1,0:T(8,128)S(1)}, f32[8,128]{1,0:T(8,128)S(1)}, u32[]{:S(2)}, u32[]{:S(2)}) collective-permute-start(f32[8,128]{1,0:T(8,128)S(1)} %three_cross.1.refs_0_), channel_id=1, source_target_pairs={{0,1},{1,0},{2,3},{3,2},{4,5},{5,4},{6,7},{7,6},{8,9},{9,8},{10,11... | collective-permute-start | bytes 12296 | tf_op jit(solution)/shard_map/ppermute | solution.py:52
  42.1 10.0 %collective-permute-start.16 = (bf16[1,1,256,256]{3,2,1,0:T(8,128)(2,1)S(1)}, bf16[1,1,256,256]{3,2,1,0:T(8,128)(2,1)S(1)}, u32[]{:S(2)}, u32[]{:S(2)}) collective-permute-start(bf16[1,1,256,256]{3,2,1,0:T(8,128)(2,1)S(1)} %get-tuple-element.57), channel_id=1, source_target_pairs={{0,4},{4,8},{8,12},{12,16},{16,20},{20,24},{24,28},{1,5},{5,9},{9,... | collective-permute-start | bytes 393224 | tf_op jit(solution)/shard_map/ppermute | solution.py:24

commit v4 on v3

--- a/solution.py
+++ b/solution.py
@@ -6,6 +6,7 @@
 from jax.experimental import pallas as pl
 from jax.experimental.pallas import tpu as pltpu
 from jax.sharding import PartitionSpec as P
+
 
 WD = 2
 NS_STEPS = 3
@@ -229,7 +230,7 @@
     weight_out[0, 0] = product(polar, x, (0, 0)).astype(BF16)
 
 
-def shards(
+def inner_shards(
     left_env, right_env, left_piece, right_piece, guess, inverse_values, precond, sector_rows
 ):
     left, right, prec = left_env[0, 0], right_env[0, 0], precond[0, 0]
@@ -239,10 +240,9 @@
     stats = jax.ShapeDtypeStruct((ROWS, LANES), F32)
     inner = pltpu.VMEM((size, channels * size), BF16)
 
-    def call(kernel, name, outs, *operands, scratch=(), in_specs=None, out_specs=None, cost=None, limit=16 << 20):
+    def call(kernel, outs, *operands, scratch=(), in_specs=None, out_specs=None, cost=None, limit=16 << 20):
         return pl.pallas_call(
             kernel,
-            name=name,
             out_shape=outs,
             in_specs=in_specs or [VMEM] * len(operands),
             out_specs=out_specs or [VMEM] * len(outs),
@@ -252,56 +252,49 @@
         )(*operands)
 
     behind = shift(right_piece[0, 0], "seg", -1)
-    (mask,) = call(
-        mask_kernel, "mask", [matrix], sector_rows[0], in_specs=[SMEM], cost=COVER
-    )
+    prec_below = rotate(prec, "sec", 1)
+    (mask,) = call(mask_kernel, [matrix], sector_rows[0], in_specs=[SMEM], cost=COVER)
     scaled = (left_piece[0, 0].astype(F32) * inverse_values[0]).astype(BF16)
 
-    y, yb = call(start_kernel, "start", [matrix, narrow], scaled, behind, guess[0, 0], mask)
-
-    def half(name, vector_b, pairs, operands, sends):
+    y, yb = call(start_kernel, [matrix, narrow], scaled, behind, guess[0, 0], mask)
+
+    def half(vector_b, pairs, operands, sends):
         outs = [matrix, matrix, stats] + [narrow] * sends
         kernel = functools.partial(lower_kernel, pairs, sends)
         low, diag, stat, *sent = call(
-            kernel, name, outs, left, right, vector_b, *operands, scratch=[inner]
+            kernel, outs, left, right, vector_b, *operands, scratch=[inner]
         )
         return low, diag, stat, rotate(sent[0], "sec", -1) if sends else None
 
-    def joined(name, below, after, diag, above):
-        (up,) = call(
-            raise_kernel, name + "_raise", [matrix], left, right, below, after, scratch=[inner]
-        )
-        return call(join_kernel, name + "_join", [matrix, narrow], diag, up, above, mask)
+    def joined(below, after, diag, above):
+        (up,) = call(raise_kernel, [matrix], left, right, below, after, scratch=[inner])
+        return call(join_kernel, [matrix, narrow], diag, up, above, mask)
 
     y_below = rotate(yb, "sec", 1)
-    low, diag, stat, above = half("one_lower", yb, [(0, 0), (0, None)], [y], 1)
-    prec_below = rotate(prec, "sec", 1)
-    (stat,) = call(cross_kernel, "one_cross", [stats], y_below, low, stat)
+    low, diag, stat, above = half(yb, [(0, 0), (0, None)], [y], 1)
+    (stat,) = call(cross_kernel, [stats], y_below, low, stat)
     parts = exchange(stat, "sec")
-    g, gb = joined("one", y_below, stat, diag, above)
+    g, gb = joined(y_below, stat, diag, above)
     g_below = rotate(gb, "sec", 1)
     kernel = functools.partial(first_kernel, len(parts))
-    p, pb = call(kernel, "first", [matrix, narrow], *parts, y, g, prec)
+    p, pb = call(kernel, [matrix, narrow], *parts, y, g, prec)
 
     pairs = [(0, 0), (0, 1), (0, 2), (2, 2), (2, 1), (2, None)]
-    low, diag, stat, above = half("two_lower", pb, pairs, [y, g, p], 1)
+    low, diag, stat, above = half(pb, pairs, [y, g, p], 1)
     kernel = functools.partial(first_cross_kernel, len(parts))
-    stat, p_below = call(
-        kernel, "two_cross", [stats, narrow], *parts, y_below, g_below, prec_below, low, stat
-    )
+    stat, p_below = call(kernel, [stats, narrow], *parts, y_below, g_below, prec_below, low, stat)
     parts = exchange(stat, "sec")
-    hp, hpb = joined("two", p_below, stat, diag, above)
+    hp, hpb = joined(p_below, stat, diag, above)
     hp_below = rotate(hpb, "sec", 1)
     kernel = functools.partial(second_kernel, len(parts))
     x, g, p, pb, coefficients = call(
-        kernel, "second", [matrix, matrix, matrix, narrow, stats], *parts, y, g, p, hp, prec
+        kernel, [matrix, matrix, matrix, narrow, stats], *parts, y, g, p, hp, prec
     )
 
     pairs = [(0, 2), (2, 2), (2, 1), (2, None)]
-    low, diag, stat, _ = half("three_lower", pb, pairs, [x, g, p], 0)
+    low, diag, stat, _ = half(pb, pairs, [x, g, p], 0)
     (stat,) = call(
         second_cross_kernel,
-        "three_cross",
         [stats],
         y_below, g_below, p_below, hp_below, prec_below, coefficients, low, stat,
     )
@@ -310,7 +303,6 @@
     block = (1, 1, size, size)
     polar, weight, energy = call(
         kernel,
-        "last",
         [
             jax.ShapeDtypeStruct(block, F32),
             jax.ShapeDtypeStruct(block, BF16),
@@ -334,7 +326,7 @@
         P("seg", "sec"),
     )
     return jax.shard_map(
-        shards,
+        inner_shards,
         mesh=mesh,
         in_specs=placed,
         out_specs=(P("seg", "sec", None, None), P("seg", "sec", None, None), P("seg")),

time: 53.8 us -> 53.8 us (level)
  no operation moved by 1% of the time
where the time goes in v4:
time: 53.8 us; the launch traced here: 52.7 us
  starting transfers between devices  24.4 us (45%)
  waiting for transfers between devices  14.9 us (28%)
  Pallas kernels  10.4 us (19%)
  local copies, waits for them, and re-layouts  1.5 us (3%)
  between operations  1.43 us (3%)
    pallas_call x15, Pallas kernels, call(): pl.pallas_call(kernel, out_shape=outs, in_specs=in_specs or [VMEM] * len(...  10.4 us
    ppermute x2, starting transfers between devices, shift(): lax.ppermute(value, axis, [(source, source + steps) for source in range(f...  9.97 us
    ppermute x9, starting transfers between devices, exchange(): parts.append(lax.ppermute(parts[0], axis, pairs))  8.55 us
    ppermute x6, starting transfers between devices, rotate(): lax.ppermute(value, axis, [(source, (source + steps) % count) for source...  5.91 us
    ppermute x2, waiting for transfers between devices, shift(): lax.ppermute(value, axis, [(source, source + steps) for source in range(f...  5.85 us
    ppermute x6, waiting for transfers between devices, rotate(): lax.ppermute(value, axis, [(source, (source + steps) % count) for source...  5.18 us
    ppermute x9, waiting for transfers between devices, exchange(): parts.append(lax.ppermute(parts[0], axis, pairs))  3.85 us
    unnamed x13, local copies, waits for them, and re-layouts  1.5 us
  transfers between devices with their start and end apart: 17, of which 8 were waited for; matrix products, arithmetic and copies ran while one was open for 0% of the time, Pallas kernels for 15%

profile of v4, /device:TPU:1, one launch (start us, length us, event | category | flops | bytes accessed | tf_op | source)
XLA Modules:
  0.0 52.7 jit_solution(902892810202546675)
XLA Ops:
  0.6 1.9 %collective-permute-start = (bf16[256,256]{1,0:T(8,128)(2,1)}, bf16[256,256]{1,0:T(8,128)(2,1)S(1)}, u32[]{:S(2)}, u32[]{:S(2)}) collective-permute-start(bf16[256,256]{1,0:T(8,128)(2,1)} %bitcast.26), channel_id=1, source_target_pairs={{4,0},{8,4},{12,8},{16,12},{20,16},{24,20},{28,24},{5,1},{9,5},{13... | collective-permute-start | bytes 393224 | tf_op jit(solution)/shard_map/ppermute | solution.py:25
  3.3 0.8 %copy-done.4 = bf16[1,1,256,256]{3,2,1,0:T(8,128)(2,1)S(1)} copy-done((bf16[1,1,256,256]{3,2,1,0:T(8,128)(2,1)S(1)}, bf16[1,1,256,256]{3,2,1,0:T(8,128)(2,1)}, u32[]{:S(2)}) %copy-start.4) | copy-done | bytes 131096
  4.1 3.9 %collective-permute-done.behind = bf16[256,256]{1,0:T(8,128)(2,1)S(1)} collective-permute-done((bf16[256,256]{1,0:T(8,128)(2,1)}, bf16[256,256]{1,0:T(8,128)(2,1)S(1)}, u32[]{:S(2)}, u32[]{:S(2)}) %collective-permute-start) | collective-permute-done | bytes 131104 | tf_op jit(solution)/shard_map/ppermute | solution.py:25
  8.3 1.3 %collective-permute-start.1 = (bf16[256,256]{1,0:T(8,128)(2,1)S(1)}, bf16[256,256]{1,0:T(8,128)(2,1)S(1)}, u32[]{:S(2)}, u32[]{:S(2)}) collective-permute-start(bf16[256,256]{1,0:T(8,128)(2,1)S(1)} %get-tuple-element.31.vector_b), channel_id=1, source_target_pairs={{0,1},{1,2},{2,3},{3,0},{4,5},{5,6},{6,7},{7,4},{8,9},{9,10},{10,1... | collective-permute-start | bytes 393224 | tf_op jit(solution)/shard_map/ppermute | solution.py:30
  9.5 1.3 %shard_map.105 = (f32[256,256]{1,0:T(8,128)S(1)}, f32[256,256]{1,0:T(8,128)S(1)}, f32[8,128]{1,0:T(8,128)S(1)}, bf16[256,256]{1,0:T(8,128)(2,1)S(1)}) custom-call(bf16[16,256,256]{2,1,0:T(8,128)(2,1)S(1)} %bitcast.11, bf16[16,256,256]{2,1,0:T(8,128)(2,1)S(1)} %bitcast.16, bf16[256,256]{1,0:T(8,128)(2,1)S(1)} %get-tuple-element.31.vector_b, ...), custom_call_target="tpu_custom_call" | custom-call | tf_op jit(solution)/shard_map/pallas_call | solution.py:244
  10.8 1.2 %collective-permute-start.2 = (bf16[256,256]{1,0:T(8,128)(2,1)S(1)}, bf16[256,256]{1,0:T(8,128)(2,1)S(1)}, u32[]{:S(2)}, u32[]{:S(2)}) collective-permute-start(bf16[256,256]{1,0:T(8,128)(2,1)S(1)} %get-tuple-element.36), channel_id=1, source_target_pairs={{0,3},{1,0},{2,1},{3,2},{4,7},{5,4},{6,5},{7,6},{8,11},{9,8},{10,9... | collective-permute-start | bytes 393224 | tf_op jit(solution)/shard_map/ppermute | solution.py:30
  12.0 1.6 %collective-permute-done.1.below.refs_4_.y = bf16[256,256]{1,0:T(8,128)(2,1)S(1)} collective-permute-done((bf16[256,256]{1,0:T(8,128)(2,1)S(1)}, bf16[256,256]{1,0:T(8,128)(2,1)S(1)}, u32[]{:S(2)}, u32[]{:S(2)}) %collective-permute-start.1) | collective-permute-done | bytes 131104 | tf_op jit(solution)/shard_map/ppermute | solution.py:30
  13.6 1.7 %collective-permute-start.6 = (f32[8,128]{1,0:T(8,128)S(1)}, f32[8,128]{1,0:T(8,128)S(1)}, u32[]{:S(2)}, u32[]{:S(2)}) collective-permute-start(f32[8,128]{1,0:T(8,128)S(1)} %shard_map.106.after.refs_0_), channel_id=1, source_target_pairs={{0,3},{1,2},{2,1},{3,0},{4,7},{5,6},{6,5},{7,4},{8,11},{9,10},{10,... | collective-permute-start | bytes 12296 | tf_op jit(solution)/shard_map/ppermute | solution.py:53
  15.4 0.3 collective-permute-start.5
  15.7 1.1 %collective-permute-start.4 = (f32[8,128]{1,0:T(8,128)S(1)}, f32[8,128]{1,0:T(8,128)S(1)}, u32[]{:S(2)}, u32[]{:S(2)}) collective-permute-start(f32[8,128]{1,0:T(8,128)S(1)} %shard_map.106.after.refs_0_), channel_id=1, source_target_pairs={{0,1},{1,0},{2,3},{3,2},{4,5},{5,4},{6,7},{7,6},{8,9},{9,8},{10,11... | collective-permute-start | bytes 12296 | tf_op jit(solution)/shard_map/ppermute | solution.py:53
  16.8 0.4 collective-permute-start.7
  17.2 1.2 %shard_map.107.up = f32[256,256]{1,0:T(8,128)S(1)} custom-call(bf16[16,256,256]{2,1,0:T(8,128)(2,1)S(1)} %bitcast.12, bf16[16,256,256]{2,1,0:T(8,128)(2,1)S(1)} %bitcast.17, bf16[256,256]{1,0:T(8,128)(2,1)S(1)} %collective-permute-done.1.below.refs_4_.y, f32[8,128]{1,0:T(8,128)S(1)} %shard_map.106.after.refs_0_), custom_call_target="tpu_custom_call" | custom-call | tf_op jit(solution)/shard_map/pallas_call | solution.py:244
  18.5 2.3 %collective-permute-start.3 = (bf16[256,256]{1,0:T(8,128)(2,1)S(1)}, bf16[256,256]{1,0:T(8,128)(2,1)S(1)}, u32[]{:S(2)}, u32[]{:S(2)}) collective-permute-start(bf16[256,256]{1,0:T(8,128)(2,1)S(1)} %get-tuple-element.37), channel_id=1, source_target_pairs={{0,1},{1,2},{2,3},{3,0},{4,5},{5,6},{6,7},{7,4},{8,9},{9,10},{10,1... | collective-permute-start | bytes 393224 | tf_op jit(solution)/shard_map/ppermute | solution.py:30
  21.1 1.3 %shard_map.110 = (f32[256,256]{1,0:T(8,128)S(1)}, f32[256,256]{1,0:T(8,128)S(1)}, f32[8,128]{1,0:T(8,128)S(1)}, bf16[256,256]{1,0:T(8,128)(2,1)S(1)}) custom-call(bf16[16,256,256]{2,1,0:T(8,128)(2,1)S(1)} %bitcast.13, bf16[16,256,256]{2,1,0:T(8,128)(2,1)S(1)} %bitcast.18, bf16[256,256]{1,0:T(8,128)(2,1)S(1)} %get-tuple-element.39.vector_b, ...), custom_call_target="tpu_custom_call" | custom-call | tf_op jit(solution)/shard_map/pallas_call | solution.py:244
  22.5 2.4 %collective-permute-done.3.refs_5_.g = bf16[256,256]{1,0:T(8,128)(2,1)S(1)} collective-permute-done((bf16[256,256]{1,0:T(8,128)(2,1)S(1)}, bf16[256,256]{1,0:T(8,128)(2,1)S(1)}, u32[]{:S(2)}, u32[]{:S(2)}) %collective-permute-start.3) | collective-permute-done | bytes 131104 | tf_op jit(solution)/shard_map/ppermute | solution.py:30
  25.1 1.2 %shard_map.112.up = f32[256,256]{1,0:T(8,128)S(1)} custom-call(bf16[16,256,256]{2,1,0:T(8,128)(2,1)S(1)} %bitcast.14, bf16[16,256,256]{2,1,0:T(8,128)(2,1)S(1)} %bitcast.19, bf16[256,256]{1,0:T(8,128)(2,1)S(1)} %get-tuple-element.43.below.p, f32[8,128]{1,0:T(8,128)S(1)} %get-tuple-element.45.after.refs_0_), custom_call_target="tpu_custom_call" | custom-call | tf_op jit(solution)/shard_map/pallas_call | solution.py:244
  26.3 1.2 %collective-permute-done.8.above = bf16[256,256]{1,0:T(8,128)(2,1)S(1)} collective-permute-done((bf16[256,256]{1,0:T(8,128)(2,1)S(1)}, bf16[256,256]{1,0:T(8,128)(2,1)S(1)}, u32[]{:S(2)}, u32[]{:S(2)}) %collective-permute-start.8) | collective-permute-done | bytes 131104 | tf_op jit(solution)/shard_map/ppermute | solution.py:30
  27.6 0.6 %collective-permute-start.9 = (bf16[256,256]{1,0:T(8,128)(2,1)S(1)}, bf16[256,256]{1,0:T(8,128)(2,1)S(1)}, u32[]{:S(2)}, u32[]{:S(2)}) collective-permute-start(bf16[256,256]{1,0:T(8,128)(2,1)S(1)} %get-tuple-element.47), channel_id=1, source_target_pairs={{0,1},{1,2},{2,3},{3,0},{4,5},{5,6},{6,7},{7,4},{8,9},{9,10},{10,1... | collective-permute-start | bytes 393224 | tf_op jit(solution)/shard_map/ppermute | solution.py:30
  28.3 1.8 %collective-permute-start.12 = (f32[8,128]{1,0:T(8,128)S(1)}, f32[8,128]{1,0:T(8,128)S(1)}, u32[]{:S(2)}, u32[]{:S(2)}) collective-permute-start(f32[8,128]{1,0:T(8,128)S(1)} %get-tuple-element.45.after.refs_0_), channel_id=1, source_target_pairs={{0,3},{1,2},{2,1},{3,0},{4,7},{5,6},{6,5},{7,4},{8,11},{9,10},{10,... | collective-permute-start | bytes 12296 | tf_op jit(solution)/shard_map/ppermute | solution.py:53
  30.1 0.5 collective-permute-start.11
  30.6 0.4 collective-permute-start.10
  30.9 2.8 %collective-permute-done.12.refs_3_ = f32[8,128]{1,0:T(8,128)S(1)} collective-permute-done((f32[8,128]{1,0:T(8,128)S(1)}, f32[8,128]{1,0:T(8,128)S(1)}, u32[]{:S(2)}, u32[]{:S(2)}) %collective-permute-start.12) | collective-permute-done | bytes 4128 | tf_op jit(solution)/shard_map/ppermute | solution.py:53
  33.7 0.4 shard_map.114
  34.1 2.0 %shard_map.115 = (f32[256,256]{1,0:T(8,128)S(1)}, f32[256,256]{1,0:T(8,128)}, f32[8,128]{1,0:T(8,128)S(1)}) custom-call(bf16[16,256,256]{2,1,0:T(8,128)(2,1)S(1)} %bitcast.15, bf16[16,256,256]{2,1,0:T(8,128)(2,1)S(1)} %bitcast.20, bf16[256,256]{1,0:T(8,128)(2,1)S(1)} %get-tuple-element.50.vector_b, f32[256,256]{1,0:T(8,128)S(1)} %get-tuple-element.51.refs_0_.refs_4_, ...), custom_call_target="tpu_custom_call" | custom-call | tf_op jit(solution)/shard_map/pallas_call | solution.py:244
  36.3 0.7 %collective-permute-start.15 = (f32[8,128]{1,0:T(8,128)S(1)}, f32[8,128]{1,0:T(8,128)S(1)}, u32[]{:S(2)}, u32[]{:S(2)}) collective-permute-start(f32[8,128]{1,0:T(8,128)S(1)} %shard_map.116.refs_0_), channel_id=1, source_target_pairs={{0,3},{1,2},{2,1},{3,0},{4,7},{5,6},{6,5},{7,4},{8,11},{9,10},{10,... | collective-permute-start | bytes 12296 | tf_op jit(solution)/shard_map/ppermute | solution.py:53
  37.0 0.6 %collective-permute-start.14 = (f32[8,128]{1,0:T(8,128)S(1)}, f32[8,128]{1,0:T(8,128)S(1)}, u32[]{:S(2)}, u32[]{:S(2)}) collective-permute-start(f32[8,128]{1,0:T(8,128)S(1)} %shard_map.116.refs_0_), channel_id=1, source_target_pairs={{0,2},{1,3},{2,0},{3,1},{4,6},{5,7},{6,4},{7,5},{8,10},{9,11},{10,... | collective-permute-start | bytes 12296 | tf_op jit(solution)/shard_map/ppermute | solution.py:53
  37.6 1.4 %collective-permute-start.13 = (f32[8,128]{1,0:T(8,128)S(1)}, f32[8,128]{1,0:T(8,128)S(1)}, u32[]{:S(2)}, u32[]{:S(2)}) collective-permute-start(f32[8,128]{1,0:T(8,128)S(1)} %shard_map.116.refs_0_), channel_id=1, source_target_pairs={{0,1},{1,0},{2,3},{3,2},{4,5},{5,4},{6,7},{7,6},{8,9},{9,8},{10,11... | collective-permute-start | bytes 12296 | tf_op jit(solution)/shard_map/ppermute | solution.py:53
  39.0 0.7 %collective-permute-done.15.refs_3_ = f32[8,128]{1,0:T(8,128)S(1)} collective-permute-done((f32[8,128]{1,0:T(8,128)S(1)}, f32[8,128]{1,0:T(8,128)S(1)}, u32[]{:S(2)}, u32[]{:S(2)}) %collective-permute-start.15) | collective-permute-done | bytes 4128 | tf_op jit(solution)/shard_map/ppermute | solution.py:53
  40.1 2.0 %shard_map.117 = (f32[1,1,256,256]{3,2,1,0:T(8,128)}, bf16[1,1,256,256]{3,2,1,0:T(8,128)(2,1)S(1)}, f32[1]{0:T(128)}) custom-call(f32[8,128]{1,0:T(8,128)S(1)} %shard_map.116.refs_0_, f32[8,128]{1,0:T(8,128)S(1)} %collective-permute-done.13.refs_1_, f32[8,128]{1,0:T(8,128)S(1)} %collective-permute-done.14.refs_2_, ...), custom_call_target="tpu_custom_call" | custom-call | tf_op jit(solution)/shard_map/pallas_call | solution.py:244
  42.1 8.0 %collective-permute-start.16 = (bf16[1,1,256,256]{3,2,1,0:T(8,128)(2,1)S(1)}, bf16[1,1,256,256]{3,2,1,0:T(8,128)(2,1)S(1)}, u32[]{:S(2)}, u32[]{:S(2)}) collective-permute-start(bf16[1,1,256,256]{3,2,1,0:T(8,128)(2,1)S(1)} %get-tuple-element.57), channel_id=1, source_target_pairs={{0,4},{4,8},{8,12},{12,16},{16,20},{20,24},{24,28},{1,5},{5,9},{9,... | collective-permute-start | bytes 393224 | tf_op jit(solution)/shard_map/ppermute | solution.py:25
  50.1 1.9 %collective-permute-done.16 = bf16[1,1,256,256]{3,2,1,0:T(8,128)(2,1)S(1)} collective-permute-done((bf16[1,1,256,256]{3,2,1,0:T(8,128)(2,1)S(1)}, bf16[1,1,256,256]{3,2,1,0:T(8,128)(2,1)S(1)}, u32[]{:S(2)}, u32[]{:S(2)}) %collective-permute-start.16) | collective-permute-done | bytes 131104 | tf_op jit(solution)/shard_map/ppermute | solution.py:25
  52.1 0.7 %copy.13 = bf16[1,1,256,256]{3,2,1,0:T(8,128)(2,1)} copy(bf16[1,1,256,256]{3,2,1,0:T(8,128)(2,1)S(1)} %collective-permute-done.16) | data formatting | bytes 262144
  (31 shorter events, 1.6 us)
Async XLA Ops:
  0.6 7.4 %collective-permute-start = (bf16[256,256]{1,0:T(8,128)(2,1)}, bf16[256,256]{1,0:T(8,128)(2,1)S(1)}, u32[]{:S(2)}, u32[]{:S(2)}) collective-permute-start(bf16[256,256]{1,0:T(8,128)(2,1)} %bitcast.26), channel_id=1, source_target_pairs={{4,0},{8,4},{12,8},{16,12},{20,16},{24,20},{28,24},{5,1},{9,5},{13... | collective-permute-start | bytes 393224 | tf_op jit(solution)/shard_map/ppermute | solution.py:25
  3.2 0.9 %copy-start.4 = (bf16[1,1,256,256]{3,2,1,0:T(8,128)(2,1)S(1)}, bf16[1,1,256,256]{3,2,1,0:T(8,128)(2,1)}, u32[]{:S(2)}) copy-start(bf16[1,1,256,256]{3,2,1,0:T(8,128)(2,1)} %param.10) | copy-start | bytes 393220
  3.2 0.9 %copy-start.5 = (f32[1,1,256]{2,1,0:T(1,128)S(1)}, f32[1,1,256]{2,1,0:T(1,128)}, u32[]{:S(2)}) copy-start(f32[1,1,256]{2,1,0:T(1,128)} %param.13) | copy-start | bytes 3076
  3.2 4.8 %copy-start.3 = (bf16[1,1,256,256]{3,2,1,0:T(8,128)(2,1)S(1)}, bf16[1,1,256,256]{3,2,1,0:T(8,128)(2,1)}, u32[]{:S(2)}) copy-start(bf16[1,1,256,256]{3,2,1,0:T(8,128)(2,1)} %param.12) | copy-start | bytes 393220
  3.2 6.3 %copy-start = (bf16[1,1,16,256,256]{4,3,2,1,0:T(8,128)(2,1)S(1)}, bf16[1,1,16,256,256]{4,3,2,1,0:T(8,128)(2,1)}, u32[]{:S(2)}) copy-start(bf16[1,1,16,256,256]{4,3,2,1,0:T(8,128)(2,1)} %param.8) | copy-start | bytes 6291460
  3.2 6.3 %copy-start.1 = (bf16[1,1,16,256,256]{4,3,2,1,0:T(8,128)(2,1)S(1)}, bf16[1,1,16,256,256]{4,3,2,1,0:T(8,128)(2,1)}, u32[]{:S(2)}) copy-start(bf16[1,1,16,256,256]{4,3,2,1,0:T(8,128)(2,1)} %param.9) | copy-start | bytes 6291460
  8.3 5.3 %collective-permute-start.1 = (bf16[256,256]{1,0:T(8,128)(2,1)S(1)}, bf16[256,256]{1,0:T(8,128)(2,1)S(1)}, u32[]{:S(2)}, u32[]{:S(2)}) collective-permute-start(bf16[256,256]{1,0:T(8,128)(2,1)S(1)} %get-tuple-element.31.vector_b), channel_id=1, source_target_pairs={{0,1},{1,2},{2,3},{3,0},{4,5},{5,6},{6,7},{7,4},{8,9},{9,10},{10,1... | collective-permute-start | bytes 393224 | tf_op jit(solution)/shard_map/ppermute | solution.py:30
  9.5 7.3 %copy-start.2 = (bf16[1,1,256,256]{3,2,1,0:T(8,128)(2,1)S(1)}, bf16[1,1,256,256]{3,2,1,0:T(8,128)(2,1)}, u32[]{:S(2)}) copy-start(bf16[1,1,256,256]{3,2,1,0:T(8,128)(2,1)} %param.14) | copy-start | bytes 393220
  10.8 7.6 %collective-permute-start.2 = (bf16[256,256]{1,0:T(8,128)(2,1)S(1)}, bf16[256,256]{1,0:T(8,128)(2,1)S(1)}, u32[]{:S(2)}, u32[]{:S(2)}) collective-permute-start(bf16[256,256]{1,0:T(8,128)(2,1)S(1)} %get-tuple-element.36), channel_id=1, source_target_pairs={{0,3},{1,0},{2,1},{3,2},{4,7},{5,4},{6,5},{7,6},{8,11},{9,8},{10,9... | collective-permute-start | bytes 393224 | tf_op jit(solution)/shard_map/ppermute | solution.py:30
  13.6 7.2 %collective-permute-start.6 = (f32[8,128]{1,0:T(8,128)S(1)}, f32[8,128]{1,0:T(8,128)S(1)}, u32[]{:S(2)}, u32[]{:S(2)}) collective-permute-start(f32[8,128]{1,0:T(8,128)S(1)} %shard_map.106.after.refs_0_), channel_id=1, source_target_pairs={{0,3},{1,2},{2,1},{3,0},{4,7},{5,6},{6,5},{7,4},{8,11},{9,10},{10,... | collective-permute-start | bytes 12296 | tf_op jit(solution)/shard_map/ppermute | solution.py:53
  15.4 5.5 %collective-permute-start.5 = (f32[8,128]{1,0:T(8,128)S(1)}, f32[8,128]{1,0:T(8,128)S(1)}, u32[]{:S(2)}, u32[]{:S(2)}) collective-permute-start(f32[8,128]{1,0:T(8,128)S(1)} %shard_map.106.after.refs_0_), channel_id=1, source_target_pairs={{0,2},{1,3},{2,0},{3,1},{4,6},{5,7},{6,4},{7,5},{8,10},{9,11},{10,... | collective-permute-start | bytes 12296 | tf_op jit(solution)/shard_map/ppermute | solution.py:53
  15.7 5.1 %collective-permute-start.4 = (f32[8,128]{1,0:T(8,128)S(1)}, f32[8,128]{1,0:T(8,128)S(1)}, u32[]{:S(2)}, u32[]{:S(2)}) collective-permute-start(f32[8,128]{1,0:T(8,128)S(1)} %shard_map.106.after.refs_0_), channel_id=1, source_target_pairs={{0,1},{1,0},{2,3},{3,2},{4,5},{5,4},{6,7},{7,6},{8,9},{9,8},{10,11... | collective-permute-start | bytes 12296 | tf_op jit(solution)/shard_map/ppermute | solution.py:53
  16.8 5.7 %collective-permute-start.7 = (bf16[256,256]{1,0:T(8,128)(2,1)S(1)}, bf16[256,256]{1,0:T(8,128)(2,1)S(1)}, u32[]{:S(2)}, u32[]{:S(2)}) collective-permute-start(bf16[256,256]{1,0:T(8,128)(2,1)S(1)} %bitcast.21), channel_id=1, source_target_pairs={{0,1},{1,2},{2,3},{3,0},{4,5},{5,6},{6,7},{7,4},{8,9},{9,10},{10,1... | collective-permute-start | bytes 393224 | tf_op jit(solution)/shard_map/ppermute | solution.py:30
  18.5 6.4 %collective-permute-start.3 = (bf16[256,256]{1,0:T(8,128)(2,1)S(1)}, bf16[256,256]{1,0:T(8,128)(2,1)S(1)}, u32[]{:S(2)}, u32[]{:S(2)}) collective-permute-start(bf16[256,256]{1,0:T(8,128)(2,1)S(1)} %get-tuple-element.37), channel_id=1, source_target_pairs={{0,1},{1,2},{2,3},{3,0},{4,5},{5,6},{6,7},{7,4},{8,9},{9,10},{10,1... | collective-permute-start | bytes 393224 | tf_op jit(solution)/shard_map/ppermute | solution.py:30
  22.4 5.2 %collective-permute-start.8 = (bf16[256,256]{1,0:T(8,128)(2,1)S(1)}, bf16[256,256]{1,0:T(8,128)(2,1)S(1)}, u32[]{:S(2)}, u32[]{:S(2)}) collective-permute-start(bf16[256,256]{1,0:T(8,128)(2,1)S(1)} %get-tuple-element.46), channel_id=1, source_target_pairs={{0,3},{1,0},{2,1},{3,2},{4,7},{5,4},{6,5},{7,6},{8,11},{9,8},{10,9... | collective-permute-start | bytes 393224 | tf_op jit(solution)/shard_map/ppermute | solution.py:30
  27.6 8.4 %collective-permute-start.9 = (bf16[256,256]{1,0:T(8,128)(2,1)S(1)}, bf16[256,256]{1,0:T(8,128)(2,1)S(1)}, u32[]{:S(2)}, u32[]{:S(2)}) collective-permute-start(bf16[256,256]{1,0:T(8,128)(2,1)S(1)} %get-tuple-element.47), channel_id=1, source_target_pairs={{0,1},{1,2},{2,3},{3,0},{4,5},{5,6},{6,7},{7,4},{8,9},{9,10},{10,1... | collective-permute-start | bytes 393224 | tf_op jit(solution)/shard_map/ppermute | solution.py:30
  28.3 5.5 %collective-permute-start.12 = (f32[8,128]{1,0:T(8,128)S(1)}, f32[8,128]{1,0:T(8,128)S(1)}, u32[]{:S(2)}, u32[]{:S(2)}) collective-permute-start(f32[8,128]{1,0:T(8,128)S(1)} %get-tuple-element.45.after.refs_0_), channel_id=1, source_target_pairs={{0,3},{1,2},{2,1},{3,0},{4,7},{5,6},{6,5},{7,4},{8,11},{9,10},{10,... | collective-permute-start | bytes 12296 | tf_op jit(solution)/shard_map/ppermute | solution.py:53
  30.1 3.6 %collective-permute-start.11 = (f32[8,128]{1,0:T(8,128)S(1)}, f32[8,128]{1,0:T(8,128)S(1)}, u32[]{:S(2)}, u32[]{:S(2)}) collective-permute-start(f32[8,128]{1,0:T(8,128)S(1)} %get-tuple-element.45.after.refs_0_), channel_id=1, source_target_pairs={{0,2},{1,3},{2,0},{3,1},{4,6},{5,7},{6,4},{7,5},{8,10},{9,11},{10,... | collective-permute-start | bytes 12296 | tf_op jit(solution)/shard_map/ppermute | solution.py:53
  30.6 3.2 %collective-permute-start.10 = (f32[8,128]{1,0:T(8,128)S(1)}, f32[8,128]{1,0:T(8,128)S(1)}, u32[]{:S(2)}, u32[]{:S(2)}) collective-permute-start(f32[8,128]{1,0:T(8,128)S(1)} %get-tuple-element.45.after.refs_0_), channel_id=1, source_target_pairs={{0,1},{1,0},{2,3},{3,2},{4,5},{5,4},{6,7},{7,6},{8,9},{9,8},{10,11... | collective-permute-start | bytes 12296 | tf_op jit(solution)/shard_map/ppermute | solution.py:53
  36.3 3.4 %collective-permute-start.15 = (f32[8,128]{1,0:T(8,128)S(1)}, f32[8,128]{1,0:T(8,128)S(1)}, u32[]{:S(2)}, u32[]{:S(2)}) collective-permute-start(f32[8,128]{1,0:T(8,128)S(1)} %shard_map.116.refs_0_), channel_id=1, source_target_pairs={{0,3},{1,2},{2,1},{3,0},{4,7},{5,6},{6,5},{7,4},{8,11},{9,10},{10,... | collective-permute-start | bytes 12296 | tf_op jit(solution)/shard_map/ppermute | solution.py:53
  37.0 2.7 %collective-permute-start.14 = (f32[8,128]{1,0:T(8,128)S(1)}, f32[8,128]{1,0:T(8,128)S(1)}, u32[]{:S(2)}, u32[]{:S(2)}) collective-permute-start(f32[8,128]{1,0:T(8,128)S(1)} %shard_map.116.refs_0_), channel_id=1, source_target_pairs={{0,2},{1,3},{2,0},{3,1},{4,6},{5,7},{6,4},{7,5},{8,10},{9,11},{10,... | collective-permute-start | bytes 12296 | tf_op jit(solution)/shard_map/ppermute | solution.py:53
  37.6 2.5 %collective-permute-start.13 = (f32[8,128]{1,0:T(8,128)S(1)}, f32[8,128]{1,0:T(8,128)S(1)}, u32[]{:S(2)}, u32[]{:S(2)}) collective-permute-start(f32[8,128]{1,0:T(8,128)S(1)} %shard_map.116.refs_0_), channel_id=1, source_target_pairs={{0,1},{1,0},{2,3},{3,2},{4,5},{5,4},{6,7},{7,6},{8,9},{9,8},{10,11... | collective-permute-start | bytes 12296 | tf_op jit(solution)/shard_map/ppermute | solution.py:53
  42.1 10.0 %collective-permute-start.16 = (bf16[1,1,256,256]{3,2,1,0:T(8,128)(2,1)S(1)}, bf16[1,1,256,256]{3,2,1,0:T(8,128)(2,1)S(1)}, u32[]{:S(2)}, u32[]{:S(2)}) collective-permute-start(bf16[1,1,256,256]{3,2,1,0:T(8,128)(2,1)S(1)} %get-tuple-element.57), channel_id=1, source_target_pairs={{0,4},{4,8},{8,12},{12,16},{16,20},{20,24},{24,28},{1,5},{5,9},{9,... | collective-permute-start | bytes 393224 | tf_op jit(solution)/shard_map/ppermute | solution.py:25

commit v5 on v4

--- a/solution.py
+++ b/solution.py
@@ -16,13 +16,29 @@
 BF16 = jnp.bfloat16
 VMEM = pl.BlockSpec(memory_space=pltpu.VMEM)
 SMEM = pl.BlockSpec(memory_space=pltpu.SMEM)
+SHORT = pl.CostEstimate(flops=0, bytes_accessed=1 << 20, transcendentals=0)
 COVER = pl.CostEstimate(flops=10**10, bytes_accessed=1 << 24, transcendentals=0)
 
 
-def shift(value, axis, steps):
+def swaps(value, axis):
     count = lax.axis_size(axis)
-    first, last = max(0, -steps), min(count, count - steps)
-    return lax.ppermute(value, axis, [(source, source + steps) for source in range(first, last)])
+
+    def partners(first):
+        pairs = {i: i for i in range(count)}
+        for i in range(first, count - 1, 2):
+            pairs[i], pairs[i + 1] = i + 1, i
+        return list(pairs.items())
+
+    far = lax.ppermute(value, axis, partners(1))
+    near = lax.ppermute(value, axis, partners(0))
+    return near, far
+
+
+def pick(near, far, axis, step):
+    place = lax.axis_index(axis)
+    inside = (place + step >= 0) & (place + step < lax.axis_size(axis))
+    paired = lax.rem(place, 2) == (0 if step > 0 else 1)
+    return jnp.where(inside, jnp.where(paired, near, far), jnp.zeros_like(near))
 
 
 def rotate(value, axis, steps):
@@ -92,9 +108,10 @@
     mask_out[...] = jnp.where((idx_r < count) & (idx_c < count), 1.0, 0.0)
 
 
-def start_kernel(scaled, behind, guess, mask, y_ref, yb_ref):
+def start_kernel(scaled, near, far, guess, mask, y_ref, yb_ref):
     size = mask.shape[-1]
-    start = jnp.dot(scaled[...], behind[...], preferred_element_type=F32) + guess[...].astype(F32)
+    behind = pick(near[...], far[...], "seg", 1)
+    start = jnp.dot(scaled[...], behind, preferred_element_type=F32) + guess[...].astype(F32)
     y = mask[...] * start * (1.0 / (1 << (size - 1).bit_length()))
     y_ref[...] = y
     yb_ref[...] = y.astype(BF16)
@@ -226,8 +243,16 @@
         narrow = polar.astype(BF16)
         gram = dot(narrow, narrow, (1, 1)).astype(BF16)
         polar = 1.5 * polar - 0.5 * dot(gram, narrow, (1, 0))
-    polar_out[0, 0] = polar
+    polar_out[...] = polar
     weight_out[0, 0] = product(polar, x, (0, 0)).astype(BF16)
+
+
+def hand_kernel(near, far, out):
+    out[...] = pick(near[...], far[...], "seg", -1)
+
+
+def store_kernel(value, out):
+    out[0, 0] = value[...]
 
 
 def inner_shards(
@@ -251,12 +276,12 @@
             compiler_params=pltpu.CompilerParams(vmem_limit_bytes=limit),
         )(*operands)
 
-    behind = shift(right_piece[0, 0], "seg", -1)
+    near, far = swaps(right_piece[0, 0], "seg")
     prec_below = rotate(prec, "sec", 1)
     (mask,) = call(mask_kernel, [matrix], sector_rows[0], in_specs=[SMEM], cost=COVER)
     scaled = (left_piece[0, 0].astype(F32) * inverse_values[0]).astype(BF16)
 
-    y, yb = call(start_kernel, [matrix, narrow], scaled, behind, guess[0, 0], mask)
+    y, yb = call(start_kernel, [matrix, narrow], scaled, near, far, guess[0, 0], mask)
 
     def half(vector_b, pairs, operands, sends):
         outs = [matrix, matrix, stats] + [narrow] * sends
@@ -304,14 +329,17 @@
     polar, weight, energy = call(
         kernel,
         [
-            jax.ShapeDtypeStruct(block, F32),
+            matrix,
             jax.ShapeDtypeStruct(block, BF16),
             jax.ShapeDtypeStruct((1,), F32),
         ],
         *parts, x, p, coefficients,
         out_specs=[VMEM, VMEM, SMEM],
     )
-    return polar, shift(weight, "seg", 1), energy
+    near, far = swaps(weight, "seg")
+    (handed,) = call(hand_kernel, [jax.ShapeDtypeStruct(block, BF16)], near, far)
+    (polar,) = call(store_kernel, [jax.ShapeDtypeStruct(block, F32)], polar, cost=SHORT)
+    return polar, handed, energy
 
 
 def solution(mesh):

time: 53.8 us -> 55.5 us (1.032); the launches traced: 52.7 us -> 55.3 us
  starting transfers between devices: 24.4 us -> 28.6 us
  waiting for transfers between devices: 14.9 us -> 12.7 us
  Pallas kernels: 10.4 us -> 11.7 us
  local copies, waits for them, and re-layouts: 1.5 us -> 0.85 us
    ppermute x2 -> x4, starting transfers between devices: 9.97 us -> 15.2 us  [the longest x2 15 us: swaps(): far = lax.ppermute(value, axis, partners(1))]
    ppermute x2 -> x4, waiting for transfers between devices: 5.85 us -> 3.03 us  [the longest x2 3.02 us: swaps(): far = lax.ppermute(value, axis, partners(1))]
    pallas_call x15 -> x17, Pallas kernels: 10.4 us -> 11.7 us  [call(): pl.pallas_call(kernel, out_shape=outs, in_specs=in_specs or [VMEM] * len(...]
    ppermute x6, waiting for transfers between devices: 5.18 us -> 6.17 us  [rotate(): lax.ppermute(value, axis, [(source, (source + steps) % count) for source...]
    unnamed x13 -> x12, local copies, waits for them, and re-layouts: 1.5 us -> 0.85 us
  transfers between devices with their start and end apart: 17 -> 19, of which waited for: 8 -> 11; matrix products, arithmetic and copies ran while one was open for 0% -> 0% of each run, Pallas kernels for 15% -> 16%
where the time goes in v5:
time: 55.5 us; the launch traced here: 55.3 us
  starting transfers between devices  28.6 us (52%)
  waiting for transfers between devices  12.7 us (23%)
  Pallas kernels  11.7 us (21%)
  between operations  1.44 us (3%)
  local copies, waits for them, and re-layouts  0.85 us (2%)
    ppermute x2, starting transfers between devices, swaps(): far = lax.ppermute(value, axis, partners(1))  15 us
    pallas_call x17, Pallas kernels, call(): pl.pallas_call(kernel, out_shape=outs, in_specs=in_specs or [VMEM] * len(...  11.7 us
    ppermute x9, starting transfers between devices, exchange(): parts.append(lax.ppermute(parts[0], axis, pairs))  8.07 us
    ppermute x6, waiting for transfers between devices, rotate(): lax.ppermute(value, axis, [(source, (source + steps) % count) for source...  6.17 us
    ppermute x6, starting transfers between devices, rotate(): lax.ppermute(value, axis, [(source, (source + steps) % count) for source...  5.4 us
    ppermute x9, waiting for transfers between devices, exchange(): parts.append(lax.ppermute(parts[0], axis, pairs))  3.48 us
    ppermute x2, waiting for transfers between devices, swaps(): far = lax.ppermute(value, axis, partners(1))  3.02 us
  transfers between devices with their start and end apart: 19, of which 11 were waited for; matrix products, arithmetic and copies ran while one was open for 0% of the time, Pallas kernels for 16%

profile of v5, /device:TPU:1, one launch (start us, length us, event | category | flops | bytes accessed | tf_op | source)
XLA Modules:
  0.0 55.3 jit_solution(1221240467074370670)
XLA Ops:
  0.6 4.6 %collective-permute-start.1 = (bf16[256,256]{1,0:T(8,128)(2,1)}, bf16[256,256]{1,0:T(8,128)(2,1)S(1)}, u32[]{:S(2)}, u32[]{:S(2)}) collective-permute-start(bf16[256,256]{1,0:T(8,128)(2,1)} %bitcast.26), channel_id=1, source_target_pairs={{0,0},{4,8},{8,4},{12,16},{16,12},{20,24},{24,20},{28,28},{1,1},{5... | collective-permute-start | bytes 393224 | tf_op jit(solution)/shard_map/ppermute | solution.py:32
  6.0 0.8 %copy-done.4 = bf16[1,1,256,256]{3,2,1,0:T(8,128)(2,1)S(1)} copy-done((bf16[1,1,256,256]{3,2,1,0:T(8,128)(2,1)S(1)}, bf16[1,1,256,256]{3,2,1,0:T(8,128)(2,1)}, u32[]{:S(2)}) %copy-start.4) | copy-done | bytes 131096
  6.9 1.2 %collective-permute-done.1.far = bf16[256,256]{1,0:T(8,128)(2,1)S(1)} collective-permute-done((bf16[256,256]{1,0:T(8,128)(2,1)}, bf16[256,256]{1,0:T(8,128)(2,1)S(1)}, u32[]{:S(2)}, u32[]{:S(2)}) %collective-permute-start.1) | collective-permute-done | bytes 131104 | tf_op jit(solution)/shard_map/ppermute | solution.py:32
  8.3 1.3 %collective-permute-start.2 = (bf16[256,256]{1,0:T(8,128)(2,1)S(1)}, bf16[256,256]{1,0:T(8,128)(2,1)S(1)}, u32[]{:S(2)}, u32[]{:S(2)}) collective-permute-start(bf16[256,256]{1,0:T(8,128)(2,1)S(1)} %get-tuple-element.31.vector_b), channel_id=1, source_target_pairs={{0,1},{1,2},{2,3},{3,0},{4,5},{5,6},{6,7},{7,4},{8,9},{9,10},{10,1... | collective-permute-start | bytes 393224 | tf_op jit(solution)/shard_map/ppermute | solution.py:46
  9.6 1.3 %shard_map.105 = (f32[256,256]{1,0:T(8,128)S(1)}, f32[256,256]{1,0:T(8,128)S(1)}, f32[8,128]{1,0:T(8,128)S(1)}, bf16[256,256]{1,0:T(8,128)(2,1)S(1)}) custom-call(bf16[16,256,256]{2,1,0:T(8,128)(2,1)S(1)} %bitcast.11, bf16[16,256,256]{2,1,0:T(8,128)(2,1)S(1)} %bitcast.16, bf16[256,256]{1,0:T(8,128)(2,1)S(1)} %get-tuple-element.31.vector_b, ...), custom_call_target="tpu_custom_call" | custom-call | tf_op jit(solution)/shard_map/pallas_call | solution.py:269
  10.8 1.2 %collective-permute-start.3 = (bf16[256,256]{1,0:T(8,128)(2,1)S(1)}, bf16[256,256]{1,0:T(8,128)(2,1)S(1)}, u32[]{:S(2)}, u32[]{:S(2)}) collective-permute-start(bf16[256,256]{1,0:T(8,128)(2,1)S(1)} %get-tuple-element.36), channel_id=1, source_target_pairs={{0,3},{1,0},{2,1},{3,2},{4,7},{5,4},{6,5},{7,6},{8,11},{9,8},{10,9... | collective-permute-start | bytes 393224 | tf_op jit(solution)/shard_map/ppermute | solution.py:46
  12.1 2.3 %collective-permute-done.2.below.refs_4_.y = bf16[256,256]{1,0:T(8,128)(2,1)S(1)} collective-permute-done((bf16[256,256]{1,0:T(8,128)(2,1)S(1)}, bf16[256,256]{1,0:T(8,128)(2,1)S(1)}, u32[]{:S(2)}, u32[]{:S(2)}) %collective-permute-start.2) | collective-permute-done | bytes 131104 | tf_op jit(solution)/shard_map/ppermute | solution.py:46
  14.4 1.3 %collective-permute-start.7 = (f32[8,128]{1,0:T(8,128)S(1)}, f32[8,128]{1,0:T(8,128)S(1)}, u32[]{:S(2)}, u32[]{:S(2)}) collective-permute-start(f32[8,128]{1,0:T(8,128)S(1)} %shard_map.106.after.refs_0_), channel_id=1, source_target_pairs={{0,3},{1,2},{2,1},{3,0},{4,7},{5,6},{6,5},{7,4},{8,11},{9,10},{10,... | collective-permute-start | bytes 12296 | tf_op jit(solution)/shard_map/ppermute | solution.py:69
  16.0 1.1 %collective-permute-start.5 = (f32[8,128]{1,0:T(8,128)S(1)}, f32[8,128]{1,0:T(8,128)S(1)}, u32[]{:S(2)}, u32[]{:S(2)}) collective-permute-start(f32[8,128]{1,0:T(8,128)S(1)} %shard_map.106.after.refs_0_), channel_id=1, source_target_pairs={{0,1},{1,0},{2,3},{3,2},{4,5},{5,4},{6,7},{7,6},{8,9},{9,8},{10,11... | collective-permute-start | bytes 12296 | tf_op jit(solution)/shard_map/ppermute | solution.py:69
  17.2 0.3 collective-permute-start.8
  17.5 1.2 %shard_map.107.up = f32[256,256]{1,0:T(8,128)S(1)} custom-call(bf16[16,256,256]{2,1,0:T(8,128)(2,1)S(1)} %bitcast.12, bf16[16,256,256]{2,1,0:T(8,128)(2,1)S(1)} %bitcast.17, bf16[256,256]{1,0:T(8,128)(2,1)S(1)} %collective-permute-done.2.below.refs_4_.y, f32[8,128]{1,0:T(8,128)S(1)} %shard_map.106.after.refs_0_), custom_call_target="tpu_custom_call" | custom-call | tf_op jit(solution)/shard_map/pallas_call | solution.py:269
  18.8 2.2 %collective-permute-start.4 = (bf16[256,256]{1,0:T(8,128)(2,1)S(1)}, bf16[256,256]{1,0:T(8,128)(2,1)S(1)}, u32[]{:S(2)}, u32[]{:S(2)}) collective-permute-start(bf16[256,256]{1,0:T(8,128)(2,1)S(1)} %get-tuple-element.37), channel_id=1, source_target_pairs={{0,1},{1,2},{2,3},{3,0},{4,5},{5,6},{6,7},{7,4},{8,9},{9,10},{10,1... | collective-permute-start | bytes 393224 | tf_op jit(solution)/shard_map/ppermute | solution.py:46
  21.2 1.3 %shard_map.110 = (f32[256,256]{1,0:T(8,128)S(1)}, f32[256,256]{1,0:T(8,128)S(1)}, f32[8,128]{1,0:T(8,128)S(1)}, bf16[256,256]{1,0:T(8,128)(2,1)S(1)}) custom-call(bf16[16,256,256]{2,1,0:T(8,128)(2,1)S(1)} %bitcast.13, bf16[16,256,256]{2,1,0:T(8,128)(2,1)S(1)} %bitcast.18, bf16[256,256]{1,0:T(8,128)(2,1)S(1)} %get-tuple-element.39.vector_b, ...), custom_call_target="tpu_custom_call" | custom-call | tf_op jit(solution)/shard_map/pallas_call | solution.py:269
  22.8 2.5 %collective-permute-done.4.refs_5_.g = bf16[256,256]{1,0:T(8,128)(2,1)S(1)} collective-permute-done((bf16[256,256]{1,0:T(8,128)(2,1)S(1)}, bf16[256,256]{1,0:T(8,128)(2,1)S(1)}, u32[]{:S(2)}, u32[]{:S(2)}) %collective-permute-start.4) | collective-permute-done | bytes 131104 | tf_op jit(solution)/shard_map/ppermute | solution.py:46
  25.5 1.2 %shard_map.112.up = f32[256,256]{1,0:T(8,128)S(1)} custom-call(bf16[16,256,256]{2,1,0:T(8,128)(2,1)S(1)} %bitcast.14, bf16[16,256,256]{2,1,0:T(8,128)(2,1)S(1)} %bitcast.19, bf16[256,256]{1,0:T(8,128)(2,1)S(1)} %get-tuple-element.43.below.p, f32[8,128]{1,0:T(8,128)S(1)} %get-tuple-element.45.after.refs_0_), custom_call_target="tpu_custom_call" | custom-call | tf_op jit(solution)/shard_map/pallas_call | solution.py:269
  26.7 1.4 %collective-permute-done.9.above = bf16[256,256]{1,0:T(8,128)(2,1)S(1)} collective-permute-done((bf16[256,256]{1,0:T(8,128)(2,1)S(1)}, bf16[256,256]{1,0:T(8,128)(2,1)S(1)}, u32[]{:S(2)}, u32[]{:S(2)}) %collective-permute-start.9) | collective-permute-done | bytes 131104 | tf_op jit(solution)/shard_map/ppermute | solution.py:46
  28.3 2.3 %collective-permute-start.13 = (f32[8,128]{1,0:T(8,128)S(1)}, f32[8,128]{1,0:T(8,128)S(1)}, u32[]{:S(2)}, u32[]{:S(2)}) collective-permute-start(f32[8,128]{1,0:T(8,128)S(1)} %get-tuple-element.45.after.refs_0_), channel_id=1, source_target_pairs={{0,3},{1,2},{2,1},{3,0},{4,7},{5,6},{6,5},{7,4},{8,11},{9,10},{10,... | collective-permute-start | bytes 12296 | tf_op jit(solution)/shard_map/ppermute | solution.py:69
  30.6 0.3 collective-permute-start.12
  30.9 2.0 %collective-permute-done.13.refs_3_ = f32[8,128]{1,0:T(8,128)S(1)} collective-permute-done((f32[8,128]{1,0:T(8,128)S(1)}, f32[8,128]{1,0:T(8,128)S(1)}, u32[]{:S(2)}, u32[]{:S(2)}) %collective-permute-start.13) | collective-permute-done | bytes 4128 | tf_op jit(solution)/shard_map/ppermute | solution.py:69
  33.0 0.3 collective-permute-done.11.refs_1_
  33.3 0.4 shard_map.114
  33.6 2.0 %shard_map.115 = (f32[256,256]{1,0:T(8,128)S(1)}, f32[256,256]{1,0:T(8,128)}, f32[8,128]{1,0:T(8,128)S(1)}) custom-call(bf16[16,256,256]{2,1,0:T(8,128)(2,1)S(1)} %bitcast.15, bf16[16,256,256]{2,1,0:T(8,128)(2,1)S(1)} %bitcast.20, bf16[256,256]{1,0:T(8,128)(2,1)S(1)} %get-tuple-element.50.vector_b, f32[256,256]{1,0:T(8,128)S(1)} %get-tuple-element.51.refs_0_.refs_4_, ...), custom_call_target="tpu_custom_call" | custom-call | tf_op jit(solution)/shard_map/pallas_call | solution.py:269
  35.6 0.2 shard_map.116.refs_0_
  35.9 1.3 %collective-permute-start.16 = (f32[8,128]{1,0:T(8,128)S(1)}, f32[8,128]{1,0:T(8,128)S(1)}, u32[]{:S(2)}, u32[]{:S(2)}) collective-permute-start(f32[8,128]{1,0:T(8,128)S(1)} %shard_map.116.refs_0_), channel_id=1, source_target_pairs={{0,3},{1,2},{2,1},{3,0},{4,7},{5,6},{6,5},{7,4},{8,11},{9,10},{10,... | collective-permute-start | bytes 12296 | tf_op jit(solution)/shard_map/ppermute | solution.py:69
  37.2 1.3 %collective-permute-start.14 = (f32[8,128]{1,0:T(8,128)S(1)}, f32[8,128]{1,0:T(8,128)S(1)}, u32[]{:S(2)}, u32[]{:S(2)}) collective-permute-start(f32[8,128]{1,0:T(8,128)S(1)} %shard_map.116.refs_0_), channel_id=1, source_target_pairs={{0,1},{1,0},{2,3},{3,2},{4,5},{5,4},{6,7},{7,6},{8,9},{9,8},{10,11... | collective-permute-start | bytes 12296 | tf_op jit(solution)/shard_map/ppermute | solution.py:69
  38.6 0.7 %collective-permute-done.16.refs_3_ = f32[8,128]{1,0:T(8,128)S(1)} collective-permute-done((f32[8,128]{1,0:T(8,128)S(1)}, f32[8,128]{1,0:T(8,128)S(1)}, u32[]{:S(2)}, u32[]{:S(2)}) %collective-permute-start.16) | collective-permute-done | bytes 4128 | tf_op jit(solution)/shard_map/ppermute | solution.py:69
  39.3 0.4 collective-permute-done.15.refs_2_
  39.7 1.8 %shard_map.117 = (f32[256,256]{1,0:T(8,128)S(1)}, bf16[1,1,256,256]{3,2,1,0:T(8,128)(2,1)S(1)}, f32[1]{0:T(128)}) custom-call(f32[8,128]{1,0:T(8,128)S(1)} %shard_map.116.refs_0_, f32[8,128]{1,0:T(8,128)S(1)} %collective-permute-done.14.refs_1_, f32[8,128]{1,0:T(8,128)S(1)} %collective-permute-done.15.refs_2_, f32[8,128]{1,0:T(8,128)S(1)} %collective-permute-done.16.refs_3_, ...), custom_call_target="tpu_custom_call" | custom-call | tf_op jit(solution)/shard_map/pallas_call | solution.py:269
  41.5 10.4 %collective-permute-start.18 = (bf16[1,1,256,256]{3,2,1,0:T(8,128)(2,1)S(1)}, bf16[1,1,256,256]{3,2,1,0:T(8,128)(2,1)S(1)}, u32[]{:S(2)}, u32[]{:S(2)}) collective-permute-start(bf16[1,1,256,256]{3,2,1,0:T(8,128)(2,1)S(1)} %get-tuple-element.57), channel_id=1, source_target_pairs={{0,0},{4,8},{8,4},{12,16},{16,12},{20,24},{24,20},{28,28},{1,1},{5... | collective-permute-start | bytes 393224 | tf_op jit(solution)/shard_map/ppermute | solution.py:32
  52.1 0.7 %shard_map.118 = f32[1,1,256,256]{3,2,1,0:T(8,128)} custom-call(f32[256,256]{1,0:T(8,128)S(1)} %get-tuple-element.56.value), custom_call_target="tpu_custom_call" | custom-call | bytes 1048576 | tf_op jit(solution)/shard_map/pallas_call | solution.py:269
  52.8 1.8 %collective-permute-done.18.far = bf16[1,1,256,256]{3,2,1,0:T(8,128)(2,1)S(1)} collective-permute-done((bf16[1,1,256,256]{3,2,1,0:T(8,128)(2,1)S(1)}, bf16[1,1,256,256]{3,2,1,0:T(8,128)(2,1)S(1)}, u32[]{:S(2)}, u32[]{:S(2)}) %collective-permute-start.18) | collective-permute-done | bytes 131104 | tf_op jit(solution)/shard_map/ppermute | solution.py:32
  54.6 0.7 %shard_map.119 = bf16[1,1,256,256]{3,2,1,0:T(8,128)(2,1)} custom-call(bf16[1,1,256,256]{3,2,1,0:T(8,128)(2,1)S(1)} %collective-permute-done.17.near, bf16[1,1,256,256]{3,2,1,0:T(8,128)(2,1)S(1)} %collective-permute-done.18.far), custom_call_target="tpu_custom_call" | custom-call | tf_op jit(solution)/shard_map/pallas_call | solution.py:269
  (36 shorter events, 2.0 us)
Async XLA Ops:
  0.6 7.4 %collective-permute-start.1 = (bf16[256,256]{1,0:T(8,128)(2,1)}, bf16[256,256]{1,0:T(8,128)(2,1)S(1)}, u32[]{:S(2)}, u32[]{:S(2)}) collective-permute-start(bf16[256,256]{1,0:T(8,128)(2,1)} %bitcast.26), channel_id=1, source_target_pairs={{0,0},{4,8},{8,4},{12,16},{16,12},{20,24},{24,20},{28,28},{1,1},{5... | collective-permute-start | bytes 393224 | tf_op jit(solution)/shard_map/ppermute | solution.py:32
  5.2 2.9 %collective-permute-start = (bf16[256,256]{1,0:T(8,128)(2,1)}, bf16[256,256]{1,0:T(8,128)(2,1)S(1)}, u32[]{:S(2)}, u32[]{:S(2)}) collective-permute-start(bf16[256,256]{1,0:T(8,128)(2,1)} %bitcast.27), channel_id=1, source_target_pairs={{0,4},{4,0},{8,12},{12,8},{16,20},{20,16},{24,28},{28,24},{1,5},{5... | collective-permute-start | bytes 393224 | tf_op jit(solution)/shard_map/ppermute | solution.py:33
  5.9 0.9 %copy-start.4 = (bf16[1,1,256,256]{3,2,1,0:T(8,128)(2,1)S(1)}, bf16[1,1,256,256]{3,2,1,0:T(8,128)(2,1)}, u32[]{:S(2)}) copy-start(bf16[1,1,256,256]{3,2,1,0:T(8,128)(2,1)} %param.10) | copy-start | bytes 393220
  6.0 0.9 %copy-start.5 = (f32[1,1,256]{2,1,0:T(1,128)S(1)}, f32[1,1,256]{2,1,0:T(1,128)}, u32[]{:S(2)}) copy-start(f32[1,1,256]{2,1,0:T(1,128)} %param.13) | copy-start | bytes 3076
  6.0 2.1 %copy-start.3 = (bf16[1,1,256,256]{3,2,1,0:T(8,128)(2,1)S(1)}, bf16[1,1,256,256]{3,2,1,0:T(8,128)(2,1)}, u32[]{:S(2)}) copy-start(bf16[1,1,256,256]{3,2,1,0:T(8,128)(2,1)} %param.12) | copy-start | bytes 393220
  6.0 3.6 %copy-start = (bf16[1,1,16,256,256]{4,3,2,1,0:T(8,128)(2,1)S(1)}, bf16[1,1,16,256,256]{4,3,2,1,0:T(8,128)(2,1)}, u32[]{:S(2)}) copy-start(bf16[1,1,16,256,256]{4,3,2,1,0:T(8,128)(2,1)} %param.8) | copy-start | bytes 6291460
  6.0 3.6 %copy-start.1 = (bf16[1,1,16,256,256]{4,3,2,1,0:T(8,128)(2,1)S(1)}, bf16[1,1,16,256,256]{4,3,2,1,0:T(8,128)(2,1)}, u32[]{:S(2)}) copy-start(bf16[1,1,16,256,256]{4,3,2,1,0:T(8,128)(2,1)} %param.9) | copy-start | bytes 6291460
  8.3 6.1 %collective-permute-start.2 = (bf16[256,256]{1,0:T(8,128)(2,1)S(1)}, bf16[256,256]{1,0:T(8,128)(2,1)S(1)}, u32[]{:S(2)}, u32[]{:S(2)}) collective-permute-start(bf16[256,256]{1,0:T(8,128)(2,1)S(1)} %get-tuple-element.31.vector_b), channel_id=1, source_target_pairs={{0,1},{1,2},{2,3},{3,0},{4,5},{5,6},{6,7},{7,4},{8,9},{9,10},{10,1... | collective-permute-start | bytes 393224 | tf_op jit(solution)/shard_map/ppermute | solution.py:46
  9.6 7.6 %copy-start.2 = (bf16[1,1,256,256]{3,2,1,0:T(8,128)(2,1)S(1)}, bf16[1,1,256,256]{3,2,1,0:T(8,128)(2,1)}, u32[]{:S(2)}) copy-start(bf16[1,1,256,256]{3,2,1,0:T(8,128)(2,1)} %param.14) | copy-start | bytes 393220
  10.8 7.9 %collective-permute-start.3 = (bf16[256,256]{1,0:T(8,128)(2,1)S(1)}, bf16[256,256]{1,0:T(8,128)(2,1)S(1)}, u32[]{:S(2)}, u32[]{:S(2)}) collective-permute-start(bf16[256,256]{1,0:T(8,128)(2,1)S(1)} %get-tuple-element.36), channel_id=1, source_target_pairs={{0,3},{1,0},{2,1},{3,2},{4,7},{5,4},{6,5},{7,6},{8,11},{9,8},{10,9... | collective-permute-start | bytes 393224 | tf_op jit(solution)/shard_map/ppermute | solution.py:46
  14.4 6.6 %collective-permute-start.7 = (f32[8,128]{1,0:T(8,128)S(1)}, f32[8,128]{1,0:T(8,128)S(1)}, u32[]{:S(2)}, u32[]{:S(2)}) collective-permute-start(f32[8,128]{1,0:T(8,128)S(1)} %shard_map.106.after.refs_0_), channel_id=1, source_target_pairs={{0,3},{1,2},{2,1},{3,0},{4,7},{5,6},{6,5},{7,4},{8,11},{9,10},{10,... | collective-permute-start | bytes 12296 | tf_op jit(solution)/shard_map/ppermute | solution.py:69
  15.8 5.3 %collective-permute-start.6 = (f32[8,128]{1,0:T(8,128)S(1)}, f32[8,128]{1,0:T(8,128)S(1)}, u32[]{:S(2)}, u32[]{:S(2)}) collective-permute-start(f32[8,128]{1,0:T(8,128)S(1)} %shard_map.106.after.refs_0_), channel_id=1, source_target_pairs={{0,2},{1,3},{2,0},{3,1},{4,6},{5,7},{6,4},{7,5},{8,10},{9,11},{10,... | collective-permute-start | bytes 12296 | tf_op jit(solution)/shard_map/ppermute | solution.py:69
  16.0 5.0 %collective-permute-start.5 = (f32[8,128]{1,0:T(8,128)S(1)}, f32[8,128]{1,0:T(8,128)S(1)}, u32[]{:S(2)}, u32[]{:S(2)}) collective-permute-start(f32[8,128]{1,0:T(8,128)S(1)} %shard_map.106.after.refs_0_), channel_id=1, source_target_pairs={{0,1},{1,0},{2,3},{3,2},{4,5},{5,4},{6,7},{7,6},{8,9},{9,8},{10,11... | collective-permute-start | bytes 12296 | tf_op jit(solution)/shard_map/ppermute | solution.py:69
  17.2 5.6 %collective-permute-start.8 = (bf16[256,256]{1,0:T(8,128)(2,1)S(1)}, bf16[256,256]{1,0:T(8,128)(2,1)S(1)}, u32[]{:S(2)}, u32[]{:S(2)}) collective-permute-start(bf16[256,256]{1,0:T(8,128)(2,1)S(1)} %bitcast.21), channel_id=1, source_target_pairs={{0,1},{1,2},{2,3},{3,0},{4,5},{5,6},{6,7},{7,4},{8,9},{9,10},{10,1... | collective-permute-start | bytes 393224 | tf_op jit(solution)/shard_map/ppermute | solution.py:46
  18.8 6.5 %collective-permute-start.4 = (bf16[256,256]{1,0:T(8,128)(2,1)S(1)}, bf16[256,256]{1,0:T(8,128)(2,1)S(1)}, u32[]{:S(2)}, u32[]{:S(2)}) collective-permute-start(bf16[256,256]{1,0:T(8,128)(2,1)S(1)} %get-tuple-element.37), channel_id=1, source_target_pairs={{0,1},{1,2},{2,3},{3,0},{4,5},{5,6},{6,7},{7,4},{8,9},{9,10},{10,1... | collective-permute-start | bytes 393224 | tf_op jit(solution)/shard_map/ppermute | solution.py:46
  22.5 5.5 %collective-permute-start.9 = (bf16[256,256]{1,0:T(8,128)(2,1)S(1)}, bf16[256,256]{1,0:T(8,128)(2,1)S(1)}, u32[]{:S(2)}, u32[]{:S(2)}) collective-permute-start(bf16[256,256]{1,0:T(8,128)(2,1)S(1)} %get-tuple-element.46), channel_id=1, source_target_pairs={{0,3},{1,0},{2,1},{3,2},{4,7},{5,4},{6,5},{7,6},{8,11},{9,8},{10,9... | collective-permute-start | bytes 393224 | tf_op jit(solution)/shard_map/ppermute | solution.py:46
  28.1 7.5 %collective-permute-start.10 = (bf16[256,256]{1,0:T(8,128)(2,1)S(1)}, bf16[256,256]{1,0:T(8,128)(2,1)S(1)}, u32[]{:S(2)}, u32[]{:S(2)}) collective-permute-start(bf16[256,256]{1,0:T(8,128)(2,1)S(1)} %get-tuple-element.47), channel_id=1, source_target_pairs={{0,1},{1,2},{2,3},{3,0},{4,5},{5,6},{6,7},{7,4},{8,9},{9,10},{10,1... | collective-permute-start | bytes 393224 | tf_op jit(solution)/shard_map/ppermute | solution.py:46
  28.3 4.7 %collective-permute-start.13 = (f32[8,128]{1,0:T(8,128)S(1)}, f32[8,128]{1,0:T(8,128)S(1)}, u32[]{:S(2)}, u32[]{:S(2)}) collective-permute-start(f32[8,128]{1,0:T(8,128)S(1)} %get-tuple-element.45.after.refs_0_), channel_id=1, source_target_pairs={{0,3},{1,2},{2,1},{3,0},{4,7},{5,6},{6,5},{7,4},{8,11},{9,10},{10,... | collective-permute-start | bytes 12296 | tf_op jit(solution)/shard_map/ppermute | solution.py:69
  30.6 2.5 %collective-permute-start.12 = (f32[8,128]{1,0:T(8,128)S(1)}, f32[8,128]{1,0:T(8,128)S(1)}, u32[]{:S(2)}, u32[]{:S(2)}) collective-permute-start(f32[8,128]{1,0:T(8,128)S(1)} %get-tuple-element.45.after.refs_0_), channel_id=1, source_target_pairs={{0,2},{1,3},{2,0},{3,1},{4,6},{5,7},{6,4},{7,5},{8,10},{9,11},{10,... | collective-permute-start | bytes 12296 | tf_op jit(solution)/shard_map/ppermute | solution.py:69
  30.8 2.5 %collective-permute-start.11 = (f32[8,128]{1,0:T(8,128)S(1)}, f32[8,128]{1,0:T(8,128)S(1)}, u32[]{:S(2)}, u32[]{:S(2)}) collective-permute-start(f32[8,128]{1,0:T(8,128)S(1)} %get-tuple-element.45.after.refs_0_), channel_id=1, source_target_pairs={{0,1},{1,0},{2,3},{3,2},{4,5},{5,4},{6,7},{7,6},{8,9},{9,8},{10,11... | collective-permute-start | bytes 12296 | tf_op jit(solution)/shard_map/ppermute | solution.py:69
  35.9 3.4 %collective-permute-start.16 = (f32[8,128]{1,0:T(8,128)S(1)}, f32[8,128]{1,0:T(8,128)S(1)}, u32[]{:S(2)}, u32[]{:S(2)}) collective-permute-start(f32[8,128]{1,0:T(8,128)S(1)} %shard_map.116.refs_0_), channel_id=1, source_target_pairs={{0,3},{1,2},{2,1},{3,0},{4,7},{5,6},{6,5},{7,4},{8,11},{9,10},{10,... | collective-permute-start | bytes 12296 | tf_op jit(solution)/shard_map/ppermute | solution.py:69
  37.2 2.5 %collective-permute-start.15 = (f32[8,128]{1,0:T(8,128)S(1)}, f32[8,128]{1,0:T(8,128)S(1)}, u32[]{:S(2)}, u32[]{:S(2)}) collective-permute-start(f32[8,128]{1,0:T(8,128)S(1)} %shard_map.116.refs_0_), channel_id=1, source_target_pairs={{0,2},{1,3},{2,0},{3,1},{4,6},{5,7},{6,4},{7,5},{8,10},{9,11},{10,... | collective-permute-start | bytes 12296 | tf_op jit(solution)/shard_map/ppermute | solution.py:69
  37.2 2.5 %collective-permute-start.14 = (f32[8,128]{1,0:T(8,128)S(1)}, f32[8,128]{1,0:T(8,128)S(1)}, u32[]{:S(2)}, u32[]{:S(2)}) collective-permute-start(f32[8,128]{1,0:T(8,128)S(1)} %shard_map.116.refs_0_), channel_id=1, source_target_pairs={{0,1},{1,0},{2,3},{3,2},{4,5},{5,4},{6,7},{7,6},{8,9},{9,8},{10,11... | collective-permute-start | bytes 12296 | tf_op jit(solution)/shard_map/ppermute | solution.py:69
  41.5 13.1 %collective-permute-start.18 = (bf16[1,1,256,256]{3,2,1,0:T(8,128)(2,1)S(1)}, bf16[1,1,256,256]{3,2,1,0:T(8,128)(2,1)S(1)}, u32[]{:S(2)}, u32[]{:S(2)}) collective-permute-start(bf16[1,1,256,256]{3,2,1,0:T(8,128)(2,1)S(1)} %get-tuple-element.57), channel_id=1, source_target_pairs={{0,0},{4,8},{8,4},{12,16},{16,12},{20,24},{24,20},{28,28},{1,1},{5... | collective-permute-start | bytes 393224 | tf_op jit(solution)/shard_map/ppermute | solution.py:32
  52.0 2.6 %collective-permute-start.17 = (bf16[1,1,256,256]{3,2,1,0:T(8,128)(2,1)S(1)}, bf16[1,1,256,256]{3,2,1,0:T(8,128)(2,1)S(1)}, u32[]{:S(2)}, u32[]{:S(2)}) collective-permute-start(bf16[1,1,256,256]{3,2,1,0:T(8,128)(2,1)S(1)} %get-tuple-element.57), channel_id=1, source_target_pairs={{0,4},{4,0},{8,12},{12,8},{16,20},{20,16},{24,28},{28,24},{1,5},{5... | collective-permute-start | bytes 393224 | tf_op jit(solution)/shard_map/ppermute | solution.py:33

commit v6 on v4

--- a/solution.py
+++ b/solution.py
@@ -16,6 +16,7 @@
 BF16 = jnp.bfloat16
 VMEM = pl.BlockSpec(memory_space=pltpu.VMEM)
 SMEM = pl.BlockSpec(memory_space=pltpu.SMEM)
+SHORT = pl.CostEstimate(flops=0, bytes_accessed=1 << 20, transcendentals=0)
 COVER = pl.CostEstimate(flops=10**10, bytes_accessed=1 << 24, transcendentals=0)
 
 
@@ -23,6 +24,14 @@
     count = lax.axis_size(axis)
     first, last = max(0, -steps), min(count, count - steps)
     return lax.ppermute(value, axis, [(source, source + steps) for source in range(first, last)])
+
+
+def swap(value, axis, first):
+    count = lax.axis_size(axis)
+    pairs = {i: i for i in range(count)}
+    for i in range(first, count - 1, 2):
+        pairs[i], pairs[i + 1] = i + 1, i
+    return lax.ppermute(value, axis, list(pairs.items()))
 
 
 def rotate(value, axis, steps):
@@ -101,17 +110,17 @@
 
 
 def lower_kernel(pairs, sends, left, right, vector_b, *refs):
-    ops, outs = refs[: len(refs) - 4 - sends], refs[len(refs) - 4 - sends :]
-    inner = outs[-1]
-    low_ref, diag_ref, stat_ref = outs[:3]
+    outs = refs[-5 if sends else -3 :]
+    ops, inner = refs[: len(refs) - len(outs)], refs[-1]
+    low_ref, stat_ref = outs[:2]
     channels = left.shape[0]
     value = vector_b[...]
     low = sandwich(left, right, value, inner, WD, channels)
     low_ref[...] = low
+    diag = sandwich(left, right, value, inner, 0, WD)
     if sends:
+        outs[2][...] = diag
         outs[3][...] = low.astype(BF16)
-    diag = sandwich(left, right, value, inner, 0, WD)
-    diag_ref[...] = diag
     stat_ref[...] = jnp.zeros(stat_ref.shape, F32)
     for row, (one, two) in enumerate(pairs):
         other = diag if two is None else ops[two][...]
@@ -207,10 +216,8 @@
     )
 
 
-def last_kernel(parts, *refs):
-    x_ref, p_ref, coefficients = refs[parts : parts + 3]
-    polar_out, weight_out, lam_out = refs[parts + 3 :]
-    xp, pp, pg, php = scalars(refs[:parts], 4)
+def finish(sums, x_ref, p_ref, coefficients):
+    xp, pp, pg, php = sums
     a = coefficients[2:3, 0:1]
     qq = pp - xp * xp
     b = (pg - xp * a) / jnp.sqrt(qq)
@@ -218,16 +225,60 @@
     lam, u, w = ritz(a, b, c)
     along_p = w / jnp.sqrt(qq)
     along_x = u - along_p * xp
-    lam_out[0] = lam[0, 0]
-    x = along_x * x_ref[...] + along_p * p_ref[...]
+    return lam, along_x * x_ref[...] + along_p * p_ref[...]
+
+
+def polarise(x, polar_out, weight_out):
     frob = jnp.sum(jnp.sum(x * x, axis=0, keepdims=True), axis=1, keepdims=True)
     polar = x * lax.rsqrt(frob + 1e-06)
     for _ in range(NS_STEPS):
         narrow = polar.astype(BF16)
         gram = dot(narrow, narrow, (1, 1)).astype(BF16)
         polar = 1.5 * polar - 0.5 * dot(gram, narrow, (1, 0))
-    polar_out[0, 0] = polar
+    polar_out[...] = polar
     weight_out[0, 0] = product(polar, x, (0, 0)).astype(BF16)
+
+
+def odd_segment():
+    return lax.rem(lax.axis_index("seg"), 2) == 1
+
+
+def odd_kernel(parts, *refs):
+    x_ref, p_ref, coefficients, polar_out, weight_out = refs[parts:]
+
+    @pl.when(odd_segment())
+    def _():
+        _, x = finish(scalars(refs[:parts], 4), x_ref, p_ref, coefficients)
+        polarise(x, polar_out, weight_out)
+
+    @pl.when(jnp.logical_not(odd_segment()))
+    def _():
+        weight_out[...] = jnp.zeros_like(weight_out)
+
+
+def even_kernel(parts, *refs):
+    x_ref, p_ref, coefficients, _, polar_out, weight_out, lam_out = refs[parts:]
+
+    @pl.when(jnp.logical_not(odd_segment()))
+    def _():
+        lam, x = finish(scalars(refs[:parts], 4), x_ref, p_ref, coefficients)
+        lam_out[0] = lam[0, 0]
+        polarise(x, polar_out, weight_out)
+
+    @pl.when(odd_segment())
+    def _():
+        lam, _ = finish(scalars(refs[:parts], 4), x_ref, p_ref, coefficients)
+        lam_out[0] = lam[0, 0]
+        weight_out[...] = jnp.zeros_like(weight_out)
+
+
+def hand_kernel(near, far, out):
+    value = jnp.where(odd_segment(), near[...], far[...])
+    out[...] = jnp.where(lax.axis_index("seg") > 0, value, jnp.zeros_like(value))
+
+
+def store_kernel(value, out):
+    out[0, 0] = value[...]
 
 
 def inner_shards(
@@ -240,7 +291,7 @@
     stats = jax.ShapeDtypeStruct((ROWS, LANES), F32)
     inner = pltpu.VMEM((size, channels * size), BF16)
 
-    def call(kernel, outs, *operands, scratch=(), in_specs=None, out_specs=None, cost=None, limit=16 << 20):
+    def call(kernel, outs, *operands, scratch=(), in_specs=None, out_specs=None, cost=None, aliases=None):
         return pl.pallas_call(
             kernel,
             out_shape=outs,
@@ -248,7 +299,8 @@
             out_specs=out_specs or [VMEM] * len(outs),
             scratch_shapes=list(scratch),
             cost_estimate=cost,
-            compiler_params=pltpu.CompilerParams(vmem_limit_bytes=limit),
+            input_output_aliases=aliases or {},
+            compiler_params=pltpu.CompilerParams(vmem_limit_bytes=16 << 20),
         )(*operands)
 
     behind = shift(right_piece[0, 0], "seg", -1)
@@ -259,19 +311,20 @@
     y, yb = call(start_kernel, [matrix, narrow], scaled, behind, guess[0, 0], mask)
 
     def half(vector_b, pairs, operands, sends):
-        outs = [matrix, matrix, stats] + [narrow] * sends
+        outs = [matrix, stats] + [matrix, narrow] * sends
         kernel = functools.partial(lower_kernel, pairs, sends)
-        low, diag, stat, *sent = call(
-            kernel, outs, left, right, vector_b, *operands, scratch=[inner]
-        )
-        return low, diag, stat, rotate(sent[0], "sec", -1) if sends else None
+        low, stat, *rest = call(kernel, outs, left, right, vector_b, *operands, scratch=[inner])
+        if not sends:
+            return low, stat
+        diag, sent = rest
+        return low, stat, diag, rotate(sent, "sec", -1)
 
     def joined(below, after, diag, above):
         (up,) = call(raise_kernel, [matrix], left, right, below, after, scratch=[inner])
         return call(join_kernel, [matrix, narrow], diag, up, above, mask)
 
     y_below = rotate(yb, "sec", 1)
-    low, diag, stat, above = half(yb, [(0, 0), (0, None)], [y], 1)
+    low, stat, diag, above = half(yb, [(0, 0), (0, None)], [y], 1)
     (stat,) = call(cross_kernel, [stats], y_below, low, stat)
     parts = exchange(stat, "sec")
     g, gb = joined(y_below, stat, diag, above)
@@ -280,7 +333,7 @@
     p, pb = call(kernel, [matrix, narrow], *parts, y, g, prec)
 
     pairs = [(0, 0), (0, 1), (0, 2), (2, 2), (2, 1), (2, None)]
-    low, diag, stat, above = half(pb, pairs, [y, g, p], 1)
+    low, stat, diag, above = half(pb, pairs, [y, g, p], 1)
     kernel = functools.partial(first_cross_kernel, len(parts))
     stat, p_below = call(kernel, [stats, narrow], *parts, y_below, g_below, prec_below, low, stat)
     parts = exchange(stat, "sec")
@@ -292,26 +345,30 @@
     )
 
     pairs = [(0, 2), (2, 2), (2, 1), (2, None)]
-    low, diag, stat, _ = half(pb, pairs, [x, g, p], 0)
+    low, stat = half(pb, pairs, [x, g, p], 0)
     (stat,) = call(
         second_cross_kernel,
         [stats],
         y_below, g_below, p_below, hp_below, prec_below, coefficients, low, stat,
     )
     parts = exchange(stat, "sec")
-    kernel = functools.partial(last_kernel, len(parts))
     block = (1, 1, size, size)
-    polar, weight, energy = call(
-        kernel,
-        [
-            jax.ShapeDtypeStruct(block, F32),
-            jax.ShapeDtypeStruct(block, BF16),
-            jax.ShapeDtypeStruct((1,), F32),
-        ],
-        *parts, x, p, coefficients,
+    weight = jax.ShapeDtypeStruct(block, BF16)
+    energy = jax.ShapeDtypeStruct((1,), F32)
+    operands = (*parts, x, p, coefficients)
+    polar, far = call(functools.partial(odd_kernel, len(parts)), [matrix, weight], *operands)
+    far = swap(far, "seg", 1)
+    polar, near, energy = call(
+        functools.partial(even_kernel, len(parts)),
+        [matrix, weight, energy],
+        *operands, polar,
         out_specs=[VMEM, VMEM, SMEM],
-    )
-    return polar, shift(weight, "seg", 1), energy
+        aliases={len(operands): 0},
+    )
+    near = swap(near, "seg", 0)
+    (handed,) = call(hand_kernel, [jax.ShapeDtypeStruct(block, BF16)], near, far)
+    (polar,) = call(store_kernel, [jax.ShapeDtypeStruct(block, F32)], polar, cost=SHORT)
+    return polar, handed, energy
 
 
 def solution(mesh):

time: 53.8 us -> 53.5 us (level); the launches traced: 52.7 us -> 53 us
  Pallas kernels: 10.4 us -> 11.5 us
  local copies, waits for them, and re-layouts: 1.5 us -> 0.85 us
    ppermute x2 -> x1, starting transfers between devices: 9.97 us -> 1.93 us  [shift(): lax.ppermute(value, axis, [(source, source + steps) for source in range(f...]
    ppermute x0 -> x2, starting transfers between devices: none -> 7.99 us  [swap(): return lax.ppermute(value, axis, list(pairs.items()))]
    ppermute x2 -> x1, waiting for transfers between devices: 5.85 us -> 3.92 us  [shift(): lax.ppermute(value, axis, [(source, source + steps) for source in range(f...]
    ppermute x0 -> x2, waiting for transfers between devices: none -> 1.91 us  [swap(): return lax.ppermute(value, axis, list(pairs.items()))]
    pallas_call x15 -> x18, Pallas kernels: 10.4 us -> 11.5 us  [call(): pl.pallas_call(kernel, out_shape=outs, in_specs=in_specs or [VMEM] * len(...]
    unnamed x13 -> x12, local copies, waits for them, and re-layouts: 1.5 us -> 0.85 us
  transfers between devices with their start and end apart: 17 -> 18, of which waited for: 8 -> 8; matrix products, arithmetic and copies ran while one was open for 0% -> 0% of each run, Pallas kernels for 15% -> 15%
where the time goes in v6:
time: 53.5 us; the launch traced here: 53 us
  starting transfers between devices  24.4 us (46%)
  waiting for transfers between devices  14.9 us (28%)
  Pallas kernels  11.5 us (21%)
  between operations  1.45 us (3%)
  local copies, waits for them, and re-layouts  0.85 us (2%)
    pallas_call x18, Pallas kernels, call(): pl.pallas_call(kernel, out_shape=outs, in_specs=in_specs or [VMEM] * len(...  11.5 us
    ppermute x9, starting transfers between devices, exchange(): parts.append(lax.ppermute(parts[0], axis, pairs))  8.55 us
    ppermute x2, starting transfers between devices, swap(): return lax.ppermute(value, axis, list(pairs.items()))  7.99 us
    ppermute x6, starting transfers between devices, rotate(): lax.ppermute(value, axis, [(source, (source + steps) % count) for source...  5.91 us
    ppermute x6, waiting for transfers between devices, rotate(): lax.ppermute(value, axis, [(source, (source + steps) % count) for source...  5.18 us
    ppermute x1, waiting for transfers between devices, shift(): lax.ppermute(value, axis, [(source, source + steps) for source in range(f...  3.92 us
    ppermute x9, waiting for transfers between devices, exchange(): parts.append(lax.ppermute(parts[0], axis, pairs))  3.85 us
    ppermute x1, starting transfers between devices, shift(): lax.ppermute(value, axis, [(source, source + steps) for source in range(f...  1.93 us
  transfers between devices with their start and end apart: 18, of which 8 were waited for; matrix products, arithmetic and copies ran while one was open for 0% of the time, Pallas kernels for 15%

profile of v6, /device:TPU:1, one launch (start us, length us, event | category | flops | bytes accessed | tf_op | source)
XLA Modules:
  0.0 53.0 jit_solution(9702609490658876417)
XLA Ops:
  0.6 1.9 %collective-permute-start = (bf16[256,256]{1,0:T(8,128)(2,1)}, bf16[256,256]{1,0:T(8,128)(2,1)S(1)}, u32[]{:S(2)}, u32[]{:S(2)}) collective-permute-start(bf16[256,256]{1,0:T(8,128)(2,1)} %bitcast.26), channel_id=1, source_target_pairs={{4,0},{8,4},{12,8},{16,12},{20,16},{24,20},{28,24},{5,1},{9,5},{13... | collective-permute-start | bytes 393224 | tf_op jit(solution)/shard_map/ppermute | solution.py:26
  3.3 0.8 %copy-done.4 = bf16[1,1,256,256]{3,2,1,0:T(8,128)(2,1)S(1)} copy-done((bf16[1,1,256,256]{3,2,1,0:T(8,128)(2,1)S(1)}, bf16[1,1,256,256]{3,2,1,0:T(8,128)(2,1)}, u32[]{:S(2)}) %copy-start.4) | copy-done | bytes 131096
  4.1 3.9 %collective-permute-done.behind = bf16[256,256]{1,0:T(8,128)(2,1)S(1)} collective-permute-done((bf16[256,256]{1,0:T(8,128)(2,1)}, bf16[256,256]{1,0:T(8,128)(2,1)S(1)}, u32[]{:S(2)}, u32[]{:S(2)}) %collective-permute-start) | collective-permute-done | bytes 131104 | tf_op jit(solution)/shard_map/ppermute | solution.py:26
  8.3 1.3 %collective-permute-start.1 = (bf16[256,256]{1,0:T(8,128)(2,1)S(1)}, bf16[256,256]{1,0:T(8,128)(2,1)S(1)}, u32[]{:S(2)}, u32[]{:S(2)}) collective-permute-start(bf16[256,256]{1,0:T(8,128)(2,1)S(1)} %get-tuple-element.33.vector_b), channel_id=1, source_target_pairs={{0,1},{1,2},{2,3},{3,0},{4,5},{5,6},{6,7},{7,4},{8,9},{9,10},{10,1... | collective-permute-start | bytes 393224 | tf_op jit(solution)/shard_map/ppermute | solution.py:39
  9.5 1.3 %shard_map.105 = (f32[256,256]{1,0:T(8,128)S(1)}, f32[8,128]{1,0:T(8,128)S(1)}, f32[256,256]{1,0:T(8,128)S(1)}, bf16[256,256]{1,0:T(8,128)(2,1)S(1)}) custom-call(bf16[16,256,256]{2,1,0:T(8,128)(2,1)S(1)} %bitcast.11, bf16[16,256,256]{2,1,0:T(8,128)(2,1)S(1)} %bitcast.16, bf16[256,256]{1,0:T(8,128)(2,1)S(1)} %get-tuple-element.33.vector_b, ...), custom_call_target="tpu_custom_call" | custom-call | tf_op jit(solution)/shard_map/pallas_call | solution.py:295
  10.8 1.2 %collective-permute-start.2 = (bf16[256,256]{1,0:T(8,128)(2,1)S(1)}, bf16[256,256]{1,0:T(8,128)(2,1)S(1)}, u32[]{:S(2)}, u32[]{:S(2)}) collective-permute-start(bf16[256,256]{1,0:T(8,128)(2,1)S(1)} %get-tuple-element.38), channel_id=1, source_target_pairs={{0,3},{1,0},{2,1},{3,2},{4,7},{5,4},{6,5},{7,6},{8,11},{9,8},{10,9... | collective-permute-start | bytes 393224 | tf_op jit(solution)/shard_map/ppermute | solution.py:39
  12.0 1.6 %collective-permute-done.1.below.refs_4_.y = bf16[256,256]{1,0:T(8,128)(2,1)S(1)} collective-permute-done((bf16[256,256]{1,0:T(8,128)(2,1)S(1)}, bf16[256,256]{1,0:T(8,128)(2,1)S(1)}, u32[]{:S(2)}, u32[]{:S(2)}) %collective-permute-start.1) | collective-permute-done | bytes 131104 | tf_op jit(solution)/shard_map/ppermute | solution.py:39
  13.6 1.7 %collective-permute-start.6 = (f32[8,128]{1,0:T(8,128)S(1)}, f32[8,128]{1,0:T(8,128)S(1)}, u32[]{:S(2)}, u32[]{:S(2)}) collective-permute-start(f32[8,128]{1,0:T(8,128)S(1)} %shard_map.106.after.refs_0_), channel_id=1, source_target_pairs={{0,3},{1,2},{2,1},{3,0},{4,7},{5,6},{6,5},{7,4},{8,11},{9,10},{10,... | collective-permute-start | bytes 12296 | tf_op jit(solution)/shard_map/ppermute | solution.py:62
  15.7 1.1 %collective-permute-start.4 = (f32[8,128]{1,0:T(8,128)S(1)}, f32[8,128]{1,0:T(8,128)S(1)}, u32[]{:S(2)}, u32[]{:S(2)}) collective-permute-start(f32[8,128]{1,0:T(8,128)S(1)} %shard_map.106.after.refs_0_), channel_id=1, source_target_pairs={{0,1},{1,0},{2,3},{3,2},{4,5},{5,4},{6,7},{7,6},{8,9},{9,8},{10,11... | collective-permute-start | bytes 12296 | tf_op jit(solution)/shard_map/ppermute | solution.py:62
  17.2 1.2 %shard_map.107.up = f32[256,256]{1,0:T(8,128)S(1)} custom-call(bf16[16,256,256]{2,1,0:T(8,128)(2,1)S(1)} %bitcast.12, bf16[16,256,256]{2,1,0:T(8,128)(2,1)S(1)} %bitcast.17, bf16[256,256]{1,0:T(8,128)(2,1)S(1)} %collective-permute-done.1.below.refs_4_.y, f32[8,128]{1,0:T(8,128)S(1)} %shard_map.106.after.refs_0_), custom_call_target="tpu_custom_call" | custom-call | tf_op jit(solution)/shard_map/pallas_call | solution.py:295
  18.5 2.3 %collective-permute-start.3 = (bf16[256,256]{1,0:T(8,128)(2,1)S(1)}, bf16[256,256]{1,0:T(8,128)(2,1)S(1)}, u32[]{:S(2)}, u32[]{:S(2)}) collective-permute-start(bf16[256,256]{1,0:T(8,128)(2,1)S(1)} %get-tuple-element.39), channel_id=1, source_target_pairs={{0,1},{1,2},{2,3},{3,0},{4,5},{5,6},{6,7},{7,4},{8,9},{9,10},{10,1... | collective-permute-start | bytes 393224 | tf_op jit(solution)/shard_map/ppermute | solution.py:39
  21.1 1.3 %shard_map.110 = (f32[256,256]{1,0:T(8,128)S(1)}, f32[8,128]{1,0:T(8,128)S(1)}, f32[256,256]{1,0:T(8,128)S(1)}, bf16[256,256]{1,0:T(8,128)(2,1)S(1)}) custom-call(bf16[16,256,256]{2,1,0:T(8,128)(2,1)S(1)} %bitcast.13, bf16[16,256,256]{2,1,0:T(8,128)(2,1)S(1)} %bitcast.18, bf16[256,256]{1,0:T(8,128)(2,1)S(1)} %get-tuple-element.41.vector_b, ...), custom_call_target="tpu_custom_call" | custom-call | tf_op jit(solution)/shard_map/pallas_call | solution.py:295
  22.5 2.4 %collective-permute-done.3.refs_5_.g = bf16[256,256]{1,0:T(8,128)(2,1)S(1)} collective-permute-done((bf16[256,256]{1,0:T(8,128)(2,1)S(1)}, bf16[256,256]{1,0:T(8,128)(2,1)S(1)}, u32[]{:S(2)}, u32[]{:S(2)}) %collective-permute-start.3) | collective-permute-done | bytes 131104 | tf_op jit(solution)/shard_map/ppermute | solution.py:39
  25.1 1.2 %shard_map.112.up = f32[256,256]{1,0:T(8,128)S(1)} custom-call(bf16[16,256,256]{2,1,0:T(8,128)(2,1)S(1)} %bitcast.14, bf16[16,256,256]{2,1,0:T(8,128)(2,1)S(1)} %bitcast.19, bf16[256,256]{1,0:T(8,128)(2,1)S(1)} %get-tuple-element.45.below.p, f32[8,128]{1,0:T(8,128)S(1)} %get-tuple-element.47.after.refs_0_), custom_call_target="tpu_custom_call" | custom-call | tf_op jit(solution)/shard_map/pallas_call | solution.py:295
  26.3 1.2 %collective-permute-done.8.above = bf16[256,256]{1,0:T(8,128)(2,1)S(1)} collective-permute-done((bf16[256,256]{1,0:T(8,128)(2,1)S(1)}, bf16[256,256]{1,0:T(8,128)(2,1)S(1)}, u32[]{:S(2)}, u32[]{:S(2)}) %collective-permute-start.8) | collective-permute-done | bytes 131104 | tf_op jit(solution)/shard_map/ppermute | solution.py:39
  27.6 0.6 %collective-permute-start.9 = (bf16[256,256]{1,0:T(8,128)(2,1)S(1)}, bf16[256,256]{1,0:T(8,128)(2,1)S(1)}, u32[]{:S(2)}, u32[]{:S(2)}) collective-permute-start(bf16[256,256]{1,0:T(8,128)(2,1)S(1)} %get-tuple-element.49), channel_id=1, source_target_pairs={{0,1},{1,2},{2,3},{3,0},{4,5},{5,6},{6,7},{7,4},{8,9},{9,10},{10,1... | collective-permute-start | bytes 393224 | tf_op jit(solution)/shard_map/ppermute | solution.py:39
  28.3 1.8 %collective-permute-start.12 = (f32[8,128]{1,0:T(8,128)S(1)}, f32[8,128]{1,0:T(8,128)S(1)}, u32[]{:S(2)}, u32[]{:S(2)}) collective-permute-start(f32[8,128]{1,0:T(8,128)S(1)} %get-tuple-element.47.after.refs_0_), channel_id=1, source_target_pairs={{0,3},{1,2},{2,1},{3,0},{4,7},{5,6},{6,5},{7,4},{8,11},{9,10},{10,... | collective-permute-start | bytes 12296 | tf_op jit(solution)/shard_map/ppermute | solution.py:62
  30.1 0.5 collective-permute-start.11
  30.9 2.8 %collective-permute-done.12.refs_3_ = f32[8,128]{1,0:T(8,128)S(1)} collective-permute-done((f32[8,128]{1,0:T(8,128)S(1)}, f32[8,128]{1,0:T(8,128)S(1)}, u32[]{:S(2)}, u32[]{:S(2)}) %collective-permute-start.12) | collective-permute-done | bytes 4128 | tf_op jit(solution)/shard_map/ppermute | solution.py:62
  33.7 0.4 shard_map.114
  34.1 1.3 %shard_map.115 = (f32[256,256]{1,0:T(8,128)S(1)}, f32[8,128]{1,0:T(8,128)S(1)}) custom-call(bf16[16,256,256]{2,1,0:T(8,128)(2,1)S(1)} %bitcast.15, bf16[16,256,256]{2,1,0:T(8,128)(2,1)S(1)} %bitcast.20, bf16[256,256]{1,0:T(8,128)(2,1)S(1)} %get-tuple-element.52.vector_b, f32[256,256]{1,0:T(8,128)S(1)} %get-tuple-element.53.refs_0_.refs_4_, ...), custom_call_target="tpu_custom_call" | custom-call | tf_op jit(solution)/shard_map/pallas_call | solution.py:295
  35.6 0.7 %collective-permute-start.15 = (f32[8,128]{1,0:T(8,128)S(1)}, f32[8,128]{1,0:T(8,128)S(1)}, u32[]{:S(2)}, u32[]{:S(2)}) collective-permute-start(f32[8,128]{1,0:T(8,128)S(1)} %shard_map.116.refs_0_), channel_id=1, source_target_pairs={{0,3},{1,2},{2,1},{3,0},{4,7},{5,6},{6,5},{7,4},{8,11},{9,10},{10,... | collective-permute-start | bytes 12296 | tf_op jit(solution)/shard_map/ppermute | solution.py:62
  36.3 0.6 %collective-permute-start.14 = (f32[8,128]{1,0:T(8,128)S(1)}, f32[8,128]{1,0:T(8,128)S(1)}, u32[]{:S(2)}, u32[]{:S(2)}) collective-permute-start(f32[8,128]{1,0:T(8,128)S(1)} %shard_map.116.refs_0_), channel_id=1, source_target_pairs={{0,2},{1,3},{2,0},{3,1},{4,6},{5,7},{6,4},{7,5},{8,10},{9,11},{10,... | collective-permute-start | bytes 12296 | tf_op jit(solution)/shard_map/ppermute | solution.py:62
  36.9 1.4 %collective-permute-start.13 = (f32[8,128]{1,0:T(8,128)S(1)}, f32[8,128]{1,0:T(8,128)S(1)}, u32[]{:S(2)}, u32[]{:S(2)}) collective-permute-start(f32[8,128]{1,0:T(8,128)S(1)} %shard_map.116.refs_0_), channel_id=1, source_target_pairs={{0,1},{1,0},{2,3},{3,2},{4,5},{5,4},{6,7},{7,6},{8,9},{9,8},{10,11... | collective-permute-start | bytes 12296 | tf_op jit(solution)/shard_map/ppermute | solution.py:62
  38.3 0.7 %collective-permute-done.15.refs_3_ = f32[8,128]{1,0:T(8,128)S(1)} collective-permute-done((f32[8,128]{1,0:T(8,128)S(1)}, f32[8,128]{1,0:T(8,128)S(1)}, u32[]{:S(2)}, u32[]{:S(2)}) %collective-permute-start.15) | collective-permute-done | bytes 4128 | tf_op jit(solution)/shard_map/ppermute | solution.py:62
  39.4 1.7 %shard_map.117 = (f32[256,256]{1,0:T(8,128)S(1)}, bf16[1,1,256,256]{3,2,1,0:T(8,128)(2,1)S(1)}) custom-call(f32[8,128]{1,0:T(8,128)S(1)} %shard_map.116.refs_0_, f32[8,128]{1,0:T(8,128)S(1)} %collective-permute-done.13.refs_1_, f32[8,128]{1,0:T(8,128)S(1)} %collective-permute-done.14.refs_2_, f32[8,128]{1,0:T(8,128)S(1)} %collective-permute-done.15.refs_3_, ...), custom_call_target="tpu_custom_call" | custom-call | tf_op jit(solution)/shard_map/pallas_call | solution.py:295
  41.0 0.7 %shard_map.118 = (f32[256,256]{1,0:T(8,128)S(1)}, bf16[1,1,256,256]{3,2,1,0:T(8,128)(2,1)S(1)}, f32[1]{0:T(128)}) custom-call(f32[8,128]{1,0:T(8,128)S(1)} %shard_map.116.refs_0_, f32[8,128]{1,0:T(8,128)S(1)} %collective-permute-done.13.refs_1_, f32[8,128]{1,0:T(8,128)S(1)} %collective-permute-done.14.refs_2_, ...), custom_call_target="tpu_custom_call", output_to_operand_aliasing={{0}: (7, {})} | custom-call | tf_op jit(solution)/shard_map/pallas_call | solution.py:295
  41.7 3.5 %collective-permute-start.16 = (bf16[1,1,256,256]{3,2,1,0:T(8,128)(2,1)S(1)}, bf16[1,1,256,256]{3,2,1,0:T(8,128)(2,1)S(1)}, u32[]{:S(2)}, u32[]{:S(2)}) collective-permute-start(bf16[1,1,256,256]{3,2,1,0:T(8,128)(2,1)S(1)} %get-tuple-element.60), channel_id=1, source_target_pairs={{0,4},{4,0},{8,12},{12,8},{16,20},{20,16},{24,28},{28,24},{1,5},{5... | collective-permute-start | bytes 393224 | tf_op jit(solution)/shard_map/ppermute | solution.py:34
  45.2 4.5 %collective-permute-start.17 = (bf16[1,1,256,256]{3,2,1,0:T(8,128)(2,1)S(1)}, bf16[1,1,256,256]{3,2,1,0:T(8,128)(2,1)S(1)}, u32[]{:S(2)}, u32[]{:S(2)}) collective-permute-start(bf16[1,1,256,256]{3,2,1,0:T(8,128)(2,1)S(1)} %get-tuple-element.61), channel_id=1, source_target_pairs={{0,0},{4,8},{8,4},{12,16},{16,12},{20,24},{24,20},{28,28},{1,1},{5... | collective-permute-start | bytes 393224 | tf_op jit(solution)/shard_map/ppermute | solution.py:34
  49.7 0.7 %shard_map.119 = f32[1,1,256,256]{3,2,1,0:T(8,128)} custom-call(f32[256,256]{1,0:T(8,128)S(1)} %get-tuple-element.59.value), custom_call_target="tpu_custom_call" | custom-call | bytes 1048576 | tf_op jit(solution)/shard_map/pallas_call | solution.py:295
  50.5 1.9 %collective-permute-done.17.far = bf16[1,1,256,256]{3,2,1,0:T(8,128)(2,1)S(1)} collective-permute-done((bf16[1,1,256,256]{3,2,1,0:T(8,128)(2,1)S(1)}, bf16[1,1,256,256]{3,2,1,0:T(8,128)(2,1)S(1)}, u32[]{:S(2)}, u32[]{:S(2)}) %collective-permute-start.17) | collective-permute-done | bytes 131104 | tf_op jit(solution)/shard_map/ppermute | solution.py:34
  52.4 0.7 %shard_map.120 = bf16[1,1,256,256]{3,2,1,0:T(8,128)(2,1)} custom-call(bf16[1,1,256,256]{3,2,1,0:T(8,128)(2,1)S(1)} %collective-permute-done.16.near, bf16[1,1,256,256]{3,2,1,0:T(8,128)(2,1)S(1)} %collective-permute-done.17.far), custom_call_target="tpu_custom_call" | custom-call | tf_op jit(solution)/shard_map/pallas_call | solution.py:295
  (35 shorter events, 2.7 us)
Async XLA Ops:
  0.6 7.4 %collective-permute-start = (bf16[256,256]{1,0:T(8,128)(2,1)}, bf16[256,256]{1,0:T(8,128)(2,1)S(1)}, u32[]{:S(2)}, u32[]{:S(2)}) collective-permute-start(bf16[256,256]{1,0:T(8,128)(2,1)} %bitcast.26), channel_id=1, source_target_pairs={{4,0},{8,4},{12,8},{16,12},{20,16},{24,20},{28,24},{5,1},{9,5},{13... | collective-permute-start | bytes 393224 | tf_op jit(solution)/shard_map/ppermute | solution.py:26
  3.2 0.9 %copy-start.4 = (bf16[1,1,256,256]{3,2,1,0:T(8,128)(2,1)S(1)}, bf16[1,1,256,256]{3,2,1,0:T(8,128)(2,1)}, u32[]{:S(2)}) copy-start(bf16[1,1,256,256]{3,2,1,0:T(8,128)(2,1)} %param.10) | copy-start | bytes 393220
  3.2 0.9 %copy-start.5 = (f32[1,1,256]{2,1,0:T(1,128)S(1)}, f32[1,1,256]{2,1,0:T(1,128)}, u32[]{:S(2)}) copy-start(f32[1,1,256]{2,1,0:T(1,128)} %param.13) | copy-start | bytes 3076
  3.2 4.8 %copy-start.3 = (bf16[1,1,256,256]{3,2,1,0:T(8,128)(2,1)S(1)}, bf16[1,1,256,256]{3,2,1,0:T(8,128)(2,1)}, u32[]{:S(2)}) copy-start(bf16[1,1,256,256]{3,2,1,0:T(8,128)(2,1)} %param.12) | copy-start | bytes 393220
  3.2 6.3 %copy-start = (bf16[1,1,16,256,256]{4,3,2,1,0:T(8,128)(2,1)S(1)}, bf16[1,1,16,256,256]{4,3,2,1,0:T(8,128)(2,1)}, u32[]{:S(2)}) copy-start(bf16[1,1,16,256,256]{4,3,2,1,0:T(8,128)(2,1)} %param.8) | copy-start | bytes 6291460
  3.2 6.3 %copy-start.1 = (bf16[1,1,16,256,256]{4,3,2,1,0:T(8,128)(2,1)S(1)}, bf16[1,1,16,256,256]{4,3,2,1,0:T(8,128)(2,1)}, u32[]{:S(2)}) copy-start(bf16[1,1,16,256,256]{4,3,2,1,0:T(8,128)(2,1)} %param.9) | copy-start | bytes 6291460
  8.3 5.3 %collective-permute-start.1 = (bf16[256,256]{1,0:T(8,128)(2,1)S(1)}, bf16[256,256]{1,0:T(8,128)(2,1)S(1)}, u32[]{:S(2)}, u32[]{:S(2)}) collective-permute-start(bf16[256,256]{1,0:T(8,128)(2,1)S(1)} %get-tuple-element.33.vector_b), channel_id=1, source_target_pairs={{0,1},{1,2},{2,3},{3,0},{4,5},{5,6},{6,7},{7,4},{8,9},{9,10},{10,1... | collective-permute-start | bytes 393224 | tf_op jit(solution)/shard_map/ppermute | solution.py:39
  9.5 7.3 %copy-start.2 = (bf16[1,1,256,256]{3,2,1,0:T(8,128)(2,1)S(1)}, bf16[1,1,256,256]{3,2,1,0:T(8,128)(2,1)}, u32[]{:S(2)}) copy-start(bf16[1,1,256,256]{3,2,1,0:T(8,128)(2,1)} %param.14) | copy-start | bytes 393220
  10.8 7.6 %collective-permute-start.2 = (bf16[256,256]{1,0:T(8,128)(2,1)S(1)}, bf16[256,256]{1,0:T(8,128)(2,1)S(1)}, u32[]{:S(2)}, u32[]{:S(2)}) collective-permute-start(bf16[256,256]{1,0:T(8,128)(2,1)S(1)} %get-tuple-element.38), channel_id=1, source_target_pairs={{0,3},{1,0},{2,1},{3,2},{4,7},{5,4},{6,5},{7,6},{8,11},{9,8},{10,9... | collective-permute-start | bytes 393224 | tf_op jit(solution)/shard_map/ppermute | solution.py:39
  13.6 7.2 %collective-permute-start.6 = (f32[8,128]{1,0:T(8,128)S(1)}, f32[8,128]{1,0:T(8,128)S(1)}, u32[]{:S(2)}, u32[]{:S(2)}) collective-permute-start(f32[8,128]{1,0:T(8,128)S(1)} %shard_map.106.after.refs_0_), channel_id=1, source_target_pairs={{0,3},{1,2},{2,1},{3,0},{4,7},{5,6},{6,5},{7,4},{8,11},{9,10},{10,... | collective-permute-start | bytes 12296 | tf_op jit(solution)/shard_map/ppermute | solution.py:62
  15.4 5.5 %collective-permute-start.5 = (f32[8,128]{1,0:T(8,128)S(1)}, f32[8,128]{1,0:T(8,128)S(1)}, u32[]{:S(2)}, u32[]{:S(2)}) collective-permute-start(f32[8,128]{1,0:T(8,128)S(1)} %shard_map.106.after.refs_0_), channel_id=1, source_target_pairs={{0,2},{1,3},{2,0},{3,1},{4,6},{5,7},{6,4},{7,5},{8,10},{9,11},{10,... | collective-permute-start | bytes 12296 | tf_op jit(solution)/shard_map/ppermute | solution.py:62
  15.7 5.1 %collective-permute-start.4 = (f32[8,128]{1,0:T(8,128)S(1)}, f32[8,128]{1,0:T(8,128)S(1)}, u32[]{:S(2)}, u32[]{:S(2)}) collective-permute-start(f32[8,128]{1,0:T(8,128)S(1)} %shard_map.106.after.refs_0_), channel_id=1, source_target_pairs={{0,1},{1,0},{2,3},{3,2},{4,5},{5,4},{6,7},{7,6},{8,9},{9,8},{10,11... | collective-permute-start | bytes 12296 | tf_op jit(solution)/shard_map/ppermute | solution.py:62
  16.8 5.7 %collective-permute-start.7 = (bf16[256,256]{1,0:T(8,128)(2,1)S(1)}, bf16[256,256]{1,0:T(8,128)(2,1)S(1)}, u32[]{:S(2)}, u32[]{:S(2)}) collective-permute-start(bf16[256,256]{1,0:T(8,128)(2,1)S(1)} %bitcast.21), channel_id=1, source_target_pairs={{0,1},{1,2},{2,3},{3,0},{4,5},{5,6},{6,7},{7,4},{8,9},{9,10},{10,1... | collective-permute-start | bytes 393224 | tf_op jit(solution)/shard_map/ppermute | solution.py:39
  18.5 6.4 %collective-permute-start.3 = (bf16[256,256]{1,0:T(8,128)(2,1)S(1)}, bf16[256,256]{1,0:T(8,128)(2,1)S(1)}, u32[]{:S(2)}, u32[]{:S(2)}) collective-permute-start(bf16[256,256]{1,0:T(8,128)(2,1)S(1)} %get-tuple-element.39), channel_id=1, source_target_pairs={{0,1},{1,2},{2,3},{3,0},{4,5},{5,6},{6,7},{7,4},{8,9},{9,10},{10,1... | collective-permute-start | bytes 393224 | tf_op jit(solution)/shard_map/ppermute | solution.py:39
  22.4 5.2 %collective-permute-start.8 = (bf16[256,256]{1,0:T(8,128)(2,1)S(1)}, bf16[256,256]{1,0:T(8,128)(2,1)S(1)}, u32[]{:S(2)}, u32[]{:S(2)}) collective-permute-start(bf16[256,256]{1,0:T(8,128)(2,1)S(1)} %get-tuple-element.48), channel_id=1, source_target_pairs={{0,3},{1,0},{2,1},{3,2},{4,7},{5,4},{6,5},{7,6},{8,11},{9,8},{10,9... | collective-permute-start | bytes 393224 | tf_op jit(solution)/shard_map/ppermute | solution.py:39
  27.6 7.7 %collective-permute-start.9 = (bf16[256,256]{1,0:T(8,128)(2,1)S(1)}, bf16[256,256]{1,0:T(8,128)(2,1)S(1)}, u32[]{:S(2)}, u32[]{:S(2)}) collective-permute-start(bf16[256,256]{1,0:T(8,128)(2,1)S(1)} %get-tuple-element.49), channel_id=1, source_target_pairs={{0,1},{1,2},{2,3},{3,0},{4,5},{5,6},{6,7},{7,4},{8,9},{9,10},{10,1... | collective-permute-start | bytes 393224 | tf_op jit(solution)/shard_map/ppermute | solution.py:39
  28.3 5.5 %collective-permute-start.12 = (f32[8,128]{1,0:T(8,128)S(1)}, f32[8,128]{1,0:T(8,128)S(1)}, u32[]{:S(2)}, u32[]{:S(2)}) collective-permute-start(f32[8,128]{1,0:T(8,128)S(1)} %get-tuple-element.47.after.refs_0_), channel_id=1, source_target_pairs={{0,3},{1,2},{2,1},{3,0},{4,7},{5,6},{6,5},{7,4},{8,11},{9,10},{10,... | collective-permute-start | bytes 12296 | tf_op jit(solution)/shard_map/ppermute | solution.py:62
  30.1 3.6 %collective-permute-start.11 = (f32[8,128]{1,0:T(8,128)S(1)}, f32[8,128]{1,0:T(8,128)S(1)}, u32[]{:S(2)}, u32[]{:S(2)}) collective-permute-start(f32[8,128]{1,0:T(8,128)S(1)} %get-tuple-element.47.after.refs_0_), channel_id=1, source_target_pairs={{0,2},{1,3},{2,0},{3,1},{4,6},{5,7},{6,4},{7,5},{8,10},{9,11},{10,... | collective-permute-start | bytes 12296 | tf_op jit(solution)/shard_map/ppermute | solution.py:62
  30.6 3.2 %collective-permute-start.10 = (f32[8,128]{1,0:T(8,128)S(1)}, f32[8,128]{1,0:T(8,128)S(1)}, u32[]{:S(2)}, u32[]{:S(2)}) collective-permute-start(f32[8,128]{1,0:T(8,128)S(1)} %get-tuple-element.47.after.refs_0_), channel_id=1, source_target_pairs={{0,1},{1,0},{2,3},{3,2},{4,5},{5,4},{6,7},{7,6},{8,9},{9,8},{10,11... | collective-permute-start | bytes 12296 | tf_op jit(solution)/shard_map/ppermute | solution.py:62
  35.6 3.4 %collective-permute-start.15 = (f32[8,128]{1,0:T(8,128)S(1)}, f32[8,128]{1,0:T(8,128)S(1)}, u32[]{:S(2)}, u32[]{:S(2)}) collective-permute-start(f32[8,128]{1,0:T(8,128)S(1)} %shard_map.116.refs_0_), channel_id=1, source_target_pairs={{0,3},{1,2},{2,1},{3,0},{4,7},{5,6},{6,5},{7,4},{8,11},{9,10},{10,... | collective-permute-start | bytes 12296 | tf_op jit(solution)/shard_map/ppermute | solution.py:62
  36.3 2.7 %collective-permute-start.14 = (f32[8,128]{1,0:T(8,128)S(1)}, f32[8,128]{1,0:T(8,128)S(1)}, u32[]{:S(2)}, u32[]{:S(2)}) collective-permute-start(f32[8,128]{1,0:T(8,128)S(1)} %shard_map.116.refs_0_), channel_id=1, source_target_pairs={{0,2},{1,3},{2,0},{3,1},{4,6},{5,7},{6,4},{7,5},{8,10},{9,11},{10,... | collective-permute-start | bytes 12296 | tf_op jit(solution)/shard_map/ppermute | solution.py:62
  36.9 2.5 %collective-permute-start.13 = (f32[8,128]{1,0:T(8,128)S(1)}, f32[8,128]{1,0:T(8,128)S(1)}, u32[]{:S(2)}, u32[]{:S(2)}) collective-permute-start(f32[8,128]{1,0:T(8,128)S(1)} %shard_map.116.refs_0_), channel_id=1, source_target_pairs={{0,1},{1,0},{2,3},{3,2},{4,5},{5,4},{6,7},{7,6},{8,9},{9,8},{10,11... | collective-permute-start | bytes 12296 | tf_op jit(solution)/shard_map/ppermute | solution.py:62
  41.7 8.7 %collective-permute-start.16 = (bf16[1,1,256,256]{3,2,1,0:T(8,128)(2,1)S(1)}, bf16[1,1,256,256]{3,2,1,0:T(8,128)(2,1)S(1)}, u32[]{:S(2)}, u32[]{:S(2)}) collective-permute-start(bf16[1,1,256,256]{3,2,1,0:T(8,128)(2,1)S(1)} %get-tuple-element.60), channel_id=1, source_target_pairs={{0,4},{4,0},{8,12},{12,8},{16,20},{20,16},{24,28},{28,24},{1,5},{5... | collective-permute-start | bytes 393224 | tf_op jit(solution)/shard_map/ppermute | solution.py:34
  45.2 7.2 %collective-permute-start.17 = (bf16[1,1,256,256]{3,2,1,0:T(8,128)(2,1)S(1)}, bf16[1,1,256,256]{3,2,1,0:T(8,128)(2,1)S(1)}, u32[]{:S(2)}, u32[]{:S(2)}) collective-permute-start(bf16[1,1,256,256]{3,2,1,0:T(8,128)(2,1)S(1)} %get-tuple-element.61), channel_id=1, source_target_pairs={{0,0},{4,8},{8,4},{12,16},{16,12},{20,24},{24,20},{28,28},{1,1},{5... | collective-permute-start | bytes 393224 | tf_op jit(solution)/shard_map/ppermute | solution.py:34

commit v7 on v6

--- a/solution.py
+++ b/solution.py
@@ -93,8 +93,12 @@
     return jnp.dot(inner[:, first * size : last * size], stacked, preferred_element_type=F32)
 
 
-def mask_kernel(rows, mask_out):
-    count = rows[0]
+def cover_kernel(out):
+    out[...] = jnp.zeros(out.shape, F32)
+
+
+def mask_kernel(rows, _, mask_out):
+    count = rows[...]
     shape = mask_out.shape
     idx_r = lax.broadcasted_iota(jnp.int32, shape, 0)
     idx_c = lax.broadcasted_iota(jnp.int32, shape, 1)
@@ -303,9 +307,10 @@
             compiler_params=pltpu.CompilerParams(vmem_limit_bytes=16 << 20),
         )(*operands)
 
+    (cover,) = call(cover_kernel, [stats], cost=COVER)
     behind = shift(right_piece[0, 0], "seg", -1)
     prec_below = rotate(prec, "sec", 1)
-    (mask,) = call(mask_kernel, [matrix], sector_rows[0], in_specs=[SMEM], cost=COVER)
+    (mask,) = call(mask_kernel, [matrix], sector_rows, cover)
     scaled = (left_piece[0, 0].astype(F32) * inverse_values[0]).astype(BF16)
 
     y, yb = call(start_kernel, [matrix, narrow], scaled, behind, guess[0, 0], mask)

time: 53.5 us -> 53.4 us (level)
  local copies, waits for them, and re-layouts: 0.85 us -> 0.02 us
    unnamed x12, local copies, waits for them, and re-layouts: 0.85 us -> 0.02 us
    ppermute x1, waiting for transfers between devices: 3.92 us -> 4.52 us  [shift(): lax.ppermute(value, axis, [(source, source + steps) for source in range(f...]
    pallas_call x18 -> x19, Pallas kernels: 11.5 us -> 11.6 us  [call(): pl.pallas_call(kernel, out_shape=outs, in_specs=in_specs or [VMEM] * len(...]
where the time goes in v7:
time: 53.4 us; the launch traced here: 53.2 us
  starting transfers between devices  24.8 us (46%)
  waiting for transfers between devices  15.2 us (28%)
  Pallas kernels  11.6 us (22%)
  between operations  1.62 us (3%)
    pallas_call x19, Pallas kernels, call(): pl.pallas_call(kernel, out_shape=outs, in_specs=in_specs or [VMEM] * len(...  11.6 us
    ppermute x9, starting transfers between devices, exchange(): parts.append(lax.ppermute(parts[0], axis, pairs))  8.55 us
    ppermute x2, starting transfers between devices, swap(): return lax.ppermute(value, axis, list(pairs.items()))  7.99 us
    ppermute x6, starting transfers between devices, rotate(): lax.ppermute(value, axis, [(source, (source + steps) % count) for source...  6.23 us
    ppermute x6, waiting for transfers between devices, rotate(): lax.ppermute(value, axis, [(source, (source + steps) % count) for source...  4.86 us
    ppermute x1, waiting for transfers between devices, shift(): lax.ppermute(value, axis, [(source, source + steps) for source in range(f...  4.52 us
    ppermute x9, waiting for transfers between devices, exchange(): parts.append(lax.ppermute(parts[0], axis, pairs))  3.86 us
    ppermute x1, starting transfers between devices, shift(): lax.ppermute(value, axis, [(source, source + steps) for source in range(f...  2.06 us
  transfers between devices with their start and end apart: 18, of which 8 were waited for; matrix products, arithmetic and copies ran while one was open for 0% of the time, Pallas kernels for 15%

profile of v7, /device:TPU:1, one launch (start us, length us, event | category | flops | bytes accessed | tf_op | source)
XLA Modules:
  0.0 53.2 jit_solution(13436547857181892711)
XLA Ops:
  0.7 2.1 %collective-permute-start = (bf16[256,256]{1,0:T(8,128)(2,1)}, bf16[256,256]{1,0:T(8,128)(2,1)S(1)}, u32[]{:S(2)}, u32[]{:S(2)}) collective-permute-start(bf16[256,256]{1,0:T(8,128)(2,1)} %bitcast.24), channel_id=1, source_target_pairs={{4,0},{8,4},{12,8},{16,12},{20,16},{24,20},{28,24},{5,1},{9,5},{13... | collective-permute-start | bytes 393224 | tf_op jit(solution)/shard_map/ppermute | solution.py:26
  3.7 4.5 %collective-permute-done.behind = bf16[256,256]{1,0:T(8,128)(2,1)S(1)} collective-permute-done((bf16[256,256]{1,0:T(8,128)(2,1)}, bf16[256,256]{1,0:T(8,128)(2,1)S(1)}, u32[]{:S(2)}, u32[]{:S(2)}) %collective-permute-start) | collective-permute-done | bytes 131104 | tf_op jit(solution)/shard_map/ppermute | solution.py:26
  8.4 1.3 %collective-permute-start.1 = (bf16[256,256]{1,0:T(8,128)(2,1)S(1)}, bf16[256,256]{1,0:T(8,128)(2,1)S(1)}, u32[]{:S(2)}, u32[]{:S(2)}) collective-permute-start(bf16[256,256]{1,0:T(8,128)(2,1)S(1)} %get-tuple-element.33.vector_b), channel_id=1, source_target_pairs={{0,1},{1,2},{2,3},{3,0},{4,5},{5,6},{6,7},{7,4},{8,9},{9,10},{10,1... | collective-permute-start | bytes 393224 | tf_op jit(solution)/shard_map/ppermute | solution.py:39
  9.7 1.3 %shard_map.106 = (f32[256,256]{1,0:T(8,128)S(1)}, f32[8,128]{1,0:T(8,128)S(1)}, f32[256,256]{1,0:T(8,128)S(1)}, bf16[256,256]{1,0:T(8,128)(2,1)S(1)}) custom-call(bf16[16,256,256]{2,1,0:T(8,128)(2,1)S(1)} %bitcast.9, bf16[16,256,256]{2,1,0:T(8,128)(2,1)S(1)} %bitcast.14, bf16[256,256]{1,0:T(8,128)(2,1)S(1)} %get-tuple-element.33.vector_b, ...), custom_call_target="tpu_custom_call" | custom-call | tf_op jit(solution)/shard_map/pallas_call | solution.py:299
  11.0 1.2 %collective-permute-start.2 = (bf16[256,256]{1,0:T(8,128)(2,1)S(1)}, bf16[256,256]{1,0:T(8,128)(2,1)S(1)}, u32[]{:S(2)}, u32[]{:S(2)}) collective-permute-start(bf16[256,256]{1,0:T(8,128)(2,1)S(1)} %get-tuple-element.38), channel_id=1, source_target_pairs={{0,3},{1,0},{2,1},{3,2},{4,7},{5,4},{6,5},{7,6},{8,11},{9,8},{10,9... | collective-permute-start | bytes 393224 | tf_op jit(solution)/shard_map/ppermute | solution.py:39
  12.2 1.6 %collective-permute-done.1.below.refs_4_.y = bf16[256,256]{1,0:T(8,128)(2,1)S(1)} collective-permute-done((bf16[256,256]{1,0:T(8,128)(2,1)S(1)}, bf16[256,256]{1,0:T(8,128)(2,1)S(1)}, u32[]{:S(2)}, u32[]{:S(2)}) %collective-permute-start.1) | collective-permute-done | bytes 131104 | tf_op jit(solution)/shard_map/ppermute | solution.py:39
  13.8 1.7 %collective-permute-start.6 = (f32[8,128]{1,0:T(8,128)S(1)}, f32[8,128]{1,0:T(8,128)S(1)}, u32[]{:S(2)}, u32[]{:S(2)}) collective-permute-start(f32[8,128]{1,0:T(8,128)S(1)} %shard_map.107.after.refs_0_), channel_id=1, source_target_pairs={{0,3},{1,2},{2,1},{3,0},{4,7},{5,6},{6,5},{7,4},{8,11},{9,10},{10,... | collective-permute-start | bytes 12296 | tf_op jit(solution)/shard_map/ppermute | solution.py:62
  15.5 0.7 %collective-permute-start.5 = (f32[8,128]{1,0:T(8,128)S(1)}, f32[8,128]{1,0:T(8,128)S(1)}, u32[]{:S(2)}, u32[]{:S(2)}) collective-permute-start(f32[8,128]{1,0:T(8,128)S(1)} %shard_map.107.after.refs_0_), channel_id=1, source_target_pairs={{0,2},{1,3},{2,0},{3,1},{4,6},{5,7},{6,4},{7,5},{8,10},{9,11},{10,... | collective-permute-start | bytes 12296 | tf_op jit(solution)/shard_map/ppermute | solution.py:62
  16.2 0.8 %collective-permute-start.4 = (f32[8,128]{1,0:T(8,128)S(1)}, f32[8,128]{1,0:T(8,128)S(1)}, u32[]{:S(2)}, u32[]{:S(2)}) collective-permute-start(f32[8,128]{1,0:T(8,128)S(1)} %shard_map.107.after.refs_0_), channel_id=1, source_target_pairs={{0,1},{1,0},{2,3},{3,2},{4,5},{5,4},{6,7},{7,6},{8,9},{9,8},{10,11... | collective-permute-start | bytes 12296 | tf_op jit(solution)/shard_map/ppermute | solution.py:62
  17.0 0.7 %collective-permute-start.7 = (bf16[256,256]{1,0:T(8,128)(2,1)S(1)}, bf16[256,256]{1,0:T(8,128)(2,1)S(1)}, u32[]{:S(2)}, u32[]{:S(2)}) collective-permute-start(bf16[256,256]{1,0:T(8,128)(2,1)S(1)} %bitcast.19), channel_id=1, source_target_pairs={{0,1},{1,2},{2,3},{3,0},{4,5},{5,6},{6,7},{7,4},{8,9},{9,10},{10,1... | collective-permute-start | bytes 393224 | tf_op jit(solution)/shard_map/ppermute | solution.py:39
  17.7 1.2 %shard_map.108.up = f32[256,256]{1,0:T(8,128)S(1)} custom-call(bf16[16,256,256]{2,1,0:T(8,128)(2,1)S(1)} %bitcast.10, bf16[16,256,256]{2,1,0:T(8,128)(2,1)S(1)} %bitcast.15, bf16[256,256]{1,0:T(8,128)(2,1)S(1)} %collective-permute-done.1.below.refs_4_.y, f32[8,128]{1,0:T(8,128)S(1)} %shard_map.107.after.refs_0_), custom_call_target="tpu_custom_call" | custom-call | tf_op jit(solution)/shard_map/pallas_call | solution.py:299
  19.0 2.0 %collective-permute-start.3 = (bf16[256,256]{1,0:T(8,128)(2,1)S(1)}, bf16[256,256]{1,0:T(8,128)(2,1)S(1)}, u32[]{:S(2)}, u32[]{:S(2)}) collective-permute-start(bf16[256,256]{1,0:T(8,128)(2,1)S(1)} %get-tuple-element.39), channel_id=1, source_target_pairs={{0,1},{1,2},{2,3},{3,0},{4,5},{5,6},{6,7},{7,4},{8,9},{9,10},{10,1... | collective-permute-start | bytes 393224 | tf_op jit(solution)/shard_map/ppermute | solution.py:39
  21.2 1.3 %shard_map.111 = (f32[256,256]{1,0:T(8,128)S(1)}, f32[8,128]{1,0:T(8,128)S(1)}, f32[256,256]{1,0:T(8,128)S(1)}, bf16[256,256]{1,0:T(8,128)(2,1)S(1)}) custom-call(bf16[16,256,256]{2,1,0:T(8,128)(2,1)S(1)} %bitcast.11, bf16[16,256,256]{2,1,0:T(8,128)(2,1)S(1)} %bitcast.16, bf16[256,256]{1,0:T(8,128)(2,1)S(1)} %get-tuple-element.41.vector_b, ...), custom_call_target="tpu_custom_call" | custom-call | tf_op jit(solution)/shard_map/pallas_call | solution.py:299
  23.0 2.2 %collective-permute-done.3.refs_5_.g = bf16[256,256]{1,0:T(8,128)(2,1)S(1)} collective-permute-done((bf16[256,256]{1,0:T(8,128)(2,1)S(1)}, bf16[256,256]{1,0:T(8,128)(2,1)S(1)}, u32[]{:S(2)}, u32[]{:S(2)}) %collective-permute-start.3) | collective-permute-done | bytes 131104 | tf_op jit(solution)/shard_map/ppermute | solution.py:39
  25.4 1.2 %shard_map.113.up = f32[256,256]{1,0:T(8,128)S(1)} custom-call(bf16[16,256,256]{2,1,0:T(8,128)(2,1)S(1)} %bitcast.12, bf16[16,256,256]{2,1,0:T(8,128)(2,1)S(1)} %bitcast.17, bf16[256,256]{1,0:T(8,128)(2,1)S(1)} %get-tuple-element.45.below.p, f32[8,128]{1,0:T(8,128)S(1)} %get-tuple-element.47.after.refs_0_), custom_call_target="tpu_custom_call" | custom-call | tf_op jit(solution)/shard_map/pallas_call | solution.py:299
  26.6 1.1 %collective-permute-done.8.above = bf16[256,256]{1,0:T(8,128)(2,1)S(1)} collective-permute-done((bf16[256,256]{1,0:T(8,128)(2,1)S(1)}, bf16[256,256]{1,0:T(8,128)(2,1)S(1)}, u32[]{:S(2)}, u32[]{:S(2)}) %collective-permute-start.8) | collective-permute-done | bytes 131104 | tf_op jit(solution)/shard_map/ppermute | solution.py:39
  27.8 0.6 %collective-permute-start.9 = (bf16[256,256]{1,0:T(8,128)(2,1)S(1)}, bf16[256,256]{1,0:T(8,128)(2,1)S(1)}, u32[]{:S(2)}, u32[]{:S(2)}) collective-permute-start(bf16[256,256]{1,0:T(8,128)(2,1)S(1)} %get-tuple-element.49), channel_id=1, source_target_pairs={{0,1},{1,2},{2,3},{3,0},{4,5},{5,6},{6,7},{7,4},{8,9},{9,10},{10,1... | collective-permute-start | bytes 393224 | tf_op jit(solution)/shard_map/ppermute | solution.py:39
  28.4 1.8 %collective-permute-start.12 = (f32[8,128]{1,0:T(8,128)S(1)}, f32[8,128]{1,0:T(8,128)S(1)}, u32[]{:S(2)}, u32[]{:S(2)}) collective-permute-start(f32[8,128]{1,0:T(8,128)S(1)} %get-tuple-element.47.after.refs_0_), channel_id=1, source_target_pairs={{0,3},{1,2},{2,1},{3,0},{4,7},{5,6},{6,5},{7,4},{8,11},{9,10},{10,... | collective-permute-start | bytes 12296 | tf_op jit(solution)/shard_map/ppermute | solution.py:62
  30.2 0.5 collective-permute-start.11
  31.1 2.8 %collective-permute-done.12.refs_3_ = f32[8,128]{1,0:T(8,128)S(1)} collective-permute-done((f32[8,128]{1,0:T(8,128)S(1)}, f32[8,128]{1,0:T(8,128)S(1)}, u32[]{:S(2)}, u32[]{:S(2)}) %collective-permute-start.12) | collective-permute-done | bytes 4128 | tf_op jit(solution)/shard_map/ppermute | solution.py:62
  34.2 1.3 %shard_map.116 = (f32[256,256]{1,0:T(8,128)S(1)}, f32[8,128]{1,0:T(8,128)S(1)}) custom-call(bf16[16,256,256]{2,1,0:T(8,128)(2,1)S(1)} %bitcast.13, bf16[16,256,256]{2,1,0:T(8,128)(2,1)S(1)} %bitcast.18, bf16[256,256]{1,0:T(8,128)(2,1)S(1)} %get-tuple-element.52.vector_b, f32[256,256]{1,0:T(8,128)S(1)} %get-tuple-element.53.refs_0_.refs_4_, ...), custom_call_target="tpu_custom_call" | custom-call | tf_op jit(solution)/shard_map/pallas_call | solution.py:299
  35.8 0.7 %collective-permute-start.15 = (f32[8,128]{1,0:T(8,128)S(1)}, f32[8,128]{1,0:T(8,128)S(1)}, u32[]{:S(2)}, u32[]{:S(2)}) collective-permute-start(f32[8,128]{1,0:T(8,128)S(1)} %shard_map.117.refs_0_), channel_id=1, source_target_pairs={{0,3},{1,2},{2,1},{3,0},{4,7},{5,6},{6,5},{7,4},{8,11},{9,10},{10,... | collective-permute-start | bytes 12296 | tf_op jit(solution)/shard_map/ppermute | solution.py:62
  36.5 0.6 %collective-permute-start.14 = (f32[8,128]{1,0:T(8,128)S(1)}, f32[8,128]{1,0:T(8,128)S(1)}, u32[]{:S(2)}, u32[]{:S(2)}) collective-permute-start(f32[8,128]{1,0:T(8,128)S(1)} %shard_map.117.refs_0_), channel_id=1, source_target_pairs={{0,2},{1,3},{2,0},{3,1},{4,6},{5,7},{6,4},{7,5},{8,10},{9,11},{10,... | collective-permute-start | bytes 12296 | tf_op jit(solution)/shard_map/ppermute | solution.py:62
  37.1 1.4 %collective-permute-start.13 = (f32[8,128]{1,0:T(8,128)S(1)}, f32[8,128]{1,0:T(8,128)S(1)}, u32[]{:S(2)}, u32[]{:S(2)}) collective-permute-start(f32[8,128]{1,0:T(8,128)S(1)} %shard_map.117.refs_0_), channel_id=1, source_target_pairs={{0,1},{1,0},{2,3},{3,2},{4,5},{5,4},{6,7},{7,6},{8,9},{9,8},{10,11... | collective-permute-start | bytes 12296 | tf_op jit(solution)/shard_map/ppermute | solution.py:62
  38.5 0.7 %collective-permute-done.15.refs_3_ = f32[8,128]{1,0:T(8,128)S(1)} collective-permute-done((f32[8,128]{1,0:T(8,128)S(1)}, f32[8,128]{1,0:T(8,128)S(1)}, u32[]{:S(2)}, u32[]{:S(2)}) %collective-permute-start.15) | collective-permute-done | bytes 4128 | tf_op jit(solution)/shard_map/ppermute | solution.py:62
  39.5 1.7 %shard_map.118 = (f32[256,256]{1,0:T(8,128)S(1)}, bf16[1,1,256,256]{3,2,1,0:T(8,128)(2,1)S(1)}) custom-call(f32[8,128]{1,0:T(8,128)S(1)} %shard_map.117.refs_0_, f32[8,128]{1,0:T(8,128)S(1)} %collective-permute-done.13.refs_1_, f32[8,128]{1,0:T(8,128)S(1)} %collective-permute-done.14.refs_2_, f32[8,128]{1,0:T(8,128)S(1)} %collective-permute-done.15.refs_3_, ...), custom_call_target="tpu_custom_call" | custom-call | tf_op jit(solution)/shard_map/pallas_call | solution.py:299
  41.2 0.7 %shard_map.119 = (f32[256,256]{1,0:T(8,128)S(1)}, bf16[1,1,256,256]{3,2,1,0:T(8,128)(2,1)S(1)}, f32[1]{0:T(128)}) custom-call(f32[8,128]{1,0:T(8,128)S(1)} %shard_map.117.refs_0_, f32[8,128]{1,0:T(8,128)S(1)} %collective-permute-done.13.refs_1_, f32[8,128]{1,0:T(8,128)S(1)} %collective-permute-done.14.refs_2_, ...), custom_call_target="tpu_custom_call", output_to_operand_aliasing={{0}: (7, {})} | custom-call | tf_op jit(solution)/shard_map/pallas_call | solution.py:299
  41.9 3.5 %collective-permute-start.16 = (bf16[1,1,256,256]{3,2,1,0:T(8,128)(2,1)S(1)}, bf16[1,1,256,256]{3,2,1,0:T(8,128)(2,1)S(1)}, u32[]{:S(2)}, u32[]{:S(2)}) collective-permute-start(bf16[1,1,256,256]{3,2,1,0:T(8,128)(2,1)S(1)} %get-tuple-element.60), channel_id=1, source_target_pairs={{0,4},{4,0},{8,12},{12,8},{16,20},{20,16},{24,28},{28,24},{1,5},{5... | collective-permute-start | bytes 393224 | tf_op jit(solution)/shard_map/ppermute | solution.py:34
  45.3 4.5 %collective-permute-start.17 = (bf16[1,1,256,256]{3,2,1,0:T(8,128)(2,1)S(1)}, bf16[1,1,256,256]{3,2,1,0:T(8,128)(2,1)S(1)}, u32[]{:S(2)}, u32[]{:S(2)}) collective-permute-start(bf16[1,1,256,256]{3,2,1,0:T(8,128)(2,1)S(1)} %get-tuple-element.61), channel_id=1, source_target_pairs={{0,0},{4,8},{8,4},{12,16},{16,12},{20,24},{24,20},{28,28},{1,1},{5... | collective-permute-start | bytes 393224 | tf_op jit(solution)/shard_map/ppermute | solution.py:34
  49.9 0.7 %shard_map.120 = f32[1,1,256,256]{3,2,1,0:T(8,128)} custom-call(f32[256,256]{1,0:T(8,128)S(1)} %get-tuple-element.59.value), custom_call_target="tpu_custom_call" | custom-call | bytes 1048576 | tf_op jit(solution)/shard_map/pallas_call | solution.py:299
  50.6 1.9 %collective-permute-done.17.far = bf16[1,1,256,256]{3,2,1,0:T(8,128)(2,1)S(1)} collective-permute-done((bf16[1,1,256,256]{3,2,1,0:T(8,128)(2,1)S(1)}, bf16[1,1,256,256]{3,2,1,0:T(8,128)(2,1)S(1)}, u32[]{:S(2)}, u32[]{:S(2)}) %collective-permute-start.17) | collective-permute-done | bytes 131104 | tf_op jit(solution)/shard_map/ppermute | solution.py:34
  52.5 0.7 %shard_map.121 = bf16[1,1,256,256]{3,2,1,0:T(8,128)(2,1)} custom-call(bf16[1,1,256,256]{3,2,1,0:T(8,128)(2,1)S(1)} %collective-permute-done.16.near, bf16[1,1,256,256]{3,2,1,0:T(8,128)(2,1)S(1)} %collective-permute-done.17.far), custom_call_target="tpu_custom_call" | custom-call | tf_op jit(solution)/shard_map/pallas_call | solution.py:299
  (36 shorter events, 2.7 us)
Async XLA Ops:
  0.6 3.0 %copy-start.4 = (bf16[1,1,256,256]{3,2,1,0:T(8,128)(2,1)S(1)}, bf16[1,1,256,256]{3,2,1,0:T(8,128)(2,1)}, u32[]{:S(2)}) copy-start(bf16[1,1,256,256]{3,2,1,0:T(8,128)(2,1)} %param.10) | copy-start | bytes 393220
  0.6 3.0 %copy-start.5 = (f32[1,1,256]{2,1,0:T(1,128)S(1)}, f32[1,1,256]{2,1,0:T(1,128)}, u32[]{:S(2)}) copy-start(f32[1,1,256]{2,1,0:T(1,128)} %param.13) | copy-start | bytes 3076
  0.7 7.6 %copy-start.3 = (bf16[1,1,256,256]{3,2,1,0:T(8,128)(2,1)S(1)}, bf16[1,1,256,256]{3,2,1,0:T(8,128)(2,1)}, u32[]{:S(2)}) copy-start(bf16[1,1,256,256]{3,2,1,0:T(8,128)(2,1)} %param.12) | copy-start | bytes 393220
  0.7 7.6 %collective-permute-start = (bf16[256,256]{1,0:T(8,128)(2,1)}, bf16[256,256]{1,0:T(8,128)(2,1)S(1)}, u32[]{:S(2)}, u32[]{:S(2)}) collective-permute-start(bf16[256,256]{1,0:T(8,128)(2,1)} %bitcast.24), channel_id=1, source_target_pairs={{4,0},{8,4},{12,8},{16,12},{20,16},{24,20},{28,24},{5,1},{9,5},{13... | collective-permute-start | bytes 393224 | tf_op jit(solution)/shard_map/ppermute | solution.py:26
  2.7 7.0 %copy-start = (bf16[1,1,16,256,256]{4,3,2,1,0:T(8,128)(2,1)S(1)}, bf16[1,1,16,256,256]{4,3,2,1,0:T(8,128)(2,1)}, u32[]{:S(2)}) copy-start(bf16[1,1,16,256,256]{4,3,2,1,0:T(8,128)(2,1)} %param.8) | copy-start | bytes 6291460
  2.7 7.0 %copy-start.1 = (bf16[1,1,16,256,256]{4,3,2,1,0:T(8,128)(2,1)S(1)}, bf16[1,1,16,256,256]{4,3,2,1,0:T(8,128)(2,1)}, u32[]{:S(2)}) copy-start(bf16[1,1,16,256,256]{4,3,2,1,0:T(8,128)(2,1)} %param.9) | copy-start | bytes 6291460
  8.4 5.3 %collective-permute-start.1 = (bf16[256,256]{1,0:T(8,128)(2,1)S(1)}, bf16[256,256]{1,0:T(8,128)(2,1)S(1)}, u32[]{:S(2)}, u32[]{:S(2)}) collective-permute-start(bf16[256,256]{1,0:T(8,128)(2,1)S(1)} %get-tuple-element.33.vector_b), channel_id=1, source_target_pairs={{0,1},{1,2},{2,3},{3,0},{4,5},{5,6},{6,7},{7,4},{8,9},{9,10},{10,1... | collective-permute-start | bytes 393224 | tf_op jit(solution)/shard_map/ppermute | solution.py:39
  9.7 7.3 %copy-start.2 = (bf16[1,1,256,256]{3,2,1,0:T(8,128)(2,1)S(1)}, bf16[1,1,256,256]{3,2,1,0:T(8,128)(2,1)}, u32[]{:S(2)}) copy-start(bf16[1,1,256,256]{3,2,1,0:T(8,128)(2,1)} %param.14) | copy-start | bytes 393220
  11.0 7.9 %collective-permute-start.2 = (bf16[256,256]{1,0:T(8,128)(2,1)S(1)}, bf16[256,256]{1,0:T(8,128)(2,1)S(1)}, u32[]{:S(2)}, u32[]{:S(2)}) collective-permute-start(bf16[256,256]{1,0:T(8,128)(2,1)S(1)} %get-tuple-element.38), channel_id=1, source_target_pairs={{0,3},{1,0},{2,1},{3,2},{4,7},{5,4},{6,5},{7,6},{8,11},{9,8},{10,9... | collective-permute-start | bytes 393224 | tf_op jit(solution)/shard_map/ppermute | solution.py:39
  13.8 7.2 %collective-permute-start.6 = (f32[8,128]{1,0:T(8,128)S(1)}, f32[8,128]{1,0:T(8,128)S(1)}, u32[]{:S(2)}, u32[]{:S(2)}) collective-permute-start(f32[8,128]{1,0:T(8,128)S(1)} %shard_map.107.after.refs_0_), channel_id=1, source_target_pairs={{0,3},{1,2},{2,1},{3,0},{4,7},{5,6},{6,5},{7,4},{8,11},{9,10},{10,... | collective-permute-start | bytes 12296 | tf_op jit(solution)/shard_map/ppermute | solution.py:62
  15.5 5.5 %collective-permute-start.5 = (f32[8,128]{1,0:T(8,128)S(1)}, f32[8,128]{1,0:T(8,128)S(1)}, u32[]{:S(2)}, u32[]{:S(2)}) collective-permute-start(f32[8,128]{1,0:T(8,128)S(1)} %shard_map.107.after.refs_0_), channel_id=1, source_target_pairs={{0,2},{1,3},{2,0},{3,1},{4,6},{5,7},{6,4},{7,5},{8,10},{9,11},{10,... | collective-permute-start | bytes 12296 | tf_op jit(solution)/shard_map/ppermute | solution.py:62
  16.2 4.8 %collective-permute-start.4 = (f32[8,128]{1,0:T(8,128)S(1)}, f32[8,128]{1,0:T(8,128)S(1)}, u32[]{:S(2)}, u32[]{:S(2)}) collective-permute-start(f32[8,128]{1,0:T(8,128)S(1)} %shard_map.107.after.refs_0_), channel_id=1, source_target_pairs={{0,1},{1,0},{2,3},{3,2},{4,5},{5,4},{6,7},{7,6},{8,9},{9,8},{10,11... | collective-permute-start | bytes 12296 | tf_op jit(solution)/shard_map/ppermute | solution.py:62
  17.0 6.0 %collective-permute-start.7 = (bf16[256,256]{1,0:T(8,128)(2,1)S(1)}, bf16[256,256]{1,0:T(8,128)(2,1)S(1)}, u32[]{:S(2)}, u32[]{:S(2)}) collective-permute-start(bf16[256,256]{1,0:T(8,128)(2,1)S(1)} %bitcast.19), channel_id=1, source_target_pairs={{0,1},{1,2},{2,3},{3,0},{4,5},{5,6},{6,7},{7,4},{8,9},{9,10},{10,1... | collective-permute-start | bytes 393224 | tf_op jit(solution)/shard_map/ppermute | solution.py:39
  19.0 6.2 %collective-permute-start.3 = (bf16[256,256]{1,0:T(8,128)(2,1)S(1)}, bf16[256,256]{1,0:T(8,128)(2,1)S(1)}, u32[]{:S(2)}, u32[]{:S(2)}) collective-permute-start(bf16[256,256]{1,0:T(8,128)(2,1)S(1)} %get-tuple-element.39), channel_id=1, source_target_pairs={{0,1},{1,2},{2,3},{3,0},{4,5},{5,6},{6,7},{7,4},{8,9},{9,10},{10,1... | collective-permute-start | bytes 393224 | tf_op jit(solution)/shard_map/ppermute | solution.py:39
  22.5 5.2 %collective-permute-start.8 = (bf16[256,256]{1,0:T(8,128)(2,1)S(1)}, bf16[256,256]{1,0:T(8,128)(2,1)S(1)}, u32[]{:S(2)}, u32[]{:S(2)}) collective-permute-start(bf16[256,256]{1,0:T(8,128)(2,1)S(1)} %get-tuple-element.48), channel_id=1, source_target_pairs={{0,3},{1,0},{2,1},{3,2},{4,7},{5,4},{6,5},{7,6},{8,11},{9,8},{10,9... | collective-permute-start | bytes 393224 | tf_op jit(solution)/shard_map/ppermute | solution.py:39
  27.8 7.7 %collective-permute-start.9 = (bf16[256,256]{1,0:T(8,128)(2,1)S(1)}, bf16[256,256]{1,0:T(8,128)(2,1)S(1)}, u32[]{:S(2)}, u32[]{:S(2)}) collective-permute-start(bf16[256,256]{1,0:T(8,128)(2,1)S(1)} %get-tuple-element.49), channel_id=1, source_target_pairs={{0,1},{1,2},{2,3},{3,0},{4,5},{5,6},{6,7},{7,4},{8,9},{9,10},{10,1... | collective-permute-start | bytes 393224 | tf_op jit(solution)/shard_map/ppermute | solution.py:39
  28.4 5.5 %collective-permute-start.12 = (f32[8,128]{1,0:T(8,128)S(1)}, f32[8,128]{1,0:T(8,128)S(1)}, u32[]{:S(2)}, u32[]{:S(2)}) collective-permute-start(f32[8,128]{1,0:T(8,128)S(1)} %get-tuple-element.47.after.refs_0_), channel_id=1, source_target_pairs={{0,3},{1,2},{2,1},{3,0},{4,7},{5,6},{6,5},{7,4},{8,11},{9,10},{10,... | collective-permute-start | bytes 12296 | tf_op jit(solution)/shard_map/ppermute | solution.py:62
  30.2 3.6 %collective-permute-start.11 = (f32[8,128]{1,0:T(8,128)S(1)}, f32[8,128]{1,0:T(8,128)S(1)}, u32[]{:S(2)}, u32[]{:S(2)}) collective-permute-start(f32[8,128]{1,0:T(8,128)S(1)} %get-tuple-element.47.after.refs_0_), channel_id=1, source_target_pairs={{0,2},{1,3},{2,0},{3,1},{4,6},{5,7},{6,4},{7,5},{8,10},{9,11},{10,... | collective-permute-start | bytes 12296 | tf_op jit(solution)/shard_map/ppermute | solution.py:62
  30.7 3.2 %collective-permute-start.10 = (f32[8,128]{1,0:T(8,128)S(1)}, f32[8,128]{1,0:T(8,128)S(1)}, u32[]{:S(2)}, u32[]{:S(2)}) collective-permute-start(f32[8,128]{1,0:T(8,128)S(1)} %get-tuple-element.47.after.refs_0_), channel_id=1, source_target_pairs={{0,1},{1,0},{2,3},{3,2},{4,5},{5,4},{6,7},{7,6},{8,9},{9,8},{10,11... | collective-permute-start | bytes 12296 | tf_op jit(solution)/shard_map/ppermute | solution.py:62
  35.8 3.4 %collective-permute-start.15 = (f32[8,128]{1,0:T(8,128)S(1)}, f32[8,128]{1,0:T(8,128)S(1)}, u32[]{:S(2)}, u32[]{:S(2)}) collective-permute-start(f32[8,128]{1,0:T(8,128)S(1)} %shard_map.117.refs_0_), channel_id=1, source_target_pairs={{0,3},{1,2},{2,1},{3,0},{4,7},{5,6},{6,5},{7,4},{8,11},{9,10},{10,... | collective-permute-start | bytes 12296 | tf_op jit(solution)/shard_map/ppermute | solution.py:62
  36.5 2.7 %collective-permute-start.14 = (f32[8,128]{1,0:T(8,128)S(1)}, f32[8,128]{1,0:T(8,128)S(1)}, u32[]{:S(2)}, u32[]{:S(2)}) collective-permute-start(f32[8,128]{1,0:T(8,128)S(1)} %shard_map.117.refs_0_), channel_id=1, source_target_pairs={{0,2},{1,3},{2,0},{3,1},{4,6},{5,7},{6,4},{7,5},{8,10},{9,11},{10,... | collective-permute-start | bytes 12296 | tf_op jit(solution)/shard_map/ppermute | solution.py:62
  37.1 2.5 %collective-permute-start.13 = (f32[8,128]{1,0:T(8,128)S(1)}, f32[8,128]{1,0:T(8,128)S(1)}, u32[]{:S(2)}, u32[]{:S(2)}) collective-permute-start(f32[8,128]{1,0:T(8,128)S(1)} %shard_map.117.refs_0_), channel_id=1, source_target_pairs={{0,1},{1,0},{2,3},{3,2},{4,5},{5,4},{6,7},{7,6},{8,9},{9,8},{10,11... | collective-permute-start | bytes 12296 | tf_op jit(solution)/shard_map/ppermute | solution.py:62
  41.9 8.7 %collective-permute-start.16 = (bf16[1,1,256,256]{3,2,1,0:T(8,128)(2,1)S(1)}, bf16[1,1,256,256]{3,2,1,0:T(8,128)(2,1)S(1)}, u32[]{:S(2)}, u32[]{:S(2)}) collective-permute-start(bf16[1,1,256,256]{3,2,1,0:T(8,128)(2,1)S(1)} %get-tuple-element.60), channel_id=1, source_target_pairs={{0,4},{4,0},{8,12},{12,8},{16,20},{20,16},{24,28},{28,24},{1,5},{5... | collective-permute-start | bytes 393224 | tf_op jit(solution)/shard_map/ppermute | solution.py:34
  45.3 7.2 %collective-permute-start.17 = (bf16[1,1,256,256]{3,2,1,0:T(8,128)(2,1)S(1)}, bf16[1,1,256,256]{3,2,1,0:T(8,128)(2,1)S(1)}, u32[]{:S(2)}, u32[]{:S(2)}) collective-permute-start(bf16[1,1,256,256]{3,2,1,0:T(8,128)(2,1)S(1)} %get-tuple-element.61), channel_id=1, source_target_pairs={{0,0},{4,8},{8,4},{12,16},{16,12},{20,24},{24,20},{28,28},{1,1},{5... | collective-permute-start | bytes 393224 | tf_op jit(solution)/shard_map/ppermute | solution.py:34

commit v8 on v7

--- a/solution.py
+++ b/solution.py
@@ -276,9 +276,18 @@
         weight_out[...] = jnp.zeros_like(weight_out)
 
 
-def hand_kernel(near, far, out):
+def hand_kernel(near, far, target, out, sems):
     value = jnp.where(odd_segment(), near[...], far[...])
     out[...] = jnp.where(lax.axis_index("seg") > 0, value, jnp.zeros_like(value))
+    count = sems.shape[0]
+    step = out.shape[2] // count
+    copies = []
+    for i in range(count):
+        part = (0, 0, pl.ds(i * step, step))
+        copies.append(pltpu.make_async_copy(out.at[part], target.at[part], sems.at[i]))
+        copies[-1].start()
+    for copy in copies:
+        copy.wait()
 
 
 def store_kernel(value, out):
@@ -371,7 +380,13 @@
         aliases={len(operands): 0},
     )
     near = swap(near, "seg", 0)
-    (handed,) = call(hand_kernel, [jax.ShapeDtypeStruct(block, BF16)], near, far)
+    (handed,) = call(
+        hand_kernel,
+        [weight],
+        near, far,
+        scratch=[pltpu.VMEM(block, BF16), pltpu.SemaphoreType.DMA((4,))],
+        out_specs=[pl.BlockSpec(memory_space=pltpu.HBM)],
+    )
     (polar,) = call(store_kernel, [jax.ShapeDtypeStruct(block, F32)], polar, cost=SHORT)
     return polar, handed, energy
 

time: 53.4 us -> 53.4 us (level)
  no operation moved by 1% of the time
where the time goes in v8:
time: 53.4 us; the launch traced here: 53.2 us
  starting transfers between devices  24.8 us (46%)
  waiting for transfers between devices  15.2 us (28%)
  Pallas kernels  11.6 us (22%)
  between operations  1.62 us (3%)
    pallas_call x19, Pallas kernels, call(): pl.pallas_call(kernel, out_shape=outs, in_specs=in_specs or [VMEM] * len(...  11.6 us
    ppermute x9, starting transfers between devices, exchange(): parts.append(lax.ppermute(parts[0], axis, pairs))  8.55 us
    ppermute x2, starting transfers between devices, swap(): return lax.ppermute(value, axis, list(pairs.items()))  7.99 us
    ppermute x6, starting transfers between devices, rotate(): lax.ppermute(value, axis, [(source, (source + steps) % count) for source...  6.23 us
    ppermute x6, waiting for transfers between devices, rotate(): lax.ppermute(value, axis, [(source, (source + steps) % count) for source...  4.86 us
    ppermute x1, waiting for transfers between devices, shift(): lax.ppermute(value, axis, [(source, source + steps) for source in range(f...  4.52 us
    ppermute x9, waiting for transfers between devices, exchange(): parts.append(lax.ppermute(parts[0], axis, pairs))  3.86 us
    ppermute x1, starting transfers between devices, shift(): lax.ppermute(value, axis, [(source, source + steps) for source in range(f...  2.06 us
  transfers between devices with their start and end apart: 18, of which 8 were waited for; matrix products, arithmetic and copies ran while one was open for 0% of the time, Pallas kernels for 15%

profile of v8, /device:TPU:1, one launch (start us, length us, event | category | flops | bytes accessed | tf_op | source)
XLA Modules:
  0.0 53.2 jit_solution(7488101223395657098)
XLA Ops:
  0.7 2.1 %collective-permute-start = (bf16[256,256]{1,0:T(8,128)(2,1)}, bf16[256,256]{1,0:T(8,128)(2,1)S(1)}, u32[]{:S(2)}, u32[]{:S(2)}) collective-permute-start(bf16[256,256]{1,0:T(8,128)(2,1)} %bitcast.24), channel_id=1, source_target_pairs={{4,0},{8,4},{12,8},{16,12},{20,16},{24,20},{28,24},{5,1},{9,5},{13... | collective-permute-start | bytes 393224 | tf_op jit(solution)/shard_map/ppermute | solution.py:26
  3.7 4.5 %collective-permute-done.behind = bf16[256,256]{1,0:T(8,128)(2,1)S(1)} collective-permute-done((bf16[256,256]{1,0:T(8,128)(2,1)}, bf16[256,256]{1,0:T(8,128)(2,1)S(1)}, u32[]{:S(2)}, u32[]{:S(2)}) %collective-permute-start) | collective-permute-done | bytes 131104 | tf_op jit(solution)/shard_map/ppermute | solution.py:26
  8.4 1.3 %collective-permute-start.1 = (bf16[256,256]{1,0:T(8,128)(2,1)S(1)}, bf16[256,256]{1,0:T(8,128)(2,1)S(1)}, u32[]{:S(2)}, u32[]{:S(2)}) collective-permute-start(bf16[256,256]{1,0:T(8,128)(2,1)S(1)} %get-tuple-element.33.vector_b), channel_id=1, source_target_pairs={{0,1},{1,2},{2,3},{3,0},{4,5},{5,6},{6,7},{7,4},{8,9},{9,10},{10,1... | collective-permute-start | bytes 393224 | tf_op jit(solution)/shard_map/ppermute | solution.py:39
  9.7 1.3 %shard_map.106 = (f32[256,256]{1,0:T(8,128)S(1)}, f32[8,128]{1,0:T(8,128)S(1)}, f32[256,256]{1,0:T(8,128)S(1)}, bf16[256,256]{1,0:T(8,128)(2,1)S(1)}) custom-call(bf16[16,256,256]{2,1,0:T(8,128)(2,1)S(1)} %bitcast.9, bf16[16,256,256]{2,1,0:T(8,128)(2,1)S(1)} %bitcast.14, bf16[256,256]{1,0:T(8,128)(2,1)S(1)} %get-tuple-element.33.vector_b, ...), custom_call_target="tpu_custom_call" | custom-call | tf_op jit(solution)/shard_map/pallas_call | solution.py:308
  11.0 1.2 %collective-permute-start.2 = (bf16[256,256]{1,0:T(8,128)(2,1)S(1)}, bf16[256,256]{1,0:T(8,128)(2,1)S(1)}, u32[]{:S(2)}, u32[]{:S(2)}) collective-permute-start(bf16[256,256]{1,0:T(8,128)(2,1)S(1)} %get-tuple-element.38), channel_id=1, source_target_pairs={{0,3},{1,0},{2,1},{3,2},{4,7},{5,4},{6,5},{7,6},{8,11},{9,8},{10,9... | collective-permute-start | bytes 393224 | tf_op jit(solution)/shard_map/ppermute | solution.py:39
  12.2 1.6 %collective-permute-done.1.below.refs_4_.y = bf16[256,256]{1,0:T(8,128)(2,1)S(1)} collective-permute-done((bf16[256,256]{1,0:T(8,128)(2,1)S(1)}, bf16[256,256]{1,0:T(8,128)(2,1)S(1)}, u32[]{:S(2)}, u32[]{:S(2)}) %collective-permute-start.1) | collective-permute-done | bytes 131104 | tf_op jit(solution)/shard_map/ppermute | solution.py:39
  13.8 1.7 %collective-permute-start.6 = (f32[8,128]{1,0:T(8,128)S(1)}, f32[8,128]{1,0:T(8,128)S(1)}, u32[]{:S(2)}, u32[]{:S(2)}) collective-permute-start(f32[8,128]{1,0:T(8,128)S(1)} %shard_map.107.after.refs_0_), channel_id=1, source_target_pairs={{0,3},{1,2},{2,1},{3,0},{4,7},{5,6},{6,5},{7,4},{8,11},{9,10},{10,... | collective-permute-start | bytes 12296 | tf_op jit(solution)/shard_map/ppermute | solution.py:62
  15.5 0.7 %collective-permute-start.5 = (f32[8,128]{1,0:T(8,128)S(1)}, f32[8,128]{1,0:T(8,128)S(1)}, u32[]{:S(2)}, u32[]{:S(2)}) collective-permute-start(f32[8,128]{1,0:T(8,128)S(1)} %shard_map.107.after.refs_0_), channel_id=1, source_target_pairs={{0,2},{1,3},{2,0},{3,1},{4,6},{5,7},{6,4},{7,5},{8,10},{9,11},{10,... | collective-permute-start | bytes 12296 | tf_op jit(solution)/shard_map/ppermute | solution.py:62
  16.2 0.8 %collective-permute-start.4 = (f32[8,128]{1,0:T(8,128)S(1)}, f32[8,128]{1,0:T(8,128)S(1)}, u32[]{:S(2)}, u32[]{:S(2)}) collective-permute-start(f32[8,128]{1,0:T(8,128)S(1)} %shard_map.107.after.refs_0_), channel_id=1, source_target_pairs={{0,1},{1,0},{2,3},{3,2},{4,5},{5,4},{6,7},{7,6},{8,9},{9,8},{10,11... | collective-permute-start | bytes 12296 | tf_op jit(solution)/shard_map/ppermute | solution.py:62
  17.0 0.7 %collective-permute-start.7 = (bf16[256,256]{1,0:T(8,128)(2,1)S(1)}, bf16[256,256]{1,0:T(8,128)(2,1)S(1)}, u32[]{:S(2)}, u32[]{:S(2)}) collective-permute-start(bf16[256,256]{1,0:T(8,128)(2,1)S(1)} %bitcast.19), channel_id=1, source_target_pairs={{0,1},{1,2},{2,3},{3,0},{4,5},{5,6},{6,7},{7,4},{8,9},{9,10},{10,1... | collective-permute-start | bytes 393224 | tf_op jit(solution)/shard_map/ppermute | solution.py:39
  17.7 1.2 %shard_map.108.up = f32[256,256]{1,0:T(8,128)S(1)} custom-call(bf16[16,256,256]{2,1,0:T(8,128)(2,1)S(1)} %bitcast.10, bf16[16,256,256]{2,1,0:T(8,128)(2,1)S(1)} %bitcast.15, bf16[256,256]{1,0:T(8,128)(2,1)S(1)} %collective-permute-done.1.below.refs_4_.y, f32[8,128]{1,0:T(8,128)S(1)} %shard_map.107.after.refs_0_), custom_call_target="tpu_custom_call" | custom-call | tf_op jit(solution)/shard_map/pallas_call | solution.py:308
  19.0 2.0 %collective-permute-start.3 = (bf16[256,256]{1,0:T(8,128)(2,1)S(1)}, bf16[256,256]{1,0:T(8,128)(2,1)S(1)}, u32[]{:S(2)}, u32[]{:S(2)}) collective-permute-start(bf16[256,256]{1,0:T(8,128)(2,1)S(1)} %get-tuple-element.39), channel_id=1, source_target_pairs={{0,1},{1,2},{2,3},{3,0},{4,5},{5,6},{6,7},{7,4},{8,9},{9,10},{10,1... | collective-permute-start | bytes 393224 | tf_op jit(solution)/shard_map/ppermute | solution.py:39
  21.2 1.3 %shard_map.111 = (f32[256,256]{1,0:T(8,128)S(1)}, f32[8,128]{1,0:T(8,128)S(1)}, f32[256,256]{1,0:T(8,128)S(1)}, bf16[256,256]{1,0:T(8,128)(2,1)S(1)}) custom-call(bf16[16,256,256]{2,1,0:T(8,128)(2,1)S(1)} %bitcast.11, bf16[16,256,256]{2,1,0:T(8,128)(2,1)S(1)} %bitcast.16, bf16[256,256]{1,0:T(8,128)(2,1)S(1)} %get-tuple-element.41.vector_b, ...), custom_call_target="tpu_custom_call" | custom-call | tf_op jit(solution)/shard_map/pallas_call | solution.py:308
  23.0 2.2 %collective-permute-done.3.refs_5_.g = bf16[256,256]{1,0:T(8,128)(2,1)S(1)} collective-permute-done((bf16[256,256]{1,0:T(8,128)(2,1)S(1)}, bf16[256,256]{1,0:T(8,128)(2,1)S(1)}, u32[]{:S(2)}, u32[]{:S(2)}) %collective-permute-start.3) | collective-permute-done | bytes 131104 | tf_op jit(solution)/shard_map/ppermute | solution.py:39
  25.4 1.2 %shard_map.113.up = f32[256,256]{1,0:T(8,128)S(1)} custom-call(bf16[16,256,256]{2,1,0:T(8,128)(2,1)S(1)} %bitcast.12, bf16[16,256,256]{2,1,0:T(8,128)(2,1)S(1)} %bitcast.17, bf16[256,256]{1,0:T(8,128)(2,1)S(1)} %get-tuple-element.45.below.p, f32[8,128]{1,0:T(8,128)S(1)} %get-tuple-element.47.after.refs_0_), custom_call_target="tpu_custom_call" | custom-call | tf_op jit(solution)/shard_map/pallas_call | solution.py:308
  26.6 1.1 %collective-permute-done.8.above = bf16[256,256]{1,0:T(8,128)(2,1)S(1)} collective-permute-done((bf16[256,256]{1,0:T(8,128)(2,1)S(1)}, bf16[256,256]{1,0:T(8,128)(2,1)S(1)}, u32[]{:S(2)}, u32[]{:S(2)}) %collective-permute-start.8) | collective-permute-done | bytes 131104 | tf_op jit(solution)/shard_map/ppermute | solution.py:39
  27.8 0.6 %collective-permute-start.9 = (bf16[256,256]{1,0:T(8,128)(2,1)S(1)}, bf16[256,256]{1,0:T(8,128)(2,1)S(1)}, u32[]{:S(2)}, u32[]{:S(2)}) collective-permute-start(bf16[256,256]{1,0:T(8,128)(2,1)S(1)} %get-tuple-element.49), channel_id=1, source_target_pairs={{0,1},{1,2},{2,3},{3,0},{4,5},{5,6},{6,7},{7,4},{8,9},{9,10},{10,1... | collective-permute-start | bytes 393224 | tf_op jit(solution)/shard_map/ppermute | solution.py:39
  28.4 1.8 %collective-permute-start.12 = (f32[8,128]{1,0:T(8,128)S(1)}, f32[8,128]{1,0:T(8,128)S(1)}, u32[]{:S(2)}, u32[]{:S(2)}) collective-permute-start(f32[8,128]{1,0:T(8,128)S(1)} %get-tuple-element.47.after.refs_0_), channel_id=1, source_target_pairs={{0,3},{1,2},{2,1},{3,0},{4,7},{5,6},{6,5},{7,4},{8,11},{9,10},{10,... | collective-permute-start | bytes 12296 | tf_op jit(solution)/shard_map/ppermute | solution.py:62
  30.2 0.5 collective-permute-start.11
  31.1 2.8 %collective-permute-done.12.refs_3_ = f32[8,128]{1,0:T(8,128)S(1)} collective-permute-done((f32[8,128]{1,0:T(8,128)S(1)}, f32[8,128]{1,0:T(8,128)S(1)}, u32[]{:S(2)}, u32[]{:S(2)}) %collective-permute-start.12) | collective-permute-done | bytes 4128 | tf_op jit(solution)/shard_map/ppermute | solution.py:62
  34.2 1.3 %shard_map.116 = (f32[256,256]{1,0:T(8,128)S(1)}, f32[8,128]{1,0:T(8,128)S(1)}) custom-call(bf16[16,256,256]{2,1,0:T(8,128)(2,1)S(1)} %bitcast.13, bf16[16,256,256]{2,1,0:T(8,128)(2,1)S(1)} %bitcast.18, bf16[256,256]{1,0:T(8,128)(2,1)S(1)} %get-tuple-element.52.vector_b, f32[256,256]{1,0:T(8,128)S(1)} %get-tuple-element.53.refs_0_.refs_4_, ...), custom_call_target="tpu_custom_call" | custom-call | tf_op jit(solution)/shard_map/pallas_call | solution.py:308
  35.8 0.7 %collective-permute-start.15 = (f32[8,128]{1,0:T(8,128)S(1)}, f32[8,128]{1,0:T(8,128)S(1)}, u32[]{:S(2)}, u32[]{:S(2)}) collective-permute-start(f32[8,128]{1,0:T(8,128)S(1)} %shard_map.117.refs_0_), channel_id=1, source_target_pairs={{0,3},{1,2},{2,1},{3,0},{4,7},{5,6},{6,5},{7,4},{8,11},{9,10},{10,... | collective-permute-start | bytes 12296 | tf_op jit(solution)/shard_map/ppermute | solution.py:62
  36.5 0.6 %collective-permute-start.14 = (f32[8,128]{1,0:T(8,128)S(1)}, f32[8,128]{1,0:T(8,128)S(1)}, u32[]{:S(2)}, u32[]{:S(2)}) collective-permute-start(f32[8,128]{1,0:T(8,128)S(1)} %shard_map.117.refs_0_), channel_id=1, source_target_pairs={{0,2},{1,3},{2,0},{3,1},{4,6},{5,7},{6,4},{7,5},{8,10},{9,11},{10,... | collective-permute-start | bytes 12296 | tf_op jit(solution)/shard_map/ppermute | solution.py:62
  37.1 1.4 %collective-permute-start.13 = (f32[8,128]{1,0:T(8,128)S(1)}, f32[8,128]{1,0:T(8,128)S(1)}, u32[]{:S(2)}, u32[]{:S(2)}) collective-permute-start(f32[8,128]{1,0:T(8,128)S(1)} %shard_map.117.refs_0_), channel_id=1, source_target_pairs={{0,1},{1,0},{2,3},{3,2},{4,5},{5,4},{6,7},{7,6},{8,9},{9,8},{10,11... | collective-permute-start | bytes 12296 | tf_op jit(solution)/shard_map/ppermute | solution.py:62
  38.5 0.7 %collective-permute-done.15.refs_3_ = f32[8,128]{1,0:T(8,128)S(1)} collective-permute-done((f32[8,128]{1,0:T(8,128)S(1)}, f32[8,128]{1,0:T(8,128)S(1)}, u32[]{:S(2)}, u32[]{:S(2)}) %collective-permute-start.15) | collective-permute-done | bytes 4128 | tf_op jit(solution)/shard_map/ppermute | solution.py:62
  39.5 1.7 %shard_map.118 = (f32[256,256]{1,0:T(8,128)S(1)}, bf16[1,1,256,256]{3,2,1,0:T(8,128)(2,1)S(1)}) custom-call(f32[8,128]{1,0:T(8,128)S(1)} %shard_map.117.refs_0_, f32[8,128]{1,0:T(8,128)S(1)} %collective-permute-done.13.refs_1_, f32[8,128]{1,0:T(8,128)S(1)} %collective-permute-done.14.refs_2_, f32[8,128]{1,0:T(8,128)S(1)} %collective-permute-done.15.refs_3_, ...), custom_call_target="tpu_custom_call" | custom-call | tf_op jit(solution)/shard_map/pallas_call | solution.py:308
  41.2 0.7 %shard_map.119 = (f32[256,256]{1,0:T(8,128)S(1)}, bf16[1,1,256,256]{3,2,1,0:T(8,128)(2,1)S(1)}, f32[1]{0:T(128)}) custom-call(f32[8,128]{1,0:T(8,128)S(1)} %shard_map.117.refs_0_, f32[8,128]{1,0:T(8,128)S(1)} %collective-permute-done.13.refs_1_, f32[8,128]{1,0:T(8,128)S(1)} %collective-permute-done.14.refs_2_, ...), custom_call_target="tpu_custom_call", output_to_operand_aliasing={{0}: (7, {})} | custom-call | tf_op jit(solution)/shard_map/pallas_call | solution.py:308
  41.9 3.5 %collective-permute-start.16 = (bf16[1,1,256,256]{3,2,1,0:T(8,128)(2,1)S(1)}, bf16[1,1,256,256]{3,2,1,0:T(8,128)(2,1)S(1)}, u32[]{:S(2)}, u32[]{:S(2)}) collective-permute-start(bf16[1,1,256,256]{3,2,1,0:T(8,128)(2,1)S(1)} %get-tuple-element.60), channel_id=1, source_target_pairs={{0,4},{4,0},{8,12},{12,8},{16,20},{20,16},{24,28},{28,24},{1,5},{5... | collective-permute-start | bytes 393224 | tf_op jit(solution)/shard_map/ppermute | solution.py:34
  45.3 4.5 %collective-permute-start.17 = (bf16[1,1,256,256]{3,2,1,0:T(8,128)(2,1)S(1)}, bf16[1,1,256,256]{3,2,1,0:T(8,128)(2,1)S(1)}, u32[]{:S(2)}, u32[]{:S(2)}) collective-permute-start(bf16[1,1,256,256]{3,2,1,0:T(8,128)(2,1)S(1)} %get-tuple-element.61), channel_id=1, source_target_pairs={{0,0},{4,8},{8,4},{12,16},{16,12},{20,24},{24,20},{28,28},{1,1},{5... | collective-permute-start | bytes 393224 | tf_op jit(solution)/shard_map/ppermute | solution.py:34
  49.9 0.7 %shard_map.120 = f32[1,1,256,256]{3,2,1,0:T(8,128)} custom-call(f32[256,256]{1,0:T(8,128)S(1)} %get-tuple-element.59.value), custom_call_target="tpu_custom_call" | custom-call | bytes 1048576 | tf_op jit(solution)/shard_map/pallas_call | solution.py:308
  50.6 1.9 %collective-permute-done.17.far = bf16[1,1,256,256]{3,2,1,0:T(8,128)(2,1)S(1)} collective-permute-done((bf16[1,1,256,256]{3,2,1,0:T(8,128)(2,1)S(1)}, bf16[1,1,256,256]{3,2,1,0:T(8,128)(2,1)S(1)}, u32[]{:S(2)}, u32[]{:S(2)}) %collective-permute-start.17) | collective-permute-done | bytes 131104 | tf_op jit(solution)/shard_map/ppermute | solution.py:34
  52.5 0.7 %shard_map.121 = bf16[1,1,256,256]{3,2,1,0:T(8,128)(2,1)} custom-call(bf16[1,1,256,256]{3,2,1,0:T(8,128)(2,1)S(1)} %collective-permute-done.16.near, bf16[1,1,256,256]{3,2,1,0:T(8,128)(2,1)S(1)} %collective-permute-done.17.far), custom_call_target="tpu_custom_call" | custom-call | tf_op jit(solution)/shard_map/pallas_call | solution.py:308
  (36 shorter events, 2.7 us)
Async XLA Ops:
  0.6 3.0 %copy-start.4 = (bf16[1,1,256,256]{3,2,1,0:T(8,128)(2,1)S(1)}, bf16[1,1,256,256]{3,2,1,0:T(8,128)(2,1)}, u32[]{:S(2)}) copy-start(bf16[1,1,256,256]{3,2,1,0:T(8,128)(2,1)} %param.10) | copy-start | bytes 393220
  0.6 3.0 %copy-start.5 = (f32[1,1,256]{2,1,0:T(1,128)S(1)}, f32[1,1,256]{2,1,0:T(1,128)}, u32[]{:S(2)}) copy-start(f32[1,1,256]{2,1,0:T(1,128)} %param.13) | copy-start | bytes 3076
  0.7 7.6 %copy-start.3 = (bf16[1,1,256,256]{3,2,1,0:T(8,128)(2,1)S(1)}, bf16[1,1,256,256]{3,2,1,0:T(8,128)(2,1)}, u32[]{:S(2)}) copy-start(bf16[1,1,256,256]{3,2,1,0:T(8,128)(2,1)} %param.12) | copy-start | bytes 393220
  0.7 7.6 %collective-permute-start = (bf16[256,256]{1,0:T(8,128)(2,1)}, bf16[256,256]{1,0:T(8,128)(2,1)S(1)}, u32[]{:S(2)}, u32[]{:S(2)}) collective-permute-start(bf16[256,256]{1,0:T(8,128)(2,1)} %bitcast.24), channel_id=1, source_target_pairs={{4,0},{8,4},{12,8},{16,12},{20,16},{24,20},{28,24},{5,1},{9,5},{13... | collective-permute-start | bytes 393224 | tf_op jit(solution)/shard_map/ppermute | solution.py:26
  2.7 7.0 %copy-start = (bf16[1,1,16,256,256]{4,3,2,1,0:T(8,128)(2,1)S(1)}, bf16[1,1,16,256,256]{4,3,2,1,0:T(8,128)(2,1)}, u32[]{:S(2)}) copy-start(bf16[1,1,16,256,256]{4,3,2,1,0:T(8,128)(2,1)} %param.8) | copy-start | bytes 6291460
  2.7 7.0 %copy-start.1 = (bf16[1,1,16,256,256]{4,3,2,1,0:T(8,128)(2,1)S(1)}, bf16[1,1,16,256,256]{4,3,2,1,0:T(8,128)(2,1)}, u32[]{:S(2)}) copy-start(bf16[1,1,16,256,256]{4,3,2,1,0:T(8,128)(2,1)} %param.9) | copy-start | bytes 6291460
  8.4 5.3 %collective-permute-start.1 = (bf16[256,256]{1,0:T(8,128)(2,1)S(1)}, bf16[256,256]{1,0:T(8,128)(2,1)S(1)}, u32[]{:S(2)}, u32[]{:S(2)}) collective-permute-start(bf16[256,256]{1,0:T(8,128)(2,1)S(1)} %get-tuple-element.33.vector_b), channel_id=1, source_target_pairs={{0,1},{1,2},{2,3},{3,0},{4,5},{5,6},{6,7},{7,4},{8,9},{9,10},{10,1... | collective-permute-start | bytes 393224 | tf_op jit(solution)/shard_map/ppermute | solution.py:39
  9.7 7.3 %copy-start.2 = (bf16[1,1,256,256]{3,2,1,0:T(8,128)(2,1)S(1)}, bf16[1,1,256,256]{3,2,1,0:T(8,128)(2,1)}, u32[]{:S(2)}) copy-start(bf16[1,1,256,256]{3,2,1,0:T(8,128)(2,1)} %param.14) | copy-start | bytes 393220
  11.0 7.9 %collective-permute-start.2 = (bf16[256,256]{1,0:T(8,128)(2,1)S(1)}, bf16[256,256]{1,0:T(8,128)(2,1)S(1)}, u32[]{:S(2)}, u32[]{:S(2)}) collective-permute-start(bf16[256,256]{1,0:T(8,128)(2,1)S(1)} %get-tuple-element.38), channel_id=1, source_target_pairs={{0,3},{1,0},{2,1},{3,2},{4,7},{5,4},{6,5},{7,6},{8,11},{9,8},{10,9... | collective-permute-start | bytes 393224 | tf_op jit(solution)/shard_map/ppermute | solution.py:39
  13.8 7.2 %collective-permute-start.6 = (f32[8,128]{1,0:T(8,128)S(1)}, f32[8,128]{1,0:T(8,128)S(1)}, u32[]{:S(2)}, u32[]{:S(2)}) collective-permute-start(f32[8,128]{1,0:T(8,128)S(1)} %shard_map.107.after.refs_0_), channel_id=1, source_target_pairs={{0,3},{1,2},{2,1},{3,0},{4,7},{5,6},{6,5},{7,4},{8,11},{9,10},{10,... | collective-permute-start | bytes 12296 | tf_op jit(solution)/shard_map/ppermute | solution.py:62
  15.5 5.5 %collective-permute-start.5 = (f32[8,128]{1,0:T(8,128)S(1)}, f32[8,128]{1,0:T(8,128)S(1)}, u32[]{:S(2)}, u32[]{:S(2)}) collective-permute-start(f32[8,128]{1,0:T(8,128)S(1)} %shard_map.107.after.refs_0_), channel_id=1, source_target_pairs={{0,2},{1,3},{2,0},{3,1},{4,6},{5,7},{6,4},{7,5},{8,10},{9,11},{10,... | collective-permute-start | bytes 12296 | tf_op jit(solution)/shard_map/ppermute | solution.py:62
  16.2 4.8 %collective-permute-start.4 = (f32[8,128]{1,0:T(8,128)S(1)}, f32[8,128]{1,0:T(8,128)S(1)}, u32[]{:S(2)}, u32[]{:S(2)}) collective-permute-start(f32[8,128]{1,0:T(8,128)S(1)} %shard_map.107.after.refs_0_), channel_id=1, source_target_pairs={{0,1},{1,0},{2,3},{3,2},{4,5},{5,4},{6,7},{7,6},{8,9},{9,8},{10,11... | collective-permute-start | bytes 12296 | tf_op jit(solution)/shard_map/ppermute | solution.py:62
  17.0 6.0 %collective-permute-start.7 = (bf16[256,256]{1,0:T(8,128)(2,1)S(1)}, bf16[256,256]{1,0:T(8,128)(2,1)S(1)}, u32[]{:S(2)}, u32[]{:S(2)}) collective-permute-start(bf16[256,256]{1,0:T(8,128)(2,1)S(1)} %bitcast.19), channel_id=1, source_target_pairs={{0,1},{1,2},{2,3},{3,0},{4,5},{5,6},{6,7},{7,4},{8,9},{9,10},{10,1... | collective-permute-start | bytes 393224 | tf_op jit(solution)/shard_map/ppermute | solution.py:39
  19.0 6.2 %collective-permute-start.3 = (bf16[256,256]{1,0:T(8,128)(2,1)S(1)}, bf16[256,256]{1,0:T(8,128)(2,1)S(1)}, u32[]{:S(2)}, u32[]{:S(2)}) collective-permute-start(bf16[256,256]{1,0:T(8,128)(2,1)S(1)} %get-tuple-element.39), channel_id=1, source_target_pairs={{0,1},{1,2},{2,3},{3,0},{4,5},{5,6},{6,7},{7,4},{8,9},{9,10},{10,1... | collective-permute-start | bytes 393224 | tf_op jit(solution)/shard_map/ppermute | solution.py:39
  22.5 5.2 %collective-permute-start.8 = (bf16[256,256]{1,0:T(8,128)(2,1)S(1)}, bf16[256,256]{1,0:T(8,128)(2,1)S(1)}, u32[]{:S(2)}, u32[]{:S(2)}) collective-permute-start(bf16[256,256]{1,0:T(8,128)(2,1)S(1)} %get-tuple-element.48), channel_id=1, source_target_pairs={{0,3},{1,0},{2,1},{3,2},{4,7},{5,4},{6,5},{7,6},{8,11},{9,8},{10,9... | collective-permute-start | bytes 393224 | tf_op jit(solution)/shard_map/ppermute | solution.py:39
  27.8 7.7 %collective-permute-start.9 = (bf16[256,256]{1,0:T(8,128)(2,1)S(1)}, bf16[256,256]{1,0:T(8,128)(2,1)S(1)}, u32[]{:S(2)}, u32[]{:S(2)}) collective-permute-start(bf16[256,256]{1,0:T(8,128)(2,1)S(1)} %get-tuple-element.49), channel_id=1, source_target_pairs={{0,1},{1,2},{2,3},{3,0},{4,5},{5,6},{6,7},{7,4},{8,9},{9,10},{10,1... | collective-permute-start | bytes 393224 | tf_op jit(solution)/shard_map/ppermute | solution.py:39
  28.4 5.5 %collective-permute-start.12 = (f32[8,128]{1,0:T(8,128)S(1)}, f32[8,128]{1,0:T(8,128)S(1)}, u32[]{:S(2)}, u32[]{:S(2)}) collective-permute-start(f32[8,128]{1,0:T(8,128)S(1)} %get-tuple-element.47.after.refs_0_), channel_id=1, source_target_pairs={{0,3},{1,2},{2,1},{3,0},{4,7},{5,6},{6,5},{7,4},{8,11},{9,10},{10,... | collective-permute-start | bytes 12296 | tf_op jit(solution)/shard_map/ppermute | solution.py:62
  30.2 3.6 %collective-permute-start.11 = (f32[8,128]{1,0:T(8,128)S(1)}, f32[8,128]{1,0:T(8,128)S(1)}, u32[]{:S(2)}, u32[]{:S(2)}) collective-permute-start(f32[8,128]{1,0:T(8,128)S(1)} %get-tuple-element.47.after.refs_0_), channel_id=1, source_target_pairs={{0,2},{1,3},{2,0},{3,1},{4,6},{5,7},{6,4},{7,5},{8,10},{9,11},{10,... | collective-permute-start | bytes 12296 | tf_op jit(solution)/shard_map/ppermute | solution.py:62
  30.7 3.2 %collective-permute-start.10 = (f32[8,128]{1,0:T(8,128)S(1)}, f32[8,128]{1,0:T(8,128)S(1)}, u32[]{:S(2)}, u32[]{:S(2)}) collective-permute-start(f32[8,128]{1,0:T(8,128)S(1)} %get-tuple-element.47.after.refs_0_), channel_id=1, source_target_pairs={{0,1},{1,0},{2,3},{3,2},{4,5},{5,4},{6,7},{7,6},{8,9},{9,8},{10,11... | collective-permute-start | bytes 12296 | tf_op jit(solution)/shard_map/ppermute | solution.py:62
  35.8 3.4 %collective-permute-start.15 = (f32[8,128]{1,0:T(8,128)S(1)}, f32[8,128]{1,0:T(8,128)S(1)}, u32[]{:S(2)}, u32[]{:S(2)}) collective-permute-start(f32[8,128]{1,0:T(8,128)S(1)} %shard_map.117.refs_0_), channel_id=1, source_target_pairs={{0,3},{1,2},{2,1},{3,0},{4,7},{5,6},{6,5},{7,4},{8,11},{9,10},{10,... | collective-permute-start | bytes 12296 | tf_op jit(solution)/shard_map/ppermute | solution.py:62
  36.5 2.7 %collective-permute-start.14 = (f32[8,128]{1,0:T(8,128)S(1)}, f32[8,128]{1,0:T(8,128)S(1)}, u32[]{:S(2)}, u32[]{:S(2)}) collective-permute-start(f32[8,128]{1,0:T(8,128)S(1)} %shard_map.117.refs_0_), channel_id=1, source_target_pairs={{0,2},{1,3},{2,0},{3,1},{4,6},{5,7},{6,4},{7,5},{8,10},{9,11},{10,... | collective-permute-start | bytes 12296 | tf_op jit(solution)/shard_map/ppermute | solution.py:62
  37.1 2.5 %collective-permute-start.13 = (f32[8,128]{1,0:T(8,128)S(1)}, f32[8,128]{1,0:T(8,128)S(1)}, u32[]{:S(2)}, u32[]{:S(2)}) collective-permute-start(f32[8,128]{1,0:T(8,128)S(1)} %shard_map.117.refs_0_), channel_id=1, source_target_pairs={{0,1},{1,0},{2,3},{3,2},{4,5},{5,4},{6,7},{7,6},{8,9},{9,8},{10,11... | collective-permute-start | bytes 12296 | tf_op jit(solution)/shard_map/ppermute | solution.py:62
  41.9 8.7 %collective-permute-start.16 = (bf16[1,1,256,256]{3,2,1,0:T(8,128)(2,1)S(1)}, bf16[1,1,256,256]{3,2,1,0:T(8,128)(2,1)S(1)}, u32[]{:S(2)}, u32[]{:S(2)}) collective-permute-start(bf16[1,1,256,256]{3,2,1,0:T(8,128)(2,1)S(1)} %get-tuple-element.60), channel_id=1, source_target_pairs={{0,4},{4,0},{8,12},{12,8},{16,20},{20,16},{24,28},{28,24},{1,5},{5... | collective-permute-start | bytes 393224 | tf_op jit(solution)/shard_map/ppermute | solution.py:34
  45.3 7.2 %collective-permute-start.17 = (bf16[1,1,256,256]{3,2,1,0:T(8,128)(2,1)S(1)}, bf16[1,1,256,256]{3,2,1,0:T(8,128)(2,1)S(1)}, u32[]{:S(2)}, u32[]{:S(2)}) collective-permute-start(bf16[1,1,256,256]{3,2,1,0:T(8,128)(2,1)S(1)} %get-tuple-element.61), channel_id=1, source_target_pairs={{0,0},{4,8},{8,4},{12,16},{16,12},{20,24},{24,20},{28,28},{1,1},{5... | collective-permute-start | bytes 393224 | tf_op jit(solution)/shard_map/ppermute | solution.py:34

commit v9 on v7

--- a/solution.py
+++ b/solution.py
@@ -61,6 +61,20 @@
             pairs = [(source, source ^ (digit * done)) for source in range(count)]
             parts.append(lax.ppermute(parts[0], axis, pairs))
         done *= radix
+    return parts
+
+
+def pairwise(value, axis):
+    count = lax.axis_size(axis)
+    if count & (count - 1) or count == 1:
+        return exchange(value, axis)
+    stride, parts = count // 2, [value]
+    while stride:
+        if len(parts) > 1:
+            parts = [total(parts)]
+        pairs = [(source, source ^ stride) for source in range(count)]
+        parts.append(lax.ppermute(parts[0], axis, pairs))
+        stride //= 2
     return parts
 
 
@@ -331,7 +345,7 @@
     y_below = rotate(yb, "sec", 1)
     low, stat, diag, above = half(yb, [(0, 0), (0, None)], [y], 1)
     (stat,) = call(cross_kernel, [stats], y_below, low, stat)
-    parts = exchange(stat, "sec")
+    parts = pairwise(stat, "sec")
     g, gb = joined(y_below, stat, diag, above)
     g_below = rotate(gb, "sec", 1)
     kernel = functools.partial(first_kernel, len(parts))
@@ -341,7 +355,7 @@
     low, stat, diag, above = half(pb, pairs, [y, g, p], 1)
     kernel = functools.partial(first_cross_kernel, len(parts))
     stat, p_below = call(kernel, [stats, narrow], *parts, y_below, g_below, prec_below, low, stat)
-    parts = exchange(stat, "sec")
+    parts = pairwise(stat, "sec")
     hp, hpb = joined(p_below, stat, diag, above)
     hp_below = rotate(hpb, "sec", 1)
     kernel = functools.partial(second_kernel, len(parts))
@@ -371,7 +385,7 @@
         aliases={len(operands): 0},
     )
     near = swap(near, "seg", 0)
-    (handed,) = call(hand_kernel, [jax.ShapeDtypeStruct(block, BF16)], near, far)
+    (handed,) = call(hand_kernel, [weight], near, far)
     (polar,) = call(store_kernel, [jax.ShapeDtypeStruct(block, F32)], polar, cost=SHORT)
     return polar, handed, energy
 

time: 53.4 us -> 55.8 us (1.045)
  waiting for transfers between devices: 15.2 us -> 19.3 us
  starting transfers between devices: 24.8 us -> 23.1 us
    ppermute x0 -> x4, waiting for transfers between devices: none -> 6.25 us  [pairwise(): parts.append(lax.ppermute(parts[0], axis, pairs))]
    ppermute x9 -> x3, starting transfers between devices: 8.55 us -> 2.71 us  [exchange(): parts.append(lax.ppermute(parts[0], axis, pairs))]
    ppermute x0 -> x4, starting transfers between devices: none -> 2.97 us  [pairwise(): parts.append(lax.ppermute(parts[0], axis, pairs))]
    ppermute x9 -> x3, waiting for transfers between devices: 3.86 us -> 0.99 us  [exchange(): parts.append(lax.ppermute(parts[0], axis, pairs))]
    ppermute x6, waiting for transfers between devices: 4.86 us -> 5.62 us  [rotate(): lax.ppermute(value, axis, [(source, (source + steps) % count) for source...]
    ppermute x2, starting transfers between devices: 7.99 us -> 8.65 us  [swap(): return lax.ppermute(value, axis, list(pairs.items()))]
  transfers between devices with their start and end apart: 18 -> 16, of which waited for: 8 -> 12; matrix products, arithmetic and copies ran while one was open for 0% -> 0% of each run, Pallas kernels for 15% -> 14%
where the time goes in v9:
time: 55.8 us; the launch traced here: 55.6 us
  starting transfers between devices  23.1 us (41%)
  waiting for transfers between devices  19.3 us (35%)
  Pallas kernels  11.6 us (21%)
  between operations  1.62 us (3%)
    pallas_call x19, Pallas kernels, call(): pl.pallas_call(kernel, out_shape=outs, in_specs=in_specs or [VMEM] * len(...  11.6 us
    ppermute x2, starting transfers between devices, swap(): return lax.ppermute(value, axis, list(pairs.items()))  8.65 us
    ppermute x6, starting transfers between devices, rotate(): lax.ppermute(value, axis, [(source, (source + steps) % count) for source...  6.68 us
    ppermute x4, waiting for transfers between devices, pairwise(): parts.append(lax.ppermute(parts[0], axis, pairs))  6.25 us
    ppermute x6, waiting for transfers between devices, rotate(): lax.ppermute(value, axis, [(source, (source + steps) % count) for source...  5.62 us
    ppermute x1, waiting for transfers between devices, shift(): lax.ppermute(value, axis, [(source, source + steps) for source in range(f...  4.52 us
    ppermute x4, starting transfers between devices, pairwise(): parts.append(lax.ppermute(parts[0], axis, pairs))  2.97 us
    ppermute x3, starting transfers between devices, exchange(): parts.append(lax.ppermute(parts[0], axis, pairs))  2.71 us
  transfers between devices with their start and end apart: 16, of which 12 were waited for; matrix products, arithmetic and copies ran while one was open for 0% of the time, Pallas kernels for 14%

profile of v9, /device:TPU:1, one launch (start us, length us, event | category | flops | bytes accessed | tf_op | source)
XLA Modules:
  0.0 55.6 jit_solution(17037852593361717611)
XLA Ops:
  0.7 2.1 %collective-permute-start = (bf16[256,256]{1,0:T(8,128)(2,1)}, bf16[256,256]{1,0:T(8,128)(2,1)S(1)}, u32[]{:S(2)}, u32[]{:S(2)}) collective-permute-start(bf16[256,256]{1,0:T(8,128)(2,1)} %bitcast.24), channel_id=1, source_target_pairs={{4,0},{8,4},{12,8},{16,12},{20,16},{24,20},{28,24},{5,1},{9,5},{13... | collective-permute-start | bytes 393224 | tf_op jit(solution)/shard_map/ppermute | solution.py:26
  3.7 4.5 %collective-permute-done.behind = bf16[256,256]{1,0:T(8,128)(2,1)S(1)} collective-permute-done((bf16[256,256]{1,0:T(8,128)(2,1)}, bf16[256,256]{1,0:T(8,128)(2,1)S(1)}, u32[]{:S(2)}, u32[]{:S(2)}) %collective-permute-start) | collective-permute-done | bytes 131104 | tf_op jit(solution)/shard_map/ppermute | solution.py:26
  8.4 1.3 %collective-permute-start.1 = (bf16[256,256]{1,0:T(8,128)(2,1)S(1)}, bf16[256,256]{1,0:T(8,128)(2,1)S(1)}, u32[]{:S(2)}, u32[]{:S(2)}) collective-permute-start(bf16[256,256]{1,0:T(8,128)(2,1)S(1)} %get-tuple-element.33.vector_b), channel_id=1, source_target_pairs={{0,1},{1,2},{2,3},{3,0},{4,5},{5,6},{6,7},{7,4},{8,9},{9,10},{10,1... | collective-permute-start | bytes 393224 | tf_op jit(solution)/shard_map/ppermute | solution.py:39
  9.7 1.3 %shard_map.106 = (f32[256,256]{1,0:T(8,128)S(1)}, f32[8,128]{1,0:T(8,128)S(1)}, f32[256,256]{1,0:T(8,128)S(1)}, bf16[256,256]{1,0:T(8,128)(2,1)S(1)}) custom-call(bf16[16,256,256]{2,1,0:T(8,128)(2,1)S(1)} %bitcast.9, bf16[16,256,256]{2,1,0:T(8,128)(2,1)S(1)} %bitcast.14, bf16[256,256]{1,0:T(8,128)(2,1)S(1)} %get-tuple-element.33.vector_b, ...), custom_call_target="tpu_custom_call" | custom-call | tf_op jit(solution)/shard_map/pallas_call | solution.py:313
  11.0 1.2 %collective-permute-start.2 = (bf16[256,256]{1,0:T(8,128)(2,1)S(1)}, bf16[256,256]{1,0:T(8,128)(2,1)S(1)}, u32[]{:S(2)}, u32[]{:S(2)}) collective-permute-start(bf16[256,256]{1,0:T(8,128)(2,1)S(1)} %get-tuple-element.38), channel_id=1, source_target_pairs={{0,3},{1,0},{2,1},{3,2},{4,7},{5,4},{6,5},{7,6},{8,11},{9,8},{10,9... | collective-permute-start | bytes 393224 | tf_op jit(solution)/shard_map/ppermute | solution.py:39
  12.2 1.6 %collective-permute-done.1.below.refs_2_.y = bf16[256,256]{1,0:T(8,128)(2,1)S(1)} collective-permute-done((bf16[256,256]{1,0:T(8,128)(2,1)S(1)}, bf16[256,256]{1,0:T(8,128)(2,1)S(1)}, u32[]{:S(2)}, u32[]{:S(2)}) %collective-permute-start.1) | collective-permute-done | bytes 131104 | tf_op jit(solution)/shard_map/ppermute | solution.py:39
  13.8 2.0 %collective-permute-start.4 = (f32[8,128]{1,0:T(8,128)S(1)}, f32[8,128]{1,0:T(8,128)S(1)}, u32[]{:S(2)}, u32[]{:S(2)}) collective-permute-start(f32[8,128]{1,0:T(8,128)S(1)} %shard_map.107.after), channel_id=1, source_target_pairs={{0,2},{1,3},{2,0},{3,1},{4,6},{5,7},{6,4},{7,5},{8,10},{9,11},{10,... | collective-permute-start | bytes 12296 | tf_op jit(solution)/shard_map/ppermute | solution.py:76
  15.8 1.0 %collective-permute-done.4 = f32[8,128]{1,0:T(8,128)S(1)} collective-permute-done((f32[8,128]{1,0:T(8,128)S(1)}, f32[8,128]{1,0:T(8,128)S(1)}, u32[]{:S(2)}, u32[]{:S(2)}) %collective-permute-start.4) | collective-permute-done | bytes 4128 | tf_op jit(solution)/shard_map/ppermute | solution.py:76
  16.8 0.7 %collective-permute-start.5 = (f32[8,128]{1,0:T(8,128)S(1)}, f32[8,128]{1,0:T(8,128)S(1)}, u32[]{:S(2)}, u32[]{:S(2)}) collective-permute-start(f32[8,128]{1,0:T(8,128)S(1)} %add.6.refs_0_), channel_id=1, source_target_pairs={{0,1},{1,0},{2,3},{3,2},{4,5},{5,4},{6,7},{7,6},{8,9},{9,8},{10,11... | collective-permute-start | bytes 12296 | tf_op jit(solution)/shard_map/ppermute | solution.py:76
  17.5 0.8 %collective-permute-start.6 = (bf16[256,256]{1,0:T(8,128)(2,1)S(1)}, bf16[256,256]{1,0:T(8,128)(2,1)S(1)}, u32[]{:S(2)}, u32[]{:S(2)}) collective-permute-start(bf16[256,256]{1,0:T(8,128)(2,1)S(1)} %bitcast.19), channel_id=1, source_target_pairs={{0,1},{1,2},{2,3},{3,0},{4,5},{5,6},{6,7},{7,4},{8,9},{9,10},{10,1... | collective-permute-start | bytes 393224 | tf_op jit(solution)/shard_map/ppermute | solution.py:39
  18.3 1.2 %shard_map.108.up = f32[256,256]{1,0:T(8,128)S(1)} custom-call(bf16[16,256,256]{2,1,0:T(8,128)(2,1)S(1)} %bitcast.10, bf16[16,256,256]{2,1,0:T(8,128)(2,1)S(1)} %bitcast.15, bf16[256,256]{1,0:T(8,128)(2,1)S(1)} %collective-permute-done.1.below.refs_2_.y, f32[8,128]{1,0:T(8,128)S(1)} %shard_map.107.after), custom_call_target="tpu_custom_call" | custom-call | tf_op jit(solution)/shard_map/pallas_call | solution.py:313
  19.6 1.3 %collective-permute-start.3 = (bf16[256,256]{1,0:T(8,128)(2,1)S(1)}, bf16[256,256]{1,0:T(8,128)(2,1)S(1)}, u32[]{:S(2)}, u32[]{:S(2)}) collective-permute-start(bf16[256,256]{1,0:T(8,128)(2,1)S(1)} %get-tuple-element.39), channel_id=1, source_target_pairs={{0,1},{1,2},{2,3},{3,0},{4,5},{5,6},{6,7},{7,4},{8,9},{9,10},{10,1... | collective-permute-start | bytes 393224 | tf_op jit(solution)/shard_map/ppermute | solution.py:39
  21.1 1.3 %shard_map.111 = (f32[256,256]{1,0:T(8,128)S(1)}, f32[8,128]{1,0:T(8,128)S(1)}, f32[256,256]{1,0:T(8,128)S(1)}, bf16[256,256]{1,0:T(8,128)(2,1)S(1)}) custom-call(bf16[16,256,256]{2,1,0:T(8,128)(2,1)S(1)} %bitcast.11, bf16[16,256,256]{2,1,0:T(8,128)(2,1)S(1)} %bitcast.16, bf16[256,256]{1,0:T(8,128)(2,1)S(1)} %get-tuple-element.41.vector_b, ...), custom_call_target="tpu_custom_call" | custom-call | tf_op jit(solution)/shard_map/pallas_call | solution.py:313
  22.4 1.2 %collective-permute-start.7 = (bf16[256,256]{1,0:T(8,128)(2,1)S(1)}, bf16[256,256]{1,0:T(8,128)(2,1)S(1)}, u32[]{:S(2)}, u32[]{:S(2)}) collective-permute-start(bf16[256,256]{1,0:T(8,128)(2,1)S(1)} %get-tuple-element.48), channel_id=1, source_target_pairs={{0,3},{1,0},{2,1},{3,2},{4,7},{5,4},{6,5},{7,6},{8,11},{9,8},{10,9... | collective-permute-start | bytes 393224 | tf_op jit(solution)/shard_map/ppermute | solution.py:39
  23.9 2.5 %collective-permute-done.3.refs_3_.g = bf16[256,256]{1,0:T(8,128)(2,1)S(1)} collective-permute-done((bf16[256,256]{1,0:T(8,128)(2,1)S(1)}, bf16[256,256]{1,0:T(8,128)(2,1)S(1)}, u32[]{:S(2)}, u32[]{:S(2)}) %collective-permute-start.3) | collective-permute-done | bytes 131104 | tf_op jit(solution)/shard_map/ppermute | solution.py:39
  26.7 1.2 %shard_map.113.up = f32[256,256]{1,0:T(8,128)S(1)} custom-call(bf16[16,256,256]{2,1,0:T(8,128)(2,1)S(1)} %bitcast.12, bf16[16,256,256]{2,1,0:T(8,128)(2,1)S(1)} %bitcast.17, bf16[256,256]{1,0:T(8,128)(2,1)S(1)} %get-tuple-element.45.below.p, f32[8,128]{1,0:T(8,128)S(1)} %get-tuple-element.47.after), custom_call_target="tpu_custom_call" | custom-call | tf_op jit(solution)/shard_map/pallas_call | solution.py:313
  27.9 1.2 %collective-permute-done.7.above = bf16[256,256]{1,0:T(8,128)(2,1)S(1)} collective-permute-done((bf16[256,256]{1,0:T(8,128)(2,1)S(1)}, bf16[256,256]{1,0:T(8,128)(2,1)S(1)}, u32[]{:S(2)}, u32[]{:S(2)}) %collective-permute-start.7) | collective-permute-done | bytes 131104 | tf_op jit(solution)/shard_map/ppermute | solution.py:39
  29.2 1.0 %collective-permute-start.8 = (bf16[256,256]{1,0:T(8,128)(2,1)S(1)}, bf16[256,256]{1,0:T(8,128)(2,1)S(1)}, u32[]{:S(2)}, u32[]{:S(2)}) collective-permute-start(bf16[256,256]{1,0:T(8,128)(2,1)S(1)} %get-tuple-element.49), channel_id=1, source_target_pairs={{0,1},{1,2},{2,3},{3,0},{4,5},{5,6},{6,7},{7,4},{8,9},{9,10},{10,1... | collective-permute-start | bytes 393224 | tf_op jit(solution)/shard_map/ppermute | solution.py:39
  30.4 2.6 %collective-permute-done.9 = f32[8,128]{1,0:T(8,128)S(1)} collective-permute-done((f32[8,128]{1,0:T(8,128)S(1)}, f32[8,128]{1,0:T(8,128)S(1)}, u32[]{:S(2)}, u32[]{:S(2)}) %collective-permute-start.9) | collective-permute-done | bytes 4128 | tf_op jit(solution)/shard_map/ppermute | solution.py:76
  33.0 2.7 %collective-permute-done.10.refs_1_ = f32[8,128]{1,0:T(8,128)S(1)} collective-permute-done((f32[8,128]{1,0:T(8,128)S(1)}, f32[8,128]{1,0:T(8,128)S(1)}, u32[]{:S(2)}, u32[]{:S(2)}) %collective-permute-start.10) | collective-permute-done | bytes 4128 | tf_op jit(solution)/shard_map/ppermute | solution.py:76
  35.7 0.4 shard_map.115
  36.1 1.3 %shard_map.116 = (f32[256,256]{1,0:T(8,128)S(1)}, f32[8,128]{1,0:T(8,128)S(1)}) custom-call(bf16[16,256,256]{2,1,0:T(8,128)(2,1)S(1)} %bitcast.13, bf16[16,256,256]{2,1,0:T(8,128)(2,1)S(1)} %bitcast.18, bf16[256,256]{1,0:T(8,128)(2,1)S(1)} %get-tuple-element.52.vector_b, f32[256,256]{1,0:T(8,128)S(1)} %get-tuple-element.53.refs_0_.refs_4_, ...), custom_call_target="tpu_custom_call" | custom-call | tf_op jit(solution)/shard_map/pallas_call | solution.py:313
  37.6 1.2 %collective-permute-start.13 = (f32[8,128]{1,0:T(8,128)S(1)}, f32[8,128]{1,0:T(8,128)S(1)}, u32[]{:S(2)}, u32[]{:S(2)}) collective-permute-start(f32[8,128]{1,0:T(8,128)S(1)} %shard_map.117.refs_0_), channel_id=1, source_target_pairs={{0,3},{1,2},{2,1},{3,0},{4,7},{5,6},{6,5},{7,4},{8,11},{9,10},{10,... | collective-permute-start | bytes 12296 | tf_op jit(solution)/shard_map/ppermute | solution.py:62
  38.8 1.5 %collective-permute-start.11 = (f32[8,128]{1,0:T(8,128)S(1)}, f32[8,128]{1,0:T(8,128)S(1)}, u32[]{:S(2)}, u32[]{:S(2)}) collective-permute-start(f32[8,128]{1,0:T(8,128)S(1)} %shard_map.117.refs_0_), channel_id=1, source_target_pairs={{0,1},{1,0},{2,3},{3,2},{4,5},{5,4},{6,7},{7,6},{8,9},{9,8},{10,11... | collective-permute-start | bytes 12296 | tf_op jit(solution)/shard_map/ppermute | solution.py:62
  40.3 0.7 %collective-permute-done.13.refs_3_ = f32[8,128]{1,0:T(8,128)S(1)} collective-permute-done((f32[8,128]{1,0:T(8,128)S(1)}, f32[8,128]{1,0:T(8,128)S(1)}, u32[]{:S(2)}, u32[]{:S(2)}) %collective-permute-start.13) | collective-permute-done | bytes 4128 | tf_op jit(solution)/shard_map/ppermute | solution.py:62
  41.3 1.7 %shard_map.118 = (f32[256,256]{1,0:T(8,128)S(1)}, bf16[1,1,256,256]{3,2,1,0:T(8,128)(2,1)S(1)}) custom-call(f32[8,128]{1,0:T(8,128)S(1)} %shard_map.117.refs_0_, f32[8,128]{1,0:T(8,128)S(1)} %collective-permute-done.11.refs_1_, f32[8,128]{1,0:T(8,128)S(1)} %collective-permute-done.12.refs_2_, f32[8,128]{1,0:T(8,128)S(1)} %collective-permute-done.13.refs_3_, ...), custom_call_target="tpu_custom_call" | custom-call | tf_op jit(solution)/shard_map/pallas_call | solution.py:313
  43.0 0.7 %shard_map.119 = (f32[256,256]{1,0:T(8,128)S(1)}, bf16[1,1,256,256]{3,2,1,0:T(8,128)(2,1)S(1)}, f32[1]{0:T(128)}) custom-call(f32[8,128]{1,0:T(8,128)S(1)} %shard_map.117.refs_0_, f32[8,128]{1,0:T(8,128)S(1)} %collective-permute-done.11.refs_1_, f32[8,128]{1,0:T(8,128)S(1)} %collective-permute-done.12.refs_2_, ...), custom_call_target="tpu_custom_call", output_to_operand_aliasing={{0}: (7, {})} | custom-call | tf_op jit(solution)/shard_map/pallas_call | solution.py:313
  43.7 4.2 %collective-permute-start.14 = (bf16[1,1,256,256]{3,2,1,0:T(8,128)(2,1)S(1)}, bf16[1,1,256,256]{3,2,1,0:T(8,128)(2,1)S(1)}, u32[]{:S(2)}, u32[]{:S(2)}) collective-permute-start(bf16[1,1,256,256]{3,2,1,0:T(8,128)(2,1)S(1)} %get-tuple-element.60), channel_id=1, source_target_pairs={{0,4},{4,0},{8,12},{12,8},{16,20},{20,16},{24,28},{28,24},{1,5},{5... | collective-permute-start | bytes 393224 | tf_op jit(solution)/shard_map/ppermute | solution.py:34
  47.8 4.5 %collective-permute-start.15 = (bf16[1,1,256,256]{3,2,1,0:T(8,128)(2,1)S(1)}, bf16[1,1,256,256]{3,2,1,0:T(8,128)(2,1)S(1)}, u32[]{:S(2)}, u32[]{:S(2)}) collective-permute-start(bf16[1,1,256,256]{3,2,1,0:T(8,128)(2,1)S(1)} %get-tuple-element.61), channel_id=1, source_target_pairs={{0,0},{4,8},{8,4},{12,16},{16,12},{20,24},{24,20},{28,28},{1,1},{5... | collective-permute-start | bytes 393224 | tf_op jit(solution)/shard_map/ppermute | solution.py:34
  52.3 0.7 %shard_map.120 = f32[1,1,256,256]{3,2,1,0:T(8,128)} custom-call(f32[256,256]{1,0:T(8,128)S(1)} %get-tuple-element.59.value), custom_call_target="tpu_custom_call" | custom-call | bytes 1048576 | tf_op jit(solution)/shard_map/pallas_call | solution.py:313
  53.0 1.9 %collective-permute-done.15.far = bf16[1,1,256,256]{3,2,1,0:T(8,128)(2,1)S(1)} collective-permute-done((bf16[1,1,256,256]{3,2,1,0:T(8,128)(2,1)S(1)}, bf16[1,1,256,256]{3,2,1,0:T(8,128)(2,1)S(1)}, u32[]{:S(2)}, u32[]{:S(2)}) %collective-permute-start.15) | collective-permute-done | bytes 131104 | tf_op jit(solution)/shard_map/ppermute | solution.py:34
  55.0 0.7 %shard_map.121 = bf16[1,1,256,256]{3,2,1,0:T(8,128)(2,1)} custom-call(bf16[1,1,256,256]{3,2,1,0:T(8,128)(2,1)S(1)} %collective-permute-done.14.near, bf16[1,1,256,256]{3,2,1,0:T(8,128)(2,1)S(1)} %collective-permute-done.15.far), custom_call_target="tpu_custom_call" | custom-call | tf_op jit(solution)/shard_map/pallas_call | solution.py:313
  (34 shorter events, 2.1 us)
Async XLA Ops:
  0.6 3.0 %copy-start.4 = (bf16[1,1,256,256]{3,2,1,0:T(8,128)(2,1)S(1)}, bf16[1,1,256,256]{3,2,1,0:T(8,128)(2,1)}, u32[]{:S(2)}) copy-start(bf16[1,1,256,256]{3,2,1,0:T(8,128)(2,1)} %param.10) | copy-start | bytes 393220
  0.6 3.0 %copy-start.5 = (f32[1,1,256]{2,1,0:T(1,128)S(1)}, f32[1,1,256]{2,1,0:T(1,128)}, u32[]{:S(2)}) copy-start(f32[1,1,256]{2,1,0:T(1,128)} %param.13) | copy-start | bytes 3076
  0.7 7.6 %copy-start.3 = (bf16[1,1,256,256]{3,2,1,0:T(8,128)(2,1)S(1)}, bf16[1,1,256,256]{3,2,1,0:T(8,128)(2,1)}, u32[]{:S(2)}) copy-start(bf16[1,1,256,256]{3,2,1,0:T(8,128)(2,1)} %param.12) | copy-start | bytes 393220
  0.7 7.6 %collective-permute-start = (bf16[256,256]{1,0:T(8,128)(2,1)}, bf16[256,256]{1,0:T(8,128)(2,1)S(1)}, u32[]{:S(2)}, u32[]{:S(2)}) collective-permute-start(bf16[256,256]{1,0:T(8,128)(2,1)} %bitcast.24), channel_id=1, source_target_pairs={{4,0},{8,4},{12,8},{16,12},{20,16},{24,20},{28,24},{5,1},{9,5},{13... | collective-permute-start | bytes 393224 | tf_op jit(solution)/shard_map/ppermute | solution.py:26
  2.7 7.0 %copy-start = (bf16[1,1,16,256,256]{4,3,2,1,0:T(8,128)(2,1)S(1)}, bf16[1,1,16,256,256]{4,3,2,1,0:T(8,128)(2,1)}, u32[]{:S(2)}) copy-start(bf16[1,1,16,256,256]{4,3,2,1,0:T(8,128)(2,1)} %param.8) | copy-start | bytes 6291460
  2.7 7.0 %copy-start.1 = (bf16[1,1,16,256,256]{4,3,2,1,0:T(8,128)(2,1)S(1)}, bf16[1,1,16,256,256]{4,3,2,1,0:T(8,128)(2,1)}, u32[]{:S(2)}) copy-start(bf16[1,1,16,256,256]{4,3,2,1,0:T(8,128)(2,1)} %param.9) | copy-start | bytes 6291460
  8.4 5.3 %collective-permute-start.1 = (bf16[256,256]{1,0:T(8,128)(2,1)S(1)}, bf16[256,256]{1,0:T(8,128)(2,1)S(1)}, u32[]{:S(2)}, u32[]{:S(2)}) collective-permute-start(bf16[256,256]{1,0:T(8,128)(2,1)S(1)} %get-tuple-element.33.vector_b), channel_id=1, source_target_pairs={{0,1},{1,2},{2,3},{3,0},{4,5},{5,6},{6,7},{7,4},{8,9},{9,10},{10,1... | collective-permute-start | bytes 393224 | tf_op jit(solution)/shard_map/ppermute | solution.py:39
  9.7 7.8 %copy-start.2 = (bf16[1,1,256,256]{3,2,1,0:T(8,128)(2,1)S(1)}, bf16[1,1,256,256]{3,2,1,0:T(8,128)(2,1)}, u32[]{:S(2)}) copy-start(bf16[1,1,256,256]{3,2,1,0:T(8,128)(2,1)} %param.14) | copy-start | bytes 393220
  11.0 8.5 %collective-permute-start.2 = (bf16[256,256]{1,0:T(8,128)(2,1)S(1)}, bf16[256,256]{1,0:T(8,128)(2,1)S(1)}, u32[]{:S(2)}, u32[]{:S(2)}) collective-permute-start(bf16[256,256]{1,0:T(8,128)(2,1)S(1)} %get-tuple-element.38), channel_id=1, source_target_pairs={{0,3},{1,0},{2,1},{3,2},{4,7},{5,4},{6,5},{7,6},{8,11},{9,8},{10,9... | collective-permute-start | bytes 393224 | tf_op jit(solution)/shard_map/ppermute | solution.py:39
  13.8 3.0 %collective-permute-start.4 = (f32[8,128]{1,0:T(8,128)S(1)}, f32[8,128]{1,0:T(8,128)S(1)}, u32[]{:S(2)}, u32[]{:S(2)}) collective-permute-start(f32[8,128]{1,0:T(8,128)S(1)} %shard_map.107.after), channel_id=1, source_target_pairs={{0,2},{1,3},{2,0},{3,1},{4,6},{5,7},{6,4},{7,5},{8,10},{9,11},{10,... | collective-permute-start | bytes 12296 | tf_op jit(solution)/shard_map/ppermute | solution.py:76
  16.8 4.1 %collective-permute-start.5 = (f32[8,128]{1,0:T(8,128)S(1)}, f32[8,128]{1,0:T(8,128)S(1)}, u32[]{:S(2)}, u32[]{:S(2)}) collective-permute-start(f32[8,128]{1,0:T(8,128)S(1)} %add.6.refs_0_), channel_id=1, source_target_pairs={{0,1},{1,0},{2,3},{3,2},{4,5},{5,4},{6,7},{7,6},{8,9},{9,8},{10,11... | collective-permute-start | bytes 12296 | tf_op jit(solution)/shard_map/ppermute | solution.py:76
  17.5 6.4 %collective-permute-start.6 = (bf16[256,256]{1,0:T(8,128)(2,1)S(1)}, bf16[256,256]{1,0:T(8,128)(2,1)S(1)}, u32[]{:S(2)}, u32[]{:S(2)}) collective-permute-start(bf16[256,256]{1,0:T(8,128)(2,1)S(1)} %bitcast.19), channel_id=1, source_target_pairs={{0,1},{1,2},{2,3},{3,0},{4,5},{5,6},{6,7},{7,4},{8,9},{9,10},{10,1... | collective-permute-start | bytes 393224 | tf_op jit(solution)/shard_map/ppermute | solution.py:39
  19.6 6.8 %collective-permute-start.3 = (bf16[256,256]{1,0:T(8,128)(2,1)S(1)}, bf16[256,256]{1,0:T(8,128)(2,1)S(1)}, u32[]{:S(2)}, u32[]{:S(2)}) collective-permute-start(bf16[256,256]{1,0:T(8,128)(2,1)S(1)} %get-tuple-element.39), channel_id=1, source_target_pairs={{0,1},{1,2},{2,3},{3,0},{4,5},{5,6},{6,7},{7,4},{8,9},{9,10},{10,1... | collective-permute-start | bytes 393224 | tf_op jit(solution)/shard_map/ppermute | solution.py:39
  22.4 6.7 %collective-permute-start.7 = (bf16[256,256]{1,0:T(8,128)(2,1)S(1)}, bf16[256,256]{1,0:T(8,128)(2,1)S(1)}, u32[]{:S(2)}, u32[]{:S(2)}) collective-permute-start(bf16[256,256]{1,0:T(8,128)(2,1)S(1)} %get-tuple-element.48), channel_id=1, source_target_pairs={{0,3},{1,0},{2,1},{3,2},{4,7},{5,4},{6,5},{7,6},{8,11},{9,8},{10,9... | collective-permute-start | bytes 393224 | tf_op jit(solution)/shard_map/ppermute | solution.py:39
  29.2 8.2 %collective-permute-start.8 = (bf16[256,256]{1,0:T(8,128)(2,1)S(1)}, bf16[256,256]{1,0:T(8,128)(2,1)S(1)}, u32[]{:S(2)}, u32[]{:S(2)}) collective-permute-start(bf16[256,256]{1,0:T(8,128)(2,1)S(1)} %get-tuple-element.49), channel_id=1, source_target_pairs={{0,1},{1,2},{2,3},{3,0},{4,5},{5,6},{6,7},{7,4},{8,9},{9,10},{10,1... | collective-permute-start | bytes 393224 | tf_op jit(solution)/shard_map/ppermute | solution.py:39
  30.1 2.9 %collective-permute-start.9 = (f32[8,128]{1,0:T(8,128)S(1)}, f32[8,128]{1,0:T(8,128)S(1)}, u32[]{:S(2)}, u32[]{:S(2)}) collective-permute-start(f32[8,128]{1,0:T(8,128)S(1)} %get-tuple-element.47.after), channel_id=1, source_target_pairs={{0,2},{1,3},{2,0},{3,1},{4,6},{5,7},{6,4},{7,5},{8,10},{9,11},{10,... | collective-permute-start | bytes 12296 | tf_op jit(solution)/shard_map/ppermute | solution.py:76
  33.0 2.7 %collective-permute-start.10 = (f32[8,128]{1,0:T(8,128)S(1)}, f32[8,128]{1,0:T(8,128)S(1)}, u32[]{:S(2)}, u32[]{:S(2)}) collective-permute-start(f32[8,128]{1,0:T(8,128)S(1)} %add.7.refs_0_), channel_id=1, source_target_pairs={{0,1},{1,0},{2,3},{3,2},{4,5},{5,4},{6,7},{7,6},{8,9},{9,8},{10,11... | collective-permute-start | bytes 12296 | tf_op jit(solution)/shard_map/ppermute | solution.py:76
  37.6 3.4 %collective-permute-start.13 = (f32[8,128]{1,0:T(8,128)S(1)}, f32[8,128]{1,0:T(8,128)S(1)}, u32[]{:S(2)}, u32[]{:S(2)}) collective-permute-start(f32[8,128]{1,0:T(8,128)S(1)} %shard_map.117.refs_0_), channel_id=1, source_target_pairs={{0,3},{1,2},{2,1},{3,0},{4,7},{5,6},{6,5},{7,4},{8,11},{9,10},{10,... | collective-permute-start | bytes 12296 | tf_op jit(solution)/shard_map/ppermute | solution.py:62
  38.8 2.5 %collective-permute-start.12 = (f32[8,128]{1,0:T(8,128)S(1)}, f32[8,128]{1,0:T(8,128)S(1)}, u32[]{:S(2)}, u32[]{:S(2)}) collective-permute-start(f32[8,128]{1,0:T(8,128)S(1)} %shard_map.117.refs_0_), channel_id=1, source_target_pairs={{0,2},{1,3},{2,0},{3,1},{4,6},{5,7},{6,4},{7,5},{8,10},{9,11},{10,... | collective-permute-start | bytes 12296 | tf_op jit(solution)/shard_map/ppermute | solution.py:62
  38.8 2.5 %collective-permute-start.11 = (f32[8,128]{1,0:T(8,128)S(1)}, f32[8,128]{1,0:T(8,128)S(1)}, u32[]{:S(2)}, u32[]{:S(2)}) collective-permute-start(f32[8,128]{1,0:T(8,128)S(1)} %shard_map.117.refs_0_), channel_id=1, source_target_pairs={{0,1},{1,0},{2,3},{3,2},{4,5},{5,4},{6,7},{7,6},{8,9},{9,8},{10,11... | collective-permute-start | bytes 12296 | tf_op jit(solution)/shard_map/ppermute | solution.py:62
  43.7 9.4 %collective-permute-start.14 = (bf16[1,1,256,256]{3,2,1,0:T(8,128)(2,1)S(1)}, bf16[1,1,256,256]{3,2,1,0:T(8,128)(2,1)S(1)}, u32[]{:S(2)}, u32[]{:S(2)}) collective-permute-start(bf16[1,1,256,256]{3,2,1,0:T(8,128)(2,1)S(1)} %get-tuple-element.60), channel_id=1, source_target_pairs={{0,4},{4,0},{8,12},{12,8},{16,20},{20,16},{24,28},{28,24},{1,5},{5... | collective-permute-start | bytes 393224 | tf_op jit(solution)/shard_map/ppermute | solution.py:34
  47.8 7.1 %collective-permute-start.15 = (bf16[1,1,256,256]{3,2,1,0:T(8,128)(2,1)S(1)}, bf16[1,1,256,256]{3,2,1,0:T(8,128)(2,1)S(1)}, u32[]{:S(2)}, u32[]{:S(2)}) collective-permute-start(bf16[1,1,256,256]{3,2,1,0:T(8,128)(2,1)S(1)} %get-tuple-element.61), channel_id=1, source_target_pairs={{0,0},{4,8},{8,4},{12,16},{16,12},{20,24},{24,20},{28,28},{1,1},{5... | collective-permute-start | bytes 393224 | tf_op jit(solution)/shard_map/ppermute | solution.py:34

commit v10 on v9

--- a/solution.py
+++ b/solution.py
@@ -68,13 +68,13 @@
     count = lax.axis_size(axis)
     if count & (count - 1) or count == 1:
         return exchange(value, axis)
-    stride, parts = count // 2, [value]
-    while stride:
+    stride, parts = 1, [value]
+    while stride < count:
         if len(parts) > 1:
             parts = [total(parts)]
         pairs = [(source, source ^ stride) for source in range(count)]
         parts.append(lax.ppermute(parts[0], axis, pairs))
-        stride //= 2
+        stride *= 2
     return parts
 
 

time: 55.8 us -> 56.2 us (level)
    ppermute x4, starting transfers between devices: 2.97 us -> 5.24 us  [pairwise(): parts.append(lax.ppermute(parts[0], axis, pairs))]
    ppermute x2, starting transfers between devices: 8.65 us -> 7.56 us  [swap(): return lax.ppermute(value, axis, list(pairs.items()))]
    ppermute x6, starting transfers between devices: 6.68 us -> 6.02 us  [rotate(): lax.ppermute(value, axis, [(source, (source + steps) % count) for source...]
  transfers between devices with their start and end apart: 16 -> 16, of which waited for: 12 -> 10; matrix products, arithmetic and copies ran while one was open for 0% -> 0% of each run, Pallas kernels for 14% -> 14%
where the time goes in v10:
time: 56.2 us; the launch traced here: 56 us
  starting transfers between devices  23.6 us (42%)
  waiting for transfers between devices  19.1 us (34%)
  Pallas kernels  11.6 us (21%)
  between operations  1.64 us (3%)
    pallas_call x19, Pallas kernels, call(): pl.pallas_call(kernel, out_shape=outs, in_specs=in_specs or [VMEM] * len(...  11.6 us
    ppermute x2, starting transfers between devices, swap(): return lax.ppermute(value, axis, list(pairs.items()))  7.56 us
    ppermute x4, waiting for transfers between devices, pairwise(): parts.append(lax.ppermute(parts[0], axis, pairs))  6.51 us
    ppermute x6, starting transfers between devices, rotate(): lax.ppermute(value, axis, [(source, (source + steps) % count) for source...  6.02 us
    ppermute x4, starting transfers between devices, pairwise(): parts.append(lax.ppermute(parts[0], axis, pairs))  5.24 us
    ppermute x6, waiting for transfers between devices, rotate(): lax.ppermute(value, axis, [(source, (source + steps) % count) for source...  5.1 us
    ppermute x1, waiting for transfers between devices, shift(): lax.ppermute(value, axis, [(source, source + steps) for source in range(f...  4.52 us
    ppermute x3, starting transfers between devices, exchange(): parts.append(lax.ppermute(parts[0], axis, pairs))  2.71 us
  transfers between devices with their start and end apart: 16, of which 10 were waited for; matrix products, arithmetic and copies ran while one was open for 0% of the time, Pallas kernels for 14%

profile of v10, /device:TPU:1, one launch (start us, length us, event | category | flops | bytes accessed | tf_op | source)
XLA Modules:
  0.0 56.0 jit_solution(10514337770479412116)
XLA Ops:
  0.7 2.1 %collective-permute-start = (bf16[256,256]{1,0:T(8,128)(2,1)}, bf16[256,256]{1,0:T(8,128)(2,1)S(1)}, u32[]{:S(2)}, u32[]{:S(2)}) collective-permute-start(bf16[256,256]{1,0:T(8,128)(2,1)} %bitcast.24), channel_id=1, source_target_pairs={{4,0},{8,4},{12,8},{16,12},{20,16},{24,20},{28,24},{5,1},{9,5},{13... | collective-permute-start | bytes 393224 | tf_op jit(solution)/shard_map/ppermute | solution.py:26
  3.7 4.5 %collective-permute-done.behind = bf16[256,256]{1,0:T(8,128)(2,1)S(1)} collective-permute-done((bf16[256,256]{1,0:T(8,128)(2,1)}, bf16[256,256]{1,0:T(8,128)(2,1)S(1)}, u32[]{:S(2)}, u32[]{:S(2)}) %collective-permute-start) | collective-permute-done | bytes 131104 | tf_op jit(solution)/shard_map/ppermute | solution.py:26
  8.4 1.3 %collective-permute-start.1 = (bf16[256,256]{1,0:T(8,128)(2,1)S(1)}, bf16[256,256]{1,0:T(8,128)(2,1)S(1)}, u32[]{:S(2)}, u32[]{:S(2)}) collective-permute-start(bf16[256,256]{1,0:T(8,128)(2,1)S(1)} %get-tuple-element.33.vector_b), channel_id=1, source_target_pairs={{0,1},{1,2},{2,3},{3,0},{4,5},{5,6},{6,7},{7,4},{8,9},{9,10},{10,1... | collective-permute-start | bytes 393224 | tf_op jit(solution)/shard_map/ppermute | solution.py:39
  9.7 1.3 %shard_map.106 = (f32[256,256]{1,0:T(8,128)S(1)}, f32[8,128]{1,0:T(8,128)S(1)}, f32[256,256]{1,0:T(8,128)S(1)}, bf16[256,256]{1,0:T(8,128)(2,1)S(1)}) custom-call(bf16[16,256,256]{2,1,0:T(8,128)(2,1)S(1)} %bitcast.9, bf16[16,256,256]{2,1,0:T(8,128)(2,1)S(1)} %bitcast.14, bf16[256,256]{1,0:T(8,128)(2,1)S(1)} %get-tuple-element.33.vector_b, ...), custom_call_target="tpu_custom_call" | custom-call | tf_op jit(solution)/shard_map/pallas_call | solution.py:313
  11.0 1.2 %collective-permute-start.2 = (bf16[256,256]{1,0:T(8,128)(2,1)S(1)}, bf16[256,256]{1,0:T(8,128)(2,1)S(1)}, u32[]{:S(2)}, u32[]{:S(2)}) collective-permute-start(bf16[256,256]{1,0:T(8,128)(2,1)S(1)} %get-tuple-element.38), channel_id=1, source_target_pairs={{0,3},{1,0},{2,1},{3,2},{4,7},{5,4},{6,5},{7,6},{8,11},{9,8},{10,9... | collective-permute-start | bytes 393224 | tf_op jit(solution)/shard_map/ppermute | solution.py:39
  12.2 1.6 %collective-permute-done.1.below.refs_2_.y = bf16[256,256]{1,0:T(8,128)(2,1)S(1)} collective-permute-done((bf16[256,256]{1,0:T(8,128)(2,1)S(1)}, bf16[256,256]{1,0:T(8,128)(2,1)S(1)}, u32[]{:S(2)}, u32[]{:S(2)}) %collective-permute-start.1) | collective-permute-done | bytes 131104 | tf_op jit(solution)/shard_map/ppermute | solution.py:39
  13.8 1.2 %collective-permute-start.4 = (f32[8,128]{1,0:T(8,128)S(1)}, f32[8,128]{1,0:T(8,128)S(1)}, u32[]{:S(2)}, u32[]{:S(2)}) collective-permute-start(f32[8,128]{1,0:T(8,128)S(1)} %shard_map.107.after), channel_id=1, source_target_pairs={{0,1},{1,0},{2,3},{3,2},{4,5},{5,4},{6,7},{7,6},{8,9},{9,8},{10,11... | collective-permute-start | bytes 12296 | tf_op jit(solution)/shard_map/ppermute | solution.py:76
  15.0 1.3 %collective-permute-done.4 = f32[8,128]{1,0:T(8,128)S(1)} collective-permute-done((f32[8,128]{1,0:T(8,128)S(1)}, f32[8,128]{1,0:T(8,128)S(1)}, u32[]{:S(2)}, u32[]{:S(2)}) %collective-permute-start.4) | collective-permute-done | bytes 4128 | tf_op jit(solution)/shard_map/ppermute | solution.py:76
  16.3 2.0 %collective-permute-start.5 = (f32[8,128]{1,0:T(8,128)S(1)}, f32[8,128]{1,0:T(8,128)S(1)}, u32[]{:S(2)}, u32[]{:S(2)}) collective-permute-start(f32[8,128]{1,0:T(8,128)S(1)} %add.6.refs_0_), channel_id=1, source_target_pairs={{0,2},{1,3},{2,0},{3,1},{4,6},{5,7},{6,4},{7,5},{8,10},{9,11},{10,... | collective-permute-start | bytes 12296 | tf_op jit(solution)/shard_map/ppermute | solution.py:76
  18.3 1.2 %shard_map.108.up = f32[256,256]{1,0:T(8,128)S(1)} custom-call(bf16[16,256,256]{2,1,0:T(8,128)(2,1)S(1)} %bitcast.10, bf16[16,256,256]{2,1,0:T(8,128)(2,1)S(1)} %bitcast.15, bf16[256,256]{1,0:T(8,128)(2,1)S(1)} %collective-permute-done.1.below.refs_2_.y, f32[8,128]{1,0:T(8,128)S(1)} %shard_map.107.after), custom_call_target="tpu_custom_call" | custom-call | tf_op jit(solution)/shard_map/pallas_call | solution.py:313
  19.6 1.3 %collective-permute-start.3 = (bf16[256,256]{1,0:T(8,128)(2,1)S(1)}, bf16[256,256]{1,0:T(8,128)(2,1)S(1)}, u32[]{:S(2)}, u32[]{:S(2)}) collective-permute-start(bf16[256,256]{1,0:T(8,128)(2,1)S(1)} %get-tuple-element.39), channel_id=1, source_target_pairs={{0,1},{1,2},{2,3},{3,0},{4,5},{5,6},{6,7},{7,4},{8,9},{9,10},{10,1... | collective-permute-start | bytes 393224 | tf_op jit(solution)/shard_map/ppermute | solution.py:39
  21.1 1.3 %shard_map.111 = (f32[256,256]{1,0:T(8,128)S(1)}, f32[8,128]{1,0:T(8,128)S(1)}, f32[256,256]{1,0:T(8,128)S(1)}, bf16[256,256]{1,0:T(8,128)(2,1)S(1)}) custom-call(bf16[16,256,256]{2,1,0:T(8,128)(2,1)S(1)} %bitcast.11, bf16[16,256,256]{2,1,0:T(8,128)(2,1)S(1)} %bitcast.16, bf16[256,256]{1,0:T(8,128)(2,1)S(1)} %get-tuple-element.41.vector_b, ...), custom_call_target="tpu_custom_call" | custom-call | tf_op jit(solution)/shard_map/pallas_call | solution.py:313
  22.5 1.2 %collective-permute-start.7 = (bf16[256,256]{1,0:T(8,128)(2,1)S(1)}, bf16[256,256]{1,0:T(8,128)(2,1)S(1)}, u32[]{:S(2)}, u32[]{:S(2)}) collective-permute-start(bf16[256,256]{1,0:T(8,128)(2,1)S(1)} %get-tuple-element.48), channel_id=1, source_target_pairs={{0,3},{1,0},{2,1},{3,2},{4,7},{5,4},{6,5},{7,6},{8,11},{9,8},{10,9... | collective-permute-start | bytes 393224 | tf_op jit(solution)/shard_map/ppermute | solution.py:39
  23.7 1.1 %collective-permute-done.6.refs_4_.prec = bf16[256,256]{1,0:T(8,128)(2,1)S(1)} collective-permute-done((bf16[256,256]{1,0:T(8,128)(2,1)S(1)}, bf16[256,256]{1,0:T(8,128)(2,1)S(1)}, u32[]{:S(2)}, u32[]{:S(2)}) %collective-permute-start.6) | collective-permute-done | bytes 131104 | tf_op jit(solution)/shard_map/ppermute | solution.py:39
  24.7 2.5 %collective-permute-done.3.refs_3_.g = bf16[256,256]{1,0:T(8,128)(2,1)S(1)} collective-permute-done((bf16[256,256]{1,0:T(8,128)(2,1)S(1)}, bf16[256,256]{1,0:T(8,128)(2,1)S(1)}, u32[]{:S(2)}, u32[]{:S(2)}) %collective-permute-start.3) | collective-permute-done | bytes 131104 | tf_op jit(solution)/shard_map/ppermute | solution.py:39
  27.4 1.2 %shard_map.113.up = f32[256,256]{1,0:T(8,128)S(1)} custom-call(bf16[16,256,256]{2,1,0:T(8,128)(2,1)S(1)} %bitcast.12, bf16[16,256,256]{2,1,0:T(8,128)(2,1)S(1)} %bitcast.17, bf16[256,256]{1,0:T(8,128)(2,1)S(1)} %get-tuple-element.45.below.p, f32[8,128]{1,0:T(8,128)S(1)} %get-tuple-element.47.after), custom_call_target="tpu_custom_call" | custom-call | tf_op jit(solution)/shard_map/pallas_call | solution.py:313
  28.7 1.1 %collective-permute-start.8 = (bf16[256,256]{1,0:T(8,128)(2,1)S(1)}, bf16[256,256]{1,0:T(8,128)(2,1)S(1)}, u32[]{:S(2)}, u32[]{:S(2)}) collective-permute-start(bf16[256,256]{1,0:T(8,128)(2,1)S(1)} %get-tuple-element.49), channel_id=1, source_target_pairs={{0,1},{1,2},{2,3},{3,0},{4,5},{5,6},{6,7},{7,4},{8,9},{9,10},{10,1... | collective-permute-start | bytes 393224 | tf_op jit(solution)/shard_map/ppermute | solution.py:39
  29.8 1.2 %collective-permute-start.9 = (f32[8,128]{1,0:T(8,128)S(1)}, f32[8,128]{1,0:T(8,128)S(1)}, u32[]{:S(2)}, u32[]{:S(2)}) collective-permute-start(f32[8,128]{1,0:T(8,128)S(1)} %get-tuple-element.47.after), channel_id=1, source_target_pairs={{0,1},{1,0},{2,3},{3,2},{4,5},{5,4},{6,7},{7,6},{8,9},{9,8},{10,11... | collective-permute-start | bytes 12296 | tf_op jit(solution)/shard_map/ppermute | solution.py:76
  31.0 3.6 %collective-permute-done.9 = f32[8,128]{1,0:T(8,128)S(1)} collective-permute-done((f32[8,128]{1,0:T(8,128)S(1)}, f32[8,128]{1,0:T(8,128)S(1)}, u32[]{:S(2)}, u32[]{:S(2)}) %collective-permute-start.9) | collective-permute-done | bytes 4128 | tf_op jit(solution)/shard_map/ppermute | solution.py:76
  34.6 0.9 %collective-permute-start.10 = (f32[8,128]{1,0:T(8,128)S(1)}, f32[8,128]{1,0:T(8,128)S(1)}, u32[]{:S(2)}, u32[]{:S(2)}) collective-permute-start(f32[8,128]{1,0:T(8,128)S(1)} %add.7.refs_0_), channel_id=1, source_target_pairs={{0,2},{1,3},{2,0},{3,1},{4,6},{5,7},{6,4},{7,5},{8,10},{9,11},{10,... | collective-permute-start | bytes 12296 | tf_op jit(solution)/shard_map/ppermute | solution.py:76
  35.5 1.6 %collective-permute-done.10.refs_1_ = f32[8,128]{1,0:T(8,128)S(1)} collective-permute-done((f32[8,128]{1,0:T(8,128)S(1)}, f32[8,128]{1,0:T(8,128)S(1)}, u32[]{:S(2)}, u32[]{:S(2)}) %collective-permute-start.10) | collective-permute-done | bytes 4128 | tf_op jit(solution)/shard_map/ppermute | solution.py:76
  37.4 1.3 %shard_map.116 = (f32[256,256]{1,0:T(8,128)S(1)}, f32[8,128]{1,0:T(8,128)S(1)}) custom-call(bf16[16,256,256]{2,1,0:T(8,128)(2,1)S(1)} %bitcast.13, bf16[16,256,256]{2,1,0:T(8,128)(2,1)S(1)} %bitcast.18, bf16[256,256]{1,0:T(8,128)(2,1)S(1)} %get-tuple-element.52.vector_b, f32[256,256]{1,0:T(8,128)S(1)} %get-tuple-element.53.refs_0_.refs_4_, ...), custom_call_target="tpu_custom_call" | custom-call | tf_op jit(solution)/shard_map/pallas_call | solution.py:313
  39.0 1.3 %collective-permute-start.12 = (f32[8,128]{1,0:T(8,128)S(1)}, f32[8,128]{1,0:T(8,128)S(1)}, u32[]{:S(2)}, u32[]{:S(2)}) collective-permute-start(f32[8,128]{1,0:T(8,128)S(1)} %shard_map.117.refs_0_), channel_id=1, source_target_pairs={{0,2},{1,3},{2,0},{3,1},{4,6},{5,7},{6,4},{7,5},{8,10},{9,11},{10,... | collective-permute-start | bytes 12296 | tf_op jit(solution)/shard_map/ppermute | solution.py:62
  40.3 1.4 %collective-permute-start.11 = (f32[8,128]{1,0:T(8,128)S(1)}, f32[8,128]{1,0:T(8,128)S(1)}, u32[]{:S(2)}, u32[]{:S(2)}) collective-permute-start(f32[8,128]{1,0:T(8,128)S(1)} %shard_map.117.refs_0_), channel_id=1, source_target_pairs={{0,1},{1,0},{2,3},{3,2},{4,5},{5,4},{6,7},{7,6},{8,9},{9,8},{10,11... | collective-permute-start | bytes 12296 | tf_op jit(solution)/shard_map/ppermute | solution.py:62
  41.7 0.7 %collective-permute-done.13.refs_3_ = f32[8,128]{1,0:T(8,128)S(1)} collective-permute-done((f32[8,128]{1,0:T(8,128)S(1)}, f32[8,128]{1,0:T(8,128)S(1)}, u32[]{:S(2)}, u32[]{:S(2)}) %collective-permute-start.13) | collective-permute-done | bytes 4128 | tf_op jit(solution)/shard_map/ppermute | solution.py:62
  42.8 1.7 %shard_map.118 = (f32[256,256]{1,0:T(8,128)S(1)}, bf16[1,1,256,256]{3,2,1,0:T(8,128)(2,1)S(1)}) custom-call(f32[8,128]{1,0:T(8,128)S(1)} %shard_map.117.refs_0_, f32[8,128]{1,0:T(8,128)S(1)} %collective-permute-done.11.refs_1_, f32[8,128]{1,0:T(8,128)S(1)} %collective-permute-done.12.refs_2_, f32[8,128]{1,0:T(8,128)S(1)} %collective-permute-done.13.refs_3_, ...), custom_call_target="tpu_custom_call" | custom-call | tf_op jit(solution)/shard_map/pallas_call | solution.py:313
  44.4 0.7 %shard_map.119 = (f32[256,256]{1,0:T(8,128)S(1)}, bf16[1,1,256,256]{3,2,1,0:T(8,128)(2,1)S(1)}, f32[1]{0:T(128)}) custom-call(f32[8,128]{1,0:T(8,128)S(1)} %shard_map.117.refs_0_, f32[8,128]{1,0:T(8,128)S(1)} %collective-permute-done.11.refs_1_, f32[8,128]{1,0:T(8,128)S(1)} %collective-permute-done.12.refs_2_, ...), custom_call_target="tpu_custom_call", output_to_operand_aliasing={{0}: (7, {})} | custom-call | tf_op jit(solution)/shard_map/pallas_call | solution.py:313
  45.1 3.9 %collective-permute-start.14 = (bf16[1,1,256,256]{3,2,1,0:T(8,128)(2,1)S(1)}, bf16[1,1,256,256]{3,2,1,0:T(8,128)(2,1)S(1)}, u32[]{:S(2)}, u32[]{:S(2)}) collective-permute-start(bf16[1,1,256,256]{3,2,1,0:T(8,128)(2,1)S(1)} %get-tuple-element.60), channel_id=1, source_target_pairs={{0,4},{4,0},{8,12},{12,8},{16,20},{20,16},{24,28},{28,24},{1,5},{5... | collective-permute-start | bytes 393224 | tf_op jit(solution)/shard_map/ppermute | solution.py:34
  49.0 3.7 %collective-permute-start.15 = (bf16[1,1,256,256]{3,2,1,0:T(8,128)(2,1)S(1)}, bf16[1,1,256,256]{3,2,1,0:T(8,128)(2,1)S(1)}, u32[]{:S(2)}, u32[]{:S(2)}) collective-permute-start(bf16[1,1,256,256]{3,2,1,0:T(8,128)(2,1)S(1)} %get-tuple-element.61), channel_id=1, source_target_pairs={{0,0},{4,8},{8,4},{12,16},{16,12},{20,24},{24,20},{28,28},{1,1},{5... | collective-permute-start | bytes 393224 | tf_op jit(solution)/shard_map/ppermute | solution.py:34
  52.7 0.7 %shard_map.120 = f32[1,1,256,256]{3,2,1,0:T(8,128)} custom-call(f32[256,256]{1,0:T(8,128)S(1)} %get-tuple-element.59.value), custom_call_target="tpu_custom_call" | custom-call | bytes 1048576 | tf_op jit(solution)/shard_map/pallas_call | solution.py:313
  53.4 1.9 %collective-permute-done.15.far = bf16[1,1,256,256]{3,2,1,0:T(8,128)(2,1)S(1)} collective-permute-done((bf16[1,1,256,256]{3,2,1,0:T(8,128)(2,1)S(1)}, bf16[1,1,256,256]{3,2,1,0:T(8,128)(2,1)S(1)}, u32[]{:S(2)}, u32[]{:S(2)}) %collective-permute-start.15) | collective-permute-done | bytes 131104 | tf_op jit(solution)/shard_map/ppermute | solution.py:34
  55.3 0.7 %shard_map.121 = bf16[1,1,256,256]{3,2,1,0:T(8,128)(2,1)} custom-call(bf16[1,1,256,256]{3,2,1,0:T(8,128)(2,1)S(1)} %collective-permute-done.14.near, bf16[1,1,256,256]{3,2,1,0:T(8,128)(2,1)S(1)} %collective-permute-done.15.far), custom_call_target="tpu_custom_call" | custom-call | tf_op jit(solution)/shard_map/pallas_call | solution.py:313
  (34 shorter events, 2.0 us)
Async XLA Ops:
  0.6 3.0 %copy-start.4 = (bf16[1,1,256,256]{3,2,1,0:T(8,128)(2,1)S(1)}, bf16[1,1,256,256]{3,2,1,0:T(8,128)(2,1)}, u32[]{:S(2)}) copy-start(bf16[1,1,256,256]{3,2,1,0:T(8,128)(2,1)} %param.10) | copy-start | bytes 393220
  0.6 3.0 %copy-start.5 = (f32[1,1,256]{2,1,0:T(1,128)S(1)}, f32[1,1,256]{2,1,0:T(1,128)}, u32[]{:S(2)}) copy-start(f32[1,1,256]{2,1,0:T(1,128)} %param.13) | copy-start | bytes 3076
  0.7 7.6 %copy-start.3 = (bf16[1,1,256,256]{3,2,1,0:T(8,128)(2,1)S(1)}, bf16[1,1,256,256]{3,2,1,0:T(8,128)(2,1)}, u32[]{:S(2)}) copy-start(bf16[1,1,256,256]{3,2,1,0:T(8,128)(2,1)} %param.12) | copy-start | bytes 393220
  0.7 7.6 %collective-permute-start = (bf16[256,256]{1,0:T(8,128)(2,1)}, bf16[256,256]{1,0:T(8,128)(2,1)S(1)}, u32[]{:S(2)}, u32[]{:S(2)}) collective-permute-start(bf16[256,256]{1,0:T(8,128)(2,1)} %bitcast.24), channel_id=1, source_target_pairs={{4,0},{8,4},{12,8},{16,12},{20,16},{24,20},{28,24},{5,1},{9,5},{13... | collective-permute-start | bytes 393224 | tf_op jit(solution)/shard_map/ppermute | solution.py:26
  2.7 7.0 %copy-start = (bf16[1,1,16,256,256]{4,3,2,1,0:T(8,128)(2,1)S(1)}, bf16[1,1,16,256,256]{4,3,2,1,0:T(8,128)(2,1)}, u32[]{:S(2)}) copy-start(bf16[1,1,16,256,256]{4,3,2,1,0:T(8,128)(2,1)} %param.8) | copy-start | bytes 6291460
  2.7 7.0 %copy-start.1 = (bf16[1,1,16,256,256]{4,3,2,1,0:T(8,128)(2,1)S(1)}, bf16[1,1,16,256,256]{4,3,2,1,0:T(8,128)(2,1)}, u32[]{:S(2)}) copy-start(bf16[1,1,16,256,256]{4,3,2,1,0:T(8,128)(2,1)} %param.9) | copy-start | bytes 6291460
  8.4 5.3 %collective-permute-start.1 = (bf16[256,256]{1,0:T(8,128)(2,1)S(1)}, bf16[256,256]{1,0:T(8,128)(2,1)S(1)}, u32[]{:S(2)}, u32[]{:S(2)}) collective-permute-start(bf16[256,256]{1,0:T(8,128)(2,1)S(1)} %get-tuple-element.33.vector_b), channel_id=1, source_target_pairs={{0,1},{1,2},{2,3},{3,0},{4,5},{5,6},{6,7},{7,4},{8,9},{9,10},{10,1... | collective-permute-start | bytes 393224 | tf_op jit(solution)/shard_map/ppermute | solution.py:39
  9.7 8.6 %copy-start.2 = (bf16[1,1,256,256]{3,2,1,0:T(8,128)(2,1)S(1)}, bf16[1,1,256,256]{3,2,1,0:T(8,128)(2,1)}, u32[]{:S(2)}) copy-start(bf16[1,1,256,256]{3,2,1,0:T(8,128)(2,1)} %param.14) | copy-start | bytes 393220
  11.0 8.6 %collective-permute-start.2 = (bf16[256,256]{1,0:T(8,128)(2,1)S(1)}, bf16[256,256]{1,0:T(8,128)(2,1)S(1)}, u32[]{:S(2)}, u32[]{:S(2)}) collective-permute-start(bf16[256,256]{1,0:T(8,128)(2,1)S(1)} %get-tuple-element.38), channel_id=1, source_target_pairs={{0,3},{1,0},{2,1},{3,2},{4,7},{5,4},{6,5},{7,6},{8,11},{9,8},{10,9... | collective-permute-start | bytes 393224 | tf_op jit(solution)/shard_map/ppermute | solution.py:39
  13.8 2.5 %collective-permute-start.4 = (f32[8,128]{1,0:T(8,128)S(1)}, f32[8,128]{1,0:T(8,128)S(1)}, u32[]{:S(2)}, u32[]{:S(2)}) collective-permute-start(f32[8,128]{1,0:T(8,128)S(1)} %shard_map.107.after), channel_id=1, source_target_pairs={{0,1},{1,0},{2,3},{3,2},{4,5},{5,4},{6,7},{7,6},{8,9},{9,8},{10,11... | collective-permute-start | bytes 12296 | tf_op jit(solution)/shard_map/ppermute | solution.py:76
  16.3 4.6 %collective-permute-start.5 = (f32[8,128]{1,0:T(8,128)S(1)}, f32[8,128]{1,0:T(8,128)S(1)}, u32[]{:S(2)}, u32[]{:S(2)}) collective-permute-start(f32[8,128]{1,0:T(8,128)S(1)} %add.6.refs_0_), channel_id=1, source_target_pairs={{0,2},{1,3},{2,0},{3,1},{4,6},{5,7},{6,4},{7,5},{8,10},{9,11},{10,... | collective-permute-start | bytes 12296 | tf_op jit(solution)/shard_map/ppermute | solution.py:76
  18.3 6.4 %collective-permute-start.6 = (bf16[256,256]{1,0:T(8,128)(2,1)S(1)}, bf16[256,256]{1,0:T(8,128)(2,1)S(1)}, u32[]{:S(2)}, u32[]{:S(2)}) collective-permute-start(bf16[256,256]{1,0:T(8,128)(2,1)S(1)} %bitcast.19), channel_id=1, source_target_pairs={{0,1},{1,2},{2,3},{3,0},{4,5},{5,6},{6,7},{7,4},{8,9},{9,10},{10,1... | collective-permute-start | bytes 393224 | tf_op jit(solution)/shard_map/ppermute | solution.py:39
  19.6 7.5 %collective-permute-start.3 = (bf16[256,256]{1,0:T(8,128)(2,1)S(1)}, bf16[256,256]{1,0:T(8,128)(2,1)S(1)}, u32[]{:S(2)}, u32[]{:S(2)}) collective-permute-start(bf16[256,256]{1,0:T(8,128)(2,1)S(1)} %get-tuple-element.39), channel_id=1, source_target_pairs={{0,1},{1,2},{2,3},{3,0},{4,5},{5,6},{6,7},{7,4},{8,9},{9,10},{10,1... | collective-permute-start | bytes 393224 | tf_op jit(solution)/shard_map/ppermute | solution.py:39
  22.5 6.2 %collective-permute-start.7 = (bf16[256,256]{1,0:T(8,128)(2,1)S(1)}, bf16[256,256]{1,0:T(8,128)(2,1)S(1)}, u32[]{:S(2)}, u32[]{:S(2)}) collective-permute-start(bf16[256,256]{1,0:T(8,128)(2,1)S(1)} %get-tuple-element.48), channel_id=1, source_target_pairs={{0,3},{1,0},{2,1},{3,2},{4,7},{5,4},{6,5},{7,6},{8,11},{9,8},{10,9... | collective-permute-start | bytes 393224 | tf_op jit(solution)/shard_map/ppermute | solution.py:39
  28.7 10.0 %collective-permute-start.8 = (bf16[256,256]{1,0:T(8,128)(2,1)S(1)}, bf16[256,256]{1,0:T(8,128)(2,1)S(1)}, u32[]{:S(2)}, u32[]{:S(2)}) collective-permute-start(bf16[256,256]{1,0:T(8,128)(2,1)S(1)} %get-tuple-element.49), channel_id=1, source_target_pairs={{0,1},{1,2},{2,3},{3,0},{4,5},{5,6},{6,7},{7,4},{8,9},{9,10},{10,1... | collective-permute-start | bytes 393224 | tf_op jit(solution)/shard_map/ppermute | solution.py:39
  29.8 4.8 %collective-permute-start.9 = (f32[8,128]{1,0:T(8,128)S(1)}, f32[8,128]{1,0:T(8,128)S(1)}, u32[]{:S(2)}, u32[]{:S(2)}) collective-permute-start(f32[8,128]{1,0:T(8,128)S(1)} %get-tuple-element.47.after), channel_id=1, source_target_pairs={{0,1},{1,0},{2,3},{3,2},{4,5},{5,4},{6,7},{7,6},{8,9},{9,8},{10,11... | collective-permute-start | bytes 12296 | tf_op jit(solution)/shard_map/ppermute | solution.py:76
  34.6 2.5 %collective-permute-start.10 = (f32[8,128]{1,0:T(8,128)S(1)}, f32[8,128]{1,0:T(8,128)S(1)}, u32[]{:S(2)}, u32[]{:S(2)}) collective-permute-start(f32[8,128]{1,0:T(8,128)S(1)} %add.7.refs_0_), channel_id=1, source_target_pairs={{0,2},{1,3},{2,0},{3,1},{4,6},{5,7},{6,4},{7,5},{8,10},{9,11},{10,... | collective-permute-start | bytes 12296 | tf_op jit(solution)/shard_map/ppermute | solution.py:76
  39.0 3.4 %collective-permute-start.13 = (f32[8,128]{1,0:T(8,128)S(1)}, f32[8,128]{1,0:T(8,128)S(1)}, u32[]{:S(2)}, u32[]{:S(2)}) collective-permute-start(f32[8,128]{1,0:T(8,128)S(1)} %shard_map.117.refs_0_), channel_id=1, source_target_pairs={{0,3},{1,2},{2,1},{3,0},{4,7},{5,6},{6,5},{7,4},{8,11},{9,10},{10,... | collective-permute-start | bytes 12296 | tf_op jit(solution)/shard_map/ppermute | solution.py:62
  39.0 3.3 %collective-permute-start.12 = (f32[8,128]{1,0:T(8,128)S(1)}, f32[8,128]{1,0:T(8,128)S(1)}, u32[]{:S(2)}, u32[]{:S(2)}) collective-permute-start(f32[8,128]{1,0:T(8,128)S(1)} %shard_map.117.refs_0_), channel_id=1, source_target_pairs={{0,2},{1,3},{2,0},{3,1},{4,6},{5,7},{6,4},{7,5},{8,10},{9,11},{10,... | collective-permute-start | bytes 12296 | tf_op jit(solution)/shard_map/ppermute | solution.py:62
  40.3 2.5 %collective-permute-start.11 = (f32[8,128]{1,0:T(8,128)S(1)}, f32[8,128]{1,0:T(8,128)S(1)}, u32[]{:S(2)}, u32[]{:S(2)}) collective-permute-start(f32[8,128]{1,0:T(8,128)S(1)} %shard_map.117.refs_0_), channel_id=1, source_target_pairs={{0,1},{1,0},{2,3},{3,2},{4,5},{5,4},{6,7},{7,6},{8,9},{9,8},{10,11... | collective-permute-start | bytes 12296 | tf_op jit(solution)/shard_map/ppermute | solution.py:62
  45.1 8.3 %collective-permute-start.14 = (bf16[1,1,256,256]{3,2,1,0:T(8,128)(2,1)S(1)}, bf16[1,1,256,256]{3,2,1,0:T(8,128)(2,1)S(1)}, u32[]{:S(2)}, u32[]{:S(2)}) collective-permute-start(bf16[1,1,256,256]{3,2,1,0:T(8,128)(2,1)S(1)} %get-tuple-element.60), channel_id=1, source_target_pairs={{0,4},{4,0},{8,12},{12,8},{16,20},{20,16},{24,28},{28,24},{1,5},{5... | collective-permute-start | bytes 393224 | tf_op jit(solution)/shard_map/ppermute | solution.py:34
  49.0 6.3 %collective-permute-start.15 = (bf16[1,1,256,256]{3,2,1,0:T(8,128)(2,1)S(1)}, bf16[1,1,256,256]{3,2,1,0:T(8,128)(2,1)S(1)}, u32[]{:S(2)}, u32[]{:S(2)}) collective-permute-start(bf16[1,1,256,256]{3,2,1,0:T(8,128)(2,1)S(1)} %get-tuple-element.61), channel_id=1, source_target_pairs={{0,0},{4,8},{8,4},{12,16},{16,12},{20,24},{24,20},{28,28},{1,1},{5... | collective-permute-start | bytes 393224 | tf_op jit(solution)/shard_map/ppermute | solution.py:34

commit v11 on v10

--- a/solution.py
+++ b/solution.py
@@ -127,22 +127,28 @@
     yb_ref[...] = y.astype(BF16)
 
 
-def lower_kernel(pairs, sends, left, right, vector_b, *refs):
-    outs = refs[-5 if sends else -3 :]
-    ops, inner = refs[: len(refs) - len(outs)], refs[-1]
-    low_ref, stat_ref = outs[:2]
+def start_lower_kernel(left, right, y, yb, prec, low_ref, stat_ref, diag_ref, sent_ref, py_ref, inner):
     channels = left.shape[0]
-    value = vector_b[...]
+    value = yb[...]
     low = sandwich(left, right, value, inner, WD, channels)
     low_ref[...] = low
+    sent_ref[...] = low.astype(BF16)
     diag = sandwich(left, right, value, inner, 0, WD)
-    if sends:
-        outs[2][...] = diag
-        outs[3][...] = low.astype(BF16)
-    stat_ref[...] = jnp.zeros(stat_ref.shape, F32)
+    diag_ref[...] = diag
+    py_ref[...] = (prec[...].astype(F32) * y[...]).astype(BF16)
+    write_sums(stat_ref, [(y, y), (y, diag)])
+
+
+def terms_kernel(left, right, value, low_ref, diag_ref, inner):
+    channels = left.shape[0]
+    low_ref[...] = sandwich(left, right, value[...], inner, WD, channels)
+    diag_ref[...] = sandwich(left, right, value[...], inner, 0, WD)
+
+
+def write_sums(out, pairs):
+    out[...] = jnp.zeros(out.shape, F32)
     for row, (one, two) in enumerate(pairs):
-        other = diag if two is None else ops[two][...]
-        stat_ref[row : row + 1] = fold(ops[one][...] * other)
+        out[row : row + 1] = fold(one[...] * two[...])
 
 
 def add_cross(row, below, low, stat, out):
@@ -169,10 +175,11 @@
     add_cross(3, prec[...].astype(F32) * (hx - lam * x), low, stat, out)
 
 
-def join_kernel(diag, up, above, mask, out, out_b):
+def join_kernel(diag, up, above, mask, prec, out, out_b, weighted_b):
     joined = mask[...] * (diag[...] + up[...] + from_above(above[...].astype(F32)))
     out[...] = joined
     out_b[...] = joined.astype(BF16)
+    weighted_b[...] = (prec[...].astype(F32) * joined).astype(BF16)
 
 
 def raise_kernel(left, right, below, after, up_ref, inner):
@@ -180,11 +187,21 @@
 
 
 def first_kernel(parts, *refs):
-    y_ref, g_ref, prec, p_ref, pb_ref = refs[parts:]
+    y, g, prec, low_g, low_y, diag_g, diag_y = refs[parts : parts + 7]
+    p_ref, low_ref, sent_ref, diag_ref, stat_ref, weighted_b, shift_ref = refs[parts + 7 :]
     yy, yhy = scalars(refs[:parts], 2)
-    p = prec[...].astype(F32) * (g_ref[...] - (yhy / yy) * y_ref[...])
+    a = yhy / yy
+    shift_ref[...] = jnp.broadcast_to(a, shift_ref.shape)
+    weights = prec[...].astype(F32)
+    low = low_g[...] - a * low_y[...]
+    low_ref[...] = low
+    sent_ref[...] = low.astype(BF16)
+    p = weights * (g[...] - a * y[...])
     p_ref[...] = p
-    pb_ref[...] = p.astype(BF16)
+    weighted_b[...] = (weights * p).astype(BF16)
+    diag = diag_g[...] - a * diag_y[...]
+    diag_ref[...] = diag
+    write_sums(stat_ref, [(y, y), (y, g), (y, p), (p, p), (p, g), (p, diag)])
 
 
 def ritz(a, b, c):
@@ -195,8 +212,9 @@
 
 
 def second_kernel(parts, *refs):
-    y_ref, g_ref, p_ref, hp_ref, prec = refs[parts : parts + 5]
-    x_out, g_out, p_out, pb_out, coefficients = refs[parts + 5 :]
+    y_ref, g_ref, p_ref, hp_ref, prec, shift_ref = refs[parts : parts + 6]
+    lows, diags = refs[parts + 6 : parts + 10], refs[parts + 10 : parts + 14]
+    x_out, p_out, coefficients, low_ref, stat_ref = refs[parts + 14 :]
     yy, yg, yp, pp, pg, php = scalars(refs[:parts], 6)
     a = yg / yy
     s = yp / yy
@@ -206,13 +224,15 @@
     lam, u, w = ritz(a, b, c)
     along_p = w / jnp.sqrt(qq)
     along_y = u / jnp.sqrt(yy) - along_p * s
+    factors = [along_y, along_y * (shift_ref[0:1, 0:1] - lam), along_p, -lam * along_p]
+    low_ref[...] = total([factor * term[...] for factor, term in zip(factors, lows)])
     x = along_y * y_ref[...] + along_p * p_ref[...]
     g = along_y * g_ref[...] + along_p * hp_ref[...]
     p = prec[...].astype(F32) * (g - lam * x)
     x_out[...] = x
-    g_out[...] = g
     p_out[...] = p
-    pb_out[...] = p.astype(BF16)
+    diag = total([factor * term[...] for factor, term in zip(factors, diags)])
+    write_sums(stat_ref, [(x, p), (p, p), (p, g), (p, diag)])
     for i, value in enumerate([along_y, along_p, lam]):
         coefficients[i : i + 1] = jnp.broadcast_to(value, (1, LANES))
 
@@ -329,42 +349,50 @@
 
     y, yb = call(start_kernel, [matrix, narrow], scaled, behind, guess[0, 0], mask)
 
-    def half(vector_b, pairs, operands, sends):
-        outs = [matrix, stats] + [matrix, narrow] * sends
-        kernel = functools.partial(lower_kernel, pairs, sends)
-        low, stat, *rest = call(kernel, outs, left, right, vector_b, *operands, scratch=[inner])
-        if not sends:
-            return low, stat
-        diag, sent = rest
-        return low, stat, diag, rotate(sent, "sec", -1)
+    def terms(value):
+        return call(terms_kernel, [matrix, matrix], left, right, value, scratch=[inner])
 
     def joined(below, after, diag, above):
         (up,) = call(raise_kernel, [matrix], left, right, below, after, scratch=[inner])
-        return call(join_kernel, [matrix, narrow], diag, up, above, mask)
+        outs = [matrix, narrow, narrow]
+        return call(join_kernel, outs, diag, up, above, mask, prec)
 
     y_below = rotate(yb, "sec", 1)
-    low, stat, diag, above = half(yb, [(0, 0), (0, None)], [y], 1)
+    low, stat, diag, sent, pyb = call(
+        start_lower_kernel,
+        [matrix, stats, matrix, narrow, narrow],
+        left, right, y, yb, prec,
+        scratch=[inner],
+    )
+    above = rotate(sent, "sec", -1)
+    low_y, diag_y = terms(pyb)
     (stat,) = call(cross_kernel, [stats], y_below, low, stat)
     parts = pairwise(stat, "sec")
-    g, gb = joined(y_below, stat, diag, above)
+    g, gb, pgb = joined(y_below, stat, diag, above)
     g_below = rotate(gb, "sec", 1)
-    kernel = functools.partial(first_kernel, len(parts))
-    p, pb = call(kernel, [matrix, narrow], *parts, y, g, prec)
-
-    pairs = [(0, 0), (0, 1), (0, 2), (2, 2), (2, 1), (2, None)]
-    low, stat, diag, above = half(pb, pairs, [y, g, p], 1)
-    kernel = functools.partial(first_cross_kernel, len(parts))
-    stat, p_below = call(kernel, [stats, narrow], *parts, y_below, g_below, prec_below, low, stat)
+    low_g, diag_g = terms(pgb)
+    p, low, sent, diag, stat, ppb, shifted = call(
+        functools.partial(first_kernel, len(parts)),
+        [matrix, matrix, narrow, matrix, stats, narrow, stats],
+        *parts, y, g, prec, low_g, low_y, diag_g, diag_y,
+    )
+    above = rotate(sent, "sec", -1)
+    stat, p_below = call(
+        functools.partial(first_cross_kernel, len(parts)),
+        [stats, narrow],
+        *parts, y_below, g_below, prec_below, low, stat,
+    )
     parts = pairwise(stat, "sec")
-    hp, hpb = joined(p_below, stat, diag, above)
+    hp, hpb, phpb = joined(p_below, stat, diag, above)
+    low_p, diag_p = terms(ppb)
     hp_below = rotate(hpb, "sec", 1)
-    kernel = functools.partial(second_kernel, len(parts))
-    x, g, p, pb, coefficients = call(
-        kernel, [matrix, matrix, matrix, narrow, stats], *parts, y, g, p, hp, prec
-    )
-
-    pairs = [(0, 2), (2, 2), (2, 1), (2, None)]
-    low, stat = half(pb, pairs, [x, g, p], 0)
+    low_hp, diag_hp = terms(phpb)
+    x, p, coefficients, low, stat = call(
+        functools.partial(second_kernel, len(parts)),
+        [matrix, matrix, stats, matrix, stats],
+        *parts, y, g, p, hp, prec, shifted,
+        low, low_y, low_hp, low_p, diag, diag_y, diag_hp, diag_p,
+    )
     (stat,) = call(
         second_cross_kernel,
         [stats],

time: 56.2 us -> 56.5 us (level)
  Pallas kernels: 11.6 us -> 14.6 us
  waiting for transfers between devices: 19.1 us -> 17.2 us
  starting transfers between devices: 23.6 us -> 22.7 us
    pallas_call x19 -> x21, Pallas kernels: 11.6 us -> 14.6 us  [call(): pl.pallas_call(kernel, out_shape=outs, in_specs=in_specs or [VMEM] * len(...]
    ppermute x4, waiting for transfers between devices: 6.51 us -> 4.59 us  [pairwise(): parts.append(lax.ppermute(parts[0], axis, pairs))]
    ppermute x6, waiting for transfers between devices: 5.1 us -> 3.89 us  [rotate(): lax.ppermute(value, axis, [(source, (source + steps) % count) for source...]
    ppermute x4, starting transfers between devices: 5.24 us -> 4.06 us  [pairwise(): parts.append(lax.ppermute(parts[0], axis, pairs))]
    ppermute x6, starting transfers between devices: 6.02 us -> 7.03 us  [rotate(): lax.ppermute(value, axis, [(source, (source + steps) % count) for source...]
    ppermute x3, waiting for transfers between devices: 1.08 us -> 2.04 us  [exchange(): parts.append(lax.ppermute(parts[0], axis, pairs))]
    ppermute x2, starting transfers between devices: 7.56 us -> 6.83 us  [swap(): return lax.ppermute(value, axis, list(pairs.items()))]
  transfers between devices with their start and end apart: 16 -> 16, of which waited for: 10 -> 10; matrix products, arithmetic and copies ran while one was open for 0% -> 0% of each run, Pallas kernels for 14% -> 20%
where the time goes in v11:
time: 56.5 us; the launch traced here: 56.3 us
  starting transfers between devices  22.7 us (40%)
  waiting for transfers between devices  17.2 us (30%)
  Pallas kernels  14.6 us (26%)
  between operations  1.66 us (3%)
    pallas_call x21, Pallas kernels, call(): pl.pallas_call(kernel, out_shape=outs, in_specs=in_specs or [VMEM] * len(...  14.6 us
    ppermute x6, starting transfers between devices, rotate(): lax.ppermute(value, axis, [(source, (source + steps) % count) for source...  7.03 us
    ppermute x2, starting transfers between devices, swap(): return lax.ppermute(value, axis, list(pairs.items()))  6.83 us
    ppermute x4, waiting for transfers between devices, pairwise(): parts.append(lax.ppermute(parts[0], axis, pairs))  4.59 us
    ppermute x1, waiting for transfers between devices, shift(): lax.ppermute(value, axis, [(source, source + steps) for source in range(f...  4.52 us
    ppermute x4, starting transfers between devices, pairwise(): parts.append(lax.ppermute(parts[0], axis, pairs))  4.06 us
    ppermute x6, waiting for transfers between devices, rotate(): lax.ppermute(value, axis, [(source, (source + steps) % count) for source...  3.89 us
    ppermute x3, starting transfers between devices, exchange(): parts.append(lax.ppermute(parts[0], axis, pairs))  2.71 us
  transfers between devices with their start and end apart: 16, of which 10 were waited for; matrix products, arithmetic and copies ran while one was open for 0% of the time, Pallas kernels for 20%

profile of v11, /device:TPU:1, one launch (start us, length us, event | category | flops | bytes accessed | tf_op | source)
XLA Modules:
  0.0 56.3 jit_solution(812992507510906986)
XLA Ops:
  0.7 2.1 %collective-permute-start = (bf16[256,256]{1,0:T(8,128)(2,1)}, bf16[256,256]{1,0:T(8,128)(2,1)S(1)}, u32[]{:S(2)}, u32[]{:S(2)}) collective-permute-start(bf16[256,256]{1,0:T(8,128)(2,1)} %bitcast.31), channel_id=1, source_target_pairs={{4,0},{8,4},{12,8},{16,12},{20,16},{24,20},{28,24},{5,1},{9,5},{13... | collective-permute-start | bytes 393224 | tf_op jit(solution)/shard_map/ppermute | solution.py:26
  3.7 4.5 %collective-permute-done.behind = bf16[256,256]{1,0:T(8,128)(2,1)S(1)} collective-permute-done((bf16[256,256]{1,0:T(8,128)(2,1)}, bf16[256,256]{1,0:T(8,128)(2,1)S(1)}, u32[]{:S(2)}, u32[]{:S(2)}) %collective-permute-start) | collective-permute-done | bytes 131104 | tf_op jit(solution)/shard_map/ppermute | solution.py:26
  8.4 1.3 %collective-permute-start.1 = (bf16[256,256]{1,0:T(8,128)(2,1)S(1)}, bf16[256,256]{1,0:T(8,128)(2,1)S(1)}, u32[]{:S(2)}, u32[]{:S(2)}) collective-permute-start(bf16[256,256]{1,0:T(8,128)(2,1)S(1)} %get-tuple-element.43.yb), channel_id=1, source_target_pairs={{0,1},{1,2},{2,3},{3,0},{4,5},{5,6},{6,7},{7,4},{8,9},{9,10},{10,1... | collective-permute-start | bytes 393224 | tf_op jit(solution)/shard_map/ppermute | solution.py:39
  9.7 1.3 %shard_map.106 = (f32[256,256]{1,0:T(8,128)S(1)}, f32[8,128]{1,0:T(8,128)S(1)}, f32[256,256]{1,0:T(8,128)S(1)}, bf16[256,256]{1,0:T(8,128)(2,1)S(1)}, bf16[256,256]{1,0:T(8,128)(2,1)S(1)}) custom-call(bf16[16,256,256]{2,1,0:T(8,128)(2,1)S(1)} %bitcast.9, bf16[16,256,256]{2,1,0:T(8,128)(2,1)S(1)} %bitcast.16, f32[256,256]{1,0:T(8,128)S(1)} %get-tuple-element.44.y.refs_2_, ...), custom_call_target="tpu_custom_call" | custom-call | tf_op jit(solution)/shard_map/pallas_call | solution.py:333
  11.0 1.2 %collective-permute-start.2 = (bf16[256,256]{1,0:T(8,128)(2,1)S(1)}, bf16[256,256]{1,0:T(8,128)(2,1)S(1)}, u32[]{:S(2)}, u32[]{:S(2)}) collective-permute-start(bf16[256,256]{1,0:T(8,128)(2,1)S(1)} %get-tuple-element.48), channel_id=1, source_target_pairs={{0,3},{1,0},{2,1},{3,2},{4,7},{5,4},{6,5},{7,6},{8,11},{9,8},{10,9... | collective-permute-start | bytes 393224 | tf_op jit(solution)/shard_map/ppermute | solution.py:39
  12.2 1.6 %collective-permute-done.1.below.refs_2_.y = bf16[256,256]{1,0:T(8,128)(2,1)S(1)} collective-permute-done((bf16[256,256]{1,0:T(8,128)(2,1)S(1)}, bf16[256,256]{1,0:T(8,128)(2,1)S(1)}, u32[]{:S(2)}, u32[]{:S(2)}) %collective-permute-start.1) | collective-permute-done | bytes 131104 | tf_op jit(solution)/shard_map/ppermute | solution.py:39
  13.8 1.2 %collective-permute-start.4 = (f32[8,128]{1,0:T(8,128)S(1)}, f32[8,128]{1,0:T(8,128)S(1)}, u32[]{:S(2)}, u32[]{:S(2)}) collective-permute-start(f32[8,128]{1,0:T(8,128)S(1)} %shard_map.107.after), channel_id=1, source_target_pairs={{0,1},{1,0},{2,3},{3,2},{4,5},{5,4},{6,7},{7,6},{8,9},{9,8},{10,11... | collective-permute-start | bytes 12296 | tf_op jit(solution)/shard_map/ppermute | solution.py:76
  15.0 1.3 %collective-permute-done.4 = f32[8,128]{1,0:T(8,128)S(1)} collective-permute-done((f32[8,128]{1,0:T(8,128)S(1)}, f32[8,128]{1,0:T(8,128)S(1)}, u32[]{:S(2)}, u32[]{:S(2)}) %collective-permute-start.4) | collective-permute-done | bytes 4128 | tf_op jit(solution)/shard_map/ppermute | solution.py:76
  16.3 2.0 %collective-permute-start.5 = (f32[8,128]{1,0:T(8,128)S(1)}, f32[8,128]{1,0:T(8,128)S(1)}, u32[]{:S(2)}, u32[]{:S(2)}) collective-permute-start(f32[8,128]{1,0:T(8,128)S(1)} %add.6.refs_0_), channel_id=1, source_target_pairs={{0,2},{1,3},{2,0},{3,1},{4,6},{5,7},{6,4},{7,5},{8,10},{9,11},{10,... | collective-permute-start | bytes 12296 | tf_op jit(solution)/shard_map/ppermute | solution.py:76
  18.3 1.3 %shard_map.111 = (f32[256,256]{1,0:T(8,128)S(1)}, f32[256,256]{1,0:T(8,128)S(1)}) custom-call(bf16[16,256,256]{2,1,0:T(8,128)(2,1)S(1)} %bitcast.10, bf16[16,256,256]{2,1,0:T(8,128)(2,1)S(1)} %bitcast.17, bf16[256,256]{1,0:T(8,128)(2,1)S(1)} %get-tuple-element.53.value), custom_call_target="tpu_custom_call" | custom-call | tf_op jit(solution)/shard_map/pallas_call | solution.py:333
  19.6 1.2 %shard_map.108.up = f32[256,256]{1,0:T(8,128)S(1)} custom-call(bf16[16,256,256]{2,1,0:T(8,128)(2,1)S(1)} %bitcast.11, bf16[16,256,256]{2,1,0:T(8,128)(2,1)S(1)} %bitcast.18, bf16[256,256]{1,0:T(8,128)(2,1)S(1)} %collective-permute-done.1.below.refs_2_.y, f32[8,128]{1,0:T(8,128)S(1)} %shard_map.107.after), custom_call_target="tpu_custom_call" | custom-call | tf_op jit(solution)/shard_map/pallas_call | solution.py:333
  20.9 1.2 %collective-permute-start.3 = (bf16[256,256]{1,0:T(8,128)(2,1)S(1)}, bf16[256,256]{1,0:T(8,128)(2,1)S(1)}, u32[]{:S(2)}, u32[]{:S(2)}) collective-permute-start(bf16[256,256]{1,0:T(8,128)(2,1)S(1)} %get-tuple-element.49), channel_id=1, source_target_pairs={{0,1},{1,2},{2,3},{3,0},{4,5},{5,6},{6,7},{7,4},{8,9},{9,10},{10,1... | collective-permute-start | bytes 393224 | tf_op jit(solution)/shard_map/ppermute | solution.py:39
  22.2 1.3 %shard_map.110 = (f32[256,256]{1,0:T(8,128)S(1)}, f32[256,256]{1,0:T(8,128)S(1)}) custom-call(bf16[16,256,256]{2,1,0:T(8,128)(2,1)S(1)} %bitcast.12, bf16[16,256,256]{2,1,0:T(8,128)(2,1)S(1)} %bitcast.19, bf16[256,256]{1,0:T(8,128)(2,1)S(1)} %get-tuple-element.51.value), custom_call_target="tpu_custom_call" | custom-call | tf_op jit(solution)/shard_map/pallas_call | solution.py:333
  23.9 1.2 %collective-permute-start.7 = (bf16[256,256]{1,0:T(8,128)(2,1)S(1)}, bf16[256,256]{1,0:T(8,128)(2,1)S(1)}, u32[]{:S(2)}, u32[]{:S(2)}) collective-permute-start(bf16[256,256]{1,0:T(8,128)(2,1)S(1)} %get-tuple-element.62), channel_id=1, source_target_pairs={{0,3},{1,0},{2,1},{3,2},{4,7},{5,4},{6,5},{7,6},{8,11},{9,8},{10,9... | collective-permute-start | bytes 393224 | tf_op jit(solution)/shard_map/ppermute | solution.py:39
  25.1 2.2 %collective-permute-done.3.refs_3_.g = bf16[256,256]{1,0:T(8,128)(2,1)S(1)} collective-permute-done((bf16[256,256]{1,0:T(8,128)(2,1)S(1)}, bf16[256,256]{1,0:T(8,128)(2,1)S(1)}, u32[]{:S(2)}, u32[]{:S(2)}) %collective-permute-start.3) | collective-permute-done | bytes 131104 | tf_op jit(solution)/shard_map/ppermute | solution.py:39
  27.5 1.2 %shard_map.114.up = f32[256,256]{1,0:T(8,128)S(1)} custom-call(bf16[16,256,256]{2,1,0:T(8,128)(2,1)S(1)} %bitcast.13, bf16[16,256,256]{2,1,0:T(8,128)(2,1)S(1)} %bitcast.20, bf16[256,256]{1,0:T(8,128)(2,1)S(1)} %get-tuple-element.59.below.p, f32[8,128]{1,0:T(8,128)S(1)} %get-tuple-element.61.after), custom_call_target="tpu_custom_call" | custom-call | tf_op jit(solution)/shard_map/pallas_call | solution.py:333
  29.0 2.1 %collective-permute-start.8 = (bf16[256,256]{1,0:T(8,128)(2,1)S(1)}, bf16[256,256]{1,0:T(8,128)(2,1)S(1)}, u32[]{:S(2)}, u32[]{:S(2)}) collective-permute-start(bf16[256,256]{1,0:T(8,128)(2,1)S(1)} %get-tuple-element.63), channel_id=1, source_target_pairs={{0,1},{1,2},{2,3},{3,0},{4,5},{5,6},{6,7},{7,4},{8,9},{9,10},{10,1... | collective-permute-start | bytes 393224 | tf_op jit(solution)/shard_map/ppermute | solution.py:39
  31.1 0.9 %collective-permute-start.9 = (f32[8,128]{1,0:T(8,128)S(1)}, f32[8,128]{1,0:T(8,128)S(1)}, u32[]{:S(2)}, u32[]{:S(2)}) collective-permute-start(f32[8,128]{1,0:T(8,128)S(1)} %get-tuple-element.61.after), channel_id=1, source_target_pairs={{0,1},{1,0},{2,3},{3,2},{4,5},{5,4},{6,7},{7,6},{8,9},{9,8},{10,11... | collective-permute-start | bytes 12296 | tf_op jit(solution)/shard_map/ppermute | solution.py:76
  32.0 3.3 %collective-permute-done.9 = f32[8,128]{1,0:T(8,128)S(1)} collective-permute-done((f32[8,128]{1,0:T(8,128)S(1)}, f32[8,128]{1,0:T(8,128)S(1)}, u32[]{:S(2)}, u32[]{:S(2)}) %collective-permute-start.9) | collective-permute-done | bytes 4128 | tf_op jit(solution)/shard_map/ppermute | solution.py:76
  35.3 1.3 %shard_map.117 = (f32[256,256]{1,0:T(8,128)S(1)}, f32[256,256]{1,0:T(8,128)S(1)}) custom-call(bf16[16,256,256]{2,1,0:T(8,128)(2,1)S(1)} %bitcast.14, bf16[16,256,256]{2,1,0:T(8,128)(2,1)S(1)} %bitcast.21, bf16[256,256]{1,0:T(8,128)(2,1)S(1)} %get-tuple-element.69.value), custom_call_target="tpu_custom_call" | custom-call | tf_op jit(solution)/shard_map/pallas_call | solution.py:333
  36.5 1.3 %shard_map.116 = (f32[256,256]{1,0:T(8,128)S(1)}, f32[256,256]{1,0:T(8,128)S(1)}) custom-call(bf16[16,256,256]{2,1,0:T(8,128)(2,1)S(1)} %bitcast.15, bf16[16,256,256]{2,1,0:T(8,128)(2,1)S(1)} %bitcast.22, bf16[256,256]{1,0:T(8,128)(2,1)S(1)} %get-tuple-element.67.value), custom_call_target="tpu_custom_call" | custom-call | tf_op jit(solution)/shard_map/pallas_call | solution.py:333
  37.8 0.7 %shard_map.118 = (f32[256,256]{1,0:T(8,128)S(1)}, f32[256,256]{1,0:T(8,128)S(1)}, f32[8,128]{1,0:T(8,128)S(1)}, f32[256,256]{1,0:T(8,128)S(1)}, f32[8,128]{1,0:T(8,128)S(1)}) custom-call(f32[8,128]{1,0:T(8,128)S(1)} %add.7.refs_0_, f32[8,128]{1,0:T(8,128)S(1)} %collective-permute-done.10.refs_1_, f32[256,256]{1,0:T(8,128)S(1)} %get-tuple-element.44.y.refs_2_, ...), custom_call_target="tpu_custom_call" | custom-call | tf_op jit(solution)/shard_map/pallas_call | solution.py:333
  38.7 2.0 %collective-permute-start.13 = (f32[8,128]{1,0:T(8,128)S(1)}, f32[8,128]{1,0:T(8,128)S(1)}, u32[]{:S(2)}, u32[]{:S(2)}) collective-permute-start(f32[8,128]{1,0:T(8,128)S(1)} %shard_map.119.refs_0_), channel_id=1, source_target_pairs={{0,3},{1,2},{2,1},{3,0},{4,7},{5,6},{6,5},{7,4},{8,11},{9,10},{10,... | collective-permute-start | bytes 12296 | tf_op jit(solution)/shard_map/ppermute | solution.py:62
  41.5 0.7 %collective-permute-done.13.refs_3_ = f32[8,128]{1,0:T(8,128)S(1)} collective-permute-done((f32[8,128]{1,0:T(8,128)S(1)}, f32[8,128]{1,0:T(8,128)S(1)}, u32[]{:S(2)}, u32[]{:S(2)}) %collective-permute-start.13) | collective-permute-done | bytes 4128 | tf_op jit(solution)/shard_map/ppermute | solution.py:62
  42.2 1.0 %collective-permute-done.12.refs_2_ = f32[8,128]{1,0:T(8,128)S(1)} collective-permute-done((f32[8,128]{1,0:T(8,128)S(1)}, f32[8,128]{1,0:T(8,128)S(1)}, u32[]{:S(2)}, u32[]{:S(2)}) %collective-permute-start.12) | collective-permute-done | bytes 4128 | tf_op jit(solution)/shard_map/ppermute | solution.py:62
  43.5 1.7 %shard_map.120 = (f32[256,256]{1,0:T(8,128)S(1)}, bf16[1,1,256,256]{3,2,1,0:T(8,128)(2,1)S(1)}) custom-call(f32[8,128]{1,0:T(8,128)S(1)} %shard_map.119.refs_0_, f32[8,128]{1,0:T(8,128)S(1)} %collective-permute-done.11.refs_1_, f32[8,128]{1,0:T(8,128)S(1)} %collective-permute-done.12.refs_2_, f32[8,128]{1,0:T(8,128)S(1)} %collective-permute-done.13.refs_3_, ...), custom_call_target="tpu_custom_call" | custom-call | tf_op jit(solution)/shard_map/pallas_call | solution.py:333
  45.2 0.7 %shard_map.121 = (f32[256,256]{1,0:T(8,128)S(1)}, bf16[1,1,256,256]{3,2,1,0:T(8,128)(2,1)S(1)}, f32[1]{0:T(128)}) custom-call(f32[8,128]{1,0:T(8,128)S(1)} %shard_map.119.refs_0_, f32[8,128]{1,0:T(8,128)S(1)} %collective-permute-done.11.refs_1_, f32[8,128]{1,0:T(8,128)S(1)} %collective-permute-done.12.refs_2_, ...), custom_call_target="tpu_custom_call", output_to_operand_aliasing={{0}: (7, {})} | custom-call | tf_op jit(solution)/shard_map/pallas_call | solution.py:333
  45.9 3.5 %collective-permute-start.14 = (bf16[1,1,256,256]{3,2,1,0:T(8,128)(2,1)S(1)}, bf16[1,1,256,256]{3,2,1,0:T(8,128)(2,1)S(1)}, u32[]{:S(2)}, u32[]{:S(2)}) collective-permute-start(bf16[1,1,256,256]{3,2,1,0:T(8,128)(2,1)S(1)} %get-tuple-element.80), channel_id=1, source_target_pairs={{0,4},{4,0},{8,12},{12,8},{16,20},{20,16},{24,28},{28,24},{1,5},{5... | collective-permute-start | bytes 393224 | tf_op jit(solution)/shard_map/ppermute | solution.py:34
  49.3 3.3 %collective-permute-start.15 = (bf16[1,1,256,256]{3,2,1,0:T(8,128)(2,1)S(1)}, bf16[1,1,256,256]{3,2,1,0:T(8,128)(2,1)S(1)}, u32[]{:S(2)}, u32[]{:S(2)}) collective-permute-start(bf16[1,1,256,256]{3,2,1,0:T(8,128)(2,1)S(1)} %get-tuple-element.81), channel_id=1, source_target_pairs={{0,0},{4,8},{8,4},{12,16},{16,12},{20,24},{24,20},{28,28},{1,1},{5... | collective-permute-start | bytes 393224 | tf_op jit(solution)/shard_map/ppermute | solution.py:34
  52.7 0.7 %shard_map.122 = f32[1,1,256,256]{3,2,1,0:T(8,128)} custom-call(f32[256,256]{1,0:T(8,128)S(1)} %get-tuple-element.79.value), custom_call_target="tpu_custom_call" | custom-call | bytes 1048576 | tf_op jit(solution)/shard_map/pallas_call | solution.py:333
  53.4 2.2 %collective-permute-done.15.far = bf16[1,1,256,256]{3,2,1,0:T(8,128)(2,1)S(1)} collective-permute-done((bf16[1,1,256,256]{3,2,1,0:T(8,128)(2,1)S(1)}, bf16[1,1,256,256]{3,2,1,0:T(8,128)(2,1)S(1)}, u32[]{:S(2)}, u32[]{:S(2)}) %collective-permute-start.15) | collective-permute-done | bytes 131104 | tf_op jit(solution)/shard_map/ppermute | solution.py:34
  55.6 0.7 %shard_map.123 = bf16[1,1,256,256]{3,2,1,0:T(8,128)(2,1)} custom-call(bf16[1,1,256,256]{3,2,1,0:T(8,128)(2,1)S(1)} %collective-permute-done.14.near, bf16[1,1,256,256]{3,2,1,0:T(8,128)(2,1)S(1)} %collective-permute-done.15.far), custom_call_target="tpu_custom_call" | custom-call | tf_op jit(solution)/shard_map/pallas_call | solution.py:333
  (36 shorter events, 2.8 us)
Async XLA Ops:
  0.6 3.0 %copy-start.4 = (bf16[1,1,256,256]{3,2,1,0:T(8,128)(2,1)S(1)}, bf16[1,1,256,256]{3,2,1,0:T(8,128)(2,1)}, u32[]{:S(2)}) copy-start(bf16[1,1,256,256]{3,2,1,0:T(8,128)(2,1)} %param.10) | copy-start | bytes 393220
  0.6 3.0 %copy-start.5 = (f32[1,1,256]{2,1,0:T(1,128)S(1)}, f32[1,1,256]{2,1,0:T(1,128)}, u32[]{:S(2)}) copy-start(f32[1,1,256]{2,1,0:T(1,128)} %param.13) | copy-start | bytes 3076
  0.7 7.6 %copy-start.3 = (bf16[1,1,256,256]{3,2,1,0:T(8,128)(2,1)S(1)}, bf16[1,1,256,256]{3,2,1,0:T(8,128)(2,1)}, u32[]{:S(2)}) copy-start(bf16[1,1,256,256]{3,2,1,0:T(8,128)(2,1)} %param.12) | copy-start | bytes 393220
  0.7 9.0 %copy-start.2 = (bf16[1,1,256,256]{3,2,1,0:T(8,128)(2,1)S(1)}, bf16[1,1,256,256]{3,2,1,0:T(8,128)(2,1)}, u32[]{:S(2)}) copy-start(bf16[1,1,256,256]{3,2,1,0:T(8,128)(2,1)} %param.14) | copy-start | bytes 393220
  0.7 7.6 %collective-permute-start = (bf16[256,256]{1,0:T(8,128)(2,1)}, bf16[256,256]{1,0:T(8,128)(2,1)S(1)}, u32[]{:S(2)}, u32[]{:S(2)}) collective-permute-start(bf16[256,256]{1,0:T(8,128)(2,1)} %bitcast.31), channel_id=1, source_target_pairs={{4,0},{8,4},{12,8},{16,12},{20,16},{24,20},{28,24},{5,1},{9,5},{13... | collective-permute-start | bytes 393224 | tf_op jit(solution)/shard_map/ppermute | solution.py:26
  2.7 7.0 %copy-start = (bf16[1,1,16,256,256]{4,3,2,1,0:T(8,128)(2,1)S(1)}, bf16[1,1,16,256,256]{4,3,2,1,0:T(8,128)(2,1)}, u32[]{:S(2)}) copy-start(bf16[1,1,16,256,256]{4,3,2,1,0:T(8,128)(2,1)} %param.8) | copy-start | bytes 6291460
  2.7 7.0 %copy-start.1 = (bf16[1,1,16,256,256]{4,3,2,1,0:T(8,128)(2,1)S(1)}, bf16[1,1,16,256,256]{4,3,2,1,0:T(8,128)(2,1)}, u32[]{:S(2)}) copy-start(bf16[1,1,16,256,256]{4,3,2,1,0:T(8,128)(2,1)} %param.9) | copy-start | bytes 6291460
  8.4 5.3 %collective-permute-start.1 = (bf16[256,256]{1,0:T(8,128)(2,1)S(1)}, bf16[256,256]{1,0:T(8,128)(2,1)S(1)}, u32[]{:S(2)}, u32[]{:S(2)}) collective-permute-start(bf16[256,256]{1,0:T(8,128)(2,1)S(1)} %get-tuple-element.43.yb), channel_id=1, source_target_pairs={{0,1},{1,2},{2,3},{3,0},{4,5},{5,6},{6,7},{7,4},{8,9},{9,10},{10,1... | collective-permute-start | bytes 393224 | tf_op jit(solution)/shard_map/ppermute | solution.py:39
  11.0 9.8 %collective-permute-start.2 = (bf16[256,256]{1,0:T(8,128)(2,1)S(1)}, bf16[256,256]{1,0:T(8,128)(2,1)S(1)}, u32[]{:S(2)}, u32[]{:S(2)}) collective-permute-start(bf16[256,256]{1,0:T(8,128)(2,1)S(1)} %get-tuple-element.48), channel_id=1, source_target_pairs={{0,3},{1,0},{2,1},{3,2},{4,7},{5,4},{6,5},{7,6},{8,11},{9,8},{10,9... | collective-permute-start | bytes 393224 | tf_op jit(solution)/shard_map/ppermute | solution.py:39
  13.8 2.5 %collective-permute-start.4 = (f32[8,128]{1,0:T(8,128)S(1)}, f32[8,128]{1,0:T(8,128)S(1)}, u32[]{:S(2)}, u32[]{:S(2)}) collective-permute-start(f32[8,128]{1,0:T(8,128)S(1)} %shard_map.107.after), channel_id=1, source_target_pairs={{0,1},{1,0},{2,3},{3,2},{4,5},{5,4},{6,7},{7,6},{8,9},{9,8},{10,11... | collective-permute-start | bytes 12296 | tf_op jit(solution)/shard_map/ppermute | solution.py:76
  16.3 7.1 %collective-permute-start.5 = (f32[8,128]{1,0:T(8,128)S(1)}, f32[8,128]{1,0:T(8,128)S(1)}, u32[]{:S(2)}, u32[]{:S(2)}) collective-permute-start(f32[8,128]{1,0:T(8,128)S(1)} %add.6.refs_0_), channel_id=1, source_target_pairs={{0,2},{1,3},{2,0},{3,1},{4,6},{5,7},{6,4},{7,5},{8,10},{9,11},{10,... | collective-permute-start | bytes 12296 | tf_op jit(solution)/shard_map/ppermute | solution.py:76
  18.3 6.8 %collective-permute-start.6 = (bf16[256,256]{1,0:T(8,128)(2,1)S(1)}, bf16[256,256]{1,0:T(8,128)(2,1)S(1)}, u32[]{:S(2)}, u32[]{:S(2)}) collective-permute-start(bf16[256,256]{1,0:T(8,128)(2,1)S(1)} %bitcast.24), channel_id=1, source_target_pairs={{0,1},{1,2},{2,3},{3,0},{4,5},{5,6},{6,7},{7,4},{8,9},{9,10},{10,1... | collective-permute-start | bytes 393224 | tf_op jit(solution)/shard_map/ppermute | solution.py:39
  20.9 6.4 %collective-permute-start.3 = (bf16[256,256]{1,0:T(8,128)(2,1)S(1)}, bf16[256,256]{1,0:T(8,128)(2,1)S(1)}, u32[]{:S(2)}, u32[]{:S(2)}) collective-permute-start(bf16[256,256]{1,0:T(8,128)(2,1)S(1)} %get-tuple-element.49), channel_id=1, source_target_pairs={{0,1},{1,2},{2,3},{3,0},{4,5},{5,6},{6,7},{7,4},{8,9},{9,10},{10,1... | collective-permute-start | bytes 393224 | tf_op jit(solution)/shard_map/ppermute | solution.py:39
  23.9 5.0 %collective-permute-start.7 = (bf16[256,256]{1,0:T(8,128)(2,1)S(1)}, bf16[256,256]{1,0:T(8,128)(2,1)S(1)}, u32[]{:S(2)}, u32[]{:S(2)}) collective-permute-start(bf16[256,256]{1,0:T(8,128)(2,1)S(1)} %get-tuple-element.62), channel_id=1, source_target_pairs={{0,3},{1,0},{2,1},{3,2},{4,7},{5,4},{6,5},{7,6},{8,11},{9,8},{10,9... | collective-permute-start | bytes 393224 | tf_op jit(solution)/shard_map/ppermute | solution.py:39
  29.0 9.5 %collective-permute-start.8 = (bf16[256,256]{1,0:T(8,128)(2,1)S(1)}, bf16[256,256]{1,0:T(8,128)(2,1)S(1)}, u32[]{:S(2)}, u32[]{:S(2)}) collective-permute-start(bf16[256,256]{1,0:T(8,128)(2,1)S(1)} %get-tuple-element.63), channel_id=1, source_target_pairs={{0,1},{1,2},{2,3},{3,0},{4,5},{5,6},{6,7},{7,4},{8,9},{9,10},{10,1... | collective-permute-start | bytes 393224 | tf_op jit(solution)/shard_map/ppermute | solution.py:39
  31.1 4.1 %collective-permute-start.9 = (f32[8,128]{1,0:T(8,128)S(1)}, f32[8,128]{1,0:T(8,128)S(1)}, u32[]{:S(2)}, u32[]{:S(2)}) collective-permute-start(f32[8,128]{1,0:T(8,128)S(1)} %get-tuple-element.61.after), channel_id=1, source_target_pairs={{0,1},{1,0},{2,3},{3,2},{4,5},{5,4},{6,7},{7,6},{8,9},{9,8},{10,11... | collective-permute-start | bytes 12296 | tf_op jit(solution)/shard_map/ppermute | solution.py:76
  35.2 2.5 %collective-permute-start.10 = (f32[8,128]{1,0:T(8,128)S(1)}, f32[8,128]{1,0:T(8,128)S(1)}, u32[]{:S(2)}, u32[]{:S(2)}) collective-permute-start(f32[8,128]{1,0:T(8,128)S(1)} %add.7.refs_0_), channel_id=1, source_target_pairs={{0,2},{1,3},{2,0},{3,1},{4,6},{5,7},{6,4},{7,5},{8,10},{9,11},{10,... | collective-permute-start | bytes 12296 | tf_op jit(solution)/shard_map/ppermute | solution.py:76
  38.7 3.4 %collective-permute-start.13 = (f32[8,128]{1,0:T(8,128)S(1)}, f32[8,128]{1,0:T(8,128)S(1)}, u32[]{:S(2)}, u32[]{:S(2)}) collective-permute-start(f32[8,128]{1,0:T(8,128)S(1)} %shard_map.119.refs_0_), channel_id=1, source_target_pairs={{0,3},{1,2},{2,1},{3,0},{4,7},{5,6},{6,5},{7,4},{8,11},{9,10},{10,... | collective-permute-start | bytes 12296 | tf_op jit(solution)/shard_map/ppermute | solution.py:62
  40.7 2.5 %collective-permute-start.12 = (f32[8,128]{1,0:T(8,128)S(1)}, f32[8,128]{1,0:T(8,128)S(1)}, u32[]{:S(2)}, u32[]{:S(2)}) collective-permute-start(f32[8,128]{1,0:T(8,128)S(1)} %shard_map.119.refs_0_), channel_id=1, source_target_pairs={{0,2},{1,3},{2,0},{3,1},{4,6},{5,7},{6,4},{7,5},{8,10},{9,11},{10,... | collective-permute-start | bytes 12296 | tf_op jit(solution)/shard_map/ppermute | solution.py:62
  41.0 2.5 %collective-permute-start.11 = (f32[8,128]{1,0:T(8,128)S(1)}, f32[8,128]{1,0:T(8,128)S(1)}, u32[]{:S(2)}, u32[]{:S(2)}) collective-permute-start(f32[8,128]{1,0:T(8,128)S(1)} %shard_map.119.refs_0_), channel_id=1, source_target_pairs={{0,1},{1,0},{2,3},{3,2},{4,5},{5,4},{6,7},{7,6},{8,9},{9,8},{10,11... | collective-permute-start | bytes 12296 | tf_op jit(solution)/shard_map/ppermute | solution.py:62
  45.9 7.6 %collective-permute-start.14 = (bf16[1,1,256,256]{3,2,1,0:T(8,128)(2,1)S(1)}, bf16[1,1,256,256]{3,2,1,0:T(8,128)(2,1)S(1)}, u32[]{:S(2)}, u32[]{:S(2)}) collective-permute-start(bf16[1,1,256,256]{3,2,1,0:T(8,128)(2,1)S(1)} %get-tuple-element.80), channel_id=1, source_target_pairs={{0,4},{4,0},{8,12},{12,8},{16,20},{20,16},{24,28},{28,24},{1,5},{5... | collective-permute-start | bytes 393224 | tf_op jit(solution)/shard_map/ppermute | solution.py:34
  49.3 6.3 %collective-permute-start.15 = (bf16[1,1,256,256]{3,2,1,0:T(8,128)(2,1)S(1)}, bf16[1,1,256,256]{3,2,1,0:T(8,128)(2,1)S(1)}, u32[]{:S(2)}, u32[]{:S(2)}) collective-permute-start(bf16[1,1,256,256]{3,2,1,0:T(8,128)(2,1)S(1)} %get-tuple-element.81), channel_id=1, source_target_pairs={{0,0},{4,8},{8,4},{12,16},{16,12},{20,24},{24,20},{28,28},{1,1},{5... | collective-permute-start | bytes 393224 | tf_op jit(solution)/shard_map/ppermute | solution.py:34

commit v12 on v11

--- a/solution.py
+++ b/solution.py
@@ -20,18 +20,18 @@
 COVER = pl.CostEstimate(flops=10**10, bytes_accessed=1 << 24, transcendentals=0)
 
 
-def shift(value, axis, steps):
-    count = lax.axis_size(axis)
-    first, last = max(0, -steps), min(count, count - steps)
-    return lax.ppermute(value, axis, [(source, source + steps) for source in range(first, last)])
-
-
-def swap(value, axis, first):
-    count = lax.axis_size(axis)
-    pairs = {i: i for i in range(count)}
+def swap(value, axis, first, other):
+    count, across = lax.axis_size(axis), lax.axis_size(other)
+    partner = {}
     for i in range(first, count - 1, 2):
-        pairs[i], pairs[i + 1] = i + 1, i
-    return lax.ppermute(value, axis, list(pairs.items()))
+        partner[i], partner[i + 1] = i + 1, i
+    pairs = []
+    for i in range(count):
+        for j in range(across):
+            beside = min(j ^ 1, across - 1) if across % 2 == 0 else j
+            target = (partner[i], j) if i in partner else (i, beside)
+            pairs.append((i * across + j, target[0] * across + target[1]))
+    return lax.ppermute(value, (axis, other), pairs)
 
 
 def rotate(value, axis, steps):
@@ -121,22 +121,28 @@
 
 def start_kernel(scaled, behind, guess, mask, y_ref, yb_ref):
     size = mask.shape[-1]
-    start = jnp.dot(scaled[...], behind[...], preferred_element_type=F32) + guess[...].astype(F32)
+    inside = lax.axis_index("seg") < lax.axis_size("seg") - 1
+    right = jnp.where(inside, behind[...], jnp.zeros_like(behind))
+    start = jnp.dot(scaled[...], right, preferred_element_type=F32) + guess[...].astype(F32)
     y = mask[...] * start * (1.0 / (1 << (size - 1).bit_length()))
     y_ref[...] = y
     yb_ref[...] = y.astype(BF16)
 
 
-def start_lower_kernel(left, right, y, yb, prec, low_ref, stat_ref, diag_ref, sent_ref, py_ref, inner):
-    channels = left.shape[0]
-    value = yb[...]
-    low = sandwich(left, right, value, inner, WD, channels)
+def start_lower_kernel(left, right, yb, low_ref, sent_ref, inner):
+    low = sandwich(left, right, yb[...], inner, WD, left.shape[0])
     low_ref[...] = low
     sent_ref[...] = low.astype(BF16)
-    diag = sandwich(left, right, value, inner, 0, WD)
+
+
+def start_terms_kernel(left, right, y, yb, prec, stat_ref, diag_ref, low_ref, diag_py_ref, inner):
+    channels = left.shape[0]
+    diag = sandwich(left, right, yb[...], inner, 0, WD)
     diag_ref[...] = diag
-    py_ref[...] = (prec[...].astype(F32) * y[...]).astype(BF16)
     write_sums(stat_ref, [(y, y), (y, diag)])
+    weighted = (prec[...].astype(F32) * y[...]).astype(BF16)
+    low_ref[...] = sandwich(left, right, weighted, inner, WD, channels)
+    diag_py_ref[...] = sandwich(left, right, weighted, inner, 0, WD)
 
 
 def terms_kernel(left, right, value, low_ref, diag_ref, inner):
@@ -186,16 +192,21 @@
     up_ref[...] = from_below(sandwich(left, right, below[...], inner, WD, left.shape[0]))
 
 
+def first_low_kernel(parts, *refs):
+    low_g, low_y, low_ref, sent_ref = refs[parts:]
+    yy, yhy = scalars(refs[:parts], 2)
+    low = low_g[...] - (yhy / yy) * low_y[...]
+    low_ref[...] = low
+    sent_ref[...] = low.astype(BF16)
+
+
 def first_kernel(parts, *refs):
-    y, g, prec, low_g, low_y, diag_g, diag_y = refs[parts : parts + 7]
-    p_ref, low_ref, sent_ref, diag_ref, stat_ref, weighted_b, shift_ref = refs[parts + 7 :]
+    y, g, prec, diag_g, diag_y = refs[parts : parts + 5]
+    p_ref, diag_ref, stat_ref, weighted_b, shift_ref = refs[parts + 5 :]
     yy, yhy = scalars(refs[:parts], 2)
     a = yhy / yy
     shift_ref[...] = jnp.broadcast_to(a, shift_ref.shape)
     weights = prec[...].astype(F32)
-    low = low_g[...] - a * low_y[...]
-    low_ref[...] = low
-    sent_ref[...] = low.astype(BF16)
     p = weights * (g[...] - a * y[...])
     p_ref[...] = p
     weighted_b[...] = (weights * p).astype(BF16)
@@ -342,7 +353,7 @@
         )(*operands)
 
     (cover,) = call(cover_kernel, [stats], cost=COVER)
-    behind = shift(right_piece[0, 0], "seg", -1)
+    behind = rotate(right_piece[0, 0], "seg", -1)
     prec_below = rotate(prec, "sec", 1)
     (mask,) = call(mask_kernel, [matrix], sector_rows, cover)
     scaled = (left_piece[0, 0].astype(F32) * inverse_values[0]).astype(BF16)
@@ -358,25 +369,30 @@
         return call(join_kernel, outs, diag, up, above, mask, prec)
 
     y_below = rotate(yb, "sec", 1)
-    low, stat, diag, sent, pyb = call(
-        start_lower_kernel,
-        [matrix, stats, matrix, narrow, narrow],
+    low, sent = call(start_lower_kernel, [matrix, narrow], left, right, yb, scratch=[inner])
+    above = rotate(sent, "sec", -1)
+    stat, diag, low_y, diag_y = call(
+        start_terms_kernel,
+        [stats, matrix, matrix, matrix],
         left, right, y, yb, prec,
         scratch=[inner],
     )
-    above = rotate(sent, "sec", -1)
-    low_y, diag_y = terms(pyb)
     (stat,) = call(cross_kernel, [stats], y_below, low, stat)
     parts = pairwise(stat, "sec")
     g, gb, pgb = joined(y_below, stat, diag, above)
     g_below = rotate(gb, "sec", 1)
     low_g, diag_g = terms(pgb)
-    p, low, sent, diag, stat, ppb, shifted = call(
+    low, sent = call(
+        functools.partial(first_low_kernel, len(parts)),
+        [matrix, narrow],
+        *parts, low_g, low_y,
+    )
+    above = rotate(sent, "sec", -1)
+    p, diag, stat, ppb, shifted = call(
         functools.partial(first_kernel, len(parts)),
-        [matrix, matrix, narrow, matrix, stats, narrow, stats],
-        *parts, y, g, prec, low_g, low_y, diag_g, diag_y,
-    )
-    above = rotate(sent, "sec", -1)
+        [matrix, matrix, stats, narrow, stats],
+        *parts, y, g, prec, diag_g, diag_y,
+    )
     stat, p_below = call(
         functools.partial(first_cross_kernel, len(parts)),
         [stats, narrow],
@@ -404,7 +420,7 @@
     energy = jax.ShapeDtypeStruct((1,), F32)
     operands = (*parts, x, p, coefficients)
     polar, far = call(functools.partial(odd_kernel, len(parts)), [matrix, weight], *operands)
-    far = swap(far, "seg", 1)
+    far = swap(far, "seg", 1, "sec")
     polar, near, energy = call(
         functools.partial(even_kernel, len(parts)),
         [matrix, weight, energy],
@@ -412,7 +428,7 @@
         out_specs=[VMEM, VMEM, SMEM],
         aliases={len(operands): 0},
     )
-    near = swap(near, "seg", 0)
+    near = swap(near, "seg", 0, "sec")
     (handed,) = call(hand_kernel, [weight], near, far)
     (polar,) = call(store_kernel, [jax.ShapeDtypeStruct(block, F32)], polar, cost=SHORT)
     return polar, handed, energy

time: 56.5 us -> 56.4 us (level)
  starting transfers between devices: 22.7 us -> 21.9 us
    ppermute x3 -> x2, waiting for transfers between devices: 6.73 us -> 3.93 us  [swap(): return lax.ppermute(value, (axis, other), pairs)]
    ppermute x6 -> x7, waiting for transfers between devices: 3.89 us -> 5.36 us  [rotate(): lax.ppermute(value, axis, [(source, (source + steps) % count) for source...]
    ppermute x4, waiting for transfers between devices: 4.59 us -> 5.86 us  [pairwise(): parts.append(lax.ppermute(parts[0], axis, pairs))]
    ppermute x3 -> x2, starting transfers between devices: 8.89 us -> 7.65 us  [swap(): return lax.ppermute(value, (axis, other), pairs)]
    ppermute x6 -> x7, starting transfers between devices: 7.03 us -> 7.97 us  [rotate(): lax.ppermute(value, axis, [(source, (source + steps) % count) for source...]
    pallas_call x21 -> x22, Pallas kernels: 14.6 us -> 14.9 us  [call(): pl.pallas_call(kernel, out_shape=outs, in_specs=in_specs or [VMEM] * len(...]
where the time goes in v12:
time: 56.4 us; the launch traced here: 55.9 us
  starting transfers between devices  21.9 us (39%)
  waiting for transfers between devices  17.4 us (31%)
  Pallas kernels  14.9 us (26%)
  between operations  1.64 us (3%)
    pallas_call x22, Pallas kernels, call(): pl.pallas_call(kernel, out_shape=outs, in_specs=in_specs or [VMEM] * len(...  14.9 us
    ppermute x7, starting transfers between devices, rotate(): lax.ppermute(value, axis, [(source, (source + steps) % count) for source...  7.97 us
    ppermute x2, starting transfers between devices, swap(): return lax.ppermute(value, (axis, other), pairs)  7.65 us
    ppermute x4, waiting for transfers between devices, pairwise(): parts.append(lax.ppermute(parts[0], axis, pairs))  5.86 us
    ppermute x7, waiting for transfers between devices, rotate(): lax.ppermute(value, axis, [(source, (source + steps) % count) for source...  5.36 us
    ppermute x2, waiting for transfers between devices, swap(): return lax.ppermute(value, (axis, other), pairs)  3.93 us
    ppermute x4, starting transfers between devices, pairwise(): parts.append(lax.ppermute(parts[0], axis, pairs))  3.52 us
    ppermute x3, starting transfers between devices, exchange(): parts.append(lax.ppermute(parts[0], axis, pairs))  2.71 us
  transfers between devices with their start and end apart: 16, of which 10 were waited for; matrix products, arithmetic and copies ran while one was open for 0% of the time, Pallas kernels for 20%

profile of v12, /device:TPU:1, one launch (start us, length us, event | category | flops | bytes accessed | tf_op | source)
XLA Modules:
  0.0 55.9 jit_solution(8470168959680509228)
XLA Ops:
  1.7 4.5 %collective-permute-done.behind = bf16[256,256]{1,0:T(8,128)(2,1)S(1)} collective-permute-done((bf16[256,256]{1,0:T(8,128)(2,1)}, bf16[256,256]{1,0:T(8,128)(2,1)S(1)}, u32[]{:S(2)}, u32[]{:S(2)}) %collective-permute-start) | collective-permute-done | bytes 131104 | tf_op jit(solution)/shard_map/ppermute | solution.py:39
  6.5 1.3 %collective-permute-start.1 = (bf16[256,256]{1,0:T(8,128)(2,1)S(1)}, bf16[256,256]{1,0:T(8,128)(2,1)S(1)}, u32[]{:S(2)}, u32[]{:S(2)}) collective-permute-start(bf16[256,256]{1,0:T(8,128)(2,1)S(1)} %get-tuple-element.42.yb), channel_id=1, source_target_pairs={{0,1},{1,2},{2,3},{3,0},{4,5},{5,6},{6,7},{7,4},{8,9},{9,10},{10,1... | collective-permute-start | bytes 393224 | tf_op jit(solution)/shard_map/ppermute | solution.py:39
  7.7 1.2 %shard_map.107 = (f32[256,256]{1,0:T(8,128)S(1)}, bf16[256,256]{1,0:T(8,128)(2,1)S(1)}) custom-call(bf16[16,256,256]{2,1,0:T(8,128)(2,1)S(1)} %bitcast.9, bf16[16,256,256]{2,1,0:T(8,128)(2,1)S(1)} %bitcast.16, bf16[256,256]{1,0:T(8,128)(2,1)S(1)} %get-tuple-element.42.yb), custom_call_target="tpu_custom_call" | custom-call | tf_op jit(solution)/shard_map/pallas_call | solution.py:344
  9.0 1.2 %collective-permute-start.2 = (bf16[256,256]{1,0:T(8,128)(2,1)S(1)}, bf16[256,256]{1,0:T(8,128)(2,1)S(1)}, u32[]{:S(2)}, u32[]{:S(2)}) collective-permute-start(bf16[256,256]{1,0:T(8,128)(2,1)S(1)} %get-tuple-element.47), channel_id=1, source_target_pairs={{0,3},{1,0},{2,1},{3,2},{4,7},{5,4},{6,5},{7,6},{8,11},{9,8},{10,9... | collective-permute-start | bytes 393224 | tf_op jit(solution)/shard_map/ppermute | solution.py:39
  10.2 1.5 %shard_map.106 = (f32[8,128]{1,0:T(8,128)S(1)}, f32[256,256]{1,0:T(8,128)S(1)}, f32[256,256]{1,0:T(8,128)S(1)}, f32[256,256]{1,0:T(8,128)S(1)}) custom-call(bf16[16,256,256]{2,1,0:T(8,128)(2,1)S(1)} %bitcast.10, bf16[16,256,256]{2,1,0:T(8,128)(2,1)S(1)} %bitcast.17, f32[256,256]{1,0:T(8,128)S(1)} %get-tuple-element.43.y.refs_2_, ...), custom_call_target="tpu_custom_call" | custom-call | tf_op jit(solution)/shard_map/pallas_call | solution.py:344
  12.1 2.5 %collective-permute-done.4 = f32[8,128]{1,0:T(8,128)S(1)} collective-permute-done((f32[8,128]{1,0:T(8,128)S(1)}, f32[8,128]{1,0:T(8,128)S(1)}, u32[]{:S(2)}, u32[]{:S(2)}) %collective-permute-start.4) | collective-permute-done | bytes 4128 | tf_op jit(solution)/shard_map/ppermute | solution.py:76
  14.6 1.2 %collective-permute-start.5 = (f32[8,128]{1,0:T(8,128)S(1)}, f32[8,128]{1,0:T(8,128)S(1)}, u32[]{:S(2)}, u32[]{:S(2)}) collective-permute-start(f32[8,128]{1,0:T(8,128)S(1)} %add.6.refs_0_), channel_id=1, source_target_pairs={{0,2},{1,3},{2,0},{3,1},{4,6},{5,7},{6,4},{7,5},{8,10},{9,11},{10,... | collective-permute-start | bytes 12296 | tf_op jit(solution)/shard_map/ppermute | solution.py:76
  15.9 1.1 %collective-permute-start.6 = (bf16[256,256]{1,0:T(8,128)(2,1)S(1)}, bf16[256,256]{1,0:T(8,128)(2,1)S(1)}, u32[]{:S(2)}, u32[]{:S(2)}) collective-permute-start(bf16[256,256]{1,0:T(8,128)(2,1)S(1)} %bitcast.24), channel_id=1, source_target_pairs={{0,1},{1,2},{2,3},{3,0},{4,5},{5,6},{6,7},{7,4},{8,9},{9,10},{10,1... | collective-permute-start | bytes 393224 | tf_op jit(solution)/shard_map/ppermute | solution.py:39
  17.0 1.2 %shard_map.109.up = f32[256,256]{1,0:T(8,128)S(1)} custom-call(bf16[16,256,256]{2,1,0:T(8,128)(2,1)S(1)} %bitcast.11, bf16[16,256,256]{2,1,0:T(8,128)(2,1)S(1)} %bitcast.18, bf16[256,256]{1,0:T(8,128)(2,1)S(1)} %collective-permute-done.1.below.refs_2_.y, f32[8,128]{1,0:T(8,128)S(1)} %shard_map.108.after), custom_call_target="tpu_custom_call" | custom-call | tf_op jit(solution)/shard_map/pallas_call | solution.py:344
  18.6 1.3 %shard_map.111 = (f32[256,256]{1,0:T(8,128)S(1)}, f32[256,256]{1,0:T(8,128)S(1)}) custom-call(bf16[16,256,256]{2,1,0:T(8,128)(2,1)S(1)} %bitcast.12, bf16[16,256,256]{2,1,0:T(8,128)(2,1)S(1)} %bitcast.19, bf16[256,256]{1,0:T(8,128)(2,1)S(1)} %get-tuple-element.49.value), custom_call_target="tpu_custom_call" | custom-call | tf_op jit(solution)/shard_map/pallas_call | solution.py:344
  20.1 2.1 %collective-permute-start.7 = (bf16[256,256]{1,0:T(8,128)(2,1)S(1)}, bf16[256,256]{1,0:T(8,128)(2,1)S(1)}, u32[]{:S(2)}, u32[]{:S(2)}) collective-permute-start(bf16[256,256]{1,0:T(8,128)(2,1)S(1)} %get-tuple-element.60), channel_id=1, source_target_pairs={{0,3},{1,0},{2,1},{3,2},{4,7},{5,4},{6,5},{7,6},{8,11},{9,8},{10,9... | collective-permute-start | bytes 393224 | tf_op jit(solution)/shard_map/ppermute | solution.py:39
  22.2 0.4 shard_map.113
  22.6 0.5 collective-permute-done.3.refs_3_.g
  23.3 1.2 %shard_map.115.up = f32[256,256]{1,0:T(8,128)S(1)} custom-call(bf16[16,256,256]{2,1,0:T(8,128)(2,1)S(1)} %bitcast.13, bf16[16,256,256]{2,1,0:T(8,128)(2,1)S(1)} %bitcast.20, bf16[256,256]{1,0:T(8,128)(2,1)S(1)} %get-tuple-element.57.below.p, f32[8,128]{1,0:T(8,128)S(1)} %get-tuple-element.59.after), custom_call_target="tpu_custom_call" | custom-call | tf_op jit(solution)/shard_map/pallas_call | solution.py:344
  24.9 1.9 %collective-permute-start.8 = (bf16[256,256]{1,0:T(8,128)(2,1)S(1)}, bf16[256,256]{1,0:T(8,128)(2,1)S(1)}, u32[]{:S(2)}, u32[]{:S(2)}) collective-permute-start(bf16[256,256]{1,0:T(8,128)(2,1)S(1)} %get-tuple-element.61), channel_id=1, source_target_pairs={{0,1},{1,2},{2,3},{3,0},{4,5},{5,6},{6,7},{7,4},{8,9},{9,10},{10,1... | collective-permute-start | bytes 393224 | tf_op jit(solution)/shard_map/ppermute | solution.py:39
  26.8 1.0 %collective-permute-start.9 = (f32[8,128]{1,0:T(8,128)S(1)}, f32[8,128]{1,0:T(8,128)S(1)}, u32[]{:S(2)}, u32[]{:S(2)}) collective-permute-start(f32[8,128]{1,0:T(8,128)S(1)} %get-tuple-element.59.after), channel_id=1, source_target_pairs={{0,1},{1,0},{2,3},{3,2},{4,5},{5,4},{6,7},{7,6},{8,9},{9,8},{10,11... | collective-permute-start | bytes 12296 | tf_op jit(solution)/shard_map/ppermute | solution.py:76
  27.8 3.4 %collective-permute-done.9 = f32[8,128]{1,0:T(8,128)S(1)} collective-permute-done((f32[8,128]{1,0:T(8,128)S(1)}, f32[8,128]{1,0:T(8,128)S(1)}, u32[]{:S(2)}, u32[]{:S(2)}) %collective-permute-start.9) | collective-permute-done | bytes 4128 | tf_op jit(solution)/shard_map/ppermute | solution.py:76
  31.2 0.9 %collective-permute-start.10 = (f32[8,128]{1,0:T(8,128)S(1)}, f32[8,128]{1,0:T(8,128)S(1)}, u32[]{:S(2)}, u32[]{:S(2)}) collective-permute-start(f32[8,128]{1,0:T(8,128)S(1)} %add.7.refs_0_), channel_id=1, source_target_pairs={{0,2},{1,3},{2,0},{3,1},{4,6},{5,7},{6,4},{7,5},{8,10},{9,11},{10,... | collective-permute-start | bytes 12296 | tf_op jit(solution)/shard_map/ppermute | solution.py:76
  32.1 1.3 %shard_map.118 = (f32[256,256]{1,0:T(8,128)S(1)}, f32[256,256]{1,0:T(8,128)S(1)}) custom-call(bf16[16,256,256]{2,1,0:T(8,128)(2,1)S(1)} %bitcast.14, bf16[16,256,256]{2,1,0:T(8,128)(2,1)S(1)} %bitcast.21, bf16[256,256]{1,0:T(8,128)(2,1)S(1)} %get-tuple-element.67.value), custom_call_target="tpu_custom_call" | custom-call | tf_op jit(solution)/shard_map/pallas_call | solution.py:344
  33.3 1.3 %shard_map.117 = (f32[256,256]{1,0:T(8,128)S(1)}, f32[256,256]{1,0:T(8,128)S(1)}) custom-call(bf16[16,256,256]{2,1,0:T(8,128)(2,1)S(1)} %bitcast.15, bf16[16,256,256]{2,1,0:T(8,128)(2,1)S(1)} %bitcast.22, bf16[256,256]{1,0:T(8,128)(2,1)S(1)} %get-tuple-element.65.value), custom_call_target="tpu_custom_call" | custom-call | tf_op jit(solution)/shard_map/pallas_call | solution.py:344
  34.6 0.7 %shard_map.119 = (f32[256,256]{1,0:T(8,128)S(1)}, f32[256,256]{1,0:T(8,128)S(1)}, f32[8,128]{1,0:T(8,128)S(1)}, f32[256,256]{1,0:T(8,128)S(1)}, f32[8,128]{1,0:T(8,128)S(1)}) custom-call(f32[8,128]{1,0:T(8,128)S(1)} %add.7.refs_0_, f32[8,128]{1,0:T(8,128)S(1)} %collective-permute-done.10.refs_1_, f32[256,256]{1,0:T(8,128)S(1)} %get-tuple-element.43.y.refs_2_, ...), custom_call_target="tpu_custom_call" | custom-call | tf_op jit(solution)/shard_map/pallas_call | solution.py:344
  35.6 1.0 %collective-permute-start.13 = (f32[8,128]{1,0:T(8,128)S(1)}, f32[8,128]{1,0:T(8,128)S(1)}, u32[]{:S(2)}, u32[]{:S(2)}) collective-permute-start(f32[8,128]{1,0:T(8,128)S(1)} %shard_map.120.refs_0_), channel_id=1, source_target_pairs={{0,3},{1,2},{2,1},{3,0},{4,7},{5,6},{6,5},{7,4},{8,11},{9,10},{10,... | collective-permute-start | bytes 12296 | tf_op jit(solution)/shard_map/ppermute | solution.py:62
  36.6 1.2 %collective-permute-start.12 = (f32[8,128]{1,0:T(8,128)S(1)}, f32[8,128]{1,0:T(8,128)S(1)}, u32[]{:S(2)}, u32[]{:S(2)}) collective-permute-start(f32[8,128]{1,0:T(8,128)S(1)} %shard_map.120.refs_0_), channel_id=1, source_target_pairs={{0,2},{1,3},{2,0},{3,1},{4,6},{5,7},{6,4},{7,5},{8,10},{9,11},{10,... | collective-permute-start | bytes 12296 | tf_op jit(solution)/shard_map/ppermute | solution.py:62
  37.8 0.5 collective-permute-start.11
  38.3 0.7 %collective-permute-done.13.refs_3_ = f32[8,128]{1,0:T(8,128)S(1)} collective-permute-done((f32[8,128]{1,0:T(8,128)S(1)}, f32[8,128]{1,0:T(8,128)S(1)}, u32[]{:S(2)}, u32[]{:S(2)}) %collective-permute-start.13) | collective-permute-done | bytes 4128 | tf_op jit(solution)/shard_map/ppermute | solution.py:62
  39.1 1.5 %collective-permute-done.11.refs_1_ = f32[8,128]{1,0:T(8,128)S(1)} collective-permute-done((f32[8,128]{1,0:T(8,128)S(1)}, f32[8,128]{1,0:T(8,128)S(1)}, u32[]{:S(2)}, u32[]{:S(2)}) %collective-permute-start.11) | collective-permute-done | bytes 4128 | tf_op jit(solution)/shard_map/ppermute | solution.py:62
  40.6 1.7 %shard_map.121 = (f32[256,256]{1,0:T(8,128)S(1)}, bf16[1,1,256,256]{3,2,1,0:T(8,128)(2,1)S(1)}) custom-call(f32[8,128]{1,0:T(8,128)S(1)} %shard_map.120.refs_0_, f32[8,128]{1,0:T(8,128)S(1)} %collective-permute-done.11.refs_1_, f32[8,128]{1,0:T(8,128)S(1)} %collective-permute-done.12.refs_2_, f32[8,128]{1,0:T(8,128)S(1)} %collective-permute-done.13.refs_3_, ...), custom_call_target="tpu_custom_call" | custom-call | tf_op jit(solution)/shard_map/pallas_call | solution.py:344
  42.2 0.7 %shard_map.122 = (f32[256,256]{1,0:T(8,128)S(1)}, bf16[1,1,256,256]{3,2,1,0:T(8,128)(2,1)S(1)}, f32[1]{0:T(128)}) custom-call(f32[8,128]{1,0:T(8,128)S(1)} %shard_map.120.refs_0_, f32[8,128]{1,0:T(8,128)S(1)} %collective-permute-done.11.refs_1_, f32[8,128]{1,0:T(8,128)S(1)} %collective-permute-done.12.refs_2_, ...), custom_call_target="tpu_custom_call", output_to_operand_aliasing={{0}: (7, {})} | custom-call | tf_op jit(solution)/shard_map/pallas_call | solution.py:344
  42.9 7.7 %collective-permute-start.14 = (bf16[1,1,256,256]{3,2,1,0:T(8,128)(2,1)S(1)}, bf16[1,1,256,256]{3,2,1,0:T(8,128)(2,1)S(1)}, u32[]{:S(2)}, u32[]{:S(2)}) collective-permute-start(bf16[1,1,256,256]{3,2,1,0:T(8,128)(2,1)S(1)} %get-tuple-element.78), channel_id=1, source_target_pairs={{0,4},{1,5},{2,6},{3,7},{4,0},{5,1},{6,2},{7,3},{8,12},{9,13},{10,... | collective-permute-start | bytes 393224 | tf_op jit(solution)/shard_map/ppermute | solution.py:34
  50.6 0.7 %shard_map.123 = f32[1,1,256,256]{3,2,1,0:T(8,128)} custom-call(f32[256,256]{1,0:T(8,128)S(1)} %get-tuple-element.77.value), custom_call_target="tpu_custom_call" | custom-call | bytes 1048576 | tf_op jit(solution)/shard_map/pallas_call | solution.py:344
  51.6 3.7 %collective-permute-done.15.far = bf16[1,1,256,256]{3,2,1,0:T(8,128)(2,1)S(1)} collective-permute-done((bf16[1,1,256,256]{3,2,1,0:T(8,128)(2,1)S(1)}, bf16[1,1,256,256]{3,2,1,0:T(8,128)(2,1)S(1)}, u32[]{:S(2)}, u32[]{:S(2)}) %collective-permute-start.15) | collective-permute-done | bytes 131104 | tf_op jit(solution)/shard_map/ppermute | solution.py:34
  55.2 0.7 %shard_map.124 = bf16[1,1,256,256]{3,2,1,0:T(8,128)(2,1)} custom-call(bf16[1,1,256,256]{3,2,1,0:T(8,128)(2,1)S(1)} %collective-permute-done.14.near, bf16[1,1,256,256]{3,2,1,0:T(8,128)(2,1)S(1)} %collective-permute-done.15.far), custom_call_target="tpu_custom_call" | custom-call | tf_op jit(solution)/shard_map/pallas_call | solution.py:344
  (37 shorter events, 2.7 us)
Async XLA Ops:
  0.6 1.0 %copy-start.4 = (bf16[1,1,256,256]{3,2,1,0:T(8,128)(2,1)S(1)}, bf16[1,1,256,256]{3,2,1,0:T(8,128)(2,1)}, u32[]{:S(2)}) copy-start(bf16[1,1,256,256]{3,2,1,0:T(8,128)(2,1)} %param.10) | copy-start | bytes 393220
  0.6 1.0 %copy-start.5 = (f32[1,1,256]{2,1,0:T(1,128)S(1)}, f32[1,1,256]{2,1,0:T(1,128)}, u32[]{:S(2)}) copy-start(f32[1,1,256]{2,1,0:T(1,128)} %param.13) | copy-start | bytes 3076
  0.7 5.6 %copy-start.3 = (bf16[1,1,256,256]{3,2,1,0:T(8,128)(2,1)S(1)}, bf16[1,1,256,256]{3,2,1,0:T(8,128)(2,1)}, u32[]{:S(2)}) copy-start(bf16[1,1,256,256]{3,2,1,0:T(8,128)(2,1)} %param.12) | copy-start | bytes 393220
  0.7 5.6 %collective-permute-start = (bf16[256,256]{1,0:T(8,128)(2,1)}, bf16[256,256]{1,0:T(8,128)(2,1)S(1)}, u32[]{:S(2)}, u32[]{:S(2)}) collective-permute-start(bf16[256,256]{1,0:T(8,128)(2,1)} %bitcast.31), channel_id=1, source_target_pairs={{0,28},{4,0},{8,4},{12,8},{16,12},{20,16},{24,20},{28,24},{1,29},{... | collective-permute-start | bytes 393224 | tf_op jit(solution)/shard_map/ppermute | solution.py:39
  0.7 7.0 %copy-start = (bf16[1,1,16,256,256]{4,3,2,1,0:T(8,128)(2,1)S(1)}, bf16[1,1,16,256,256]{4,3,2,1,0:T(8,128)(2,1)}, u32[]{:S(2)}) copy-start(bf16[1,1,16,256,256]{4,3,2,1,0:T(8,128)(2,1)} %param.8) | copy-start | bytes 6291460
  0.7 7.0 %copy-start.1 = (bf16[1,1,16,256,256]{4,3,2,1,0:T(8,128)(2,1)S(1)}, bf16[1,1,16,256,256]{4,3,2,1,0:T(8,128)(2,1)}, u32[]{:S(2)}) copy-start(bf16[1,1,16,256,256]{4,3,2,1,0:T(8,128)(2,1)} %param.9) | copy-start | bytes 6291460
  6.5 5.2 %collective-permute-start.1 = (bf16[256,256]{1,0:T(8,128)(2,1)S(1)}, bf16[256,256]{1,0:T(8,128)(2,1)S(1)}, u32[]{:S(2)}, u32[]{:S(2)}) collective-permute-start(bf16[256,256]{1,0:T(8,128)(2,1)S(1)} %get-tuple-element.42.yb), channel_id=1, source_target_pairs={{0,1},{1,2},{2,3},{3,0},{4,5},{5,6},{6,7},{7,4},{8,9},{9,10},{10,1... | collective-permute-start | bytes 393224 | tf_op jit(solution)/shard_map/ppermute | solution.py:39
  7.7 2.4 %copy-start.2 = (bf16[1,1,256,256]{3,2,1,0:T(8,128)(2,1)S(1)}, bf16[1,1,256,256]{3,2,1,0:T(8,128)(2,1)}, u32[]{:S(2)}) copy-start(bf16[1,1,256,256]{3,2,1,0:T(8,128)(2,1)} %param.14) | copy-start | bytes 393220
  9.0 9.2 %collective-permute-start.2 = (bf16[256,256]{1,0:T(8,128)(2,1)S(1)}, bf16[256,256]{1,0:T(8,128)(2,1)S(1)}, u32[]{:S(2)}, u32[]{:S(2)}) collective-permute-start(bf16[256,256]{1,0:T(8,128)(2,1)S(1)} %get-tuple-element.47), channel_id=1, source_target_pairs={{0,3},{1,0},{2,1},{3,2},{4,7},{5,4},{6,5},{7,6},{8,11},{9,8},{10,9... | collective-permute-start | bytes 393224 | tf_op jit(solution)/shard_map/ppermute | solution.py:39
  11.8 2.9 %collective-permute-start.4 = (f32[8,128]{1,0:T(8,128)S(1)}, f32[8,128]{1,0:T(8,128)S(1)}, u32[]{:S(2)}, u32[]{:S(2)}) collective-permute-start(f32[8,128]{1,0:T(8,128)S(1)} %shard_map.108.after), channel_id=1, source_target_pairs={{0,1},{1,0},{2,3},{3,2},{4,5},{5,4},{6,7},{7,6},{8,9},{9,8},{10,11... | collective-permute-start | bytes 12296 | tf_op jit(solution)/shard_map/ppermute | solution.py:76
  14.6 5.3 %collective-permute-start.5 = (f32[8,128]{1,0:T(8,128)S(1)}, f32[8,128]{1,0:T(8,128)S(1)}, u32[]{:S(2)}, u32[]{:S(2)}) collective-permute-start(f32[8,128]{1,0:T(8,128)S(1)} %add.6.refs_0_), channel_id=1, source_target_pairs={{0,2},{1,3},{2,0},{3,1},{4,6},{5,7},{6,4},{7,5},{8,10},{9,11},{10,... | collective-permute-start | bytes 12296 | tf_op jit(solution)/shard_map/ppermute | solution.py:76
  15.9 6.7 %collective-permute-start.6 = (bf16[256,256]{1,0:T(8,128)(2,1)S(1)}, bf16[256,256]{1,0:T(8,128)(2,1)S(1)}, u32[]{:S(2)}, u32[]{:S(2)}) collective-permute-start(bf16[256,256]{1,0:T(8,128)(2,1)S(1)} %bitcast.24), channel_id=1, source_target_pairs={{0,1},{1,2},{2,3},{3,0},{4,5},{5,6},{6,7},{7,4},{8,9},{9,10},{10,1... | collective-permute-start | bytes 393224 | tf_op jit(solution)/shard_map/ppermute | solution.py:39
  18.3 4.8 %collective-permute-start.3 = (bf16[256,256]{1,0:T(8,128)(2,1)S(1)}, bf16[256,256]{1,0:T(8,128)(2,1)S(1)}, u32[]{:S(2)}, u32[]{:S(2)}) collective-permute-start(bf16[256,256]{1,0:T(8,128)(2,1)S(1)} %get-tuple-element.48), channel_id=1, source_target_pairs={{0,1},{1,2},{2,3},{3,0},{4,5},{5,6},{6,7},{7,4},{8,9},{9,10},{10,1... | collective-permute-start | bytes 393224 | tf_op jit(solution)/shard_map/ppermute | solution.py:39
  20.1 4.8 %collective-permute-start.7 = (bf16[256,256]{1,0:T(8,128)(2,1)S(1)}, bf16[256,256]{1,0:T(8,128)(2,1)S(1)}, u32[]{:S(2)}, u32[]{:S(2)}) collective-permute-start(bf16[256,256]{1,0:T(8,128)(2,1)S(1)} %get-tuple-element.60), channel_id=1, source_target_pairs={{0,3},{1,0},{2,1},{3,2},{4,7},{5,4},{6,5},{7,6},{8,11},{9,8},{10,9... | collective-permute-start | bytes 393224 | tf_op jit(solution)/shard_map/ppermute | solution.py:39
  24.9 10.4 %collective-permute-start.8 = (bf16[256,256]{1,0:T(8,128)(2,1)S(1)}, bf16[256,256]{1,0:T(8,128)(2,1)S(1)}, u32[]{:S(2)}, u32[]{:S(2)}) collective-permute-start(bf16[256,256]{1,0:T(8,128)(2,1)S(1)} %get-tuple-element.61), channel_id=1, source_target_pairs={{0,1},{1,2},{2,3},{3,0},{4,5},{5,6},{6,7},{7,4},{8,9},{9,10},{10,1... | collective-permute-start | bytes 393224 | tf_op jit(solution)/shard_map/ppermute | solution.py:39
  26.8 4.4 %collective-permute-start.9 = (f32[8,128]{1,0:T(8,128)S(1)}, f32[8,128]{1,0:T(8,128)S(1)}, u32[]{:S(2)}, u32[]{:S(2)}) collective-permute-start(f32[8,128]{1,0:T(8,128)S(1)} %get-tuple-element.59.after), channel_id=1, source_target_pairs={{0,1},{1,0},{2,3},{3,2},{4,5},{5,4},{6,7},{7,6},{8,9},{9,8},{10,11... | collective-permute-start | bytes 12296 | tf_op jit(solution)/shard_map/ppermute | solution.py:76
  31.2 3.4 %collective-permute-start.10 = (f32[8,128]{1,0:T(8,128)S(1)}, f32[8,128]{1,0:T(8,128)S(1)}, u32[]{:S(2)}, u32[]{:S(2)}) collective-permute-start(f32[8,128]{1,0:T(8,128)S(1)} %add.7.refs_0_), channel_id=1, source_target_pairs={{0,2},{1,3},{2,0},{3,1},{4,6},{5,7},{6,4},{7,5},{8,10},{9,11},{10,... | collective-permute-start | bytes 12296 | tf_op jit(solution)/shard_map/ppermute | solution.py:76
  35.6 3.4 %collective-permute-start.13 = (f32[8,128]{1,0:T(8,128)S(1)}, f32[8,128]{1,0:T(8,128)S(1)}, u32[]{:S(2)}, u32[]{:S(2)}) collective-permute-start(f32[8,128]{1,0:T(8,128)S(1)} %shard_map.120.refs_0_), channel_id=1, source_target_pairs={{0,3},{1,2},{2,1},{3,0},{4,7},{5,6},{6,5},{7,4},{8,11},{9,10},{10,... | collective-permute-start | bytes 12296 | tf_op jit(solution)/shard_map/ppermute | solution.py:62
  36.6 2.5 %collective-permute-start.12 = (f32[8,128]{1,0:T(8,128)S(1)}, f32[8,128]{1,0:T(8,128)S(1)}, u32[]{:S(2)}, u32[]{:S(2)}) collective-permute-start(f32[8,128]{1,0:T(8,128)S(1)} %shard_map.120.refs_0_), channel_id=1, source_target_pairs={{0,2},{1,3},{2,0},{3,1},{4,6},{5,7},{6,4},{7,5},{8,10},{9,11},{10,... | collective-permute-start | bytes 12296 | tf_op jit(solution)/shard_map/ppermute | solution.py:62
  37.8 2.7 %collective-permute-start.11 = (f32[8,128]{1,0:T(8,128)S(1)}, f32[8,128]{1,0:T(8,128)S(1)}, u32[]{:S(2)}, u32[]{:S(2)}) collective-permute-start(f32[8,128]{1,0:T(8,128)S(1)} %shard_map.120.refs_0_), channel_id=1, source_target_pairs={{0,1},{1,0},{2,3},{3,2},{4,5},{5,4},{6,7},{7,6},{8,9},{9,8},{10,11... | collective-permute-start | bytes 12296 | tf_op jit(solution)/shard_map/ppermute | solution.py:62
  42.9 8.6 %collective-permute-start.14 = (bf16[1,1,256,256]{3,2,1,0:T(8,128)(2,1)S(1)}, bf16[1,1,256,256]{3,2,1,0:T(8,128)(2,1)S(1)}, u32[]{:S(2)}, u32[]{:S(2)}) collective-permute-start(bf16[1,1,256,256]{3,2,1,0:T(8,128)(2,1)S(1)} %get-tuple-element.78), channel_id=1, source_target_pairs={{0,4},{1,5},{2,6},{3,7},{4,0},{5,1},{6,2},{7,3},{8,12},{9,13},{10,... | collective-permute-start | bytes 393224 | tf_op jit(solution)/shard_map/ppermute | solution.py:34
  50.6 4.7 %collective-permute-start.15 = (bf16[1,1,256,256]{3,2,1,0:T(8,128)(2,1)S(1)}, bf16[1,1,256,256]{3,2,1,0:T(8,128)(2,1)S(1)}, u32[]{:S(2)}, u32[]{:S(2)}) collective-permute-start(bf16[1,1,256,256]{3,2,1,0:T(8,128)(2,1)S(1)} %get-tuple-element.79), channel_id=1, source_target_pairs={{0,1},{1,0},{2,3},{3,2},{4,8},{5,9},{6,10},{7,11},{8,4},{9,5},{10,... | collective-permute-start | bytes 393224 | tf_op jit(solution)/shard_map/ppermute | solution.py:34

commit v13 on v12

--- a/solution.py
+++ b/solution.py
@@ -119,10 +119,11 @@
     mask_out[...] = jnp.where((idx_r < count) & (idx_c < count), 1.0, 0.0)
 
 
-def start_kernel(scaled, behind, guess, mask, y_ref, yb_ref):
+def start_kernel(scaled, near, far, guess, mask, y_ref, yb_ref):
     size = mask.shape[-1]
     inside = lax.axis_index("seg") < lax.axis_size("seg") - 1
-    right = jnp.where(inside, behind[...], jnp.zeros_like(behind))
+    behind = jnp.where(odd_segment(), far[...], near[...])
+    right = jnp.where(inside, behind, jnp.zeros_like(behind))
     start = jnp.dot(scaled[...], right, preferred_element_type=F32) + guess[...].astype(F32)
     y = mask[...] * start * (1.0 / (1 << (size - 1).bit_length()))
     y_ref[...] = y
@@ -353,12 +354,13 @@
         )(*operands)
 
     (cover,) = call(cover_kernel, [stats], cost=COVER)
-    behind = rotate(right_piece[0, 0], "seg", -1)
+    far = swap(right_piece[0, 0], "seg", 1, "sec")
+    near = swap(right_piece[0, 0], "seg", 0, "sec")
     prec_below = rotate(prec, "sec", 1)
     (mask,) = call(mask_kernel, [matrix], sector_rows, cover)
     scaled = (left_piece[0, 0].astype(F32) * inverse_values[0]).astype(BF16)
 
-    y, yb = call(start_kernel, [matrix, narrow], scaled, behind, guess[0, 0], mask)
+    y, yb = call(start_kernel, [matrix, narrow], scaled, near, far, guess[0, 0], mask)
 
     def terms(value):
         return call(terms_kernel, [matrix, matrix], left, right, value, scratch=[inner])

time: 56.4 us -> 55.2 us (0.979)
  waiting for transfers between devices: 17.4 us -> 14.4 us
  starting transfers between devices: 21.9 us -> 23.6 us
    ppermute x2 -> x4, starting transfers between devices: 7.65 us -> 11.3 us  [swap(): return lax.ppermute(value, (axis, other), pairs)]
    ppermute x7 -> x6, waiting for transfers between devices: 5.36 us -> 2.99 us  [rotate(): lax.ppermute(value, axis, [(source, (source + steps) % count) for source...]
    ppermute x7 -> x6, starting transfers between devices: 7.97 us -> 5.63 us  [rotate(): lax.ppermute(value, axis, [(source, (source + steps) % count) for source...]
    ppermute x2 -> x4, waiting for transfers between devices: 3.93 us -> 5.29 us  [swap(): return lax.ppermute(value, (axis, other), pairs)]
    ppermute x3, waiting for transfers between devices: 2.28 us -> 1.01 us  [exchange(): parts.append(lax.ppermute(parts[0], axis, pairs))]
    ppermute x4, waiting for transfers between devices: 5.86 us -> 5.12 us  [pairwise(): parts.append(lax.ppermute(parts[0], axis, pairs))]
  transfers between devices with their start and end apart: 16 -> 17, of which waited for: 10 -> 9; matrix products, arithmetic and copies ran while one was open for 0% -> 0% of each run, Pallas kernels for 20% -> 21%
where the time goes in v13:
time: 55.2 us; the launch traced here: 54.6 us
  starting transfers between devices  23.6 us (43%)
  Pallas kernels  14.9 us (27%)
  waiting for transfers between devices  14.4 us (26%)
  between operations  1.62 us (3%)
    pallas_call x22, Pallas kernels, call(): pl.pallas_call(kernel, out_shape=outs, in_specs=in_specs or [VMEM] * len(...  14.9 us
    ppermute x4, starting transfers between devices, swap(): return lax.ppermute(value, (axis, other), pairs)  11.3 us
    ppermute x6, starting transfers between devices, rotate(): lax.ppermute(value, axis, [(source, (source + steps) % count) for source...  5.63 us
    ppermute x4, waiting for transfers between devices, swap(): return lax.ppermute(value, (axis, other), pairs)  5.29 us
    ppermute x4, waiting for transfers between devices, pairwise(): parts.append(lax.ppermute(parts[0], axis, pairs))  5.12 us
    ppermute x4, starting transfers between devices, pairwise(): parts.append(lax.ppermute(parts[0], axis, pairs))  4.01 us
    ppermute x6, waiting for transfers between devices, rotate(): lax.ppermute(value, axis, [(source, (source + steps) % count) for source...  2.99 us
    ppermute x3, starting transfers between devices, exchange(): parts.append(lax.ppermute(parts[0], axis, pairs))  2.71 us
  transfers between devices with their start and end apart: 17, of which 9 were waited for; matrix products, arithmetic and copies ran while one was open for 0% of the time, Pallas kernels for 21%

profile of v13, /device:TPU:1, one launch (start us, length us, event | category | flops | bytes accessed | tf_op | source)
XLA Modules:
  0.0 54.6 jit_solution(10673831750262765088)
XLA Ops:
  0.7 2.7 %collective-permute-start.1 = (bf16[256,256]{1,0:T(8,128)(2,1)}, bf16[256,256]{1,0:T(8,128)(2,1)S(1)}, u32[]{:S(2)}, u32[]{:S(2)}) collective-permute-start(bf16[256,256]{1,0:T(8,128)(2,1)} %bitcast.31), channel_id=1, source_target_pairs={{0,1},{1,0},{2,3},{3,2},{4,8},{5,9},{6,10},{7,11},{8,4},{9,5},{10,... | collective-permute-start | bytes 393224 | tf_op jit(solution)/shard_map/ppermute | solution.py:34
  4.7 1.8 %collective-permute-done.1.far = bf16[256,256]{1,0:T(8,128)(2,1)S(1)} collective-permute-done((bf16[256,256]{1,0:T(8,128)(2,1)}, bf16[256,256]{1,0:T(8,128)(2,1)S(1)}, u32[]{:S(2)}, u32[]{:S(2)}) %collective-permute-start.1) | collective-permute-done | bytes 131104 | tf_op jit(solution)/shard_map/ppermute | solution.py:34
  6.7 1.3 %collective-permute-start.2 = (bf16[256,256]{1,0:T(8,128)(2,1)S(1)}, bf16[256,256]{1,0:T(8,128)(2,1)S(1)}, u32[]{:S(2)}, u32[]{:S(2)}) collective-permute-start(bf16[256,256]{1,0:T(8,128)(2,1)S(1)} %get-tuple-element.42.yb), channel_id=1, source_target_pairs={{0,1},{1,2},{2,3},{3,0},{4,5},{5,6},{6,7},{7,4},{8,9},{9,10},{10,1... | collective-permute-start | bytes 393224 | tf_op jit(solution)/shard_map/ppermute | solution.py:39
  8.0 1.2 %shard_map.107 = (f32[256,256]{1,0:T(8,128)S(1)}, bf16[256,256]{1,0:T(8,128)(2,1)S(1)}) custom-call(bf16[16,256,256]{2,1,0:T(8,128)(2,1)S(1)} %bitcast.9, bf16[16,256,256]{2,1,0:T(8,128)(2,1)S(1)} %bitcast.16, bf16[256,256]{1,0:T(8,128)(2,1)S(1)} %get-tuple-element.42.yb), custom_call_target="tpu_custom_call" | custom-call | tf_op jit(solution)/shard_map/pallas_call | solution.py:345
  9.3 1.1 %collective-permute-start.3 = (bf16[256,256]{1,0:T(8,128)(2,1)S(1)}, bf16[256,256]{1,0:T(8,128)(2,1)S(1)}, u32[]{:S(2)}, u32[]{:S(2)}) collective-permute-start(bf16[256,256]{1,0:T(8,128)(2,1)S(1)} %get-tuple-element.47), channel_id=1, source_target_pairs={{0,3},{1,0},{2,1},{3,2},{4,7},{5,4},{6,5},{7,6},{8,11},{9,8},{10,9... | collective-permute-start | bytes 393224 | tf_op jit(solution)/shard_map/ppermute | solution.py:39
  10.4 1.5 %shard_map.106 = (f32[8,128]{1,0:T(8,128)S(1)}, f32[256,256]{1,0:T(8,128)S(1)}, f32[256,256]{1,0:T(8,128)S(1)}, f32[256,256]{1,0:T(8,128)S(1)}) custom-call(bf16[16,256,256]{2,1,0:T(8,128)(2,1)S(1)} %bitcast.10, bf16[16,256,256]{2,1,0:T(8,128)(2,1)S(1)} %bitcast.17, f32[256,256]{1,0:T(8,128)S(1)} %get-tuple-element.43.y.refs_2_, ...), custom_call_target="tpu_custom_call" | custom-call | tf_op jit(solution)/shard_map/pallas_call | solution.py:345
  12.4 2.7 %collective-permute-done.5 = f32[8,128]{1,0:T(8,128)S(1)} collective-permute-done((f32[8,128]{1,0:T(8,128)S(1)}, f32[8,128]{1,0:T(8,128)S(1)}, u32[]{:S(2)}, u32[]{:S(2)}) %collective-permute-start.5) | collective-permute-done | bytes 4128 | tf_op jit(solution)/shard_map/ppermute | solution.py:76
  15.2 1.0 %collective-permute-start.6 = (f32[8,128]{1,0:T(8,128)S(1)}, f32[8,128]{1,0:T(8,128)S(1)}, u32[]{:S(2)}, u32[]{:S(2)}) collective-permute-start(f32[8,128]{1,0:T(8,128)S(1)} %add.6.refs_0_), channel_id=1, source_target_pairs={{0,2},{1,3},{2,0},{3,1},{4,6},{5,7},{6,4},{7,5},{8,10},{9,11},{10,... | collective-permute-start | bytes 12296 | tf_op jit(solution)/shard_map/ppermute | solution.py:76
  16.5 1.2 %shard_map.109.up = f32[256,256]{1,0:T(8,128)S(1)} custom-call(bf16[16,256,256]{2,1,0:T(8,128)(2,1)S(1)} %bitcast.11, bf16[16,256,256]{2,1,0:T(8,128)(2,1)S(1)} %bitcast.18, bf16[256,256]{1,0:T(8,128)(2,1)S(1)} %collective-permute-done.2.below.refs_2_.y, f32[8,128]{1,0:T(8,128)S(1)} %shard_map.108.after), custom_call_target="tpu_custom_call" | custom-call | tf_op jit(solution)/shard_map/pallas_call | solution.py:345
  17.8 1.4 %collective-permute-start.4 = (bf16[256,256]{1,0:T(8,128)(2,1)S(1)}, bf16[256,256]{1,0:T(8,128)(2,1)S(1)}, u32[]{:S(2)}, u32[]{:S(2)}) collective-permute-start(bf16[256,256]{1,0:T(8,128)(2,1)S(1)} %get-tuple-element.48), channel_id=1, source_target_pairs={{0,1},{1,2},{2,3},{3,0},{4,5},{5,6},{6,7},{7,4},{8,9},{9,10},{10,1... | collective-permute-start | bytes 393224 | tf_op jit(solution)/shard_map/ppermute | solution.py:39
  19.2 1.3 %shard_map.111 = (f32[256,256]{1,0:T(8,128)S(1)}, f32[256,256]{1,0:T(8,128)S(1)}) custom-call(bf16[16,256,256]{2,1,0:T(8,128)(2,1)S(1)} %bitcast.12, bf16[16,256,256]{2,1,0:T(8,128)(2,1)S(1)} %bitcast.19, bf16[256,256]{1,0:T(8,128)(2,1)S(1)} %get-tuple-element.49.value), custom_call_target="tpu_custom_call" | custom-call | tf_op jit(solution)/shard_map/pallas_call | solution.py:345
  20.6 1.1 %collective-permute-start.8 = (bf16[256,256]{1,0:T(8,128)(2,1)S(1)}, bf16[256,256]{1,0:T(8,128)(2,1)S(1)}, u32[]{:S(2)}, u32[]{:S(2)}) collective-permute-start(bf16[256,256]{1,0:T(8,128)(2,1)S(1)} %get-tuple-element.60), channel_id=1, source_target_pairs={{0,3},{1,0},{2,1},{3,2},{4,7},{5,4},{6,5},{7,6},{8,11},{9,8},{10,9... | collective-permute-start | bytes 393224 | tf_op jit(solution)/shard_map/ppermute | solution.py:39
  22.1 0.5 collective-permute-done.4.refs_3_.g
  22.8 1.2 %shard_map.115.up = f32[256,256]{1,0:T(8,128)S(1)} custom-call(bf16[16,256,256]{2,1,0:T(8,128)(2,1)S(1)} %bitcast.13, bf16[16,256,256]{2,1,0:T(8,128)(2,1)S(1)} %bitcast.20, bf16[256,256]{1,0:T(8,128)(2,1)S(1)} %get-tuple-element.57.below.p, f32[8,128]{1,0:T(8,128)S(1)} %get-tuple-element.59.after), custom_call_target="tpu_custom_call" | custom-call | tf_op jit(solution)/shard_map/pallas_call | solution.py:345
  24.0 2.2 %collective-permute-done.8.above = bf16[256,256]{1,0:T(8,128)(2,1)S(1)} collective-permute-done((bf16[256,256]{1,0:T(8,128)(2,1)S(1)}, bf16[256,256]{1,0:T(8,128)(2,1)S(1)}, u32[]{:S(2)}, u32[]{:S(2)}) %collective-permute-start.8) | collective-permute-done | bytes 131104 | tf_op jit(solution)/shard_map/ppermute | solution.py:39
  26.7 1.8 %collective-permute-start.10 = (f32[8,128]{1,0:T(8,128)S(1)}, f32[8,128]{1,0:T(8,128)S(1)}, u32[]{:S(2)}, u32[]{:S(2)}) collective-permute-start(f32[8,128]{1,0:T(8,128)S(1)} %get-tuple-element.59.after), channel_id=1, source_target_pairs={{0,1},{1,0},{2,3},{3,2},{4,5},{5,4},{6,7},{7,6},{8,9},{9,8},{10,11... | collective-permute-start | bytes 12296 | tf_op jit(solution)/shard_map/ppermute | solution.py:76
  28.5 2.4 %collective-permute-done.10 = f32[8,128]{1,0:T(8,128)S(1)} collective-permute-done((f32[8,128]{1,0:T(8,128)S(1)}, f32[8,128]{1,0:T(8,128)S(1)}, u32[]{:S(2)}, u32[]{:S(2)}) %collective-permute-start.10) | collective-permute-done | bytes 4128 | tf_op jit(solution)/shard_map/ppermute | solution.py:76
  30.9 1.1 %collective-permute-start.11 = (f32[8,128]{1,0:T(8,128)S(1)}, f32[8,128]{1,0:T(8,128)S(1)}, u32[]{:S(2)}, u32[]{:S(2)}) collective-permute-start(f32[8,128]{1,0:T(8,128)S(1)} %add.7.refs_0_), channel_id=1, source_target_pairs={{0,2},{1,3},{2,0},{3,1},{4,6},{5,7},{6,4},{7,5},{8,10},{9,11},{10,... | collective-permute-start | bytes 12296 | tf_op jit(solution)/shard_map/ppermute | solution.py:76
  32.0 1.3 %shard_map.118 = (f32[256,256]{1,0:T(8,128)S(1)}, f32[256,256]{1,0:T(8,128)S(1)}) custom-call(bf16[16,256,256]{2,1,0:T(8,128)(2,1)S(1)} %bitcast.14, bf16[16,256,256]{2,1,0:T(8,128)(2,1)S(1)} %bitcast.21, bf16[256,256]{1,0:T(8,128)(2,1)S(1)} %get-tuple-element.67.value), custom_call_target="tpu_custom_call" | custom-call | tf_op jit(solution)/shard_map/pallas_call | solution.py:345
  33.2 1.3 %shard_map.117 = (f32[256,256]{1,0:T(8,128)S(1)}, f32[256,256]{1,0:T(8,128)S(1)}) custom-call(bf16[16,256,256]{2,1,0:T(8,128)(2,1)S(1)} %bitcast.15, bf16[16,256,256]{2,1,0:T(8,128)(2,1)S(1)} %bitcast.22, bf16[256,256]{1,0:T(8,128)(2,1)S(1)} %get-tuple-element.65.value), custom_call_target="tpu_custom_call" | custom-call | tf_op jit(solution)/shard_map/pallas_call | solution.py:345
  34.5 0.7 %shard_map.119 = (f32[256,256]{1,0:T(8,128)S(1)}, f32[256,256]{1,0:T(8,128)S(1)}, f32[8,128]{1,0:T(8,128)S(1)}, f32[256,256]{1,0:T(8,128)S(1)}, f32[8,128]{1,0:T(8,128)S(1)}) custom-call(f32[8,128]{1,0:T(8,128)S(1)} %add.7.refs_0_, f32[8,128]{1,0:T(8,128)S(1)} %collective-permute-done.11.refs_1_, f32[256,256]{1,0:T(8,128)S(1)} %get-tuple-element.43.y.refs_2_, ...), custom_call_target="tpu_custom_call" | custom-call | tf_op jit(solution)/shard_map/pallas_call | solution.py:345
  35.5 0.7 %collective-permute-start.14 = (f32[8,128]{1,0:T(8,128)S(1)}, f32[8,128]{1,0:T(8,128)S(1)}, u32[]{:S(2)}, u32[]{:S(2)}) collective-permute-start(f32[8,128]{1,0:T(8,128)S(1)} %shard_map.120.refs_0_), channel_id=1, source_target_pairs={{0,3},{1,2},{2,1},{3,0},{4,7},{5,6},{6,5},{7,4},{8,11},{9,10},{10,... | collective-permute-start | bytes 12296 | tf_op jit(solution)/shard_map/ppermute | solution.py:62
  36.1 0.6 %collective-permute-start.13 = (f32[8,128]{1,0:T(8,128)S(1)}, f32[8,128]{1,0:T(8,128)S(1)}, u32[]{:S(2)}, u32[]{:S(2)}) collective-permute-start(f32[8,128]{1,0:T(8,128)S(1)} %shard_map.120.refs_0_), channel_id=1, source_target_pairs={{0,2},{1,3},{2,0},{3,1},{4,6},{5,7},{6,4},{7,5},{8,10},{9,11},{10,... | collective-permute-start | bytes 12296 | tf_op jit(solution)/shard_map/ppermute | solution.py:62
  36.7 1.4 %collective-permute-start.12 = (f32[8,128]{1,0:T(8,128)S(1)}, f32[8,128]{1,0:T(8,128)S(1)}, u32[]{:S(2)}, u32[]{:S(2)}) collective-permute-start(f32[8,128]{1,0:T(8,128)S(1)} %shard_map.120.refs_0_), channel_id=1, source_target_pairs={{0,1},{1,0},{2,3},{3,2},{4,5},{5,4},{6,7},{7,6},{8,9},{9,8},{10,11... | collective-permute-start | bytes 12296 | tf_op jit(solution)/shard_map/ppermute | solution.py:62
  38.2 0.7 %collective-permute-done.14.refs_3_ = f32[8,128]{1,0:T(8,128)S(1)} collective-permute-done((f32[8,128]{1,0:T(8,128)S(1)}, f32[8,128]{1,0:T(8,128)S(1)}, u32[]{:S(2)}, u32[]{:S(2)}) %collective-permute-start.14) | collective-permute-done | bytes 4128 | tf_op jit(solution)/shard_map/ppermute | solution.py:62
  39.2 1.7 %shard_map.121 = (f32[256,256]{1,0:T(8,128)S(1)}, bf16[1,1,256,256]{3,2,1,0:T(8,128)(2,1)S(1)}) custom-call(f32[8,128]{1,0:T(8,128)S(1)} %shard_map.120.refs_0_, f32[8,128]{1,0:T(8,128)S(1)} %collective-permute-done.12.refs_1_, f32[8,128]{1,0:T(8,128)S(1)} %collective-permute-done.13.refs_2_, f32[8,128]{1,0:T(8,128)S(1)} %collective-permute-done.14.refs_3_, ...), custom_call_target="tpu_custom_call" | custom-call | tf_op jit(solution)/shard_map/pallas_call | solution.py:345
  40.8 0.7 %shard_map.122 = (f32[256,256]{1,0:T(8,128)S(1)}, bf16[1,1,256,256]{3,2,1,0:T(8,128)(2,1)S(1)}, f32[1]{0:T(128)}) custom-call(f32[8,128]{1,0:T(8,128)S(1)} %shard_map.120.refs_0_, f32[8,128]{1,0:T(8,128)S(1)} %collective-permute-done.12.refs_1_, f32[8,128]{1,0:T(8,128)S(1)} %collective-permute-done.13.refs_2_, ...), custom_call_target="tpu_custom_call", output_to_operand_aliasing={{0}: (7, {})} | custom-call | tf_op jit(solution)/shard_map/pallas_call | solution.py:345
  41.5 7.8 %collective-permute-start.15 = (bf16[1,1,256,256]{3,2,1,0:T(8,128)(2,1)S(1)}, bf16[1,1,256,256]{3,2,1,0:T(8,128)(2,1)S(1)}, u32[]{:S(2)}, u32[]{:S(2)}) collective-permute-start(bf16[1,1,256,256]{3,2,1,0:T(8,128)(2,1)S(1)} %get-tuple-element.78), channel_id=1, source_target_pairs={{0,4},{1,5},{2,6},{3,7},{4,0},{5,1},{6,2},{7,3},{8,12},{9,13},{10,... | collective-permute-start | bytes 393224 | tf_op jit(solution)/shard_map/ppermute | solution.py:34
  49.3 0.4 collective-permute-start.16
  49.8 0.7 %shard_map.123 = f32[1,1,256,256]{3,2,1,0:T(8,128)} custom-call(f32[256,256]{1,0:T(8,128)S(1)} %get-tuple-element.77.value), custom_call_target="tpu_custom_call" | custom-call | bytes 1048576 | tf_op jit(solution)/shard_map/pallas_call | solution.py:345
  50.5 3.5 %collective-permute-done.16.far = bf16[1,1,256,256]{3,2,1,0:T(8,128)(2,1)S(1)} collective-permute-done((bf16[1,1,256,256]{3,2,1,0:T(8,128)(2,1)S(1)}, bf16[1,1,256,256]{3,2,1,0:T(8,128)(2,1)S(1)}, u32[]{:S(2)}, u32[]{:S(2)}) %collective-permute-start.16) | collective-permute-done | bytes 131104 | tf_op jit(solution)/shard_map/ppermute | solution.py:34
  54.0 0.7 %shard_map.124 = bf16[1,1,256,256]{3,2,1,0:T(8,128)(2,1)} custom-call(bf16[1,1,256,256]{3,2,1,0:T(8,128)(2,1)S(1)} %collective-permute-done.15.near, bf16[1,1,256,256]{3,2,1,0:T(8,128)(2,1)S(1)} %collective-permute-done.16.far), custom_call_target="tpu_custom_call" | custom-call | tf_op jit(solution)/shard_map/pallas_call | solution.py:345
  (39 shorter events, 3.4 us)
Async XLA Ops:
  0.6 4.0 %copy-start.4 = (bf16[1,1,256,256]{3,2,1,0:T(8,128)(2,1)S(1)}, bf16[1,1,256,256]{3,2,1,0:T(8,128)(2,1)}, u32[]{:S(2)}) copy-start(bf16[1,1,256,256]{3,2,1,0:T(8,128)(2,1)} %param.10) | copy-start | bytes 393220
  0.6 4.0 %copy-start.5 = (f32[1,1,256]{2,1,0:T(1,128)S(1)}, f32[1,1,256]{2,1,0:T(1,128)}, u32[]{:S(2)}) copy-start(f32[1,1,256]{2,1,0:T(1,128)} %param.13) | copy-start | bytes 3076
  0.7 5.8 %copy-start.3 = (bf16[1,1,256,256]{3,2,1,0:T(8,128)(2,1)S(1)}, bf16[1,1,256,256]{3,2,1,0:T(8,128)(2,1)}, u32[]{:S(2)}) copy-start(bf16[1,1,256,256]{3,2,1,0:T(8,128)(2,1)} %param.12) | copy-start | bytes 393220
  0.7 5.8 %collective-permute-start.1 = (bf16[256,256]{1,0:T(8,128)(2,1)}, bf16[256,256]{1,0:T(8,128)(2,1)S(1)}, u32[]{:S(2)}, u32[]{:S(2)}) collective-permute-start(bf16[256,256]{1,0:T(8,128)(2,1)} %bitcast.31), channel_id=1, source_target_pairs={{0,1},{1,0},{2,3},{3,2},{4,8},{5,9},{6,10},{7,11},{8,4},{9,5},{10,... | collective-permute-start | bytes 393224 | tf_op jit(solution)/shard_map/ppermute | solution.py:34
  3.4 3.1 %collective-permute-start = (bf16[256,256]{1,0:T(8,128)(2,1)}, bf16[256,256]{1,0:T(8,128)(2,1)S(1)}, u32[]{:S(2)}, u32[]{:S(2)}) collective-permute-start(bf16[256,256]{1,0:T(8,128)(2,1)} %bitcast.32), channel_id=1, source_target_pairs={{0,4},{1,5},{2,6},{3,7},{4,0},{5,1},{6,2},{7,3},{8,12},{9,13},{10,... | collective-permute-start | bytes 393224 | tf_op jit(solution)/shard_map/ppermute | solution.py:34
  3.7 4.3 %copy-start = (bf16[1,1,16,256,256]{4,3,2,1,0:T(8,128)(2,1)S(1)}, bf16[1,1,16,256,256]{4,3,2,1,0:T(8,128)(2,1)}, u32[]{:S(2)}) copy-start(bf16[1,1,16,256,256]{4,3,2,1,0:T(8,128)(2,1)} %param.8) | copy-start | bytes 6291460
  3.7 4.3 %copy-start.1 = (bf16[1,1,16,256,256]{4,3,2,1,0:T(8,128)(2,1)S(1)}, bf16[1,1,16,256,256]{4,3,2,1,0:T(8,128)(2,1)}, u32[]{:S(2)}) copy-start(bf16[1,1,16,256,256]{4,3,2,1,0:T(8,128)(2,1)} %param.9) | copy-start | bytes 6291460
  6.7 5.6 %collective-permute-start.2 = (bf16[256,256]{1,0:T(8,128)(2,1)S(1)}, bf16[256,256]{1,0:T(8,128)(2,1)S(1)}, u32[]{:S(2)}, u32[]{:S(2)}) collective-permute-start(bf16[256,256]{1,0:T(8,128)(2,1)S(1)} %get-tuple-element.42.yb), channel_id=1, source_target_pairs={{0,1},{1,2},{2,3},{3,0},{4,5},{5,6},{6,7},{7,4},{8,9},{9,10},{10,1... | collective-permute-start | bytes 393224 | tf_op jit(solution)/shard_map/ppermute | solution.py:39
  8.0 2.4 %copy-start.2 = (bf16[1,1,256,256]{3,2,1,0:T(8,128)(2,1)S(1)}, bf16[1,1,256,256]{3,2,1,0:T(8,128)(2,1)}, u32[]{:S(2)}) copy-start(bf16[1,1,256,256]{3,2,1,0:T(8,128)(2,1)} %param.14) | copy-start | bytes 393220
  9.3 8.4 %collective-permute-start.3 = (bf16[256,256]{1,0:T(8,128)(2,1)S(1)}, bf16[256,256]{1,0:T(8,128)(2,1)S(1)}, u32[]{:S(2)}, u32[]{:S(2)}) collective-permute-start(bf16[256,256]{1,0:T(8,128)(2,1)S(1)} %get-tuple-element.47), channel_id=1, source_target_pairs={{0,3},{1,0},{2,1},{3,2},{4,7},{5,4},{6,5},{7,6},{8,11},{9,8},{10,9... | collective-permute-start | bytes 393224 | tf_op jit(solution)/shard_map/ppermute | solution.py:39
  12.3 2.9 %collective-permute-start.5 = (f32[8,128]{1,0:T(8,128)S(1)}, f32[8,128]{1,0:T(8,128)S(1)}, u32[]{:S(2)}, u32[]{:S(2)}) collective-permute-start(f32[8,128]{1,0:T(8,128)S(1)} %shard_map.108.after), channel_id=1, source_target_pairs={{0,1},{1,0},{2,3},{3,2},{4,5},{5,4},{6,7},{7,6},{8,9},{9,8},{10,11... | collective-permute-start | bytes 12296 | tf_op jit(solution)/shard_map/ppermute | solution.py:76
  15.2 5.3 %collective-permute-start.6 = (f32[8,128]{1,0:T(8,128)S(1)}, f32[8,128]{1,0:T(8,128)S(1)}, u32[]{:S(2)}, u32[]{:S(2)}) collective-permute-start(f32[8,128]{1,0:T(8,128)S(1)} %add.6.refs_0_), channel_id=1, source_target_pairs={{0,2},{1,3},{2,0},{3,1},{4,6},{5,7},{6,4},{7,5},{8,10},{9,11},{10,... | collective-permute-start | bytes 12296 | tf_op jit(solution)/shard_map/ppermute | solution.py:76
  16.2 5.9 %collective-permute-start.7 = (bf16[256,256]{1,0:T(8,128)(2,1)S(1)}, bf16[256,256]{1,0:T(8,128)(2,1)S(1)}, u32[]{:S(2)}, u32[]{:S(2)}) collective-permute-start(bf16[256,256]{1,0:T(8,128)(2,1)S(1)} %bitcast.24), channel_id=1, source_target_pairs={{0,1},{1,2},{2,3},{3,0},{4,5},{5,6},{6,7},{7,4},{8,9},{9,10},{10,1... | collective-permute-start | bytes 393224 | tf_op jit(solution)/shard_map/ppermute | solution.py:39
  17.8 4.8 %collective-permute-start.4 = (bf16[256,256]{1,0:T(8,128)(2,1)S(1)}, bf16[256,256]{1,0:T(8,128)(2,1)S(1)}, u32[]{:S(2)}, u32[]{:S(2)}) collective-permute-start(bf16[256,256]{1,0:T(8,128)(2,1)S(1)} %get-tuple-element.48), channel_id=1, source_target_pairs={{0,1},{1,2},{2,3},{3,0},{4,5},{5,6},{6,7},{7,4},{8,9},{9,10},{10,1... | collective-permute-start | bytes 393224 | tf_op jit(solution)/shard_map/ppermute | solution.py:39
  20.6 5.6 %collective-permute-start.8 = (bf16[256,256]{1,0:T(8,128)(2,1)S(1)}, bf16[256,256]{1,0:T(8,128)(2,1)S(1)}, u32[]{:S(2)}, u32[]{:S(2)}) collective-permute-start(bf16[256,256]{1,0:T(8,128)(2,1)S(1)} %get-tuple-element.60), channel_id=1, source_target_pairs={{0,3},{1,0},{2,1},{3,2},{4,7},{5,4},{6,5},{7,6},{8,11},{9,8},{10,9... | collective-permute-start | bytes 393224 | tf_op jit(solution)/shard_map/ppermute | solution.py:39
  26.3 8.9 %collective-permute-start.9 = (bf16[256,256]{1,0:T(8,128)(2,1)S(1)}, bf16[256,256]{1,0:T(8,128)(2,1)S(1)}, u32[]{:S(2)}, u32[]{:S(2)}) collective-permute-start(bf16[256,256]{1,0:T(8,128)(2,1)S(1)} %get-tuple-element.61), channel_id=1, source_target_pairs={{0,1},{1,2},{2,3},{3,0},{4,5},{5,6},{6,7},{7,4},{8,9},{9,10},{10,1... | collective-permute-start | bytes 393224 | tf_op jit(solution)/shard_map/ppermute | solution.py:39
  26.7 4.2 %collective-permute-start.10 = (f32[8,128]{1,0:T(8,128)S(1)}, f32[8,128]{1,0:T(8,128)S(1)}, u32[]{:S(2)}, u32[]{:S(2)}) collective-permute-start(f32[8,128]{1,0:T(8,128)S(1)} %get-tuple-element.59.after), channel_id=1, source_target_pairs={{0,1},{1,0},{2,3},{3,2},{4,5},{5,4},{6,7},{7,6},{8,9},{9,8},{10,11... | collective-permute-start | bytes 12296 | tf_op jit(solution)/shard_map/ppermute | solution.py:76
  30.9 3.6 %collective-permute-start.11 = (f32[8,128]{1,0:T(8,128)S(1)}, f32[8,128]{1,0:T(8,128)S(1)}, u32[]{:S(2)}, u32[]{:S(2)}) collective-permute-start(f32[8,128]{1,0:T(8,128)S(1)} %add.7.refs_0_), channel_id=1, source_target_pairs={{0,2},{1,3},{2,0},{3,1},{4,6},{5,7},{6,4},{7,5},{8,10},{9,11},{10,... | collective-permute-start | bytes 12296 | tf_op jit(solution)/shard_map/ppermute | solution.py:76
  35.5 3.4 %collective-permute-start.14 = (f32[8,128]{1,0:T(8,128)S(1)}, f32[8,128]{1,0:T(8,128)S(1)}, u32[]{:S(2)}, u32[]{:S(2)}) collective-permute-start(f32[8,128]{1,0:T(8,128)S(1)} %shard_map.120.refs_0_), channel_id=1, source_target_pairs={{0,3},{1,2},{2,1},{3,0},{4,7},{5,6},{6,5},{7,4},{8,11},{9,10},{10,... | collective-permute-start | bytes 12296 | tf_op jit(solution)/shard_map/ppermute | solution.py:62
  36.1 2.7 %collective-permute-start.13 = (f32[8,128]{1,0:T(8,128)S(1)}, f32[8,128]{1,0:T(8,128)S(1)}, u32[]{:S(2)}, u32[]{:S(2)}) collective-permute-start(f32[8,128]{1,0:T(8,128)S(1)} %shard_map.120.refs_0_), channel_id=1, source_target_pairs={{0,2},{1,3},{2,0},{3,1},{4,6},{5,7},{6,4},{7,5},{8,10},{9,11},{10,... | collective-permute-start | bytes 12296 | tf_op jit(solution)/shard_map/ppermute | solution.py:62
  36.7 2.5 %collective-permute-start.12 = (f32[8,128]{1,0:T(8,128)S(1)}, f32[8,128]{1,0:T(8,128)S(1)}, u32[]{:S(2)}, u32[]{:S(2)}) collective-permute-start(f32[8,128]{1,0:T(8,128)S(1)} %shard_map.120.refs_0_), channel_id=1, source_target_pairs={{0,1},{1,0},{2,3},{3,2},{4,5},{5,4},{6,7},{7,6},{8,9},{9,8},{10,11... | collective-permute-start | bytes 12296 | tf_op jit(solution)/shard_map/ppermute | solution.py:62
  41.5 9.0 %collective-permute-start.15 = (bf16[1,1,256,256]{3,2,1,0:T(8,128)(2,1)S(1)}, bf16[1,1,256,256]{3,2,1,0:T(8,128)(2,1)S(1)}, u32[]{:S(2)}, u32[]{:S(2)}) collective-permute-start(bf16[1,1,256,256]{3,2,1,0:T(8,128)(2,1)S(1)} %get-tuple-element.78), channel_id=1, source_target_pairs={{0,4},{1,5},{2,6},{3,7},{4,0},{5,1},{6,2},{7,3},{8,12},{9,13},{10,... | collective-permute-start | bytes 393224 | tf_op jit(solution)/shard_map/ppermute | solution.py:34
  49.3 4.7 %collective-permute-start.16 = (bf16[1,1,256,256]{3,2,1,0:T(8,128)(2,1)S(1)}, bf16[1,1,256,256]{3,2,1,0:T(8,128)(2,1)S(1)}, u32[]{:S(2)}, u32[]{:S(2)}) collective-permute-start(bf16[1,1,256,256]{3,2,1,0:T(8,128)(2,1)S(1)} %get-tuple-element.79), channel_id=1, source_target_pairs={{0,1},{1,0},{2,3},{3,2},{4,8},{5,9},{6,10},{7,11},{8,4},{9,5},{10,... | collective-permute-start | bytes 393224 | tf_op jit(solution)/shard_map/ppermute | solution.py:34

commit v14 on v12

--- a/solution.py
+++ b/solution.py
@@ -18,6 +18,12 @@
 SMEM = pl.BlockSpec(memory_space=pltpu.SMEM)
 SHORT = pl.CostEstimate(flops=0, bytes_accessed=1 << 20, transcendentals=0)
 COVER = pl.CostEstimate(flops=10**10, bytes_accessed=1 << 24, transcendentals=0)
+
+
+def shift(value, axis, steps):
+    count = lax.axis_size(axis)
+    first, last = max(0, -steps), min(count, count - steps)
+    return lax.ppermute(value, axis, [(source, source + steps) for source in range(first, last)])
 
 
 def swap(value, axis, first, other):
@@ -121,9 +127,7 @@
 
 def start_kernel(scaled, behind, guess, mask, y_ref, yb_ref):
     size = mask.shape[-1]
-    inside = lax.axis_index("seg") < lax.axis_size("seg") - 1
-    right = jnp.where(inside, behind[...], jnp.zeros_like(behind))
-    start = jnp.dot(scaled[...], right, preferred_element_type=F32) + guess[...].astype(F32)
+    start = jnp.dot(scaled[...], behind[...], preferred_element_type=F32) + guess[...].astype(F32)
     y = mask[...] * start * (1.0 / (1 << (size - 1).bit_length()))
     y_ref[...] = y
     yb_ref[...] = y.astype(BF16)
@@ -353,7 +357,7 @@
         )(*operands)
 
     (cover,) = call(cover_kernel, [stats], cost=COVER)
-    behind = rotate(right_piece[0, 0], "seg", -1)
+    behind = shift(right_piece[0, 0], "seg", -1)
     prec_below = rotate(prec, "sec", 1)
     (mask,) = call(mask_kernel, [matrix], sector_rows, cover)
     scaled = (left_piece[0, 0].astype(F32) * inverse_values[0]).astype(BF16)

time: 56.4 us -> 53.9 us (0.956)
  waiting for transfers between devices: 17.4 us -> 15.8 us
  starting transfers between devices: 21.9 us -> 20.9 us
    ppermute x0 -> x1, waiting for transfers between devices: none -> 4.52 us  [shift(): lax.ppermute(value, axis, [(source, source + steps) for source in range(f...]
    ppermute x2, starting transfers between devices: 7.65 us -> 4.91 us  [swap(): return lax.ppermute(value, (axis, other), pairs)]
    ppermute x0 -> x1, starting transfers between devices: none -> 2.06 us  [shift(): lax.ppermute(value, axis, [(source, source + steps) for source in range(f...]
    ppermute x7 -> x6, waiting for transfers between devices: 5.36 us -> 3.39 us  [rotate(): lax.ppermute(value, axis, [(source, (source + steps) % count) for source...]
    ppermute x2, waiting for transfers between devices: 3.93 us -> 1.97 us  [swap(): return lax.ppermute(value, (axis, other), pairs)]
    ppermute x7 -> x6, starting transfers between devices: 7.97 us -> 6.06 us  [rotate(): lax.ppermute(value, axis, [(source, (source + steps) % count) for source...]
    ppermute x4, starting transfers between devices: 3.52 us -> 5.2 us  [pairwise(): parts.append(lax.ppermute(parts[0], axis, pairs))]
    ppermute x3, waiting for transfers between devices: 2.28 us -> 0.99 us  [exchange(): parts.append(lax.ppermute(parts[0], axis, pairs))]
  transfers between devices with their start and end apart: 16 -> 16, of which waited for: 10 -> 9; matrix products, arithmetic and copies ran while one was open for 0% -> 0% of each run, Pallas kernels for 20% -> 21%
where the time goes in v14:
time: 53.9 us; the launch traced here: 53.4 us
  starting transfers between devices  20.9 us (39%)
  waiting for transfers between devices  15.8 us (29%)
  Pallas kernels  14.9 us (28%)
  between operations  1.65 us (3%)
    pallas_call x22, Pallas kernels, call(): pl.pallas_call(kernel, out_shape=outs, in_specs=in_specs or [VMEM] * len(...  14.9 us
    ppermute x6, starting transfers between devices, rotate(): lax.ppermute(value, axis, [(source, (source + steps) % count) for source...  6.06 us
    ppermute x4, starting transfers between devices, pairwise(): parts.append(lax.ppermute(parts[0], axis, pairs))  5.2 us
    ppermute x4, waiting for transfers between devices, pairwise(): parts.append(lax.ppermute(parts[0], axis, pairs))  4.95 us
    ppermute x2, starting transfers between devices, swap(): return lax.ppermute(value, (axis, other), pairs)  4.91 us
    ppermute x1, waiting for transfers between devices, shift(): lax.ppermute(value, axis, [(source, source + steps) for source in range(f...  4.52 us
    ppermute x6, waiting for transfers between devices, rotate(): lax.ppermute(value, axis, [(source, (source + steps) % count) for source...  3.39 us
    ppermute x3, starting transfers between devices, exchange(): parts.append(lax.ppermute(parts[0], axis, pairs))  2.71 us
  transfers between devices with their start and end apart: 16, of which 9 were waited for; matrix products, arithmetic and copies ran while one was open for 0% of the time, Pallas kernels for 21%

profile of v14, /device:TPU:1, one launch (start us, length us, event | category | flops | bytes accessed | tf_op | source)
XLA Modules:
  0.0 53.4 jit_solution(7685988344563582621)
XLA Ops:
  0.7 2.1 %collective-permute-start = (bf16[256,256]{1,0:T(8,128)(2,1)}, bf16[256,256]{1,0:T(8,128)(2,1)S(1)}, u32[]{:S(2)}, u32[]{:S(2)}) collective-permute-start(bf16[256,256]{1,0:T(8,128)(2,1)} %bitcast.31), channel_id=1, source_target_pairs={{4,0},{8,4},{12,8},{16,12},{20,16},{24,20},{28,24},{5,1},{9,5},{13... | collective-permute-start | bytes 393224 | tf_op jit(solution)/shard_map/ppermute | solution.py:26
  3.7 4.5 %collective-permute-done.behind = bf16[256,256]{1,0:T(8,128)(2,1)S(1)} collective-permute-done((bf16[256,256]{1,0:T(8,128)(2,1)}, bf16[256,256]{1,0:T(8,128)(2,1)S(1)}, u32[]{:S(2)}, u32[]{:S(2)}) %collective-permute-start) | collective-permute-done | bytes 131104 | tf_op jit(solution)/shard_map/ppermute | solution.py:26
  8.4 1.3 %collective-permute-start.1 = (bf16[256,256]{1,0:T(8,128)(2,1)S(1)}, bf16[256,256]{1,0:T(8,128)(2,1)S(1)}, u32[]{:S(2)}, u32[]{:S(2)}) collective-permute-start(bf16[256,256]{1,0:T(8,128)(2,1)S(1)} %get-tuple-element.42.yb), channel_id=1, source_target_pairs={{0,1},{1,2},{2,3},{3,0},{4,5},{5,6},{6,7},{7,4},{8,9},{9,10},{10,1... | collective-permute-start | bytes 393224 | tf_op jit(solution)/shard_map/ppermute | solution.py:45
  9.7 1.2 %shard_map.107 = (f32[256,256]{1,0:T(8,128)S(1)}, bf16[256,256]{1,0:T(8,128)(2,1)S(1)}) custom-call(bf16[16,256,256]{2,1,0:T(8,128)(2,1)S(1)} %bitcast.9, bf16[16,256,256]{2,1,0:T(8,128)(2,1)S(1)} %bitcast.16, bf16[256,256]{1,0:T(8,128)(2,1)S(1)} %get-tuple-element.42.yb), custom_call_target="tpu_custom_call" | custom-call | tf_op jit(solution)/shard_map/pallas_call | solution.py:348
  10.9 1.2 %collective-permute-start.2 = (bf16[256,256]{1,0:T(8,128)(2,1)S(1)}, bf16[256,256]{1,0:T(8,128)(2,1)S(1)}, u32[]{:S(2)}, u32[]{:S(2)}) collective-permute-start(bf16[256,256]{1,0:T(8,128)(2,1)S(1)} %get-tuple-element.47), channel_id=1, source_target_pairs={{0,3},{1,0},{2,1},{3,2},{4,7},{5,4},{6,5},{7,6},{8,11},{9,8},{10,9... | collective-permute-start | bytes 393224 | tf_op jit(solution)/shard_map/ppermute | solution.py:45
  12.1 1.5 %shard_map.106 = (f32[8,128]{1,0:T(8,128)S(1)}, f32[256,256]{1,0:T(8,128)S(1)}, f32[256,256]{1,0:T(8,128)S(1)}, f32[256,256]{1,0:T(8,128)S(1)}) custom-call(bf16[16,256,256]{2,1,0:T(8,128)(2,1)S(1)} %bitcast.10, bf16[16,256,256]{2,1,0:T(8,128)(2,1)S(1)} %bitcast.17, f32[256,256]{1,0:T(8,128)S(1)} %get-tuple-element.43.y.refs_2_, ...), custom_call_target="tpu_custom_call" | custom-call | tf_op jit(solution)/shard_map/pallas_call | solution.py:348
  13.9 1.2 %collective-permute-start.4 = (f32[8,128]{1,0:T(8,128)S(1)}, f32[8,128]{1,0:T(8,128)S(1)}, u32[]{:S(2)}, u32[]{:S(2)}) collective-permute-start(f32[8,128]{1,0:T(8,128)S(1)} %shard_map.108.after), channel_id=1, source_target_pairs={{0,1},{1,0},{2,3},{3,2},{4,5},{5,4},{6,7},{7,6},{8,9},{9,8},{10,11... | collective-permute-start | bytes 12296 | tf_op jit(solution)/shard_map/ppermute | solution.py:82
  15.1 1.3 %collective-permute-done.4 = f32[8,128]{1,0:T(8,128)S(1)} collective-permute-done((f32[8,128]{1,0:T(8,128)S(1)}, f32[8,128]{1,0:T(8,128)S(1)}, u32[]{:S(2)}, u32[]{:S(2)}) %collective-permute-start.4) | collective-permute-done | bytes 4128 | tf_op jit(solution)/shard_map/ppermute | solution.py:82
  16.4 1.9 %collective-permute-start.5 = (f32[8,128]{1,0:T(8,128)S(1)}, f32[8,128]{1,0:T(8,128)S(1)}, u32[]{:S(2)}, u32[]{:S(2)}) collective-permute-start(f32[8,128]{1,0:T(8,128)S(1)} %add.6.refs_0_), channel_id=1, source_target_pairs={{0,2},{1,3},{2,0},{3,1},{4,6},{5,7},{6,4},{7,5},{8,10},{9,11},{10,... | collective-permute-start | bytes 12296 | tf_op jit(solution)/shard_map/ppermute | solution.py:82
  18.3 1.2 %shard_map.109.up = f32[256,256]{1,0:T(8,128)S(1)} custom-call(bf16[16,256,256]{2,1,0:T(8,128)(2,1)S(1)} %bitcast.11, bf16[16,256,256]{2,1,0:T(8,128)(2,1)S(1)} %bitcast.18, bf16[256,256]{1,0:T(8,128)(2,1)S(1)} %collective-permute-done.1.below.refs_2_.y, f32[8,128]{1,0:T(8,128)S(1)} %shard_map.108.after), custom_call_target="tpu_custom_call" | custom-call | tf_op jit(solution)/shard_map/pallas_call | solution.py:348
  19.7 1.2 %collective-permute-start.3 = (bf16[256,256]{1,0:T(8,128)(2,1)S(1)}, bf16[256,256]{1,0:T(8,128)(2,1)S(1)}, u32[]{:S(2)}, u32[]{:S(2)}) collective-permute-start(bf16[256,256]{1,0:T(8,128)(2,1)S(1)} %get-tuple-element.48), channel_id=1, source_target_pairs={{0,1},{1,2},{2,3},{3,0},{4,5},{5,6},{6,7},{7,4},{8,9},{9,10},{10,1... | collective-permute-start | bytes 393224 | tf_op jit(solution)/shard_map/ppermute | solution.py:45
  20.8 1.3 %shard_map.111 = (f32[256,256]{1,0:T(8,128)S(1)}, f32[256,256]{1,0:T(8,128)S(1)}) custom-call(bf16[16,256,256]{2,1,0:T(8,128)(2,1)S(1)} %bitcast.12, bf16[16,256,256]{2,1,0:T(8,128)(2,1)S(1)} %bitcast.19, bf16[256,256]{1,0:T(8,128)(2,1)S(1)} %get-tuple-element.49.value), custom_call_target="tpu_custom_call" | custom-call | tf_op jit(solution)/shard_map/pallas_call | solution.py:348
  22.3 1.3 %collective-permute-start.7 = (bf16[256,256]{1,0:T(8,128)(2,1)S(1)}, bf16[256,256]{1,0:T(8,128)(2,1)S(1)}, u32[]{:S(2)}, u32[]{:S(2)}) collective-permute-start(bf16[256,256]{1,0:T(8,128)(2,1)S(1)} %get-tuple-element.60), channel_id=1, source_target_pairs={{0,3},{1,0},{2,1},{3,2},{4,7},{5,4},{6,5},{7,6},{8,11},{9,8},{10,9... | collective-permute-start | bytes 393224 | tf_op jit(solution)/shard_map/ppermute | solution.py:45
  24.0 0.7 %collective-permute-done.6.refs_4_.prec = bf16[256,256]{1,0:T(8,128)(2,1)S(1)} collective-permute-done((bf16[256,256]{1,0:T(8,128)(2,1)S(1)}, bf16[256,256]{1,0:T(8,128)(2,1)S(1)}, u32[]{:S(2)}, u32[]{:S(2)}) %collective-permute-start.6) | collective-permute-done | bytes 131104 | tf_op jit(solution)/shard_map/ppermute | solution.py:45
  24.7 2.5 %collective-permute-done.3.refs_3_.g = bf16[256,256]{1,0:T(8,128)(2,1)S(1)} collective-permute-done((bf16[256,256]{1,0:T(8,128)(2,1)S(1)}, bf16[256,256]{1,0:T(8,128)(2,1)S(1)}, u32[]{:S(2)}, u32[]{:S(2)}) %collective-permute-start.3) | collective-permute-done | bytes 131104 | tf_op jit(solution)/shard_map/ppermute | solution.py:45
  27.4 1.2 %shard_map.115.up = f32[256,256]{1,0:T(8,128)S(1)} custom-call(bf16[16,256,256]{2,1,0:T(8,128)(2,1)S(1)} %bitcast.13, bf16[16,256,256]{2,1,0:T(8,128)(2,1)S(1)} %bitcast.20, bf16[256,256]{1,0:T(8,128)(2,1)S(1)} %get-tuple-element.57.below.p, f32[8,128]{1,0:T(8,128)S(1)} %get-tuple-element.59.after), custom_call_target="tpu_custom_call" | custom-call | tf_op jit(solution)/shard_map/pallas_call | solution.py:348
  28.8 1.1 %collective-permute-start.8 = (bf16[256,256]{1,0:T(8,128)(2,1)S(1)}, bf16[256,256]{1,0:T(8,128)(2,1)S(1)}, u32[]{:S(2)}, u32[]{:S(2)}) collective-permute-start(bf16[256,256]{1,0:T(8,128)(2,1)S(1)} %get-tuple-element.61), channel_id=1, source_target_pairs={{0,1},{1,2},{2,3},{3,0},{4,5},{5,6},{6,7},{7,4},{8,9},{9,10},{10,1... | collective-permute-start | bytes 393224 | tf_op jit(solution)/shard_map/ppermute | solution.py:45
  29.8 1.2 %collective-permute-start.9 = (f32[8,128]{1,0:T(8,128)S(1)}, f32[8,128]{1,0:T(8,128)S(1)}, u32[]{:S(2)}, u32[]{:S(2)}) collective-permute-start(f32[8,128]{1,0:T(8,128)S(1)} %get-tuple-element.59.after), channel_id=1, source_target_pairs={{0,1},{1,0},{2,3},{3,2},{4,5},{5,4},{6,7},{7,6},{8,9},{9,8},{10,11... | collective-permute-start | bytes 12296 | tf_op jit(solution)/shard_map/ppermute | solution.py:82
  31.0 3.6 %collective-permute-done.9 = f32[8,128]{1,0:T(8,128)S(1)} collective-permute-done((f32[8,128]{1,0:T(8,128)S(1)}, f32[8,128]{1,0:T(8,128)S(1)}, u32[]{:S(2)}, u32[]{:S(2)}) %collective-permute-start.9) | collective-permute-done | bytes 4128 | tf_op jit(solution)/shard_map/ppermute | solution.py:82
  34.6 0.9 %collective-permute-start.10 = (f32[8,128]{1,0:T(8,128)S(1)}, f32[8,128]{1,0:T(8,128)S(1)}, u32[]{:S(2)}, u32[]{:S(2)}) collective-permute-start(f32[8,128]{1,0:T(8,128)S(1)} %add.7.refs_0_), channel_id=1, source_target_pairs={{0,2},{1,3},{2,0},{3,1},{4,6},{5,7},{6,4},{7,5},{8,10},{9,11},{10,... | collective-permute-start | bytes 12296 | tf_op jit(solution)/shard_map/ppermute | solution.py:82
  35.6 1.3 %shard_map.118 = (f32[256,256]{1,0:T(8,128)S(1)}, f32[256,256]{1,0:T(8,128)S(1)}) custom-call(bf16[16,256,256]{2,1,0:T(8,128)(2,1)S(1)} %bitcast.14, bf16[16,256,256]{2,1,0:T(8,128)(2,1)S(1)} %bitcast.21, bf16[256,256]{1,0:T(8,128)(2,1)S(1)} %get-tuple-element.67.value), custom_call_target="tpu_custom_call" | custom-call | tf_op jit(solution)/shard_map/pallas_call | solution.py:348
  36.8 1.3 %shard_map.117 = (f32[256,256]{1,0:T(8,128)S(1)}, f32[256,256]{1,0:T(8,128)S(1)}) custom-call(bf16[16,256,256]{2,1,0:T(8,128)(2,1)S(1)} %bitcast.15, bf16[16,256,256]{2,1,0:T(8,128)(2,1)S(1)} %bitcast.22, bf16[256,256]{1,0:T(8,128)(2,1)S(1)} %get-tuple-element.65.value), custom_call_target="tpu_custom_call" | custom-call | tf_op jit(solution)/shard_map/pallas_call | solution.py:348
  38.1 0.7 %shard_map.119 = (f32[256,256]{1,0:T(8,128)S(1)}, f32[256,256]{1,0:T(8,128)S(1)}, f32[8,128]{1,0:T(8,128)S(1)}, f32[256,256]{1,0:T(8,128)S(1)}, f32[8,128]{1,0:T(8,128)S(1)}) custom-call(f32[8,128]{1,0:T(8,128)S(1)} %add.7.refs_0_, f32[8,128]{1,0:T(8,128)S(1)} %collective-permute-done.10.refs_1_, f32[256,256]{1,0:T(8,128)S(1)} %get-tuple-element.43.y.refs_2_, ...), custom_call_target="tpu_custom_call" | custom-call | tf_op jit(solution)/shard_map/pallas_call | solution.py:348
  39.7 2.0 %collective-permute-start.11 = (f32[8,128]{1,0:T(8,128)S(1)}, f32[8,128]{1,0:T(8,128)S(1)}, u32[]{:S(2)}, u32[]{:S(2)}) collective-permute-start(f32[8,128]{1,0:T(8,128)S(1)} %shard_map.120.refs_0_), channel_id=1, source_target_pairs={{0,1},{1,0},{2,3},{3,2},{4,5},{5,4},{6,7},{7,6},{8,9},{9,8},{10,11... | collective-permute-start | bytes 12296 | tf_op jit(solution)/shard_map/ppermute | solution.py:68
  41.8 0.7 %collective-permute-done.13.refs_3_ = f32[8,128]{1,0:T(8,128)S(1)} collective-permute-done((f32[8,128]{1,0:T(8,128)S(1)}, f32[8,128]{1,0:T(8,128)S(1)}, u32[]{:S(2)}, u32[]{:S(2)}) %collective-permute-start.13) | collective-permute-done | bytes 4128 | tf_op jit(solution)/shard_map/ppermute | solution.py:68
  42.8 1.7 %shard_map.121 = (f32[256,256]{1,0:T(8,128)S(1)}, bf16[1,1,256,256]{3,2,1,0:T(8,128)(2,1)S(1)}) custom-call(f32[8,128]{1,0:T(8,128)S(1)} %shard_map.120.refs_0_, f32[8,128]{1,0:T(8,128)S(1)} %collective-permute-done.11.refs_1_, f32[8,128]{1,0:T(8,128)S(1)} %collective-permute-done.12.refs_2_, f32[8,128]{1,0:T(8,128)S(1)} %collective-permute-done.13.refs_3_, ...), custom_call_target="tpu_custom_call" | custom-call | tf_op jit(solution)/shard_map/pallas_call | solution.py:348
  44.4 0.7 %shard_map.122 = (f32[256,256]{1,0:T(8,128)S(1)}, bf16[1,1,256,256]{3,2,1,0:T(8,128)(2,1)S(1)}, f32[1]{0:T(128)}) custom-call(f32[8,128]{1,0:T(8,128)S(1)} %shard_map.120.refs_0_, f32[8,128]{1,0:T(8,128)S(1)} %collective-permute-done.11.refs_1_, f32[8,128]{1,0:T(8,128)S(1)} %collective-permute-done.12.refs_2_, ...), custom_call_target="tpu_custom_call", output_to_operand_aliasing={{0}: (7, {})} | custom-call | tf_op jit(solution)/shard_map/pallas_call | solution.py:348
  45.1 3.0 %collective-permute-start.14 = (bf16[1,1,256,256]{3,2,1,0:T(8,128)(2,1)S(1)}, bf16[1,1,256,256]{3,2,1,0:T(8,128)(2,1)S(1)}, u32[]{:S(2)}, u32[]{:S(2)}) collective-permute-start(bf16[1,1,256,256]{3,2,1,0:T(8,128)(2,1)S(1)} %get-tuple-element.78), channel_id=1, source_target_pairs={{0,4},{1,5},{2,6},{3,7},{4,0},{5,1},{6,2},{7,3},{8,12},{9,13},{10,... | collective-permute-start | bytes 393224 | tf_op jit(solution)/shard_map/ppermute | solution.py:40
  48.1 2.0 %collective-permute-start.15 = (bf16[1,1,256,256]{3,2,1,0:T(8,128)(2,1)S(1)}, bf16[1,1,256,256]{3,2,1,0:T(8,128)(2,1)S(1)}, u32[]{:S(2)}, u32[]{:S(2)}) collective-permute-start(bf16[1,1,256,256]{3,2,1,0:T(8,128)(2,1)S(1)} %get-tuple-element.79), channel_id=1, source_target_pairs={{0,1},{1,0},{2,3},{3,2},{4,8},{5,9},{6,10},{7,11},{8,4},{9,5},{10,... | collective-permute-start | bytes 393224 | tf_op jit(solution)/shard_map/ppermute | solution.py:40
  50.0 0.7 %shard_map.123 = f32[1,1,256,256]{3,2,1,0:T(8,128)} custom-call(f32[256,256]{1,0:T(8,128)S(1)} %get-tuple-element.77.value), custom_call_target="tpu_custom_call" | custom-call | bytes 1048576 | tf_op jit(solution)/shard_map/pallas_call | solution.py:348
  50.7 2.0 %collective-permute-done.15.far = bf16[1,1,256,256]{3,2,1,0:T(8,128)(2,1)S(1)} collective-permute-done((bf16[1,1,256,256]{3,2,1,0:T(8,128)(2,1)S(1)}, bf16[1,1,256,256]{3,2,1,0:T(8,128)(2,1)S(1)}, u32[]{:S(2)}, u32[]{:S(2)}) %collective-permute-start.15) | collective-permute-done | bytes 131104 | tf_op jit(solution)/shard_map/ppermute | solution.py:40
  52.7 0.7 %shard_map.124 = bf16[1,1,256,256]{3,2,1,0:T(8,128)(2,1)} custom-call(bf16[1,1,256,256]{3,2,1,0:T(8,128)(2,1)S(1)} %collective-permute-done.14.near, bf16[1,1,256,256]{3,2,1,0:T(8,128)(2,1)S(1)} %collective-permute-done.15.far), custom_call_target="tpu_custom_call" | custom-call | tf_op jit(solution)/shard_map/pallas_call | solution.py:348
  (37 shorter events, 2.8 us)
Async XLA Ops:
  0.6 3.0 %copy-start.4 = (bf16[1,1,256,256]{3,2,1,0:T(8,128)(2,1)S(1)}, bf16[1,1,256,256]{3,2,1,0:T(8,128)(2,1)}, u32[]{:S(2)}) copy-start(bf16[1,1,256,256]{3,2,1,0:T(8,128)(2,1)} %param.10) | copy-start | bytes 393220
  0.6 3.0 %copy-start.5 = (f32[1,1,256]{2,1,0:T(1,128)S(1)}, f32[1,1,256]{2,1,0:T(1,128)}, u32[]{:S(2)}) copy-start(f32[1,1,256]{2,1,0:T(1,128)} %param.13) | copy-start | bytes 3076
  0.7 7.6 %copy-start.3 = (bf16[1,1,256,256]{3,2,1,0:T(8,128)(2,1)S(1)}, bf16[1,1,256,256]{3,2,1,0:T(8,128)(2,1)}, u32[]{:S(2)}) copy-start(bf16[1,1,256,256]{3,2,1,0:T(8,128)(2,1)} %param.12) | copy-start | bytes 393220
  0.7 7.6 %collective-permute-start = (bf16[256,256]{1,0:T(8,128)(2,1)}, bf16[256,256]{1,0:T(8,128)(2,1)S(1)}, u32[]{:S(2)}, u32[]{:S(2)}) collective-permute-start(bf16[256,256]{1,0:T(8,128)(2,1)} %bitcast.31), channel_id=1, source_target_pairs={{4,0},{8,4},{12,8},{16,12},{20,16},{24,20},{28,24},{5,1},{9,5},{13... | collective-permute-start | bytes 393224 | tf_op jit(solution)/shard_map/ppermute | solution.py:26
  2.7 7.0 %copy-start = (bf16[1,1,16,256,256]{4,3,2,1,0:T(8,128)(2,1)S(1)}, bf16[1,1,16,256,256]{4,3,2,1,0:T(8,128)(2,1)}, u32[]{:S(2)}) copy-start(bf16[1,1,16,256,256]{4,3,2,1,0:T(8,128)(2,1)} %param.8) | copy-start | bytes 6291460
  2.7 7.0 %copy-start.1 = (bf16[1,1,16,256,256]{4,3,2,1,0:T(8,128)(2,1)S(1)}, bf16[1,1,16,256,256]{4,3,2,1,0:T(8,128)(2,1)}, u32[]{:S(2)}) copy-start(bf16[1,1,16,256,256]{4,3,2,1,0:T(8,128)(2,1)} %param.9) | copy-start | bytes 6291460
  8.4 5.4 %collective-permute-start.1 = (bf16[256,256]{1,0:T(8,128)(2,1)S(1)}, bf16[256,256]{1,0:T(8,128)(2,1)S(1)}, u32[]{:S(2)}, u32[]{:S(2)}) collective-permute-start(bf16[256,256]{1,0:T(8,128)(2,1)S(1)} %get-tuple-element.42.yb), channel_id=1, source_target_pairs={{0,1},{1,2},{2,3},{3,0},{4,5},{5,6},{6,7},{7,4},{8,9},{9,10},{10,1... | collective-permute-start | bytes 393224 | tf_op jit(solution)/shard_map/ppermute | solution.py:45
  9.7 2.4 %copy-start.2 = (bf16[1,1,256,256]{3,2,1,0:T(8,128)(2,1)S(1)}, bf16[1,1,256,256]{3,2,1,0:T(8,128)(2,1)}, u32[]{:S(2)}) copy-start(bf16[1,1,256,256]{3,2,1,0:T(8,128)(2,1)} %param.14) | copy-start | bytes 393220
  10.9 8.6 %collective-permute-start.2 = (bf16[256,256]{1,0:T(8,128)(2,1)S(1)}, bf16[256,256]{1,0:T(8,128)(2,1)S(1)}, u32[]{:S(2)}, u32[]{:S(2)}) collective-permute-start(bf16[256,256]{1,0:T(8,128)(2,1)S(1)} %get-tuple-element.47), channel_id=1, source_target_pairs={{0,3},{1,0},{2,1},{3,2},{4,7},{5,4},{6,5},{7,6},{8,11},{9,8},{10,9... | collective-permute-start | bytes 393224 | tf_op jit(solution)/shard_map/ppermute | solution.py:45
  13.9 2.5 %collective-permute-start.4 = (f32[8,128]{1,0:T(8,128)S(1)}, f32[8,128]{1,0:T(8,128)S(1)}, u32[]{:S(2)}, u32[]{:S(2)}) collective-permute-start(f32[8,128]{1,0:T(8,128)S(1)} %shard_map.108.after), channel_id=1, source_target_pairs={{0,1},{1,0},{2,3},{3,2},{4,5},{5,4},{6,7},{7,6},{8,9},{9,8},{10,11... | collective-permute-start | bytes 12296 | tf_op jit(solution)/shard_map/ppermute | solution.py:82
  16.4 5.7 %collective-permute-start.5 = (f32[8,128]{1,0:T(8,128)S(1)}, f32[8,128]{1,0:T(8,128)S(1)}, u32[]{:S(2)}, u32[]{:S(2)}) collective-permute-start(f32[8,128]{1,0:T(8,128)S(1)} %add.6.refs_0_), channel_id=1, source_target_pairs={{0,2},{1,3},{2,0},{3,1},{4,6},{5,7},{6,4},{7,5},{8,10},{9,11},{10,... | collective-permute-start | bytes 12296 | tf_op jit(solution)/shard_map/ppermute | solution.py:82
  18.3 6.4 %collective-permute-start.6 = (bf16[256,256]{1,0:T(8,128)(2,1)S(1)}, bf16[256,256]{1,0:T(8,128)(2,1)S(1)}, u32[]{:S(2)}, u32[]{:S(2)}) collective-permute-start(bf16[256,256]{1,0:T(8,128)(2,1)S(1)} %bitcast.24), channel_id=1, source_target_pairs={{0,1},{1,2},{2,3},{3,0},{4,5},{5,6},{6,7},{7,4},{8,9},{9,10},{10,1... | collective-permute-start | bytes 393224 | tf_op jit(solution)/shard_map/ppermute | solution.py:45
  19.7 7.5 %collective-permute-start.3 = (bf16[256,256]{1,0:T(8,128)(2,1)S(1)}, bf16[256,256]{1,0:T(8,128)(2,1)S(1)}, u32[]{:S(2)}, u32[]{:S(2)}) collective-permute-start(bf16[256,256]{1,0:T(8,128)(2,1)S(1)} %get-tuple-element.48), channel_id=1, source_target_pairs={{0,1},{1,2},{2,3},{3,0},{4,5},{5,6},{6,7},{7,4},{8,9},{9,10},{10,1... | collective-permute-start | bytes 393224 | tf_op jit(solution)/shard_map/ppermute | solution.py:45
  22.3 6.4 %collective-permute-start.7 = (bf16[256,256]{1,0:T(8,128)(2,1)S(1)}, bf16[256,256]{1,0:T(8,128)(2,1)S(1)}, u32[]{:S(2)}, u32[]{:S(2)}) collective-permute-start(bf16[256,256]{1,0:T(8,128)(2,1)S(1)} %get-tuple-element.60), channel_id=1, source_target_pairs={{0,3},{1,0},{2,1},{3,2},{4,7},{5,4},{6,5},{7,6},{8,11},{9,8},{10,9... | collective-permute-start | bytes 393224 | tf_op jit(solution)/shard_map/ppermute | solution.py:45
  28.8 10.0 %collective-permute-start.8 = (bf16[256,256]{1,0:T(8,128)(2,1)S(1)}, bf16[256,256]{1,0:T(8,128)(2,1)S(1)}, u32[]{:S(2)}, u32[]{:S(2)}) collective-permute-start(bf16[256,256]{1,0:T(8,128)(2,1)S(1)} %get-tuple-element.61), channel_id=1, source_target_pairs={{0,1},{1,2},{2,3},{3,0},{4,5},{5,6},{6,7},{7,4},{8,9},{9,10},{10,1... | collective-permute-start | bytes 393224 | tf_op jit(solution)/shard_map/ppermute | solution.py:45
  29.8 4.8 %collective-permute-start.9 = (f32[8,128]{1,0:T(8,128)S(1)}, f32[8,128]{1,0:T(8,128)S(1)}, u32[]{:S(2)}, u32[]{:S(2)}) collective-permute-start(f32[8,128]{1,0:T(8,128)S(1)} %get-tuple-element.59.after), channel_id=1, source_target_pairs={{0,1},{1,0},{2,3},{3,2},{4,5},{5,4},{6,7},{7,6},{8,9},{9,8},{10,11... | collective-permute-start | bytes 12296 | tf_op jit(solution)/shard_map/ppermute | solution.py:82
  34.6 3.5 %collective-permute-start.10 = (f32[8,128]{1,0:T(8,128)S(1)}, f32[8,128]{1,0:T(8,128)S(1)}, u32[]{:S(2)}, u32[]{:S(2)}) collective-permute-start(f32[8,128]{1,0:T(8,128)S(1)} %add.7.refs_0_), channel_id=1, source_target_pairs={{0,2},{1,3},{2,0},{3,1},{4,6},{5,7},{6,4},{7,5},{8,10},{9,11},{10,... | collective-permute-start | bytes 12296 | tf_op jit(solution)/shard_map/ppermute | solution.py:82
  39.0 3.4 %collective-permute-start.13 = (f32[8,128]{1,0:T(8,128)S(1)}, f32[8,128]{1,0:T(8,128)S(1)}, u32[]{:S(2)}, u32[]{:S(2)}) collective-permute-start(f32[8,128]{1,0:T(8,128)S(1)} %shard_map.120.refs_0_), channel_id=1, source_target_pairs={{0,3},{1,2},{2,1},{3,0},{4,7},{5,6},{6,5},{7,4},{8,11},{9,10},{10,... | collective-permute-start | bytes 12296 | tf_op jit(solution)/shard_map/ppermute | solution.py:68
  39.4 3.1 %collective-permute-start.12 = (f32[8,128]{1,0:T(8,128)S(1)}, f32[8,128]{1,0:T(8,128)S(1)}, u32[]{:S(2)}, u32[]{:S(2)}) collective-permute-start(f32[8,128]{1,0:T(8,128)S(1)} %shard_map.120.refs_0_), channel_id=1, source_target_pairs={{0,2},{1,3},{2,0},{3,1},{4,6},{5,7},{6,4},{7,5},{8,10},{9,11},{10,... | collective-permute-start | bytes 12296 | tf_op jit(solution)/shard_map/ppermute | solution.py:68
  39.7 3.0 %collective-permute-start.11 = (f32[8,128]{1,0:T(8,128)S(1)}, f32[8,128]{1,0:T(8,128)S(1)}, u32[]{:S(2)}, u32[]{:S(2)}) collective-permute-start(f32[8,128]{1,0:T(8,128)S(1)} %shard_map.120.refs_0_), channel_id=1, source_target_pairs={{0,1},{1,0},{2,3},{3,2},{4,5},{5,4},{6,7},{7,6},{8,9},{9,8},{10,11... | collective-permute-start | bytes 12296 | tf_op jit(solution)/shard_map/ppermute | solution.py:68
  45.1 5.6 %collective-permute-start.14 = (bf16[1,1,256,256]{3,2,1,0:T(8,128)(2,1)S(1)}, bf16[1,1,256,256]{3,2,1,0:T(8,128)(2,1)S(1)}, u32[]{:S(2)}, u32[]{:S(2)}) collective-permute-start(bf16[1,1,256,256]{3,2,1,0:T(8,128)(2,1)S(1)} %get-tuple-element.78), channel_id=1, source_target_pairs={{0,4},{1,5},{2,6},{3,7},{4,0},{5,1},{6,2},{7,3},{8,12},{9,13},{10,... | collective-permute-start | bytes 393224 | tf_op jit(solution)/shard_map/ppermute | solution.py:40
  48.1 4.7 %collective-permute-start.15 = (bf16[1,1,256,256]{3,2,1,0:T(8,128)(2,1)S(1)}, bf16[1,1,256,256]{3,2,1,0:T(8,128)(2,1)S(1)}, u32[]{:S(2)}, u32[]{:S(2)}) collective-permute-start(bf16[1,1,256,256]{3,2,1,0:T(8,128)(2,1)S(1)} %get-tuple-element.79), channel_id=1, source_target_pairs={{0,1},{1,0},{2,3},{3,2},{4,8},{5,9},{6,10},{7,11},{8,4},{9,5},{10,... | collective-permute-start | bytes 393224 | tf_op jit(solution)/shard_map/ppermute | solution.py:40

commit v15 on v14

--- a/solution.py
+++ b/solution.py
@@ -196,21 +196,16 @@
     up_ref[...] = from_below(sandwich(left, right, below[...], inner, WD, left.shape[0]))
 
 
-def first_low_kernel(parts, *refs):
-    low_g, low_y, low_ref, sent_ref = refs[parts:]
-    yy, yhy = scalars(refs[:parts], 2)
-    low = low_g[...] - (yhy / yy) * low_y[...]
-    low_ref[...] = low
-    sent_ref[...] = low.astype(BF16)
-
-
 def first_kernel(parts, *refs):
-    y, g, prec, diag_g, diag_y = refs[parts : parts + 5]
-    p_ref, diag_ref, stat_ref, weighted_b, shift_ref = refs[parts + 5 :]
+    y, g, prec, low_g, low_y, diag_g, diag_y = refs[parts : parts + 7]
+    p_ref, low_ref, sent_ref, diag_ref, stat_ref, weighted_b, shift_ref = refs[parts + 7 :]
     yy, yhy = scalars(refs[:parts], 2)
     a = yhy / yy
     shift_ref[...] = jnp.broadcast_to(a, shift_ref.shape)
     weights = prec[...].astype(F32)
+    low = low_g[...] - a * low_y[...]
+    low_ref[...] = low
+    sent_ref[...] = low.astype(BF16)
     p = weights * (g[...] - a * y[...])
     p_ref[...] = p
     weighted_b[...] = (weights * p).astype(BF16)
@@ -220,10 +215,11 @@
 
 
 def ritz(a, b, c):
-    lam = 0.5 * (a + c) - jnp.sqrt((0.5 * (a - c)) ** 2 + b * b)
-    u, w = c - lam, -b
-    n = jnp.sqrt(u * u + w * w)
-    return lam, u / n, w / n
+    half = 0.5 * (a - c)
+    root = jnp.sqrt(half * half + b * b)
+    u, w = root - half, -b
+    inverse = lax.rsqrt(u * u + w * w)
+    return 0.5 * (a + c) - root, u * inverse, w * inverse
 
 
 def second_kernel(parts, *refs):
@@ -231,14 +227,16 @@
     lows, diags = refs[parts + 6 : parts + 10], refs[parts + 10 : parts + 14]
     x_out, p_out, coefficients, low_ref, stat_ref = refs[parts + 14 :]
     yy, yg, yp, pp, pg, php = scalars(refs[:parts], 6)
-    a = yg / yy
-    s = yp / yy
-    qq = pp - 2.0 * s * yp + s * s * yy
-    b = (pg - s * yg) / jnp.sqrt(qq * yy)
-    c = (php - 2.0 * s * pg + s * s * yg) / qq
+    inverse_y = lax.rsqrt(yy)
+    per_y = inverse_y * inverse_y
+    a = yg * per_y
+    s = yp * per_y
+    inverse_q = lax.rsqrt(pp - 2.0 * s * yp + s * s * yy)
+    b = (pg - s * yg) * (inverse_q * inverse_y)
+    c = (php - 2.0 * s * pg + s * s * yg) * (inverse_q * inverse_q)
     lam, u, w = ritz(a, b, c)
-    along_p = w / jnp.sqrt(qq)
-    along_y = u / jnp.sqrt(yy) - along_p * s
+    along_p = w * inverse_q
+    along_y = u * inverse_y - along_p * s
     factors = [along_y, along_y * (shift_ref[0:1, 0:1] - lam), along_p, -lam * along_p]
     low_ref[...] = total([factor * term[...] for factor, term in zip(factors, lows)])
     x = along_y * y_ref[...] + along_p * p_ref[...]
@@ -272,11 +270,11 @@
 def finish(sums, x_ref, p_ref, coefficients):
     xp, pp, pg, php = sums
     a = coefficients[2:3, 0:1]
-    qq = pp - xp * xp
-    b = (pg - xp * a) / jnp.sqrt(qq)
-    c = (php - 2.0 * xp * pg + xp * xp * a) / qq
+    inverse_q = lax.rsqrt(pp - xp * xp)
+    b = (pg - xp * a) * inverse_q
+    c = (php - 2.0 * xp * pg + xp * xp * a) * (inverse_q * inverse_q)
     lam, u, w = ritz(a, b, c)
-    along_p = w / jnp.sqrt(qq)
+    along_p = w * inverse_q
     along_x = u - along_p * xp
     return lam, along_x * x_ref[...] + along_p * p_ref[...]
 
@@ -315,8 +313,8 @@
     @pl.when(jnp.logical_not(odd_segment()))
     def _():
         lam, x = finish(scalars(refs[:parts], 4), x_ref, p_ref, coefficients)
+        polarise(x, polar_out, weight_out)
         lam_out[0] = lam[0, 0]
-        polarise(x, polar_out, weight_out)
 
     @pl.when(odd_segment())
     def _():
@@ -386,17 +384,12 @@
     g, gb, pgb = joined(y_below, stat, diag, above)
     g_below = rotate(gb, "sec", 1)
     low_g, diag_g = terms(pgb)
-    low, sent = call(
-        functools.partial(first_low_kernel, len(parts)),
-        [matrix, narrow],
-        *parts, low_g, low_y,
+    p, low, sent, diag, stat, ppb, shifted = call(
+        functools.partial(first_kernel, len(parts)),
+        [matrix, matrix, narrow, matrix, stats, narrow, stats],
+        *parts, y, g, prec, low_g, low_y, diag_g, diag_y,
     )
     above = rotate(sent, "sec", -1)
-    p, diag, stat, ppb, shifted = call(
-        functools.partial(first_kernel, len(parts)),
-        [matrix, matrix, stats, narrow, stats],
-        *parts, y, g, prec, diag_g, diag_y,
-    )
     stat, p_below = call(
         functools.partial(first_cross_kernel, len(parts)),
         [stats, narrow],

time: 53.9 us -> 53.9 us (level)
    pallas_call x22 -> x21, Pallas kernels: 14.9 us -> 14.8 us  [call(): pl.pallas_call(kernel, out_shape=outs, in_specs=in_specs or [VMEM] * len(...]
where the time goes in v15:
time: 53.9 us; the launch traced here: 53.4 us
  starting transfers between devices  21.3 us (40%)
  waiting for transfers between devices  15.6 us (29%)
  Pallas kernels  14.8 us (27%)
  between operations  1.65 us (3%)
    pallas_call x21, Pallas kernels, call(): pl.pallas_call(kernel, out_shape=outs, in_specs=in_specs or [VMEM] * len(...  14.8 us
    ppermute x6, starting transfers between devices, rotate(): lax.ppermute(value, axis, [(source, (source + steps) % count) for source...  6.27 us
    ppermute x2, starting transfers between devices, swap(): return lax.ppermute(value, (axis, other), pairs)  5.25 us
    ppermute x4, starting transfers between devices, pairwise(): parts.append(lax.ppermute(parts[0], axis, pairs))  4.99 us
    ppermute x4, waiting for transfers between devices, pairwise(): parts.append(lax.ppermute(parts[0], axis, pairs))  4.73 us
    ppermute x1, waiting for transfers between devices, shift(): lax.ppermute(value, axis, [(source, source + steps) for source in range(f...  4.52 us
    ppermute x6, waiting for transfers between devices, rotate(): lax.ppermute(value, axis, [(source, (source + steps) % count) for source...  3.28 us
    ppermute x3, starting transfers between devices, exchange(): parts.append(lax.ppermute(parts[0], axis, pairs))  2.71 us
  transfers between devices with their start and end apart: 16, of which 9 were waited for; matrix products, arithmetic and copies ran while one was open for 0% of the time, Pallas kernels for 21%

profile of v15, /device:TPU:1, one launch (start us, length us, event | category | flops | bytes accessed | tf_op | source)
XLA Modules:
  0.0 53.4 jit_solution(8476543755050377899)
XLA Ops:
  0.7 2.1 %collective-permute-start = (bf16[256,256]{1,0:T(8,128)(2,1)}, bf16[256,256]{1,0:T(8,128)(2,1)S(1)}, u32[]{:S(2)}, u32[]{:S(2)}) collective-permute-start(bf16[256,256]{1,0:T(8,128)(2,1)} %bitcast.31), channel_id=1, source_target_pairs={{4,0},{8,4},{12,8},{16,12},{20,16},{24,20},{28,24},{5,1},{9,5},{13... | collective-permute-start | bytes 393224 | tf_op jit(solution)/shard_map/ppermute | solution.py:26
  3.7 4.5 %collective-permute-done.behind = bf16[256,256]{1,0:T(8,128)(2,1)S(1)} collective-permute-done((bf16[256,256]{1,0:T(8,128)(2,1)}, bf16[256,256]{1,0:T(8,128)(2,1)S(1)}, u32[]{:S(2)}, u32[]{:S(2)}) %collective-permute-start) | collective-permute-done | bytes 131104 | tf_op jit(solution)/shard_map/ppermute | solution.py:26
  8.4 1.3 %collective-permute-start.1 = (bf16[256,256]{1,0:T(8,128)(2,1)S(1)}, bf16[256,256]{1,0:T(8,128)(2,1)S(1)}, u32[]{:S(2)}, u32[]{:S(2)}) collective-permute-start(bf16[256,256]{1,0:T(8,128)(2,1)S(1)} %get-tuple-element.42.yb), channel_id=1, source_target_pairs={{0,1},{1,2},{2,3},{3,0},{4,5},{5,6},{6,7},{7,4},{8,9},{9,10},{10,1... | collective-permute-start | bytes 393224 | tf_op jit(solution)/shard_map/ppermute | solution.py:45
  9.7 1.2 %shard_map.107 = (f32[256,256]{1,0:T(8,128)S(1)}, bf16[256,256]{1,0:T(8,128)(2,1)S(1)}) custom-call(bf16[16,256,256]{2,1,0:T(8,128)(2,1)S(1)} %bitcast.9, bf16[16,256,256]{2,1,0:T(8,128)(2,1)S(1)} %bitcast.16, bf16[256,256]{1,0:T(8,128)(2,1)S(1)} %get-tuple-element.42.yb), custom_call_target="tpu_custom_call" | custom-call | tf_op jit(solution)/shard_map/pallas_call | solution.py:346
  10.9 1.2 %collective-permute-start.2 = (bf16[256,256]{1,0:T(8,128)(2,1)S(1)}, bf16[256,256]{1,0:T(8,128)(2,1)S(1)}, u32[]{:S(2)}, u32[]{:S(2)}) collective-permute-start(bf16[256,256]{1,0:T(8,128)(2,1)S(1)} %get-tuple-element.47), channel_id=1, source_target_pairs={{0,3},{1,0},{2,1},{3,2},{4,7},{5,4},{6,5},{7,6},{8,11},{9,8},{10,9... | collective-permute-start | bytes 393224 | tf_op jit(solution)/shard_map/ppermute | solution.py:45
  12.1 1.5 %shard_map.106 = (f32[8,128]{1,0:T(8,128)S(1)}, f32[256,256]{1,0:T(8,128)S(1)}, f32[256,256]{1,0:T(8,128)S(1)}, f32[256,256]{1,0:T(8,128)S(1)}) custom-call(bf16[16,256,256]{2,1,0:T(8,128)(2,1)S(1)} %bitcast.10, bf16[16,256,256]{2,1,0:T(8,128)(2,1)S(1)} %bitcast.17, f32[256,256]{1,0:T(8,128)S(1)} %get-tuple-element.43.y.refs_2_, ...), custom_call_target="tpu_custom_call" | custom-call | tf_op jit(solution)/shard_map/pallas_call | solution.py:346
  13.9 1.2 %collective-permute-start.4 = (f32[8,128]{1,0:T(8,128)S(1)}, f32[8,128]{1,0:T(8,128)S(1)}, u32[]{:S(2)}, u32[]{:S(2)}) collective-permute-start(f32[8,128]{1,0:T(8,128)S(1)} %shard_map.108.after), channel_id=1, source_target_pairs={{0,1},{1,0},{2,3},{3,2},{4,5},{5,4},{6,7},{7,6},{8,9},{9,8},{10,11... | collective-permute-start | bytes 12296 | tf_op jit(solution)/shard_map/ppermute | solution.py:82
  15.1 1.3 %collective-permute-done.4 = f32[8,128]{1,0:T(8,128)S(1)} collective-permute-done((f32[8,128]{1,0:T(8,128)S(1)}, f32[8,128]{1,0:T(8,128)S(1)}, u32[]{:S(2)}, u32[]{:S(2)}) %collective-permute-start.4) | collective-permute-done | bytes 4128 | tf_op jit(solution)/shard_map/ppermute | solution.py:82
  16.4 1.9 %collective-permute-start.5 = (f32[8,128]{1,0:T(8,128)S(1)}, f32[8,128]{1,0:T(8,128)S(1)}, u32[]{:S(2)}, u32[]{:S(2)}) collective-permute-start(f32[8,128]{1,0:T(8,128)S(1)} %add.6.refs_0_), channel_id=1, source_target_pairs={{0,2},{1,3},{2,0},{3,1},{4,6},{5,7},{6,4},{7,5},{8,10},{9,11},{10,... | collective-permute-start | bytes 12296 | tf_op jit(solution)/shard_map/ppermute | solution.py:82
  18.3 1.2 %shard_map.109.up = f32[256,256]{1,0:T(8,128)S(1)} custom-call(bf16[16,256,256]{2,1,0:T(8,128)(2,1)S(1)} %bitcast.11, bf16[16,256,256]{2,1,0:T(8,128)(2,1)S(1)} %bitcast.18, bf16[256,256]{1,0:T(8,128)(2,1)S(1)} %collective-permute-done.1.below.refs_2_.y, f32[8,128]{1,0:T(8,128)S(1)} %shard_map.108.after), custom_call_target="tpu_custom_call" | custom-call | tf_op jit(solution)/shard_map/pallas_call | solution.py:346
  19.7 1.2 %collective-permute-start.3 = (bf16[256,256]{1,0:T(8,128)(2,1)S(1)}, bf16[256,256]{1,0:T(8,128)(2,1)S(1)}, u32[]{:S(2)}, u32[]{:S(2)}) collective-permute-start(bf16[256,256]{1,0:T(8,128)(2,1)S(1)} %get-tuple-element.48), channel_id=1, source_target_pairs={{0,1},{1,2},{2,3},{3,0},{4,5},{5,6},{6,7},{7,4},{8,9},{9,10},{10,1... | collective-permute-start | bytes 393224 | tf_op jit(solution)/shard_map/ppermute | solution.py:45
  20.8 1.3 %shard_map.111 = (f32[256,256]{1,0:T(8,128)S(1)}, f32[256,256]{1,0:T(8,128)S(1)}) custom-call(bf16[16,256,256]{2,1,0:T(8,128)(2,1)S(1)} %bitcast.12, bf16[16,256,256]{2,1,0:T(8,128)(2,1)S(1)} %bitcast.19, bf16[256,256]{1,0:T(8,128)(2,1)S(1)} %get-tuple-element.50.value), custom_call_target="tpu_custom_call" | custom-call | tf_op jit(solution)/shard_map/pallas_call | solution.py:346
  22.6 1.3 %collective-permute-start.7 = (bf16[256,256]{1,0:T(8,128)(2,1)S(1)}, bf16[256,256]{1,0:T(8,128)(2,1)S(1)}, u32[]{:S(2)}, u32[]{:S(2)}) collective-permute-start(bf16[256,256]{1,0:T(8,128)(2,1)S(1)} %get-tuple-element.60), channel_id=1, source_target_pairs={{0,3},{1,0},{2,1},{3,2},{4,7},{5,4},{6,5},{7,6},{8,11},{9,8},{10,9... | collective-permute-start | bytes 393224 | tf_op jit(solution)/shard_map/ppermute | solution.py:45
  23.9 0.8 %collective-permute-done.6.refs_4_.prec = bf16[256,256]{1,0:T(8,128)(2,1)S(1)} collective-permute-done((bf16[256,256]{1,0:T(8,128)(2,1)S(1)}, bf16[256,256]{1,0:T(8,128)(2,1)S(1)}, u32[]{:S(2)}, u32[]{:S(2)}) %collective-permute-start.6) | collective-permute-done | bytes 131104 | tf_op jit(solution)/shard_map/ppermute | solution.py:45
  24.7 2.3 %collective-permute-done.3.refs_3_.g = bf16[256,256]{1,0:T(8,128)(2,1)S(1)} collective-permute-done((bf16[256,256]{1,0:T(8,128)(2,1)S(1)}, bf16[256,256]{1,0:T(8,128)(2,1)S(1)}, u32[]{:S(2)}, u32[]{:S(2)}) %collective-permute-start.3) | collective-permute-done | bytes 131104 | tf_op jit(solution)/shard_map/ppermute | solution.py:45
  27.2 1.2 %shard_map.114.up = f32[256,256]{1,0:T(8,128)S(1)} custom-call(bf16[16,256,256]{2,1,0:T(8,128)(2,1)S(1)} %bitcast.13, bf16[16,256,256]{2,1,0:T(8,128)(2,1)S(1)} %bitcast.20, bf16[256,256]{1,0:T(8,128)(2,1)S(1)} %get-tuple-element.57.below.p, f32[8,128]{1,0:T(8,128)S(1)} %get-tuple-element.59.after), custom_call_target="tpu_custom_call" | custom-call | tf_op jit(solution)/shard_map/pallas_call | solution.py:346
  28.6 1.3 %collective-permute-start.8 = (bf16[256,256]{1,0:T(8,128)(2,1)S(1)}, bf16[256,256]{1,0:T(8,128)(2,1)S(1)}, u32[]{:S(2)}, u32[]{:S(2)}) collective-permute-start(bf16[256,256]{1,0:T(8,128)(2,1)S(1)} %get-tuple-element.61), channel_id=1, source_target_pairs={{0,1},{1,2},{2,3},{3,0},{4,5},{5,6},{6,7},{7,4},{8,9},{9,10},{10,1... | collective-permute-start | bytes 393224 | tf_op jit(solution)/shard_map/ppermute | solution.py:45
  29.8 1.2 %collective-permute-start.9 = (f32[8,128]{1,0:T(8,128)S(1)}, f32[8,128]{1,0:T(8,128)S(1)}, u32[]{:S(2)}, u32[]{:S(2)}) collective-permute-start(f32[8,128]{1,0:T(8,128)S(1)} %get-tuple-element.59.after), channel_id=1, source_target_pairs={{0,1},{1,0},{2,3},{3,2},{4,5},{5,4},{6,7},{7,6},{8,9},{9,8},{10,11... | collective-permute-start | bytes 12296 | tf_op jit(solution)/shard_map/ppermute | solution.py:82
  31.0 3.4 %collective-permute-done.9 = f32[8,128]{1,0:T(8,128)S(1)} collective-permute-done((f32[8,128]{1,0:T(8,128)S(1)}, f32[8,128]{1,0:T(8,128)S(1)}, u32[]{:S(2)}, u32[]{:S(2)}) %collective-permute-start.9) | collective-permute-done | bytes 4128 | tf_op jit(solution)/shard_map/ppermute | solution.py:82
  34.4 0.7 %collective-permute-start.10 = (f32[8,128]{1,0:T(8,128)S(1)}, f32[8,128]{1,0:T(8,128)S(1)}, u32[]{:S(2)}, u32[]{:S(2)}) collective-permute-start(f32[8,128]{1,0:T(8,128)S(1)} %add.7.refs_0_), channel_id=1, source_target_pairs={{0,2},{1,3},{2,0},{3,1},{4,6},{5,7},{6,4},{7,5},{8,10},{9,11},{10,... | collective-permute-start | bytes 12296 | tf_op jit(solution)/shard_map/ppermute | solution.py:82
  35.1 1.3 %shard_map.117 = (f32[256,256]{1,0:T(8,128)S(1)}, f32[256,256]{1,0:T(8,128)S(1)}) custom-call(bf16[16,256,256]{2,1,0:T(8,128)(2,1)S(1)} %bitcast.14, bf16[16,256,256]{2,1,0:T(8,128)(2,1)S(1)} %bitcast.21, bf16[256,256]{1,0:T(8,128)(2,1)S(1)} %get-tuple-element.67.value), custom_call_target="tpu_custom_call" | custom-call | tf_op jit(solution)/shard_map/pallas_call | solution.py:346
  36.4 1.3 %shard_map.116 = (f32[256,256]{1,0:T(8,128)S(1)}, f32[256,256]{1,0:T(8,128)S(1)}) custom-call(bf16[16,256,256]{2,1,0:T(8,128)(2,1)S(1)} %bitcast.15, bf16[16,256,256]{2,1,0:T(8,128)(2,1)S(1)} %bitcast.22, bf16[256,256]{1,0:T(8,128)(2,1)S(1)} %get-tuple-element.65.value), custom_call_target="tpu_custom_call" | custom-call | tf_op jit(solution)/shard_map/pallas_call | solution.py:346
  38.6 0.8 %collective-permute-start.13 = (f32[8,128]{1,0:T(8,128)S(1)}, f32[8,128]{1,0:T(8,128)S(1)}, u32[]{:S(2)}, u32[]{:S(2)}) collective-permute-start(f32[8,128]{1,0:T(8,128)S(1)} %shard_map.119.refs_0_), channel_id=1, source_target_pairs={{0,3},{1,2},{2,1},{3,0},{4,7},{5,6},{6,5},{7,4},{8,11},{9,10},{10,... | collective-permute-start | bytes 12296 | tf_op jit(solution)/shard_map/ppermute | solution.py:68
  39.6 1.7 %collective-permute-start.11 = (f32[8,128]{1,0:T(8,128)S(1)}, f32[8,128]{1,0:T(8,128)S(1)}, u32[]{:S(2)}, u32[]{:S(2)}) collective-permute-start(f32[8,128]{1,0:T(8,128)S(1)} %shard_map.119.refs_0_), channel_id=1, source_target_pairs={{0,1},{1,0},{2,3},{3,2},{4,5},{5,4},{6,7},{7,6},{8,9},{9,8},{10,11... | collective-permute-start | bytes 12296 | tf_op jit(solution)/shard_map/ppermute | solution.py:68
  41.3 0.7 %collective-permute-done.13.refs_3_ = f32[8,128]{1,0:T(8,128)S(1)} collective-permute-done((f32[8,128]{1,0:T(8,128)S(1)}, f32[8,128]{1,0:T(8,128)S(1)}, u32[]{:S(2)}, u32[]{:S(2)}) %collective-permute-start.13) | collective-permute-done | bytes 4128 | tf_op jit(solution)/shard_map/ppermute | solution.py:68
  42.3 1.6 %shard_map.120 = (f32[256,256]{1,0:T(8,128)S(1)}, bf16[1,1,256,256]{3,2,1,0:T(8,128)(2,1)S(1)}) custom-call(f32[8,128]{1,0:T(8,128)S(1)} %shard_map.119.refs_0_, f32[8,128]{1,0:T(8,128)S(1)} %collective-permute-done.11.refs_1_, f32[8,128]{1,0:T(8,128)S(1)} %collective-permute-done.12.refs_2_, f32[8,128]{1,0:T(8,128)S(1)} %collective-permute-done.13.refs_3_, ...), custom_call_target="tpu_custom_call" | custom-call | tf_op jit(solution)/shard_map/pallas_call | solution.py:346
  44.0 0.7 %shard_map.121 = (f32[256,256]{1,0:T(8,128)S(1)}, bf16[1,1,256,256]{3,2,1,0:T(8,128)(2,1)S(1)}, f32[1]{0:T(128)}) custom-call(f32[8,128]{1,0:T(8,128)S(1)} %shard_map.119.refs_0_, f32[8,128]{1,0:T(8,128)S(1)} %collective-permute-done.11.refs_1_, f32[8,128]{1,0:T(8,128)S(1)} %collective-permute-done.12.refs_2_, ...), custom_call_target="tpu_custom_call", output_to_operand_aliasing={{0}: (7, {})} | custom-call | tf_op jit(solution)/shard_map/pallas_call | solution.py:346
  44.7 3.4 %collective-permute-start.14 = (bf16[1,1,256,256]{3,2,1,0:T(8,128)(2,1)S(1)}, bf16[1,1,256,256]{3,2,1,0:T(8,128)(2,1)S(1)}, u32[]{:S(2)}, u32[]{:S(2)}) collective-permute-start(bf16[1,1,256,256]{3,2,1,0:T(8,128)(2,1)S(1)} %get-tuple-element.78), channel_id=1, source_target_pairs={{0,4},{1,5},{2,6},{3,7},{4,0},{5,1},{6,2},{7,3},{8,12},{9,13},{10,... | collective-permute-start | bytes 393224 | tf_op jit(solution)/shard_map/ppermute | solution.py:40
  48.0 1.9 %collective-permute-start.15 = (bf16[1,1,256,256]{3,2,1,0:T(8,128)(2,1)S(1)}, bf16[1,1,256,256]{3,2,1,0:T(8,128)(2,1)S(1)}, u32[]{:S(2)}, u32[]{:S(2)}) collective-permute-start(bf16[1,1,256,256]{3,2,1,0:T(8,128)(2,1)S(1)} %get-tuple-element.79), channel_id=1, source_target_pairs={{0,1},{1,0},{2,3},{3,2},{4,8},{5,9},{6,10},{7,11},{8,4},{9,5},{10,... | collective-permute-start | bytes 393224 | tf_op jit(solution)/shard_map/ppermute | solution.py:40
  49.9 0.7 %shard_map.122 = f32[1,1,256,256]{3,2,1,0:T(8,128)} custom-call(f32[256,256]{1,0:T(8,128)S(1)} %get-tuple-element.77.value), custom_call_target="tpu_custom_call" | custom-call | bytes 1048576 | tf_op jit(solution)/shard_map/pallas_call | solution.py:346
  50.6 2.1 %collective-permute-done.15.far = bf16[1,1,256,256]{3,2,1,0:T(8,128)(2,1)S(1)} collective-permute-done((bf16[1,1,256,256]{3,2,1,0:T(8,128)(2,1)S(1)}, bf16[1,1,256,256]{3,2,1,0:T(8,128)(2,1)S(1)}, u32[]{:S(2)}, u32[]{:S(2)}) %collective-permute-start.15) | collective-permute-done | bytes 131104 | tf_op jit(solution)/shard_map/ppermute | solution.py:40
  52.7 0.7 %shard_map.123 = bf16[1,1,256,256]{3,2,1,0:T(8,128)(2,1)} custom-call(bf16[1,1,256,256]{3,2,1,0:T(8,128)(2,1)S(1)} %collective-permute-done.14.near, bf16[1,1,256,256]{3,2,1,0:T(8,128)(2,1)S(1)} %collective-permute-done.15.far), custom_call_target="tpu_custom_call" | custom-call | tf_op jit(solution)/shard_map/pallas_call | solution.py:346
  (36 shorter events, 3.0 us)
Async XLA Ops:
  0.6 3.0 %copy-start.4 = (bf16[1,1,256,256]{3,2,1,0:T(8,128)(2,1)S(1)}, bf16[1,1,256,256]{3,2,1,0:T(8,128)(2,1)}, u32[]{:S(2)}) copy-start(bf16[1,1,256,256]{3,2,1,0:T(8,128)(2,1)} %param.10) | copy-start | bytes 393220
  0.6 3.0 %copy-start.5 = (f32[1,1,256]{2,1,0:T(1,128)S(1)}, f32[1,1,256]{2,1,0:T(1,128)}, u32[]{:S(2)}) copy-start(f32[1,1,256]{2,1,0:T(1,128)} %param.13) | copy-start | bytes 3076
  0.7 7.6 %copy-start.3 = (bf16[1,1,256,256]{3,2,1,0:T(8,128)(2,1)S(1)}, bf16[1,1,256,256]{3,2,1,0:T(8,128)(2,1)}, u32[]{:S(2)}) copy-start(bf16[1,1,256,256]{3,2,1,0:T(8,128)(2,1)} %param.12) | copy-start | bytes 393220
  0.7 7.6 %collective-permute-start = (bf16[256,256]{1,0:T(8,128)(2,1)}, bf16[256,256]{1,0:T(8,128)(2,1)S(1)}, u32[]{:S(2)}, u32[]{:S(2)}) collective-permute-start(bf16[256,256]{1,0:T(8,128)(2,1)} %bitcast.31), channel_id=1, source_target_pairs={{4,0},{8,4},{12,8},{16,12},{20,16},{24,20},{28,24},{5,1},{9,5},{13... | collective-permute-start | bytes 393224 | tf_op jit(solution)/shard_map/ppermute | solution.py:26
  2.7 7.0 %copy-start = (bf16[1,1,16,256,256]{4,3,2,1,0:T(8,128)(2,1)S(1)}, bf16[1,1,16,256,256]{4,3,2,1,0:T(8,128)(2,1)}, u32[]{:S(2)}) copy-start(bf16[1,1,16,256,256]{4,3,2,1,0:T(8,128)(2,1)} %param.8) | copy-start | bytes 6291460
  2.7 7.0 %copy-start.1 = (bf16[1,1,16,256,256]{4,3,2,1,0:T(8,128)(2,1)S(1)}, bf16[1,1,16,256,256]{4,3,2,1,0:T(8,128)(2,1)}, u32[]{:S(2)}) copy-start(bf16[1,1,16,256,256]{4,3,2,1,0:T(8,128)(2,1)} %param.9) | copy-start | bytes 6291460
  8.4 5.4 %collective-permute-start.1 = (bf16[256,256]{1,0:T(8,128)(2,1)S(1)}, bf16[256,256]{1,0:T(8,128)(2,1)S(1)}, u32[]{:S(2)}, u32[]{:S(2)}) collective-permute-start(bf16[256,256]{1,0:T(8,128)(2,1)S(1)} %get-tuple-element.42.yb), channel_id=1, source_target_pairs={{0,1},{1,2},{2,3},{3,0},{4,5},{5,6},{6,7},{7,4},{8,9},{9,10},{10,1... | collective-permute-start | bytes 393224 | tf_op jit(solution)/shard_map/ppermute | solution.py:45
  9.7 2.4 %copy-start.2 = (bf16[1,1,256,256]{3,2,1,0:T(8,128)(2,1)S(1)}, bf16[1,1,256,256]{3,2,1,0:T(8,128)(2,1)}, u32[]{:S(2)}) copy-start(bf16[1,1,256,256]{3,2,1,0:T(8,128)(2,1)} %param.14) | copy-start | bytes 393220
  10.9 8.6 %collective-permute-start.2 = (bf16[256,256]{1,0:T(8,128)(2,1)S(1)}, bf16[256,256]{1,0:T(8,128)(2,1)S(1)}, u32[]{:S(2)}, u32[]{:S(2)}) collective-permute-start(bf16[256,256]{1,0:T(8,128)(2,1)S(1)} %get-tuple-element.47), channel_id=1, source_target_pairs={{0,3},{1,0},{2,1},{3,2},{4,7},{5,4},{6,5},{7,6},{8,11},{9,8},{10,9... | collective-permute-start | bytes 393224 | tf_op jit(solution)/shard_map/ppermute | solution.py:45
  13.9 2.5 %collective-permute-start.4 = (f32[8,128]{1,0:T(8,128)S(1)}, f32[8,128]{1,0:T(8,128)S(1)}, u32[]{:S(2)}, u32[]{:S(2)}) collective-permute-start(f32[8,128]{1,0:T(8,128)S(1)} %shard_map.108.after), channel_id=1, source_target_pairs={{0,1},{1,0},{2,3},{3,2},{4,5},{5,4},{6,7},{7,6},{8,9},{9,8},{10,11... | collective-permute-start | bytes 12296 | tf_op jit(solution)/shard_map/ppermute | solution.py:82
  16.4 5.7 %collective-permute-start.5 = (f32[8,128]{1,0:T(8,128)S(1)}, f32[8,128]{1,0:T(8,128)S(1)}, u32[]{:S(2)}, u32[]{:S(2)}) collective-permute-start(f32[8,128]{1,0:T(8,128)S(1)} %add.6.refs_0_), channel_id=1, source_target_pairs={{0,2},{1,3},{2,0},{3,1},{4,6},{5,7},{6,4},{7,5},{8,10},{9,11},{10,... | collective-permute-start | bytes 12296 | tf_op jit(solution)/shard_map/ppermute | solution.py:82
  18.3 6.4 %collective-permute-start.6 = (bf16[256,256]{1,0:T(8,128)(2,1)S(1)}, bf16[256,256]{1,0:T(8,128)(2,1)S(1)}, u32[]{:S(2)}, u32[]{:S(2)}) collective-permute-start(bf16[256,256]{1,0:T(8,128)(2,1)S(1)} %bitcast.24), channel_id=1, source_target_pairs={{0,1},{1,2},{2,3},{3,0},{4,5},{5,6},{6,7},{7,4},{8,9},{9,10},{10,1... | collective-permute-start | bytes 393224 | tf_op jit(solution)/shard_map/ppermute | solution.py:45
  19.7 7.3 %collective-permute-start.3 = (bf16[256,256]{1,0:T(8,128)(2,1)S(1)}, bf16[256,256]{1,0:T(8,128)(2,1)S(1)}, u32[]{:S(2)}, u32[]{:S(2)}) collective-permute-start(bf16[256,256]{1,0:T(8,128)(2,1)S(1)} %get-tuple-element.48), channel_id=1, source_target_pairs={{0,1},{1,2},{2,3},{3,0},{4,5},{5,6},{6,7},{7,4},{8,9},{9,10},{10,1... | collective-permute-start | bytes 393224 | tf_op jit(solution)/shard_map/ppermute | solution.py:45
  22.6 5.9 %collective-permute-start.7 = (bf16[256,256]{1,0:T(8,128)(2,1)S(1)}, bf16[256,256]{1,0:T(8,128)(2,1)S(1)}, u32[]{:S(2)}, u32[]{:S(2)}) collective-permute-start(bf16[256,256]{1,0:T(8,128)(2,1)S(1)} %get-tuple-element.60), channel_id=1, source_target_pairs={{0,3},{1,0},{2,1},{3,2},{4,7},{5,4},{6,5},{7,6},{8,11},{9,8},{10,9... | collective-permute-start | bytes 393224 | tf_op jit(solution)/shard_map/ppermute | solution.py:45
  28.6 9.8 %collective-permute-start.8 = (bf16[256,256]{1,0:T(8,128)(2,1)S(1)}, bf16[256,256]{1,0:T(8,128)(2,1)S(1)}, u32[]{:S(2)}, u32[]{:S(2)}) collective-permute-start(bf16[256,256]{1,0:T(8,128)(2,1)S(1)} %get-tuple-element.61), channel_id=1, source_target_pairs={{0,1},{1,2},{2,3},{3,0},{4,5},{5,6},{6,7},{7,4},{8,9},{9,10},{10,1... | collective-permute-start | bytes 393224 | tf_op jit(solution)/shard_map/ppermute | solution.py:45
  29.8 4.6 %collective-permute-start.9 = (f32[8,128]{1,0:T(8,128)S(1)}, f32[8,128]{1,0:T(8,128)S(1)}, u32[]{:S(2)}, u32[]{:S(2)}) collective-permute-start(f32[8,128]{1,0:T(8,128)S(1)} %get-tuple-element.59.after), channel_id=1, source_target_pairs={{0,1},{1,0},{2,3},{3,2},{4,5},{5,4},{6,7},{7,6},{8,9},{9,8},{10,11... | collective-permute-start | bytes 12296 | tf_op jit(solution)/shard_map/ppermute | solution.py:82
  34.4 3.3 %collective-permute-start.10 = (f32[8,128]{1,0:T(8,128)S(1)}, f32[8,128]{1,0:T(8,128)S(1)}, u32[]{:S(2)}, u32[]{:S(2)}) collective-permute-start(f32[8,128]{1,0:T(8,128)S(1)} %add.7.refs_0_), channel_id=1, source_target_pairs={{0,2},{1,3},{2,0},{3,1},{4,6},{5,7},{6,4},{7,5},{8,10},{9,11},{10,... | collective-permute-start | bytes 12296 | tf_op jit(solution)/shard_map/ppermute | solution.py:82
  38.6 3.4 %collective-permute-start.13 = (f32[8,128]{1,0:T(8,128)S(1)}, f32[8,128]{1,0:T(8,128)S(1)}, u32[]{:S(2)}, u32[]{:S(2)}) collective-permute-start(f32[8,128]{1,0:T(8,128)S(1)} %shard_map.119.refs_0_), channel_id=1, source_target_pairs={{0,3},{1,2},{2,1},{3,0},{4,7},{5,6},{6,5},{7,4},{8,11},{9,10},{10,... | collective-permute-start | bytes 12296 | tf_op jit(solution)/shard_map/ppermute | solution.py:68
  39.4 2.7 %collective-permute-start.12 = (f32[8,128]{1,0:T(8,128)S(1)}, f32[8,128]{1,0:T(8,128)S(1)}, u32[]{:S(2)}, u32[]{:S(2)}) collective-permute-start(f32[8,128]{1,0:T(8,128)S(1)} %shard_map.119.refs_0_), channel_id=1, source_target_pairs={{0,2},{1,3},{2,0},{3,1},{4,6},{5,7},{6,4},{7,5},{8,10},{9,11},{10,... | collective-permute-start | bytes 12296 | tf_op jit(solution)/shard_map/ppermute | solution.py:68
  39.6 2.7 %collective-permute-start.11 = (f32[8,128]{1,0:T(8,128)S(1)}, f32[8,128]{1,0:T(8,128)S(1)}, u32[]{:S(2)}, u32[]{:S(2)}) collective-permute-start(f32[8,128]{1,0:T(8,128)S(1)} %shard_map.119.refs_0_), channel_id=1, source_target_pairs={{0,1},{1,0},{2,3},{3,2},{4,5},{5,4},{6,7},{7,6},{8,9},{9,8},{10,11... | collective-permute-start | bytes 12296 | tf_op jit(solution)/shard_map/ppermute | solution.py:68
  44.7 6.0 %collective-permute-start.14 = (bf16[1,1,256,256]{3,2,1,0:T(8,128)(2,1)S(1)}, bf16[1,1,256,256]{3,2,1,0:T(8,128)(2,1)S(1)}, u32[]{:S(2)}, u32[]{:S(2)}) collective-permute-start(bf16[1,1,256,256]{3,2,1,0:T(8,128)(2,1)S(1)} %get-tuple-element.78), channel_id=1, source_target_pairs={{0,4},{1,5},{2,6},{3,7},{4,0},{5,1},{6,2},{7,3},{8,12},{9,13},{10,... | collective-permute-start | bytes 393224 | tf_op jit(solution)/shard_map/ppermute | solution.py:40
  48.0 4.7 %collective-permute-start.15 = (bf16[1,1,256,256]{3,2,1,0:T(8,128)(2,1)S(1)}, bf16[1,1,256,256]{3,2,1,0:T(8,128)(2,1)S(1)}, u32[]{:S(2)}, u32[]{:S(2)}) collective-permute-start(bf16[1,1,256,256]{3,2,1,0:T(8,128)(2,1)S(1)} %get-tuple-element.79), channel_id=1, source_target_pairs={{0,1},{1,0},{2,3},{3,2},{4,8},{5,9},{6,10},{7,11},{8,4},{9,5},{10,... | collective-permute-start | bytes 393224 | tf_op jit(solution)/shard_map/ppermute | solution.py:40

commit v16 on v14

--- a/solution.py
+++ b/solution.py
@@ -196,21 +196,16 @@
     up_ref[...] = from_below(sandwich(left, right, below[...], inner, WD, left.shape[0]))
 
 
-def first_low_kernel(parts, *refs):
-    low_g, low_y, low_ref, sent_ref = refs[parts:]
-    yy, yhy = scalars(refs[:parts], 2)
-    low = low_g[...] - (yhy / yy) * low_y[...]
-    low_ref[...] = low
-    sent_ref[...] = low.astype(BF16)
-
-
 def first_kernel(parts, *refs):
-    y, g, prec, diag_g, diag_y = refs[parts : parts + 5]
-    p_ref, diag_ref, stat_ref, weighted_b, shift_ref = refs[parts + 5 :]
+    y, g, prec, low_g, low_y, diag_g, diag_y = refs[parts : parts + 7]
+    p_ref, low_ref, sent_ref, diag_ref, stat_ref, weighted_b, shift_ref = refs[parts + 7 :]
     yy, yhy = scalars(refs[:parts], 2)
     a = yhy / yy
     shift_ref[...] = jnp.broadcast_to(a, shift_ref.shape)
     weights = prec[...].astype(F32)
+    low = low_g[...] - a * low_y[...]
+    low_ref[...] = low
+    sent_ref[...] = low.astype(BF16)
     p = weights * (g[...] - a * y[...])
     p_ref[...] = p
     weighted_b[...] = (weights * p).astype(BF16)
@@ -382,21 +377,16 @@
         scratch=[inner],
     )
     (stat,) = call(cross_kernel, [stats], y_below, low, stat)
-    parts = pairwise(stat, "sec")
+    parts = exchange(stat, "sec")
     g, gb, pgb = joined(y_below, stat, diag, above)
     g_below = rotate(gb, "sec", 1)
     low_g, diag_g = terms(pgb)
-    low, sent = call(
-        functools.partial(first_low_kernel, len(parts)),
-        [matrix, narrow],
-        *parts, low_g, low_y,
+    p, low, sent, diag, stat, ppb, shifted = call(
+        functools.partial(first_kernel, len(parts)),
+        [matrix, matrix, narrow, matrix, stats, narrow, stats],
+        *parts, y, g, prec, low_g, low_y, diag_g, diag_y,
     )
     above = rotate(sent, "sec", -1)
-    p, diag, stat, ppb, shifted = call(
-        functools.partial(first_kernel, len(parts)),
-        [matrix, matrix, stats, narrow, stats],
-        *parts, y, g, prec, diag_g, diag_y,
-    )
     stat, p_below = call(
         functools.partial(first_cross_kernel, len(parts)),
         [stats, narrow],

time: 53.9 us -> 52.9 us (0.981)
  waiting for transfers between devices: 15.8 us -> 14.9 us
    ppermute x4 -> x2, starting transfers between devices: 5.2 us -> 1.35 us  [pairwise(): parts.append(lax.ppermute(parts[0], axis, pairs))]
    ppermute x3 -> x6, starting transfers between devices: 2.71 us -> 5.8 us  [exchange(): parts.append(lax.ppermute(parts[0], axis, pairs))]
    ppermute x4 -> x2, waiting for transfers between devices: 4.95 us -> 3.91 us  [pairwise(): parts.append(lax.ppermute(parts[0], axis, pairs))]
    ppermute x3 -> x6, waiting for transfers between devices: 0.99 us -> 1.38 us  [exchange(): parts.append(lax.ppermute(parts[0], axis, pairs))]
    pallas_call x22 -> x21, Pallas kernels: 14.9 us -> 14.8 us  [call(): pl.pallas_call(kernel, out_shape=outs, in_specs=in_specs or [VMEM] * len(...]
  transfers between devices with their start and end apart: 16 -> 17, of which waited for: 9 -> 8; matrix products, arithmetic and copies ran while one was open for 0% -> 0% of each run, Pallas kernels for 21% -> 21%
where the time goes in v16:
time: 52.9 us; the launch traced here: 52.6 us
  starting transfers between devices  21.2 us (40%)
  waiting for transfers between devices  14.9 us (28%)
  Pallas kernels  14.8 us (28%)
  between operations  1.65 us (3%)
    pallas_call x21, Pallas kernels, call(): pl.pallas_call(kernel, out_shape=outs, in_specs=in_specs or [VMEM] * len(...  14.8 us
    ppermute x6, starting transfers between devices, rotate(): lax.ppermute(value, axis, [(source, (source + steps) % count) for source...  6.57 us
    ppermute x6, starting transfers between devices, exchange(): parts.append(lax.ppermute(parts[0], axis, pairs))  5.8 us
    ppermute x2, starting transfers between devices, swap(): return lax.ppermute(value, (axis, other), pairs)  5.41 us
    ppermute x1, waiting for transfers between devices, shift(): lax.ppermute(value, axis, [(source, source + steps) for source in range(f...  4.52 us
    ppermute x2, waiting for transfers between devices, pairwise(): parts.append(lax.ppermute(parts[0], axis, pairs))  3.91 us
    ppermute x6, waiting for transfers between devices, rotate(): lax.ppermute(value, axis, [(source, (source + steps) % count) for source...  3.14 us
    ppermute x1, starting transfers between devices, shift(): lax.ppermute(value, axis, [(source, source + steps) for source in range(f...  2.06 us
  transfers between devices with their start and end apart: 17, of which 8 were waited for; matrix products, arithmetic and copies ran while one was open for 0% of the time, Pallas kernels for 21%

profile of v16, /device:TPU:1, one launch (start us, length us, event | category | flops | bytes accessed | tf_op | source)
XLA Modules:
  0.0 52.6 jit_solution(15916534505618014401)
XLA Ops:
  0.7 2.1 %collective-permute-start = (bf16[256,256]{1,0:T(8,128)(2,1)}, bf16[256,256]{1,0:T(8,128)(2,1)S(1)}, u32[]{:S(2)}, u32[]{:S(2)}) collective-permute-start(bf16[256,256]{1,0:T(8,128)(2,1)} %bitcast.31), channel_id=1, source_target_pairs={{4,0},{8,4},{12,8},{16,12},{20,16},{24,20},{28,24},{5,1},{9,5},{13... | collective-permute-start | bytes 393224 | tf_op jit(solution)/shard_map/ppermute | solution.py:26
  3.7 4.5 %collective-permute-done.behind = bf16[256,256]{1,0:T(8,128)(2,1)S(1)} collective-permute-done((bf16[256,256]{1,0:T(8,128)(2,1)}, bf16[256,256]{1,0:T(8,128)(2,1)S(1)}, u32[]{:S(2)}, u32[]{:S(2)}) %collective-permute-start) | collective-permute-done | bytes 131104 | tf_op jit(solution)/shard_map/ppermute | solution.py:26
  8.4 1.3 %collective-permute-start.1 = (bf16[256,256]{1,0:T(8,128)(2,1)S(1)}, bf16[256,256]{1,0:T(8,128)(2,1)S(1)}, u32[]{:S(2)}, u32[]{:S(2)}) collective-permute-start(bf16[256,256]{1,0:T(8,128)(2,1)S(1)} %get-tuple-element.42.yb), channel_id=1, source_target_pairs={{0,1},{1,2},{2,3},{3,0},{4,5},{5,6},{6,7},{7,4},{8,9},{9,10},{10,1... | collective-permute-start | bytes 393224 | tf_op jit(solution)/shard_map/ppermute | solution.py:45
  9.7 1.2 %shard_map.107 = (f32[256,256]{1,0:T(8,128)S(1)}, bf16[256,256]{1,0:T(8,128)(2,1)S(1)}) custom-call(bf16[16,256,256]{2,1,0:T(8,128)(2,1)S(1)} %bitcast.9, bf16[16,256,256]{2,1,0:T(8,128)(2,1)S(1)} %bitcast.16, bf16[256,256]{1,0:T(8,128)(2,1)S(1)} %get-tuple-element.42.yb), custom_call_target="tpu_custom_call" | custom-call | tf_op jit(solution)/shard_map/pallas_call | solution.py:343
  10.9 1.2 %collective-permute-start.2 = (bf16[256,256]{1,0:T(8,128)(2,1)S(1)}, bf16[256,256]{1,0:T(8,128)(2,1)S(1)}, u32[]{:S(2)}, u32[]{:S(2)}) collective-permute-start(bf16[256,256]{1,0:T(8,128)(2,1)S(1)} %get-tuple-element.47), channel_id=1, source_target_pairs={{0,3},{1,0},{2,1},{3,2},{4,7},{5,4},{6,5},{7,6},{8,11},{9,8},{10,9... | collective-permute-start | bytes 393224 | tf_op jit(solution)/shard_map/ppermute | solution.py:45
  12.1 1.5 %shard_map.106 = (f32[8,128]{1,0:T(8,128)S(1)}, f32[256,256]{1,0:T(8,128)S(1)}, f32[256,256]{1,0:T(8,128)S(1)}, f32[256,256]{1,0:T(8,128)S(1)}) custom-call(bf16[16,256,256]{2,1,0:T(8,128)(2,1)S(1)} %bitcast.10, bf16[16,256,256]{2,1,0:T(8,128)(2,1)S(1)} %bitcast.17, f32[256,256]{1,0:T(8,128)S(1)} %get-tuple-element.43.y.refs_4_.refs_2_, ...), custom_call_target="tpu_custom_call" | custom-call | tf_op jit(solution)/shard_map/pallas_call | solution.py:343
  13.9 1.7 %collective-permute-start.6 = (f32[8,128]{1,0:T(8,128)S(1)}, f32[8,128]{1,0:T(8,128)S(1)}, u32[]{:S(2)}, u32[]{:S(2)}) collective-permute-start(f32[8,128]{1,0:T(8,128)S(1)} %shard_map.108.after.refs_0_), channel_id=1, source_target_pairs={{0,3},{1,2},{2,1},{3,0},{4,7},{5,6},{6,5},{7,4},{8,11},{9,10},{10,... | collective-permute-start | bytes 12296 | tf_op jit(solution)/shard_map/ppermute | solution.py:68
  15.6 0.7 %collective-permute-start.5 = (f32[8,128]{1,0:T(8,128)S(1)}, f32[8,128]{1,0:T(8,128)S(1)}, u32[]{:S(2)}, u32[]{:S(2)}) collective-permute-start(f32[8,128]{1,0:T(8,128)S(1)} %shard_map.108.after.refs_0_), channel_id=1, source_target_pairs={{0,2},{1,3},{2,0},{3,1},{4,6},{5,7},{6,4},{7,5},{8,10},{9,11},{10,... | collective-permute-start | bytes 12296 | tf_op jit(solution)/shard_map/ppermute | solution.py:68
  16.3 0.7 %collective-permute-start.4 = (f32[8,128]{1,0:T(8,128)S(1)}, f32[8,128]{1,0:T(8,128)S(1)}, u32[]{:S(2)}, u32[]{:S(2)}) collective-permute-start(f32[8,128]{1,0:T(8,128)S(1)} %shard_map.108.after.refs_0_), channel_id=1, source_target_pairs={{0,1},{1,0},{2,3},{3,2},{4,5},{5,4},{6,7},{7,6},{8,9},{9,8},{10,11... | collective-permute-start | bytes 12296 | tf_op jit(solution)/shard_map/ppermute | solution.py:68
  16.9 0.8 %collective-permute-start.7 = (bf16[256,256]{1,0:T(8,128)(2,1)S(1)}, bf16[256,256]{1,0:T(8,128)(2,1)S(1)}, u32[]{:S(2)}, u32[]{:S(2)}) collective-permute-start(bf16[256,256]{1,0:T(8,128)(2,1)S(1)} %bitcast.24), channel_id=1, source_target_pairs={{0,1},{1,2},{2,3},{3,0},{4,5},{5,6},{6,7},{7,4},{8,9},{9,10},{10,1... | collective-permute-start | bytes 393224 | tf_op jit(solution)/shard_map/ppermute | solution.py:45
  17.7 1.2 %shard_map.109.up = f32[256,256]{1,0:T(8,128)S(1)} custom-call(bf16[16,256,256]{2,1,0:T(8,128)(2,1)S(1)} %bitcast.11, bf16[16,256,256]{2,1,0:T(8,128)(2,1)S(1)} %bitcast.18, bf16[256,256]{1,0:T(8,128)(2,1)S(1)} %collective-permute-done.1.below.refs_4_.y, f32[8,128]{1,0:T(8,128)S(1)} %shard_map.108.after.refs_0_), custom_call_target="tpu_custom_call" | custom-call | tf_op jit(solution)/shard_map/pallas_call | solution.py:343
  19.1 1.9 %collective-permute-start.3 = (bf16[256,256]{1,0:T(8,128)(2,1)S(1)}, bf16[256,256]{1,0:T(8,128)(2,1)S(1)}, u32[]{:S(2)}, u32[]{:S(2)}) collective-permute-start(bf16[256,256]{1,0:T(8,128)(2,1)S(1)} %get-tuple-element.48), channel_id=1, source_target_pairs={{0,1},{1,2},{2,3},{3,0},{4,5},{5,6},{6,7},{7,4},{8,9},{9,10},{10,1... | collective-permute-start | bytes 393224 | tf_op jit(solution)/shard_map/ppermute | solution.py:45
  21.0 1.3 %shard_map.111 = (f32[256,256]{1,0:T(8,128)S(1)}, f32[256,256]{1,0:T(8,128)S(1)}) custom-call(bf16[16,256,256]{2,1,0:T(8,128)(2,1)S(1)} %bitcast.12, bf16[16,256,256]{2,1,0:T(8,128)(2,1)S(1)} %bitcast.19, bf16[256,256]{1,0:T(8,128)(2,1)S(1)} %get-tuple-element.50.value), custom_call_target="tpu_custom_call" | custom-call | tf_op jit(solution)/shard_map/pallas_call | solution.py:343
  23.3 1.7 %collective-permute-done.3.refs_5_.g = bf16[256,256]{1,0:T(8,128)(2,1)S(1)} collective-permute-done((bf16[256,256]{1,0:T(8,128)(2,1)S(1)}, bf16[256,256]{1,0:T(8,128)(2,1)S(1)}, u32[]{:S(2)}, u32[]{:S(2)}) %collective-permute-start.3) | collective-permute-done | bytes 131104 | tf_op jit(solution)/shard_map/ppermute | solution.py:45
  25.2 1.2 %shard_map.114.up = f32[256,256]{1,0:T(8,128)S(1)} custom-call(bf16[16,256,256]{2,1,0:T(8,128)(2,1)S(1)} %bitcast.13, bf16[16,256,256]{2,1,0:T(8,128)(2,1)S(1)} %bitcast.20, bf16[256,256]{1,0:T(8,128)(2,1)S(1)} %get-tuple-element.57.below.p, f32[8,128]{1,0:T(8,128)S(1)} %get-tuple-element.59.after), custom_call_target="tpu_custom_call" | custom-call | tf_op jit(solution)/shard_map/pallas_call | solution.py:343
  26.4 1.3 %collective-permute-done.8.above = bf16[256,256]{1,0:T(8,128)(2,1)S(1)} collective-permute-done((bf16[256,256]{1,0:T(8,128)(2,1)S(1)}, bf16[256,256]{1,0:T(8,128)(2,1)S(1)}, u32[]{:S(2)}, u32[]{:S(2)}) %collective-permute-start.8) | collective-permute-done | bytes 131104 | tf_op jit(solution)/shard_map/ppermute | solution.py:45
  27.8 0.8 %collective-permute-start.9 = (bf16[256,256]{1,0:T(8,128)(2,1)S(1)}, bf16[256,256]{1,0:T(8,128)(2,1)S(1)}, u32[]{:S(2)}, u32[]{:S(2)}) collective-permute-start(bf16[256,256]{1,0:T(8,128)(2,1)S(1)} %get-tuple-element.61), channel_id=1, source_target_pairs={{0,1},{1,2},{2,3},{3,0},{4,5},{5,6},{6,7},{7,4},{8,9},{9,10},{10,1... | collective-permute-start | bytes 393224 | tf_op jit(solution)/shard_map/ppermute | solution.py:45
  29.3 3.9 %collective-permute-done.10 = f32[8,128]{1,0:T(8,128)S(1)} collective-permute-done((f32[8,128]{1,0:T(8,128)S(1)}, f32[8,128]{1,0:T(8,128)S(1)}, u32[]{:S(2)}, u32[]{:S(2)}) %collective-permute-start.10) | collective-permute-done | bytes 4128 | tf_op jit(solution)/shard_map/ppermute | solution.py:82
  33.2 0.7 %collective-permute-start.11 = (f32[8,128]{1,0:T(8,128)S(1)}, f32[8,128]{1,0:T(8,128)S(1)}, u32[]{:S(2)}, u32[]{:S(2)}) collective-permute-start(f32[8,128]{1,0:T(8,128)S(1)} %add.3.refs_0_), channel_id=1, source_target_pairs={{0,2},{1,3},{2,0},{3,1},{4,6},{5,7},{6,4},{7,5},{8,10},{9,11},{10,... | collective-permute-start | bytes 12296 | tf_op jit(solution)/shard_map/ppermute | solution.py:82
  33.9 1.3 %shard_map.117 = (f32[256,256]{1,0:T(8,128)S(1)}, f32[256,256]{1,0:T(8,128)S(1)}) custom-call(bf16[16,256,256]{2,1,0:T(8,128)(2,1)S(1)} %bitcast.14, bf16[16,256,256]{2,1,0:T(8,128)(2,1)S(1)} %bitcast.21, bf16[256,256]{1,0:T(8,128)(2,1)S(1)} %get-tuple-element.67.value), custom_call_target="tpu_custom_call" | custom-call | tf_op jit(solution)/shard_map/pallas_call | solution.py:343
  35.2 1.3 %shard_map.116 = (f32[256,256]{1,0:T(8,128)S(1)}, f32[256,256]{1,0:T(8,128)S(1)}) custom-call(bf16[16,256,256]{2,1,0:T(8,128)(2,1)S(1)} %bitcast.15, bf16[16,256,256]{2,1,0:T(8,128)(2,1)S(1)} %bitcast.22, bf16[256,256]{1,0:T(8,128)(2,1)S(1)} %get-tuple-element.65.value), custom_call_target="tpu_custom_call" | custom-call | tf_op jit(solution)/shard_map/pallas_call | solution.py:343
  36.5 0.7 %shard_map.118 = (f32[256,256]{1,0:T(8,128)S(1)}, f32[256,256]{1,0:T(8,128)S(1)}, f32[8,128]{1,0:T(8,128)S(1)}, f32[256,256]{1,0:T(8,128)S(1)}, f32[8,128]{1,0:T(8,128)S(1)}) custom-call(f32[8,128]{1,0:T(8,128)S(1)} %add.3.refs_0_, f32[8,128]{1,0:T(8,128)S(1)} %collective-permute-done.11.refs_1_, f32[256,256]{1,0:T(8,128)S(1)} %get-tuple-element.43.y.refs_4_.refs_2_, ...), custom_call_target="tpu_custom_call" | custom-call | tf_op jit(solution)/shard_map/pallas_call | solution.py:343
  37.4 0.9 %collective-permute-start.14 = (f32[8,128]{1,0:T(8,128)S(1)}, f32[8,128]{1,0:T(8,128)S(1)}, u32[]{:S(2)}, u32[]{:S(2)}) collective-permute-start(f32[8,128]{1,0:T(8,128)S(1)} %shard_map.119.refs_0_), channel_id=1, source_target_pairs={{0,3},{1,2},{2,1},{3,0},{4,7},{5,6},{6,5},{7,4},{8,11},{9,10},{10,... | collective-permute-start | bytes 12296 | tf_op jit(solution)/shard_map/ppermute | solution.py:68
  38.3 0.7 %collective-permute-start.13 = (f32[8,128]{1,0:T(8,128)S(1)}, f32[8,128]{1,0:T(8,128)S(1)}, u32[]{:S(2)}, u32[]{:S(2)}) collective-permute-start(f32[8,128]{1,0:T(8,128)S(1)} %shard_map.119.refs_0_), channel_id=1, source_target_pairs={{0,2},{1,3},{2,0},{3,1},{4,6},{5,7},{6,4},{7,5},{8,10},{9,11},{10,... | collective-permute-start | bytes 12296 | tf_op jit(solution)/shard_map/ppermute | solution.py:68
  39.0 1.1 %collective-permute-start.12 = (f32[8,128]{1,0:T(8,128)S(1)}, f32[8,128]{1,0:T(8,128)S(1)}, u32[]{:S(2)}, u32[]{:S(2)}) collective-permute-start(f32[8,128]{1,0:T(8,128)S(1)} %shard_map.119.refs_0_), channel_id=1, source_target_pairs={{0,1},{1,0},{2,3},{3,2},{4,5},{5,4},{6,7},{7,6},{8,9},{9,8},{10,11... | collective-permute-start | bytes 12296 | tf_op jit(solution)/shard_map/ppermute | solution.py:68
  40.1 0.7 %collective-permute-done.14.refs_3_ = f32[8,128]{1,0:T(8,128)S(1)} collective-permute-done((f32[8,128]{1,0:T(8,128)S(1)}, f32[8,128]{1,0:T(8,128)S(1)}, u32[]{:S(2)}, u32[]{:S(2)}) %collective-permute-start.14) | collective-permute-done | bytes 4128 | tf_op jit(solution)/shard_map/ppermute | solution.py:68
  41.5 1.7 %shard_map.120 = (f32[256,256]{1,0:T(8,128)S(1)}, bf16[1,1,256,256]{3,2,1,0:T(8,128)(2,1)S(1)}) custom-call(f32[8,128]{1,0:T(8,128)S(1)} %shard_map.119.refs_0_, f32[8,128]{1,0:T(8,128)S(1)} %collective-permute-done.12.refs_1_, f32[8,128]{1,0:T(8,128)S(1)} %collective-permute-done.13.refs_2_, f32[8,128]{1,0:T(8,128)S(1)} %collective-permute-done.14.refs_3_, ...), custom_call_target="tpu_custom_call" | custom-call | tf_op jit(solution)/shard_map/pallas_call | solution.py:343
  43.2 0.7 %shard_map.121 = (f32[256,256]{1,0:T(8,128)S(1)}, bf16[1,1,256,256]{3,2,1,0:T(8,128)(2,1)S(1)}, f32[1]{0:T(128)}) custom-call(f32[8,128]{1,0:T(8,128)S(1)} %shard_map.119.refs_0_, f32[8,128]{1,0:T(8,128)S(1)} %collective-permute-done.12.refs_1_, f32[8,128]{1,0:T(8,128)S(1)} %collective-permute-done.13.refs_2_, ...), custom_call_target="tpu_custom_call", output_to_operand_aliasing={{0}: (7, {})} | custom-call | tf_op jit(solution)/shard_map/pallas_call | solution.py:343
  43.9 3.1 %collective-permute-start.15 = (bf16[1,1,256,256]{3,2,1,0:T(8,128)(2,1)S(1)}, bf16[1,1,256,256]{3,2,1,0:T(8,128)(2,1)S(1)}, u32[]{:S(2)}, u32[]{:S(2)}) collective-permute-start(bf16[1,1,256,256]{3,2,1,0:T(8,128)(2,1)S(1)} %get-tuple-element.78), channel_id=1, source_target_pairs={{0,4},{1,5},{2,6},{3,7},{4,0},{5,1},{6,2},{7,3},{8,12},{9,13},{10,... | collective-permute-start | bytes 393224 | tf_op jit(solution)/shard_map/ppermute | solution.py:40
  46.9 2.3 %collective-permute-start.16 = (bf16[1,1,256,256]{3,2,1,0:T(8,128)(2,1)S(1)}, bf16[1,1,256,256]{3,2,1,0:T(8,128)(2,1)S(1)}, u32[]{:S(2)}, u32[]{:S(2)}) collective-permute-start(bf16[1,1,256,256]{3,2,1,0:T(8,128)(2,1)S(1)} %get-tuple-element.79), channel_id=1, source_target_pairs={{0,1},{1,0},{2,3},{3,2},{4,8},{5,9},{6,10},{7,11},{8,4},{9,5},{10,... | collective-permute-start | bytes 393224 | tf_op jit(solution)/shard_map/ppermute | solution.py:40
  49.3 0.7 %shard_map.122 = f32[1,1,256,256]{3,2,1,0:T(8,128)} custom-call(f32[256,256]{1,0:T(8,128)S(1)} %get-tuple-element.77.value), custom_call_target="tpu_custom_call" | custom-call | bytes 1048576 | tf_op jit(solution)/shard_map/pallas_call | solution.py:343
  50.0 1.9 %collective-permute-done.16.far = bf16[1,1,256,256]{3,2,1,0:T(8,128)(2,1)S(1)} collective-permute-done((bf16[1,1,256,256]{3,2,1,0:T(8,128)(2,1)S(1)}, bf16[1,1,256,256]{3,2,1,0:T(8,128)(2,1)S(1)}, u32[]{:S(2)}, u32[]{:S(2)}) %collective-permute-start.16) | collective-permute-done | bytes 131104 | tf_op jit(solution)/shard_map/ppermute | solution.py:40
  (37 shorter events, 4.2 us)
Async XLA Ops:
  0.6 3.0 %copy-start.4 = (bf16[1,1,256,256]{3,2,1,0:T(8,128)(2,1)S(1)}, bf16[1,1,256,256]{3,2,1,0:T(8,128)(2,1)}, u32[]{:S(2)}) copy-start(bf16[1,1,256,256]{3,2,1,0:T(8,128)(2,1)} %param.10) | copy-start | bytes 393220
  0.6 3.0 %copy-start.5 = (f32[1,1,256]{2,1,0:T(1,128)S(1)}, f32[1,1,256]{2,1,0:T(1,128)}, u32[]{:S(2)}) copy-start(f32[1,1,256]{2,1,0:T(1,128)} %param.13) | copy-start | bytes 3076
  0.7 7.6 %copy-start.3 = (bf16[1,1,256,256]{3,2,1,0:T(8,128)(2,1)S(1)}, bf16[1,1,256,256]{3,2,1,0:T(8,128)(2,1)}, u32[]{:S(2)}) copy-start(bf16[1,1,256,256]{3,2,1,0:T(8,128)(2,1)} %param.12) | copy-start | bytes 393220
  0.7 7.6 %collective-permute-start = (bf16[256,256]{1,0:T(8,128)(2,1)}, bf16[256,256]{1,0:T(8,128)(2,1)S(1)}, u32[]{:S(2)}, u32[]{:S(2)}) collective-permute-start(bf16[256,256]{1,0:T(8,128)(2,1)} %bitcast.31), channel_id=1, source_target_pairs={{4,0},{8,4},{12,8},{16,12},{20,16},{24,20},{28,24},{5,1},{9,5},{13... | collective-permute-start | bytes 393224 | tf_op jit(solution)/shard_map/ppermute | solution.py:26
  2.7 7.0 %copy-start = (bf16[1,1,16,256,256]{4,3,2,1,0:T(8,128)(2,1)S(1)}, bf16[1,1,16,256,256]{4,3,2,1,0:T(8,128)(2,1)}, u32[]{:S(2)}) copy-start(bf16[1,1,16,256,256]{4,3,2,1,0:T(8,128)(2,1)} %param.8) | copy-start | bytes 6291460
  2.7 7.0 %copy-start.1 = (bf16[1,1,16,256,256]{4,3,2,1,0:T(8,128)(2,1)S(1)}, bf16[1,1,16,256,256]{4,3,2,1,0:T(8,128)(2,1)}, u32[]{:S(2)}) copy-start(bf16[1,1,16,256,256]{4,3,2,1,0:T(8,128)(2,1)} %param.9) | copy-start | bytes 6291460
  8.4 5.4 %collective-permute-start.1 = (bf16[256,256]{1,0:T(8,128)(2,1)S(1)}, bf16[256,256]{1,0:T(8,128)(2,1)S(1)}, u32[]{:S(2)}, u32[]{:S(2)}) collective-permute-start(bf16[256,256]{1,0:T(8,128)(2,1)S(1)} %get-tuple-element.42.yb), channel_id=1, source_target_pairs={{0,1},{1,2},{2,3},{3,0},{4,5},{5,6},{6,7},{7,4},{8,9},{9,10},{10,1... | collective-permute-start | bytes 393224 | tf_op jit(solution)/shard_map/ppermute | solution.py:45
  9.7 2.4 %copy-start.2 = (bf16[1,1,256,256]{3,2,1,0:T(8,128)(2,1)S(1)}, bf16[1,1,256,256]{3,2,1,0:T(8,128)(2,1)}, u32[]{:S(2)}) copy-start(bf16[1,1,256,256]{3,2,1,0:T(8,128)(2,1)} %param.14) | copy-start | bytes 393220
  10.9 8.0 %collective-permute-start.2 = (bf16[256,256]{1,0:T(8,128)(2,1)S(1)}, bf16[256,256]{1,0:T(8,128)(2,1)S(1)}, u32[]{:S(2)}, u32[]{:S(2)}) collective-permute-start(bf16[256,256]{1,0:T(8,128)(2,1)S(1)} %get-tuple-element.47), channel_id=1, source_target_pairs={{0,3},{1,0},{2,1},{3,2},{4,7},{5,4},{6,5},{7,6},{8,11},{9,8},{10,9... | collective-permute-start | bytes 393224 | tf_op jit(solution)/shard_map/ppermute | solution.py:45
  13.9 8.4 %collective-permute-start.6 = (f32[8,128]{1,0:T(8,128)S(1)}, f32[8,128]{1,0:T(8,128)S(1)}, u32[]{:S(2)}, u32[]{:S(2)}) collective-permute-start(f32[8,128]{1,0:T(8,128)S(1)} %shard_map.108.after.refs_0_), channel_id=1, source_target_pairs={{0,3},{1,2},{2,1},{3,0},{4,7},{5,6},{6,5},{7,4},{8,11},{9,10},{10,... | collective-permute-start | bytes 12296 | tf_op jit(solution)/shard_map/ppermute | solution.py:68
  15.6 6.7 %collective-permute-start.5 = (f32[8,128]{1,0:T(8,128)S(1)}, f32[8,128]{1,0:T(8,128)S(1)}, u32[]{:S(2)}, u32[]{:S(2)}) collective-permute-start(f32[8,128]{1,0:T(8,128)S(1)} %shard_map.108.after.refs_0_), channel_id=1, source_target_pairs={{0,2},{1,3},{2,0},{3,1},{4,6},{5,7},{6,4},{7,5},{8,10},{9,11},{10,... | collective-permute-start | bytes 12296 | tf_op jit(solution)/shard_map/ppermute | solution.py:68
  16.3 6.0 %collective-permute-start.4 = (f32[8,128]{1,0:T(8,128)S(1)}, f32[8,128]{1,0:T(8,128)S(1)}, u32[]{:S(2)}, u32[]{:S(2)}) collective-permute-start(f32[8,128]{1,0:T(8,128)S(1)} %shard_map.108.after.refs_0_), channel_id=1, source_target_pairs={{0,1},{1,0},{2,3},{3,2},{4,5},{5,4},{6,7},{7,6},{8,9},{9,8},{10,11... | collective-permute-start | bytes 12296 | tf_op jit(solution)/shard_map/ppermute | solution.py:68
  16.9 6.3 %collective-permute-start.7 = (bf16[256,256]{1,0:T(8,128)(2,1)S(1)}, bf16[256,256]{1,0:T(8,128)(2,1)S(1)}, u32[]{:S(2)}, u32[]{:S(2)}) collective-permute-start(bf16[256,256]{1,0:T(8,128)(2,1)S(1)} %bitcast.24), channel_id=1, source_target_pairs={{0,1},{1,2},{2,3},{3,0},{4,5},{5,6},{6,7},{7,4},{8,9},{9,10},{10,1... | collective-permute-start | bytes 393224 | tf_op jit(solution)/shard_map/ppermute | solution.py:45
  19.1 5.9 %collective-permute-start.3 = (bf16[256,256]{1,0:T(8,128)(2,1)S(1)}, bf16[256,256]{1,0:T(8,128)(2,1)S(1)}, u32[]{:S(2)}, u32[]{:S(2)}) collective-permute-start(bf16[256,256]{1,0:T(8,128)(2,1)S(1)} %get-tuple-element.48), channel_id=1, source_target_pairs={{0,1},{1,2},{2,3},{3,0},{4,5},{5,6},{6,7},{7,4},{8,9},{9,10},{10,1... | collective-permute-start | bytes 393224 | tf_op jit(solution)/shard_map/ppermute | solution.py:45
  22.7 5.0 %collective-permute-start.8 = (bf16[256,256]{1,0:T(8,128)(2,1)S(1)}, bf16[256,256]{1,0:T(8,128)(2,1)S(1)}, u32[]{:S(2)}, u32[]{:S(2)}) collective-permute-start(bf16[256,256]{1,0:T(8,128)(2,1)S(1)} %get-tuple-element.60), channel_id=1, source_target_pairs={{0,3},{1,0},{2,1},{3,2},{4,7},{5,4},{6,5},{7,6},{8,11},{9,8},{10,9... | collective-permute-start | bytes 393224 | tf_op jit(solution)/shard_map/ppermute | solution.py:45
  27.8 9.3 %collective-permute-start.9 = (bf16[256,256]{1,0:T(8,128)(2,1)S(1)}, bf16[256,256]{1,0:T(8,128)(2,1)S(1)}, u32[]{:S(2)}, u32[]{:S(2)}) collective-permute-start(bf16[256,256]{1,0:T(8,128)(2,1)S(1)} %get-tuple-element.61), channel_id=1, source_target_pairs={{0,1},{1,2},{2,3},{3,0},{4,5},{5,6},{6,7},{7,4},{8,9},{9,10},{10,1... | collective-permute-start | bytes 393224 | tf_op jit(solution)/shard_map/ppermute | solution.py:45
  28.7 4.5 %collective-permute-start.10 = (f32[8,128]{1,0:T(8,128)S(1)}, f32[8,128]{1,0:T(8,128)S(1)}, u32[]{:S(2)}, u32[]{:S(2)}) collective-permute-start(f32[8,128]{1,0:T(8,128)S(1)} %get-tuple-element.59.after), channel_id=1, source_target_pairs={{0,1},{1,0},{2,3},{3,2},{4,5},{5,4},{6,7},{7,6},{8,9},{9,8},{10,11... | collective-permute-start | bytes 12296 | tf_op jit(solution)/shard_map/ppermute | solution.py:82
  33.2 3.2 %collective-permute-start.11 = (f32[8,128]{1,0:T(8,128)S(1)}, f32[8,128]{1,0:T(8,128)S(1)}, u32[]{:S(2)}, u32[]{:S(2)}) collective-permute-start(f32[8,128]{1,0:T(8,128)S(1)} %add.3.refs_0_), channel_id=1, source_target_pairs={{0,2},{1,3},{2,0},{3,1},{4,6},{5,7},{6,4},{7,5},{8,10},{9,11},{10,... | collective-permute-start | bytes 12296 | tf_op jit(solution)/shard_map/ppermute | solution.py:82
  37.4 3.4 %collective-permute-start.14 = (f32[8,128]{1,0:T(8,128)S(1)}, f32[8,128]{1,0:T(8,128)S(1)}, u32[]{:S(2)}, u32[]{:S(2)}) collective-permute-start(f32[8,128]{1,0:T(8,128)S(1)} %shard_map.119.refs_0_), channel_id=1, source_target_pairs={{0,3},{1,2},{2,1},{3,0},{4,7},{5,6},{6,5},{7,4},{8,11},{9,10},{10,... | collective-permute-start | bytes 12296 | tf_op jit(solution)/shard_map/ppermute | solution.py:68
  38.3 2.5 %collective-permute-start.13 = (f32[8,128]{1,0:T(8,128)S(1)}, f32[8,128]{1,0:T(8,128)S(1)}, u32[]{:S(2)}, u32[]{:S(2)}) collective-permute-start(f32[8,128]{1,0:T(8,128)S(1)} %shard_map.119.refs_0_), channel_id=1, source_target_pairs={{0,2},{1,3},{2,0},{3,1},{4,6},{5,7},{6,4},{7,5},{8,10},{9,11},{10,... | collective-permute-start | bytes 12296 | tf_op jit(solution)/shard_map/ppermute | solution.py:68
  39.0 2.5 %collective-permute-start.12 = (f32[8,128]{1,0:T(8,128)S(1)}, f32[8,128]{1,0:T(8,128)S(1)}, u32[]{:S(2)}, u32[]{:S(2)}) collective-permute-start(f32[8,128]{1,0:T(8,128)S(1)} %shard_map.119.refs_0_), channel_id=1, source_target_pairs={{0,1},{1,0},{2,3},{3,2},{4,5},{5,4},{6,7},{7,6},{8,9},{9,8},{10,11... | collective-permute-start | bytes 12296 | tf_op jit(solution)/shard_map/ppermute | solution.py:68
  43.9 6.1 %collective-permute-start.15 = (bf16[1,1,256,256]{3,2,1,0:T(8,128)(2,1)S(1)}, bf16[1,1,256,256]{3,2,1,0:T(8,128)(2,1)S(1)}, u32[]{:S(2)}, u32[]{:S(2)}) collective-permute-start(bf16[1,1,256,256]{3,2,1,0:T(8,128)(2,1)S(1)} %get-tuple-element.78), channel_id=1, source_target_pairs={{0,4},{1,5},{2,6},{3,7},{4,0},{5,1},{6,2},{7,3},{8,12},{9,13},{10,... | collective-permute-start | bytes 393224 | tf_op jit(solution)/shard_map/ppermute | solution.py:40
  46.9 5.0 %collective-permute-start.16 = (bf16[1,1,256,256]{3,2,1,0:T(8,128)(2,1)S(1)}, bf16[1,1,256,256]{3,2,1,0:T(8,128)(2,1)S(1)}, u32[]{:S(2)}, u32[]{:S(2)}) collective-permute-start(bf16[1,1,256,256]{3,2,1,0:T(8,128)(2,1)S(1)} %get-tuple-element.79), channel_id=1, source_target_pairs={{0,1},{1,0},{2,3},{3,2},{4,8},{5,9},{6,10},{7,11},{8,4},{9,5},{10,... | collective-permute-start | bytes 393224 | tf_op jit(solution)/shard_map/ppermute | solution.py:40

commit v17 on v15

--- a/solution.py
+++ b/solution.py
@@ -11,6 +11,7 @@
 WD = 2
 NS_STEPS = 3
 ROWS = 8
+BAND = 32
 LANES = 128
 F32 = jnp.float32
 BF16 = jnp.bfloat16
@@ -238,14 +239,24 @@
     along_p = w * inverse_q
     along_y = u * inverse_y - along_p * s
     factors = [along_y, along_y * (shift_ref[0:1, 0:1] - lam), along_p, -lam * along_p]
-    low_ref[...] = total([factor * term[...] for factor, term in zip(factors, lows)])
-    x = along_y * y_ref[...] + along_p * p_ref[...]
-    g = along_y * g_ref[...] + along_p * hp_ref[...]
-    p = prec[...].astype(F32) * (g - lam * x)
-    x_out[...] = x
-    p_out[...] = p
-    diag = total([factor * term[...] for factor, term in zip(factors, diags)])
-    write_sums(stat_ref, [(x, p), (p, p), (p, g), (p, diag)])
+    size = low_ref.shape[0]
+    step = BAND if size % BAND == 0 else size
+    sums = None
+    for start in range(0, size, step):
+        band = slice(start, start + step)
+        low_ref[band] = total([factor * term[band] for factor, term in zip(factors, lows)])
+        x = along_y * y_ref[band] + along_p * p_ref[band]
+        g = along_y * g_ref[band] + along_p * hp_ref[band]
+        p = prec[band].astype(F32) * (g - lam * x)
+        x_out[band] = x
+        p_out[band] = p
+        diag = total([factor * term[band] for factor, term in zip(factors, diags)])
+        products = [x * p, p * p, p * g, p * diag]
+        parts_of = [jnp.sum(value.reshape(-1, ROWS, size), axis=0) for value in products]
+        sums = parts_of if sums is None else [one + two for one, two in zip(sums, parts_of)]
+    stat_ref[...] = jnp.zeros(stat_ref.shape, F32)
+    for row, value in enumerate(sums):
+        stat_ref[row : row + 1] = fold(value)
     for i, value in enumerate([along_y, along_p, lam]):
         coefficients[i : i + 1] = jnp.broadcast_to(value, (1, LANES))
 
@@ -313,8 +324,8 @@
     @pl.when(jnp.logical_not(odd_segment()))
     def _():
         lam, x = finish(scalars(refs[:parts], 4), x_ref, p_ref, coefficients)
+        lam_out[0] = lam[0, 0]
         polarise(x, polar_out, weight_out)
-        lam_out[0] = lam[0, 0]
 
     @pl.when(odd_segment())
     def _():

time: 53.9 us -> 53.7 us (level)
  no operation moved by 1% of the time
where the time goes in v17:
time: 53.7 us; the launch traced here: 53.2 us
  starting transfers between devices  21.3 us (40%)
  waiting for transfers between devices  15.6 us (29%)
  Pallas kernels  14.6 us (27%)
  between operations  1.65 us (3%)
    pallas_call x21, Pallas kernels, call(): pl.pallas_call(kernel, out_shape=outs, in_specs=in_specs or [VMEM] * len(...  14.6 us
    ppermute x6, starting transfers between devices, rotate(): lax.ppermute(value, axis, [(source, (source + steps) % count) for source...  6.27 us
    ppermute x2, starting transfers between devices, swap(): return lax.ppermute(value, (axis, other), pairs)  5.25 us
    ppermute x4, starting transfers between devices, pairwise(): parts.append(lax.ppermute(parts[0], axis, pairs))  4.99 us
    ppermute x4, waiting for transfers between devices, pairwise(): parts.append(lax.ppermute(parts[0], axis, pairs))  4.73 us
    ppermute x1, waiting for transfers between devices, shift(): lax.ppermute(value, axis, [(source, source + steps) for source in range(f...  4.52 us
    ppermute x6, waiting for transfers between devices, rotate(): lax.ppermute(value, axis, [(source, (source + steps) % count) for source...  3.28 us
    ppermute x3, starting transfers between devices, exchange(): parts.append(lax.ppermute(parts[0], axis, pairs))  2.71 us
  transfers between devices with their start and end apart: 16, of which 9 were waited for; matrix products, arithmetic and copies ran while one was open for 0% of the time, Pallas kernels for 21%

profile of v17, /device:TPU:1, one launch (start us, length us, event | category | flops | bytes accessed | tf_op | source)
XLA Modules:
  0.0 53.2 jit_solution(13072905207051652302)
XLA Ops:
  0.7 2.1 %collective-permute-start = (bf16[256,256]{1,0:T(8,128)(2,1)}, bf16[256,256]{1,0:T(8,128)(2,1)S(1)}, u32[]{:S(2)}, u32[]{:S(2)}) collective-permute-start(bf16[256,256]{1,0:T(8,128)(2,1)} %bitcast.31), channel_id=1, source_target_pairs={{4,0},{8,4},{12,8},{16,12},{20,16},{24,20},{28,24},{5,1},{9,5},{13... | collective-permute-start | bytes 393224 | tf_op jit(solution)/shard_map/ppermute | solution.py:27
  3.7 4.5 %collective-permute-done.behind = bf16[256,256]{1,0:T(8,128)(2,1)S(1)} collective-permute-done((bf16[256,256]{1,0:T(8,128)(2,1)}, bf16[256,256]{1,0:T(8,128)(2,1)S(1)}, u32[]{:S(2)}, u32[]{:S(2)}) %collective-permute-start) | collective-permute-done | bytes 131104 | tf_op jit(solution)/shard_map/ppermute | solution.py:27
  8.4 1.3 %collective-permute-start.1 = (bf16[256,256]{1,0:T(8,128)(2,1)S(1)}, bf16[256,256]{1,0:T(8,128)(2,1)S(1)}, u32[]{:S(2)}, u32[]{:S(2)}) collective-permute-start(bf16[256,256]{1,0:T(8,128)(2,1)S(1)} %get-tuple-element.42.yb), channel_id=1, source_target_pairs={{0,1},{1,2},{2,3},{3,0},{4,5},{5,6},{6,7},{7,4},{8,9},{9,10},{10,1... | collective-permute-start | bytes 393224 | tf_op jit(solution)/shard_map/ppermute | solution.py:46
  9.7 1.2 %shard_map.107 = (f32[256,256]{1,0:T(8,128)S(1)}, bf16[256,256]{1,0:T(8,128)(2,1)S(1)}) custom-call(bf16[16,256,256]{2,1,0:T(8,128)(2,1)S(1)} %bitcast.9, bf16[16,256,256]{2,1,0:T(8,128)(2,1)S(1)} %bitcast.16, bf16[256,256]{1,0:T(8,128)(2,1)S(1)} %get-tuple-element.42.yb), custom_call_target="tpu_custom_call" | custom-call | tf_op jit(solution)/shard_map/pallas_call | solution.py:357
  10.9 1.2 %collective-permute-start.2 = (bf16[256,256]{1,0:T(8,128)(2,1)S(1)}, bf16[256,256]{1,0:T(8,128)(2,1)S(1)}, u32[]{:S(2)}, u32[]{:S(2)}) collective-permute-start(bf16[256,256]{1,0:T(8,128)(2,1)S(1)} %get-tuple-element.47), channel_id=1, source_target_pairs={{0,3},{1,0},{2,1},{3,2},{4,7},{5,4},{6,5},{7,6},{8,11},{9,8},{10,9... | collective-permute-start | bytes 393224 | tf_op jit(solution)/shard_map/ppermute | solution.py:46
  12.1 1.5 %shard_map.106 = (f32[8,128]{1,0:T(8,128)S(1)}, f32[256,256]{1,0:T(8,128)S(1)}, f32[256,256]{1,0:T(8,128)S(1)}, f32[256,256]{1,0:T(8,128)S(1)}) custom-call(bf16[16,256,256]{2,1,0:T(8,128)(2,1)S(1)} %bitcast.10, bf16[16,256,256]{2,1,0:T(8,128)(2,1)S(1)} %bitcast.17, f32[256,256]{1,0:T(8,128)S(1)} %get-tuple-element.43.y.refs_2_, ...), custom_call_target="tpu_custom_call" | custom-call | tf_op jit(solution)/shard_map/pallas_call | solution.py:357
  13.9 1.2 %collective-permute-start.4 = (f32[8,128]{1,0:T(8,128)S(1)}, f32[8,128]{1,0:T(8,128)S(1)}, u32[]{:S(2)}, u32[]{:S(2)}) collective-permute-start(f32[8,128]{1,0:T(8,128)S(1)} %shard_map.108.after), channel_id=1, source_target_pairs={{0,1},{1,0},{2,3},{3,2},{4,5},{5,4},{6,7},{7,6},{8,9},{9,8},{10,11... | collective-permute-start | bytes 12296 | tf_op jit(solution)/shard_map/ppermute | solution.py:83
  15.1 1.3 %collective-permute-done.4 = f32[8,128]{1,0:T(8,128)S(1)} collective-permute-done((f32[8,128]{1,0:T(8,128)S(1)}, f32[8,128]{1,0:T(8,128)S(1)}, u32[]{:S(2)}, u32[]{:S(2)}) %collective-permute-start.4) | collective-permute-done | bytes 4128 | tf_op jit(solution)/shard_map/ppermute | solution.py:83
  16.4 1.9 %collective-permute-start.5 = (f32[8,128]{1,0:T(8,128)S(1)}, f32[8,128]{1,0:T(8,128)S(1)}, u32[]{:S(2)}, u32[]{:S(2)}) collective-permute-start(f32[8,128]{1,0:T(8,128)S(1)} %add.6.refs_0_), channel_id=1, source_target_pairs={{0,2},{1,3},{2,0},{3,1},{4,6},{5,7},{6,4},{7,5},{8,10},{9,11},{10,... | collective-permute-start | bytes 12296 | tf_op jit(solution)/shard_map/ppermute | solution.py:83
  18.3 1.2 %shard_map.109.up = f32[256,256]{1,0:T(8,128)S(1)} custom-call(bf16[16,256,256]{2,1,0:T(8,128)(2,1)S(1)} %bitcast.11, bf16[16,256,256]{2,1,0:T(8,128)(2,1)S(1)} %bitcast.18, bf16[256,256]{1,0:T(8,128)(2,1)S(1)} %collective-permute-done.1.below.refs_2_.y, f32[8,128]{1,0:T(8,128)S(1)} %shard_map.108.after), custom_call_target="tpu_custom_call" | custom-call | tf_op jit(solution)/shard_map/pallas_call | solution.py:357
  19.7 1.2 %collective-permute-start.3 = (bf16[256,256]{1,0:T(8,128)(2,1)S(1)}, bf16[256,256]{1,0:T(8,128)(2,1)S(1)}, u32[]{:S(2)}, u32[]{:S(2)}) collective-permute-start(bf16[256,256]{1,0:T(8,128)(2,1)S(1)} %get-tuple-element.48), channel_id=1, source_target_pairs={{0,1},{1,2},{2,3},{3,0},{4,5},{5,6},{6,7},{7,4},{8,9},{9,10},{10,1... | collective-permute-start | bytes 393224 | tf_op jit(solution)/shard_map/ppermute | solution.py:46
  20.8 1.3 %shard_map.111 = (f32[256,256]{1,0:T(8,128)S(1)}, f32[256,256]{1,0:T(8,128)S(1)}) custom-call(bf16[16,256,256]{2,1,0:T(8,128)(2,1)S(1)} %bitcast.12, bf16[16,256,256]{2,1,0:T(8,128)(2,1)S(1)} %bitcast.19, bf16[256,256]{1,0:T(8,128)(2,1)S(1)} %get-tuple-element.50.value), custom_call_target="tpu_custom_call" | custom-call | tf_op jit(solution)/shard_map/pallas_call | solution.py:357
  22.6 1.3 %collective-permute-start.7 = (bf16[256,256]{1,0:T(8,128)(2,1)S(1)}, bf16[256,256]{1,0:T(8,128)(2,1)S(1)}, u32[]{:S(2)}, u32[]{:S(2)}) collective-permute-start(bf16[256,256]{1,0:T(8,128)(2,1)S(1)} %get-tuple-element.60), channel_id=1, source_target_pairs={{0,3},{1,0},{2,1},{3,2},{4,7},{5,4},{6,5},{7,6},{8,11},{9,8},{10,9... | collective-permute-start | bytes 393224 | tf_op jit(solution)/shard_map/ppermute | solution.py:46
  23.9 0.8 %collective-permute-done.6.refs_4_.prec = bf16[256,256]{1,0:T(8,128)(2,1)S(1)} collective-permute-done((bf16[256,256]{1,0:T(8,128)(2,1)S(1)}, bf16[256,256]{1,0:T(8,128)(2,1)S(1)}, u32[]{:S(2)}, u32[]{:S(2)}) %collective-permute-start.6) | collective-permute-done | bytes 131104 | tf_op jit(solution)/shard_map/ppermute | solution.py:46
  24.7 2.3 %collective-permute-done.3.refs_3_.g = bf16[256,256]{1,0:T(8,128)(2,1)S(1)} collective-permute-done((bf16[256,256]{1,0:T(8,128)(2,1)S(1)}, bf16[256,256]{1,0:T(8,128)(2,1)S(1)}, u32[]{:S(2)}, u32[]{:S(2)}) %collective-permute-start.3) | collective-permute-done | bytes 131104 | tf_op jit(solution)/shard_map/ppermute | solution.py:46
  27.2 1.2 %shard_map.114.up = f32[256,256]{1,0:T(8,128)S(1)} custom-call(bf16[16,256,256]{2,1,0:T(8,128)(2,1)S(1)} %bitcast.13, bf16[16,256,256]{2,1,0:T(8,128)(2,1)S(1)} %bitcast.20, bf16[256,256]{1,0:T(8,128)(2,1)S(1)} %get-tuple-element.57.below.p, f32[8,128]{1,0:T(8,128)S(1)} %get-tuple-element.59.after), custom_call_target="tpu_custom_call" | custom-call | tf_op jit(solution)/shard_map/pallas_call | solution.py:357
  28.6 1.3 %collective-permute-start.8 = (bf16[256,256]{1,0:T(8,128)(2,1)S(1)}, bf16[256,256]{1,0:T(8,128)(2,1)S(1)}, u32[]{:S(2)}, u32[]{:S(2)}) collective-permute-start(bf16[256,256]{1,0:T(8,128)(2,1)S(1)} %get-tuple-element.61), channel_id=1, source_target_pairs={{0,1},{1,2},{2,3},{3,0},{4,5},{5,6},{6,7},{7,4},{8,9},{9,10},{10,1... | collective-permute-start | bytes 393224 | tf_op jit(solution)/shard_map/ppermute | solution.py:46
  29.8 1.2 %collective-permute-start.9 = (f32[8,128]{1,0:T(8,128)S(1)}, f32[8,128]{1,0:T(8,128)S(1)}, u32[]{:S(2)}, u32[]{:S(2)}) collective-permute-start(f32[8,128]{1,0:T(8,128)S(1)} %get-tuple-element.59.after), channel_id=1, source_target_pairs={{0,1},{1,0},{2,3},{3,2},{4,5},{5,4},{6,7},{7,6},{8,9},{9,8},{10,11... | collective-permute-start | bytes 12296 | tf_op jit(solution)/shard_map/ppermute | solution.py:83
  31.0 3.4 %collective-permute-done.9 = f32[8,128]{1,0:T(8,128)S(1)} collective-permute-done((f32[8,128]{1,0:T(8,128)S(1)}, f32[8,128]{1,0:T(8,128)S(1)}, u32[]{:S(2)}, u32[]{:S(2)}) %collective-permute-start.9) | collective-permute-done | bytes 4128 | tf_op jit(solution)/shard_map/ppermute | solution.py:83
  34.4 0.7 %collective-permute-start.10 = (f32[8,128]{1,0:T(8,128)S(1)}, f32[8,128]{1,0:T(8,128)S(1)}, u32[]{:S(2)}, u32[]{:S(2)}) collective-permute-start(f32[8,128]{1,0:T(8,128)S(1)} %add.7.refs_0_), channel_id=1, source_target_pairs={{0,2},{1,3},{2,0},{3,1},{4,6},{5,7},{6,4},{7,5},{8,10},{9,11},{10,... | collective-permute-start | bytes 12296 | tf_op jit(solution)/shard_map/ppermute | solution.py:83
  35.1 1.3 %shard_map.117 = (f32[256,256]{1,0:T(8,128)S(1)}, f32[256,256]{1,0:T(8,128)S(1)}) custom-call(bf16[16,256,256]{2,1,0:T(8,128)(2,1)S(1)} %bitcast.14, bf16[16,256,256]{2,1,0:T(8,128)(2,1)S(1)} %bitcast.21, bf16[256,256]{1,0:T(8,128)(2,1)S(1)} %get-tuple-element.67.value), custom_call_target="tpu_custom_call" | custom-call | tf_op jit(solution)/shard_map/pallas_call | solution.py:357
  36.4 1.3 %shard_map.116 = (f32[256,256]{1,0:T(8,128)S(1)}, f32[256,256]{1,0:T(8,128)S(1)}) custom-call(bf16[16,256,256]{2,1,0:T(8,128)(2,1)S(1)} %bitcast.15, bf16[16,256,256]{2,1,0:T(8,128)(2,1)S(1)} %bitcast.22, bf16[256,256]{1,0:T(8,128)(2,1)S(1)} %get-tuple-element.65.value), custom_call_target="tpu_custom_call" | custom-call | tf_op jit(solution)/shard_map/pallas_call | solution.py:357
  38.4 0.8 %collective-permute-start.13 = (f32[8,128]{1,0:T(8,128)S(1)}, f32[8,128]{1,0:T(8,128)S(1)}, u32[]{:S(2)}, u32[]{:S(2)}) collective-permute-start(f32[8,128]{1,0:T(8,128)S(1)} %shard_map.119.refs_0_), channel_id=1, source_target_pairs={{0,3},{1,2},{2,1},{3,0},{4,7},{5,6},{6,5},{7,4},{8,11},{9,10},{10,... | collective-permute-start | bytes 12296 | tf_op jit(solution)/shard_map/ppermute | solution.py:69
  39.5 1.7 %collective-permute-start.11 = (f32[8,128]{1,0:T(8,128)S(1)}, f32[8,128]{1,0:T(8,128)S(1)}, u32[]{:S(2)}, u32[]{:S(2)}) collective-permute-start(f32[8,128]{1,0:T(8,128)S(1)} %shard_map.119.refs_0_), channel_id=1, source_target_pairs={{0,1},{1,0},{2,3},{3,2},{4,5},{5,4},{6,7},{7,6},{8,9},{9,8},{10,11... | collective-permute-start | bytes 12296 | tf_op jit(solution)/shard_map/ppermute | solution.py:69
  41.2 0.7 %collective-permute-done.13.refs_3_ = f32[8,128]{1,0:T(8,128)S(1)} collective-permute-done((f32[8,128]{1,0:T(8,128)S(1)}, f32[8,128]{1,0:T(8,128)S(1)}, u32[]{:S(2)}, u32[]{:S(2)}) %collective-permute-start.13) | collective-permute-done | bytes 4128 | tf_op jit(solution)/shard_map/ppermute | solution.py:69
  42.2 1.6 %shard_map.120 = (f32[256,256]{1,0:T(8,128)S(1)}, bf16[1,1,256,256]{3,2,1,0:T(8,128)(2,1)S(1)}) custom-call(f32[8,128]{1,0:T(8,128)S(1)} %shard_map.119.refs_0_, f32[8,128]{1,0:T(8,128)S(1)} %collective-permute-done.11.refs_1_, f32[8,128]{1,0:T(8,128)S(1)} %collective-permute-done.12.refs_2_, f32[8,128]{1,0:T(8,128)S(1)} %collective-permute-done.13.refs_3_, ...), custom_call_target="tpu_custom_call" | custom-call | tf_op jit(solution)/shard_map/pallas_call | solution.py:357
  43.8 0.7 %shard_map.121 = (f32[256,256]{1,0:T(8,128)S(1)}, bf16[1,1,256,256]{3,2,1,0:T(8,128)(2,1)S(1)}, f32[1]{0:T(128)}) custom-call(f32[8,128]{1,0:T(8,128)S(1)} %shard_map.119.refs_0_, f32[8,128]{1,0:T(8,128)S(1)} %collective-permute-done.11.refs_1_, f32[8,128]{1,0:T(8,128)S(1)} %collective-permute-done.12.refs_2_, ...), custom_call_target="tpu_custom_call", output_to_operand_aliasing={{0}: (7, {})} | custom-call | tf_op jit(solution)/shard_map/pallas_call | solution.py:357
  44.5 3.4 %collective-permute-start.14 = (bf16[1,1,256,256]{3,2,1,0:T(8,128)(2,1)S(1)}, bf16[1,1,256,256]{3,2,1,0:T(8,128)(2,1)S(1)}, u32[]{:S(2)}, u32[]{:S(2)}) collective-permute-start(bf16[1,1,256,256]{3,2,1,0:T(8,128)(2,1)S(1)} %get-tuple-element.78), channel_id=1, source_target_pairs={{0,4},{1,5},{2,6},{3,7},{4,0},{5,1},{6,2},{7,3},{8,12},{9,13},{10,... | collective-permute-start | bytes 393224 | tf_op jit(solution)/shard_map/ppermute | solution.py:41
  47.9 1.9 %collective-permute-start.15 = (bf16[1,1,256,256]{3,2,1,0:T(8,128)(2,1)S(1)}, bf16[1,1,256,256]{3,2,1,0:T(8,128)(2,1)S(1)}, u32[]{:S(2)}, u32[]{:S(2)}) collective-permute-start(bf16[1,1,256,256]{3,2,1,0:T(8,128)(2,1)S(1)} %get-tuple-element.79), channel_id=1, source_target_pairs={{0,1},{1,0},{2,3},{3,2},{4,8},{5,9},{6,10},{7,11},{8,4},{9,5},{10,... | collective-permute-start | bytes 393224 | tf_op jit(solution)/shard_map/ppermute | solution.py:41
  49.7 0.7 %shard_map.122 = f32[1,1,256,256]{3,2,1,0:T(8,128)} custom-call(f32[256,256]{1,0:T(8,128)S(1)} %get-tuple-element.77.value), custom_call_target="tpu_custom_call" | custom-call | bytes 1048576 | tf_op jit(solution)/shard_map/pallas_call | solution.py:357
  50.5 2.1 %collective-permute-done.15.far = bf16[1,1,256,256]{3,2,1,0:T(8,128)(2,1)S(1)} collective-permute-done((bf16[1,1,256,256]{3,2,1,0:T(8,128)(2,1)S(1)}, bf16[1,1,256,256]{3,2,1,0:T(8,128)(2,1)S(1)}, u32[]{:S(2)}, u32[]{:S(2)}) %collective-permute-start.15) | collective-permute-done | bytes 131104 | tf_op jit(solution)/shard_map/ppermute | solution.py:41
  52.5 0.7 %shard_map.123 = bf16[1,1,256,256]{3,2,1,0:T(8,128)(2,1)} custom-call(bf16[1,1,256,256]{3,2,1,0:T(8,128)(2,1)S(1)} %collective-permute-done.14.near, bf16[1,1,256,256]{3,2,1,0:T(8,128)(2,1)S(1)} %collective-permute-done.15.far), custom_call_target="tpu_custom_call" | custom-call | tf_op jit(solution)/shard_map/pallas_call | solution.py:357
  (36 shorter events, 2.8 us)
Async XLA Ops:
  0.6 3.0 %copy-start.4 = (bf16[1,1,256,256]{3,2,1,0:T(8,128)(2,1)S(1)}, bf16[1,1,256,256]{3,2,1,0:T(8,128)(2,1)}, u32[]{:S(2)}) copy-start(bf16[1,1,256,256]{3,2,1,0:T(8,128)(2,1)} %param.10) | copy-start | bytes 393220
  0.6 3.0 %copy-start.5 = (f32[1,1,256]{2,1,0:T(1,128)S(1)}, f32[1,1,256]{2,1,0:T(1,128)}, u32[]{:S(2)}) copy-start(f32[1,1,256]{2,1,0:T(1,128)} %param.13) | copy-start | bytes 3076
  0.7 7.6 %copy-start.3 = (bf16[1,1,256,256]{3,2,1,0:T(8,128)(2,1)S(1)}, bf16[1,1,256,256]{3,2,1,0:T(8,128)(2,1)}, u32[]{:S(2)}) copy-start(bf16[1,1,256,256]{3,2,1,0:T(8,128)(2,1)} %param.12) | copy-start | bytes 393220
  0.7 7.6 %collective-permute-start = (bf16[256,256]{1,0:T(8,128)(2,1)}, bf16[256,256]{1,0:T(8,128)(2,1)S(1)}, u32[]{:S(2)}, u32[]{:S(2)}) collective-permute-start(bf16[256,256]{1,0:T(8,128)(2,1)} %bitcast.31), channel_id=1, source_target_pairs={{4,0},{8,4},{12,8},{16,12},{20,16},{24,20},{28,24},{5,1},{9,5},{13... | collective-permute-start | bytes 393224 | tf_op jit(solution)/shard_map/ppermute | solution.py:27
  2.7 7.0 %copy-start = (bf16[1,1,16,256,256]{4,3,2,1,0:T(8,128)(2,1)S(1)}, bf16[1,1,16,256,256]{4,3,2,1,0:T(8,128)(2,1)}, u32[]{:S(2)}) copy-start(bf16[1,1,16,256,256]{4,3,2,1,0:T(8,128)(2,1)} %param.8) | copy-start | bytes 6291460
  2.7 7.0 %copy-start.1 = (bf16[1,1,16,256,256]{4,3,2,1,0:T(8,128)(2,1)S(1)}, bf16[1,1,16,256,256]{4,3,2,1,0:T(8,128)(2,1)}, u32[]{:S(2)}) copy-start(bf16[1,1,16,256,256]{4,3,2,1,0:T(8,128)(2,1)} %param.9) | copy-start | bytes 6291460
  8.4 5.4 %collective-permute-start.1 = (bf16[256,256]{1,0:T(8,128)(2,1)S(1)}, bf16[256,256]{1,0:T(8,128)(2,1)S(1)}, u32[]{:S(2)}, u32[]{:S(2)}) collective-permute-start(bf16[256,256]{1,0:T(8,128)(2,1)S(1)} %get-tuple-element.42.yb), channel_id=1, source_target_pairs={{0,1},{1,2},{2,3},{3,0},{4,5},{5,6},{6,7},{7,4},{8,9},{9,10},{10,1... | collective-permute-start | bytes 393224 | tf_op jit(solution)/shard_map/ppermute | solution.py:46
  9.7 2.4 %copy-start.2 = (bf16[1,1,256,256]{3,2,1,0:T(8,128)(2,1)S(1)}, bf16[1,1,256,256]{3,2,1,0:T(8,128)(2,1)}, u32[]{:S(2)}) copy-start(bf16[1,1,256,256]{3,2,1,0:T(8,128)(2,1)} %param.14) | copy-start | bytes 393220
  10.9 8.6 %collective-permute-start.2 = (bf16[256,256]{1,0:T(8,128)(2,1)S(1)}, bf16[256,256]{1,0:T(8,128)(2,1)S(1)}, u32[]{:S(2)}, u32[]{:S(2)}) collective-permute-start(bf16[256,256]{1,0:T(8,128)(2,1)S(1)} %get-tuple-element.47), channel_id=1, source_target_pairs={{0,3},{1,0},{2,1},{3,2},{4,7},{5,4},{6,5},{7,6},{8,11},{9,8},{10,9... | collective-permute-start | bytes 393224 | tf_op jit(solution)/shard_map/ppermute | solution.py:46
  13.9 2.5 %collective-permute-start.4 = (f32[8,128]{1,0:T(8,128)S(1)}, f32[8,128]{1,0:T(8,128)S(1)}, u32[]{:S(2)}, u32[]{:S(2)}) collective-permute-start(f32[8,128]{1,0:T(8,128)S(1)} %shard_map.108.after), channel_id=1, source_target_pairs={{0,1},{1,0},{2,3},{3,2},{4,5},{5,4},{6,7},{7,6},{8,9},{9,8},{10,11... | collective-permute-start | bytes 12296 | tf_op jit(solution)/shard_map/ppermute | solution.py:83
  16.4 5.7 %collective-permute-start.5 = (f32[8,128]{1,0:T(8,128)S(1)}, f32[8,128]{1,0:T(8,128)S(1)}, u32[]{:S(2)}, u32[]{:S(2)}) collective-permute-start(f32[8,128]{1,0:T(8,128)S(1)} %add.6.refs_0_), channel_id=1, source_target_pairs={{0,2},{1,3},{2,0},{3,1},{4,6},{5,7},{6,4},{7,5},{8,10},{9,11},{10,... | collective-permute-start | bytes 12296 | tf_op jit(solution)/shard_map/ppermute | solution.py:83
  18.3 6.4 %collective-permute-start.6 = (bf16[256,256]{1,0:T(8,128)(2,1)S(1)}, bf16[256,256]{1,0:T(8,128)(2,1)S(1)}, u32[]{:S(2)}, u32[]{:S(2)}) collective-permute-start(bf16[256,256]{1,0:T(8,128)(2,1)S(1)} %bitcast.24), channel_id=1, source_target_pairs={{0,1},{1,2},{2,3},{3,0},{4,5},{5,6},{6,7},{7,4},{8,9},{9,10},{10,1... | collective-permute-start | bytes 393224 | tf_op jit(solution)/shard_map/ppermute | solution.py:46
  19.7 7.3 %collective-permute-start.3 = (bf16[256,256]{1,0:T(8,128)(2,1)S(1)}, bf16[256,256]{1,0:T(8,128)(2,1)S(1)}, u32[]{:S(2)}, u32[]{:S(2)}) collective-permute-start(bf16[256,256]{1,0:T(8,128)(2,1)S(1)} %get-tuple-element.48), channel_id=1, source_target_pairs={{0,1},{1,2},{2,3},{3,0},{4,5},{5,6},{6,7},{7,4},{8,9},{9,10},{10,1... | collective-permute-start | bytes 393224 | tf_op jit(solution)/shard_map/ppermute | solution.py:46
  22.6 5.9 %collective-permute-start.7 = (bf16[256,256]{1,0:T(8,128)(2,1)S(1)}, bf16[256,256]{1,0:T(8,128)(2,1)S(1)}, u32[]{:S(2)}, u32[]{:S(2)}) collective-permute-start(bf16[256,256]{1,0:T(8,128)(2,1)S(1)} %get-tuple-element.60), channel_id=1, source_target_pairs={{0,3},{1,0},{2,1},{3,2},{4,7},{5,4},{6,5},{7,6},{8,11},{9,8},{10,9... | collective-permute-start | bytes 393224 | tf_op jit(solution)/shard_map/ppermute | solution.py:46
  28.6 9.6 %collective-permute-start.8 = (bf16[256,256]{1,0:T(8,128)(2,1)S(1)}, bf16[256,256]{1,0:T(8,128)(2,1)S(1)}, u32[]{:S(2)}, u32[]{:S(2)}) collective-permute-start(bf16[256,256]{1,0:T(8,128)(2,1)S(1)} %get-tuple-element.61), channel_id=1, source_target_pairs={{0,1},{1,2},{2,3},{3,0},{4,5},{5,6},{6,7},{7,4},{8,9},{9,10},{10,1... | collective-permute-start | bytes 393224 | tf_op jit(solution)/shard_map/ppermute | solution.py:46
  29.8 4.6 %collective-permute-start.9 = (f32[8,128]{1,0:T(8,128)S(1)}, f32[8,128]{1,0:T(8,128)S(1)}, u32[]{:S(2)}, u32[]{:S(2)}) collective-permute-start(f32[8,128]{1,0:T(8,128)S(1)} %get-tuple-element.59.after), channel_id=1, source_target_pairs={{0,1},{1,0},{2,3},{3,2},{4,5},{5,4},{6,7},{7,6},{8,9},{9,8},{10,11... | collective-permute-start | bytes 12296 | tf_op jit(solution)/shard_map/ppermute | solution.py:83
  34.4 3.3 %collective-permute-start.10 = (f32[8,128]{1,0:T(8,128)S(1)}, f32[8,128]{1,0:T(8,128)S(1)}, u32[]{:S(2)}, u32[]{:S(2)}) collective-permute-start(f32[8,128]{1,0:T(8,128)S(1)} %add.7.refs_0_), channel_id=1, source_target_pairs={{0,2},{1,3},{2,0},{3,1},{4,6},{5,7},{6,4},{7,5},{8,10},{9,11},{10,... | collective-permute-start | bytes 12296 | tf_op jit(solution)/shard_map/ppermute | solution.py:83
  38.4 3.4 %collective-permute-start.13 = (f32[8,128]{1,0:T(8,128)S(1)}, f32[8,128]{1,0:T(8,128)S(1)}, u32[]{:S(2)}, u32[]{:S(2)}) collective-permute-start(f32[8,128]{1,0:T(8,128)S(1)} %shard_map.119.refs_0_), channel_id=1, source_target_pairs={{0,3},{1,2},{2,1},{3,0},{4,7},{5,6},{6,5},{7,4},{8,11},{9,10},{10,... | collective-permute-start | bytes 12296 | tf_op jit(solution)/shard_map/ppermute | solution.py:69
  39.2 2.7 %collective-permute-start.12 = (f32[8,128]{1,0:T(8,128)S(1)}, f32[8,128]{1,0:T(8,128)S(1)}, u32[]{:S(2)}, u32[]{:S(2)}) collective-permute-start(f32[8,128]{1,0:T(8,128)S(1)} %shard_map.119.refs_0_), channel_id=1, source_target_pairs={{0,2},{1,3},{2,0},{3,1},{4,6},{5,7},{6,4},{7,5},{8,10},{9,11},{10,... | collective-permute-start | bytes 12296 | tf_op jit(solution)/shard_map/ppermute | solution.py:69
  39.5 2.7 %collective-permute-start.11 = (f32[8,128]{1,0:T(8,128)S(1)}, f32[8,128]{1,0:T(8,128)S(1)}, u32[]{:S(2)}, u32[]{:S(2)}) collective-permute-start(f32[8,128]{1,0:T(8,128)S(1)} %shard_map.119.refs_0_), channel_id=1, source_target_pairs={{0,1},{1,0},{2,3},{3,2},{4,5},{5,4},{6,7},{7,6},{8,9},{9,8},{10,11... | collective-permute-start | bytes 12296 | tf_op jit(solution)/shard_map/ppermute | solution.py:69
  44.5 6.0 %collective-permute-start.14 = (bf16[1,1,256,256]{3,2,1,0:T(8,128)(2,1)S(1)}, bf16[1,1,256,256]{3,2,1,0:T(8,128)(2,1)S(1)}, u32[]{:S(2)}, u32[]{:S(2)}) collective-permute-start(bf16[1,1,256,256]{3,2,1,0:T(8,128)(2,1)S(1)} %get-tuple-element.78), channel_id=1, source_target_pairs={{0,4},{1,5},{2,6},{3,7},{4,0},{5,1},{6,2},{7,3},{8,12},{9,13},{10,... | collective-permute-start | bytes 393224 | tf_op jit(solution)/shard_map/ppermute | solution.py:41
  47.9 4.7 %collective-permute-start.15 = (bf16[1,1,256,256]{3,2,1,0:T(8,128)(2,1)S(1)}, bf16[1,1,256,256]{3,2,1,0:T(8,128)(2,1)S(1)}, u32[]{:S(2)}, u32[]{:S(2)}) collective-permute-start(bf16[1,1,256,256]{3,2,1,0:T(8,128)(2,1)S(1)} %get-tuple-element.79), channel_id=1, source_target_pairs={{0,1},{1,0},{2,3},{3,2},{4,8},{5,9},{6,10},{7,11},{8,4},{9,5},{10,... | collective-permute-start | bytes 393224 | tf_op jit(solution)/shard_map/ppermute | solution.py:41

commit v18 on v16

--- a/solution.py
+++ b/solution.py
@@ -11,6 +11,7 @@
 WD = 2
 NS_STEPS = 3
 ROWS = 8
+BAND = 32
 LANES = 128
 F32 = jnp.float32
 BF16 = jnp.bfloat16
@@ -235,14 +236,24 @@
     along_p = w / jnp.sqrt(qq)
     along_y = u / jnp.sqrt(yy) - along_p * s
     factors = [along_y, along_y * (shift_ref[0:1, 0:1] - lam), along_p, -lam * along_p]
-    low_ref[...] = total([factor * term[...] for factor, term in zip(factors, lows)])
-    x = along_y * y_ref[...] + along_p * p_ref[...]
-    g = along_y * g_ref[...] + along_p * hp_ref[...]
-    p = prec[...].astype(F32) * (g - lam * x)
-    x_out[...] = x
-    p_out[...] = p
-    diag = total([factor * term[...] for factor, term in zip(factors, diags)])
-    write_sums(stat_ref, [(x, p), (p, p), (p, g), (p, diag)])
+    size = low_ref.shape[0]
+    step = BAND if size % BAND == 0 else size
+    sums = None
+    for start in range(0, size, step):
+        band = slice(start, start + step)
+        low_ref[band] = total([factor * term[band] for factor, term in zip(factors, lows)])
+        x = along_y * y_ref[band] + along_p * p_ref[band]
+        g = along_y * g_ref[band] + along_p * hp_ref[band]
+        p = prec[band].astype(F32) * (g - lam * x)
+        x_out[band] = x
+        p_out[band] = p
+        diag = total([factor * term[band] for factor, term in zip(factors, diags)])
+        products = [x * p, p * p, p * g, p * diag]
+        parts_of = [jnp.sum(value.reshape(-1, ROWS, size), axis=0) for value in products]
+        sums = parts_of if sums is None else [one + two for one, two in zip(sums, parts_of)]
+    stat_ref[...] = jnp.zeros(stat_ref.shape, F32)
+    for row, value in enumerate(sums):
+        stat_ref[row : row + 1] = fold(value)
     for i, value in enumerate([along_y, along_p, lam]):
         coefficients[i : i + 1] = jnp.broadcast_to(value, (1, LANES))
 
@@ -377,7 +388,7 @@
         scratch=[inner],
     )
     (stat,) = call(cross_kernel, [stats], y_below, low, stat)
-    parts = exchange(stat, "sec")
+    parts = pairwise(stat, "sec")
     g, gb, pgb = joined(y_below, stat, diag, above)
     g_below = rotate(gb, "sec", 1)
     low_g, diag_g = terms(pgb)

time: 52.9 us -> 53.8 us (1.017)
  waiting for transfers between devices: 14.9 us -> 15.6 us
    ppermute x2 -> x4, starting transfers between devices: 1.35 us -> 4.99 us  [pairwise(): parts.append(lax.ppermute(parts[0], axis, pairs))]
    ppermute x6 -> x3, starting transfers between devices: 5.8 us -> 2.71 us  [exchange(): parts.append(lax.ppermute(parts[0], axis, pairs))]
    ppermute x2 -> x4, waiting for transfers between devices: 3.91 us -> 4.73 us  [pairwise(): parts.append(lax.ppermute(parts[0], axis, pairs))]
    ppermute x6 -> x3, waiting for transfers between devices: 1.38 us -> 0.99 us  [exchange(): parts.append(lax.ppermute(parts[0], axis, pairs))]
  transfers between devices with their start and end apart: 17 -> 16, of which waited for: 8 -> 9; matrix products, arithmetic and copies ran while one was open for 0% -> 0% of each run, Pallas kernels for 21% -> 21%
where the time goes in v18:
time: 53.8 us; the launch traced here: 53.2 us
  starting transfers between devices  21.3 us (40%)
  waiting for transfers between devices  15.6 us (29%)
  Pallas kernels  14.7 us (27%)
  between operations  1.65 us (3%)
    pallas_call x21, Pallas kernels, call(): pl.pallas_call(kernel, out_shape=outs, in_specs=in_specs or [VMEM] * len(...  14.7 us
    ppermute x6, starting transfers between devices, rotate(): lax.ppermute(value, axis, [(source, (source + steps) % count) for source...  6.27 us
    ppermute x2, starting transfers between devices, swap(): return lax.ppermute(value, (axis, other), pairs)  5.25 us
    ppermute x4, starting transfers between devices, pairwise(): parts.append(lax.ppermute(parts[0], axis, pairs))  4.99 us
    ppermute x4, waiting for transfers between devices, pairwise(): parts.append(lax.ppermute(parts[0], axis, pairs))  4.73 us
    ppermute x1, waiting for transfers between devices, shift(): lax.ppermute(value, axis, [(source, source + steps) for source in range(f...  4.52 us
    ppermute x6, waiting for transfers between devices, rotate(): lax.ppermute(value, axis, [(source, (source + steps) % count) for source...  3.28 us
    ppermute x3, starting transfers between devices, exchange(): parts.append(lax.ppermute(parts[0], axis, pairs))  2.71 us
  transfers between devices with their start and end apart: 16, of which 9 were waited for; matrix products, arithmetic and copies ran while one was open for 0% of the time, Pallas kernels for 21%

profile of v18, /device:TPU:1, one launch (start us, length us, event | category | flops | bytes accessed | tf_op | source)
XLA Modules:
  0.0 53.2 jit_solution(9479522875823717602)
XLA Ops:
  0.7 2.1 %collective-permute-start = (bf16[256,256]{1,0:T(8,128)(2,1)}, bf16[256,256]{1,0:T(8,128)(2,1)S(1)}, u32[]{:S(2)}, u32[]{:S(2)}) collective-permute-start(bf16[256,256]{1,0:T(8,128)(2,1)} %bitcast.31), channel_id=1, source_target_pairs={{4,0},{8,4},{12,8},{16,12},{20,16},{24,20},{28,24},{5,1},{9,5},{13... | collective-permute-start | bytes 393224 | tf_op jit(solution)/shard_map/ppermute | solution.py:27
  3.7 4.5 %collective-permute-done.behind = bf16[256,256]{1,0:T(8,128)(2,1)S(1)} collective-permute-done((bf16[256,256]{1,0:T(8,128)(2,1)}, bf16[256,256]{1,0:T(8,128)(2,1)S(1)}, u32[]{:S(2)}, u32[]{:S(2)}) %collective-permute-start) | collective-permute-done | bytes 131104 | tf_op jit(solution)/shard_map/ppermute | solution.py:27
  8.4 1.3 %collective-permute-start.1 = (bf16[256,256]{1,0:T(8,128)(2,1)S(1)}, bf16[256,256]{1,0:T(8,128)(2,1)S(1)}, u32[]{:S(2)}, u32[]{:S(2)}) collective-permute-start(bf16[256,256]{1,0:T(8,128)(2,1)S(1)} %get-tuple-element.42.yb), channel_id=1, source_target_pairs={{0,1},{1,2},{2,3},{3,0},{4,5},{5,6},{6,7},{7,4},{8,9},{9,10},{10,1... | collective-permute-start | bytes 393224 | tf_op jit(solution)/shard_map/ppermute | solution.py:46
  9.7 1.2 %shard_map.107 = (f32[256,256]{1,0:T(8,128)S(1)}, bf16[256,256]{1,0:T(8,128)(2,1)S(1)}) custom-call(bf16[16,256,256]{2,1,0:T(8,128)(2,1)S(1)} %bitcast.9, bf16[16,256,256]{2,1,0:T(8,128)(2,1)S(1)} %bitcast.16, bf16[256,256]{1,0:T(8,128)(2,1)S(1)} %get-tuple-element.42.yb), custom_call_target="tpu_custom_call" | custom-call | tf_op jit(solution)/shard_map/pallas_call | solution.py:354
  10.9 1.2 %collective-permute-start.2 = (bf16[256,256]{1,0:T(8,128)(2,1)S(1)}, bf16[256,256]{1,0:T(8,128)(2,1)S(1)}, u32[]{:S(2)}, u32[]{:S(2)}) collective-permute-start(bf16[256,256]{1,0:T(8,128)(2,1)S(1)} %get-tuple-element.47), channel_id=1, source_target_pairs={{0,3},{1,0},{2,1},{3,2},{4,7},{5,4},{6,5},{7,6},{8,11},{9,8},{10,9... | collective-permute-start | bytes 393224 | tf_op jit(solution)/shard_map/ppermute | solution.py:46
  12.1 1.5 %shard_map.106 = (f32[8,128]{1,0:T(8,128)S(1)}, f32[256,256]{1,0:T(8,128)S(1)}, f32[256,256]{1,0:T(8,128)S(1)}, f32[256,256]{1,0:T(8,128)S(1)}) custom-call(bf16[16,256,256]{2,1,0:T(8,128)(2,1)S(1)} %bitcast.10, bf16[16,256,256]{2,1,0:T(8,128)(2,1)S(1)} %bitcast.17, f32[256,256]{1,0:T(8,128)S(1)} %get-tuple-element.43.y.refs_2_, ...), custom_call_target="tpu_custom_call" | custom-call | tf_op jit(solution)/shard_map/pallas_call | solution.py:354
  13.9 1.2 %collective-permute-start.4 = (f32[8,128]{1,0:T(8,128)S(1)}, f32[8,128]{1,0:T(8,128)S(1)}, u32[]{:S(2)}, u32[]{:S(2)}) collective-permute-start(f32[8,128]{1,0:T(8,128)S(1)} %shard_map.108.after), channel_id=1, source_target_pairs={{0,1},{1,0},{2,3},{3,2},{4,5},{5,4},{6,7},{7,6},{8,9},{9,8},{10,11... | collective-permute-start | bytes 12296 | tf_op jit(solution)/shard_map/ppermute | solution.py:83
  15.1 1.3 %collective-permute-done.4 = f32[8,128]{1,0:T(8,128)S(1)} collective-permute-done((f32[8,128]{1,0:T(8,128)S(1)}, f32[8,128]{1,0:T(8,128)S(1)}, u32[]{:S(2)}, u32[]{:S(2)}) %collective-permute-start.4) | collective-permute-done | bytes 4128 | tf_op jit(solution)/shard_map/ppermute | solution.py:83
  16.4 1.9 %collective-permute-start.5 = (f32[8,128]{1,0:T(8,128)S(1)}, f32[8,128]{1,0:T(8,128)S(1)}, u32[]{:S(2)}, u32[]{:S(2)}) collective-permute-start(f32[8,128]{1,0:T(8,128)S(1)} %add.6.refs_0_), channel_id=1, source_target_pairs={{0,2},{1,3},{2,0},{3,1},{4,6},{5,7},{6,4},{7,5},{8,10},{9,11},{10,... | collective-permute-start | bytes 12296 | tf_op jit(solution)/shard_map/ppermute | solution.py:83
  18.3 1.2 %shard_map.109.up = f32[256,256]{1,0:T(8,128)S(1)} custom-call(bf16[16,256,256]{2,1,0:T(8,128)(2,1)S(1)} %bitcast.11, bf16[16,256,256]{2,1,0:T(8,128)(2,1)S(1)} %bitcast.18, bf16[256,256]{1,0:T(8,128)(2,1)S(1)} %collective-permute-done.1.below.refs_2_.y, f32[8,128]{1,0:T(8,128)S(1)} %shard_map.108.after), custom_call_target="tpu_custom_call" | custom-call | tf_op jit(solution)/shard_map/pallas_call | solution.py:354
  19.7 1.2 %collective-permute-start.3 = (bf16[256,256]{1,0:T(8,128)(2,1)S(1)}, bf16[256,256]{1,0:T(8,128)(2,1)S(1)}, u32[]{:S(2)}, u32[]{:S(2)}) collective-permute-start(bf16[256,256]{1,0:T(8,128)(2,1)S(1)} %get-tuple-element.48), channel_id=1, source_target_pairs={{0,1},{1,2},{2,3},{3,0},{4,5},{5,6},{6,7},{7,4},{8,9},{9,10},{10,1... | collective-permute-start | bytes 393224 | tf_op jit(solution)/shard_map/ppermute | solution.py:46
  20.8 1.3 %shard_map.111 = (f32[256,256]{1,0:T(8,128)S(1)}, f32[256,256]{1,0:T(8,128)S(1)}) custom-call(bf16[16,256,256]{2,1,0:T(8,128)(2,1)S(1)} %bitcast.12, bf16[16,256,256]{2,1,0:T(8,128)(2,1)S(1)} %bitcast.19, bf16[256,256]{1,0:T(8,128)(2,1)S(1)} %get-tuple-element.50.value), custom_call_target="tpu_custom_call" | custom-call | tf_op jit(solution)/shard_map/pallas_call | solution.py:354
  22.6 1.3 %collective-permute-start.7 = (bf16[256,256]{1,0:T(8,128)(2,1)S(1)}, bf16[256,256]{1,0:T(8,128)(2,1)S(1)}, u32[]{:S(2)}, u32[]{:S(2)}) collective-permute-start(bf16[256,256]{1,0:T(8,128)(2,1)S(1)} %get-tuple-element.60), channel_id=1, source_target_pairs={{0,3},{1,0},{2,1},{3,2},{4,7},{5,4},{6,5},{7,6},{8,11},{9,8},{10,9... | collective-permute-start | bytes 393224 | tf_op jit(solution)/shard_map/ppermute | solution.py:46
  23.9 0.8 %collective-permute-done.6.refs_4_.prec = bf16[256,256]{1,0:T(8,128)(2,1)S(1)} collective-permute-done((bf16[256,256]{1,0:T(8,128)(2,1)S(1)}, bf16[256,256]{1,0:T(8,128)(2,1)S(1)}, u32[]{:S(2)}, u32[]{:S(2)}) %collective-permute-start.6) | collective-permute-done | bytes 131104 | tf_op jit(solution)/shard_map/ppermute | solution.py:46
  24.7 2.3 %collective-permute-done.3.refs_3_.g = bf16[256,256]{1,0:T(8,128)(2,1)S(1)} collective-permute-done((bf16[256,256]{1,0:T(8,128)(2,1)S(1)}, bf16[256,256]{1,0:T(8,128)(2,1)S(1)}, u32[]{:S(2)}, u32[]{:S(2)}) %collective-permute-start.3) | collective-permute-done | bytes 131104 | tf_op jit(solution)/shard_map/ppermute | solution.py:46
  27.2 1.2 %shard_map.114.up = f32[256,256]{1,0:T(8,128)S(1)} custom-call(bf16[16,256,256]{2,1,0:T(8,128)(2,1)S(1)} %bitcast.13, bf16[16,256,256]{2,1,0:T(8,128)(2,1)S(1)} %bitcast.20, bf16[256,256]{1,0:T(8,128)(2,1)S(1)} %get-tuple-element.57.below.p, f32[8,128]{1,0:T(8,128)S(1)} %get-tuple-element.59.after), custom_call_target="tpu_custom_call" | custom-call | tf_op jit(solution)/shard_map/pallas_call | solution.py:354
  28.6 1.3 %collective-permute-start.8 = (bf16[256,256]{1,0:T(8,128)(2,1)S(1)}, bf16[256,256]{1,0:T(8,128)(2,1)S(1)}, u32[]{:S(2)}, u32[]{:S(2)}) collective-permute-start(bf16[256,256]{1,0:T(8,128)(2,1)S(1)} %get-tuple-element.61), channel_id=1, source_target_pairs={{0,1},{1,2},{2,3},{3,0},{4,5},{5,6},{6,7},{7,4},{8,9},{9,10},{10,1... | collective-permute-start | bytes 393224 | tf_op jit(solution)/shard_map/ppermute | solution.py:46
  29.8 1.2 %collective-permute-start.9 = (f32[8,128]{1,0:T(8,128)S(1)}, f32[8,128]{1,0:T(8,128)S(1)}, u32[]{:S(2)}, u32[]{:S(2)}) collective-permute-start(f32[8,128]{1,0:T(8,128)S(1)} %get-tuple-element.59.after), channel_id=1, source_target_pairs={{0,1},{1,0},{2,3},{3,2},{4,5},{5,4},{6,7},{7,6},{8,9},{9,8},{10,11... | collective-permute-start | bytes 12296 | tf_op jit(solution)/shard_map/ppermute | solution.py:83
  31.0 3.4 %collective-permute-done.9 = f32[8,128]{1,0:T(8,128)S(1)} collective-permute-done((f32[8,128]{1,0:T(8,128)S(1)}, f32[8,128]{1,0:T(8,128)S(1)}, u32[]{:S(2)}, u32[]{:S(2)}) %collective-permute-start.9) | collective-permute-done | bytes 4128 | tf_op jit(solution)/shard_map/ppermute | solution.py:83
  34.4 0.7 %collective-permute-start.10 = (f32[8,128]{1,0:T(8,128)S(1)}, f32[8,128]{1,0:T(8,128)S(1)}, u32[]{:S(2)}, u32[]{:S(2)}) collective-permute-start(f32[8,128]{1,0:T(8,128)S(1)} %add.7.refs_0_), channel_id=1, source_target_pairs={{0,2},{1,3},{2,0},{3,1},{4,6},{5,7},{6,4},{7,5},{8,10},{9,11},{10,... | collective-permute-start | bytes 12296 | tf_op jit(solution)/shard_map/ppermute | solution.py:83
  35.1 1.3 %shard_map.117 = (f32[256,256]{1,0:T(8,128)S(1)}, f32[256,256]{1,0:T(8,128)S(1)}) custom-call(bf16[16,256,256]{2,1,0:T(8,128)(2,1)S(1)} %bitcast.14, bf16[16,256,256]{2,1,0:T(8,128)(2,1)S(1)} %bitcast.21, bf16[256,256]{1,0:T(8,128)(2,1)S(1)} %get-tuple-element.67.value), custom_call_target="tpu_custom_call" | custom-call | tf_op jit(solution)/shard_map/pallas_call | solution.py:354
  36.4 1.3 %shard_map.116 = (f32[256,256]{1,0:T(8,128)S(1)}, f32[256,256]{1,0:T(8,128)S(1)}) custom-call(bf16[16,256,256]{2,1,0:T(8,128)(2,1)S(1)} %bitcast.15, bf16[16,256,256]{2,1,0:T(8,128)(2,1)S(1)} %bitcast.22, bf16[256,256]{1,0:T(8,128)(2,1)S(1)} %get-tuple-element.65.value), custom_call_target="tpu_custom_call" | custom-call | tf_op jit(solution)/shard_map/pallas_call | solution.py:354
  38.5 0.8 %collective-permute-start.13 = (f32[8,128]{1,0:T(8,128)S(1)}, f32[8,128]{1,0:T(8,128)S(1)}, u32[]{:S(2)}, u32[]{:S(2)}) collective-permute-start(f32[8,128]{1,0:T(8,128)S(1)} %shard_map.119.refs_0_), channel_id=1, source_target_pairs={{0,3},{1,2},{2,1},{3,0},{4,7},{5,6},{6,5},{7,4},{8,11},{9,10},{10,... | collective-permute-start | bytes 12296 | tf_op jit(solution)/shard_map/ppermute | solution.py:69
  39.5 1.7 %collective-permute-start.11 = (f32[8,128]{1,0:T(8,128)S(1)}, f32[8,128]{1,0:T(8,128)S(1)}, u32[]{:S(2)}, u32[]{:S(2)}) collective-permute-start(f32[8,128]{1,0:T(8,128)S(1)} %shard_map.119.refs_0_), channel_id=1, source_target_pairs={{0,1},{1,0},{2,3},{3,2},{4,5},{5,4},{6,7},{7,6},{8,9},{9,8},{10,11... | collective-permute-start | bytes 12296 | tf_op jit(solution)/shard_map/ppermute | solution.py:69
  41.2 0.7 %collective-permute-done.13.refs_3_ = f32[8,128]{1,0:T(8,128)S(1)} collective-permute-done((f32[8,128]{1,0:T(8,128)S(1)}, f32[8,128]{1,0:T(8,128)S(1)}, u32[]{:S(2)}, u32[]{:S(2)}) %collective-permute-start.13) | collective-permute-done | bytes 4128 | tf_op jit(solution)/shard_map/ppermute | solution.py:69
  42.2 1.7 %shard_map.120 = (f32[256,256]{1,0:T(8,128)S(1)}, bf16[1,1,256,256]{3,2,1,0:T(8,128)(2,1)S(1)}) custom-call(f32[8,128]{1,0:T(8,128)S(1)} %shard_map.119.refs_0_, f32[8,128]{1,0:T(8,128)S(1)} %collective-permute-done.11.refs_1_, f32[8,128]{1,0:T(8,128)S(1)} %collective-permute-done.12.refs_2_, f32[8,128]{1,0:T(8,128)S(1)} %collective-permute-done.13.refs_3_, ...), custom_call_target="tpu_custom_call" | custom-call | tf_op jit(solution)/shard_map/pallas_call | solution.py:354
  43.8 0.7 %shard_map.121 = (f32[256,256]{1,0:T(8,128)S(1)}, bf16[1,1,256,256]{3,2,1,0:T(8,128)(2,1)S(1)}, f32[1]{0:T(128)}) custom-call(f32[8,128]{1,0:T(8,128)S(1)} %shard_map.119.refs_0_, f32[8,128]{1,0:T(8,128)S(1)} %collective-permute-done.11.refs_1_, f32[8,128]{1,0:T(8,128)S(1)} %collective-permute-done.12.refs_2_, ...), custom_call_target="tpu_custom_call", output_to_operand_aliasing={{0}: (7, {})} | custom-call | tf_op jit(solution)/shard_map/pallas_call | solution.py:354
  44.5 3.4 %collective-permute-start.14 = (bf16[1,1,256,256]{3,2,1,0:T(8,128)(2,1)S(1)}, bf16[1,1,256,256]{3,2,1,0:T(8,128)(2,1)S(1)}, u32[]{:S(2)}, u32[]{:S(2)}) collective-permute-start(bf16[1,1,256,256]{3,2,1,0:T(8,128)(2,1)S(1)} %get-tuple-element.78), channel_id=1, source_target_pairs={{0,4},{1,5},{2,6},{3,7},{4,0},{5,1},{6,2},{7,3},{8,12},{9,13},{10,... | collective-permute-start | bytes 393224 | tf_op jit(solution)/shard_map/ppermute | solution.py:41
  47.9 1.9 %collective-permute-start.15 = (bf16[1,1,256,256]{3,2,1,0:T(8,128)(2,1)S(1)}, bf16[1,1,256,256]{3,2,1,0:T(8,128)(2,1)S(1)}, u32[]{:S(2)}, u32[]{:S(2)}) collective-permute-start(bf16[1,1,256,256]{3,2,1,0:T(8,128)(2,1)S(1)} %get-tuple-element.79), channel_id=1, source_target_pairs={{0,1},{1,0},{2,3},{3,2},{4,8},{5,9},{6,10},{7,11},{8,4},{9,5},{10,... | collective-permute-start | bytes 393224 | tf_op jit(solution)/shard_map/ppermute | solution.py:41
  49.8 0.7 %shard_map.122 = f32[1,1,256,256]{3,2,1,0:T(8,128)} custom-call(f32[256,256]{1,0:T(8,128)S(1)} %get-tuple-element.77.value), custom_call_target="tpu_custom_call" | custom-call | bytes 1048576 | tf_op jit(solution)/shard_map/pallas_call | solution.py:354
  50.5 2.1 %collective-permute-done.15.far = bf16[1,1,256,256]{3,2,1,0:T(8,128)(2,1)S(1)} collective-permute-done((bf16[1,1,256,256]{3,2,1,0:T(8,128)(2,1)S(1)}, bf16[1,1,256,256]{3,2,1,0:T(8,128)(2,1)S(1)}, u32[]{:S(2)}, u32[]{:S(2)}) %collective-permute-start.15) | collective-permute-done | bytes 131104 | tf_op jit(solution)/shard_map/ppermute | solution.py:41
  52.6 0.7 %shard_map.123 = bf16[1,1,256,256]{3,2,1,0:T(8,128)(2,1)} custom-call(bf16[1,1,256,256]{3,2,1,0:T(8,128)(2,1)S(1)} %collective-permute-done.14.near, bf16[1,1,256,256]{3,2,1,0:T(8,128)(2,1)S(1)} %collective-permute-done.15.far), custom_call_target="tpu_custom_call" | custom-call | tf_op jit(solution)/shard_map/pallas_call | solution.py:354
  (36 shorter events, 2.8 us)
Async XLA Ops:
  0.6 3.0 %copy-start.4 = (bf16[1,1,256,256]{3,2,1,0:T(8,128)(2,1)S(1)}, bf16[1,1,256,256]{3,2,1,0:T(8,128)(2,1)}, u32[]{:S(2)}) copy-start(bf16[1,1,256,256]{3,2,1,0:T(8,128)(2,1)} %param.10) | copy-start | bytes 393220
  0.6 3.0 %copy-start.5 = (f32[1,1,256]{2,1,0:T(1,128)S(1)}, f32[1,1,256]{2,1,0:T(1,128)}, u32[]{:S(2)}) copy-start(f32[1,1,256]{2,1,0:T(1,128)} %param.13) | copy-start | bytes 3076
  0.7 7.6 %copy-start.3 = (bf16[1,1,256,256]{3,2,1,0:T(8,128)(2,1)S(1)}, bf16[1,1,256,256]{3,2,1,0:T(8,128)(2,1)}, u32[]{:S(2)}) copy-start(bf16[1,1,256,256]{3,2,1,0:T(8,128)(2,1)} %param.12) | copy-start | bytes 393220
  0.7 7.6 %collective-permute-start = (bf16[256,256]{1,0:T(8,128)(2,1)}, bf16[256,256]{1,0:T(8,128)(2,1)S(1)}, u32[]{:S(2)}, u32[]{:S(2)}) collective-permute-start(bf16[256,256]{1,0:T(8,128)(2,1)} %bitcast.31), channel_id=1, source_target_pairs={{4,0},{8,4},{12,8},{16,12},{20,16},{24,20},{28,24},{5,1},{9,5},{13... | collective-permute-start | bytes 393224 | tf_op jit(solution)/shard_map/ppermute | solution.py:27
  2.7 7.0 %copy-start = (bf16[1,1,16,256,256]{4,3,2,1,0:T(8,128)(2,1)S(1)}, bf16[1,1,16,256,256]{4,3,2,1,0:T(8,128)(2,1)}, u32[]{:S(2)}) copy-start(bf16[1,1,16,256,256]{4,3,2,1,0:T(8,128)(2,1)} %param.8) | copy-start | bytes 6291460
  2.7 7.0 %copy-start.1 = (bf16[1,1,16,256,256]{4,3,2,1,0:T(8,128)(2,1)S(1)}, bf16[1,1,16,256,256]{4,3,2,1,0:T(8,128)(2,1)}, u32[]{:S(2)}) copy-start(bf16[1,1,16,256,256]{4,3,2,1,0:T(8,128)(2,1)} %param.9) | copy-start | bytes 6291460
  8.4 5.4 %collective-permute-start.1 = (bf16[256,256]{1,0:T(8,128)(2,1)S(1)}, bf16[256,256]{1,0:T(8,128)(2,1)S(1)}, u32[]{:S(2)}, u32[]{:S(2)}) collective-permute-start(bf16[256,256]{1,0:T(8,128)(2,1)S(1)} %get-tuple-element.42.yb), channel_id=1, source_target_pairs={{0,1},{1,2},{2,3},{3,0},{4,5},{5,6},{6,7},{7,4},{8,9},{9,10},{10,1... | collective-permute-start | bytes 393224 | tf_op jit(solution)/shard_map/ppermute | solution.py:46
  9.7 2.4 %copy-start.2 = (bf16[1,1,256,256]{3,2,1,0:T(8,128)(2,1)S(1)}, bf16[1,1,256,256]{3,2,1,0:T(8,128)(2,1)}, u32[]{:S(2)}) copy-start(bf16[1,1,256,256]{3,2,1,0:T(8,128)(2,1)} %param.14) | copy-start | bytes 393220
  10.9 8.6 %collective-permute-start.2 = (bf16[256,256]{1,0:T(8,128)(2,1)S(1)}, bf16[256,256]{1,0:T(8,128)(2,1)S(1)}, u32[]{:S(2)}, u32[]{:S(2)}) collective-permute-start(bf16[256,256]{1,0:T(8,128)(2,1)S(1)} %get-tuple-element.47), channel_id=1, source_target_pairs={{0,3},{1,0},{2,1},{3,2},{4,7},{5,4},{6,5},{7,6},{8,11},{9,8},{10,9... | collective-permute-start | bytes 393224 | tf_op jit(solution)/shard_map/ppermute | solution.py:46
  13.9 2.5 %collective-permute-start.4 = (f32[8,128]{1,0:T(8,128)S(1)}, f32[8,128]{1,0:T(8,128)S(1)}, u32[]{:S(2)}, u32[]{:S(2)}) collective-permute-start(f32[8,128]{1,0:T(8,128)S(1)} %shard_map.108.after), channel_id=1, source_target_pairs={{0,1},{1,0},{2,3},{3,2},{4,5},{5,4},{6,7},{7,6},{8,9},{9,8},{10,11... | collective-permute-start | bytes 12296 | tf_op jit(solution)/shard_map/ppermute | solution.py:83
  16.4 5.7 %collective-permute-start.5 = (f32[8,128]{1,0:T(8,128)S(1)}, f32[8,128]{1,0:T(8,128)S(1)}, u32[]{:S(2)}, u32[]{:S(2)}) collective-permute-start(f32[8,128]{1,0:T(8,128)S(1)} %add.6.refs_0_), channel_id=1, source_target_pairs={{0,2},{1,3},{2,0},{3,1},{4,6},{5,7},{6,4},{7,5},{8,10},{9,11},{10,... | collective-permute-start | bytes 12296 | tf_op jit(solution)/shard_map/ppermute | solution.py:83
  18.3 6.4 %collective-permute-start.6 = (bf16[256,256]{1,0:T(8,128)(2,1)S(1)}, bf16[256,256]{1,0:T(8,128)(2,1)S(1)}, u32[]{:S(2)}, u32[]{:S(2)}) collective-permute-start(bf16[256,256]{1,0:T(8,128)(2,1)S(1)} %bitcast.24), channel_id=1, source_target_pairs={{0,1},{1,2},{2,3},{3,0},{4,5},{5,6},{6,7},{7,4},{8,9},{9,10},{10,1... | collective-permute-start | bytes 393224 | tf_op jit(solution)/shard_map/ppermute | solution.py:46
  19.7 7.3 %collective-permute-start.3 = (bf16[256,256]{1,0:T(8,128)(2,1)S(1)}, bf16[256,256]{1,0:T(8,128)(2,1)S(1)}, u32[]{:S(2)}, u32[]{:S(2)}) collective-permute-start(bf16[256,256]{1,0:T(8,128)(2,1)S(1)} %get-tuple-element.48), channel_id=1, source_target_pairs={{0,1},{1,2},{2,3},{3,0},{4,5},{5,6},{6,7},{7,4},{8,9},{9,10},{10,1... | collective-permute-start | bytes 393224 | tf_op jit(solution)/shard_map/ppermute | solution.py:46
  22.6 5.9 %collective-permute-start.7 = (bf16[256,256]{1,0:T(8,128)(2,1)S(1)}, bf16[256,256]{1,0:T(8,128)(2,1)S(1)}, u32[]{:S(2)}, u32[]{:S(2)}) collective-permute-start(bf16[256,256]{1,0:T(8,128)(2,1)S(1)} %get-tuple-element.60), channel_id=1, source_target_pairs={{0,3},{1,0},{2,1},{3,2},{4,7},{5,4},{6,5},{7,6},{8,11},{9,8},{10,9... | collective-permute-start | bytes 393224 | tf_op jit(solution)/shard_map/ppermute | solution.py:46
  28.6 9.7 %collective-permute-start.8 = (bf16[256,256]{1,0:T(8,128)(2,1)S(1)}, bf16[256,256]{1,0:T(8,128)(2,1)S(1)}, u32[]{:S(2)}, u32[]{:S(2)}) collective-permute-start(bf16[256,256]{1,0:T(8,128)(2,1)S(1)} %get-tuple-element.61), channel_id=1, source_target_pairs={{0,1},{1,2},{2,3},{3,0},{4,5},{5,6},{6,7},{7,4},{8,9},{9,10},{10,1... | collective-permute-start | bytes 393224 | tf_op jit(solution)/shard_map/ppermute | solution.py:46
  29.8 4.6 %collective-permute-start.9 = (f32[8,128]{1,0:T(8,128)S(1)}, f32[8,128]{1,0:T(8,128)S(1)}, u32[]{:S(2)}, u32[]{:S(2)}) collective-permute-start(f32[8,128]{1,0:T(8,128)S(1)} %get-tuple-element.59.after), channel_id=1, source_target_pairs={{0,1},{1,0},{2,3},{3,2},{4,5},{5,4},{6,7},{7,6},{8,9},{9,8},{10,11... | collective-permute-start | bytes 12296 | tf_op jit(solution)/shard_map/ppermute | solution.py:83
  34.4 3.3 %collective-permute-start.10 = (f32[8,128]{1,0:T(8,128)S(1)}, f32[8,128]{1,0:T(8,128)S(1)}, u32[]{:S(2)}, u32[]{:S(2)}) collective-permute-start(f32[8,128]{1,0:T(8,128)S(1)} %add.7.refs_0_), channel_id=1, source_target_pairs={{0,2},{1,3},{2,0},{3,1},{4,6},{5,7},{6,4},{7,5},{8,10},{9,11},{10,... | collective-permute-start | bytes 12296 | tf_op jit(solution)/shard_map/ppermute | solution.py:83
  38.5 3.4 %collective-permute-start.13 = (f32[8,128]{1,0:T(8,128)S(1)}, f32[8,128]{1,0:T(8,128)S(1)}, u32[]{:S(2)}, u32[]{:S(2)}) collective-permute-start(f32[8,128]{1,0:T(8,128)S(1)} %shard_map.119.refs_0_), channel_id=1, source_target_pairs={{0,3},{1,2},{2,1},{3,0},{4,7},{5,6},{6,5},{7,4},{8,11},{9,10},{10,... | collective-permute-start | bytes 12296 | tf_op jit(solution)/shard_map/ppermute | solution.py:69
  39.2 2.7 %collective-permute-start.12 = (f32[8,128]{1,0:T(8,128)S(1)}, f32[8,128]{1,0:T(8,128)S(1)}, u32[]{:S(2)}, u32[]{:S(2)}) collective-permute-start(f32[8,128]{1,0:T(8,128)S(1)} %shard_map.119.refs_0_), channel_id=1, source_target_pairs={{0,2},{1,3},{2,0},{3,1},{4,6},{5,7},{6,4},{7,5},{8,10},{9,11},{10,... | collective-permute-start | bytes 12296 | tf_op jit(solution)/shard_map/ppermute | solution.py:69
  39.5 2.7 %collective-permute-start.11 = (f32[8,128]{1,0:T(8,128)S(1)}, f32[8,128]{1,0:T(8,128)S(1)}, u32[]{:S(2)}, u32[]{:S(2)}) collective-permute-start(f32[8,128]{1,0:T(8,128)S(1)} %shard_map.119.refs_0_), channel_id=1, source_target_pairs={{0,1},{1,0},{2,3},{3,2},{4,5},{5,4},{6,7},{7,6},{8,9},{9,8},{10,11... | collective-permute-start | bytes 12296 | tf_op jit(solution)/shard_map/ppermute | solution.py:69
  44.5 6.0 %collective-permute-start.14 = (bf16[1,1,256,256]{3,2,1,0:T(8,128)(2,1)S(1)}, bf16[1,1,256,256]{3,2,1,0:T(8,128)(2,1)S(1)}, u32[]{:S(2)}, u32[]{:S(2)}) collective-permute-start(bf16[1,1,256,256]{3,2,1,0:T(8,128)(2,1)S(1)} %get-tuple-element.78), channel_id=1, source_target_pairs={{0,4},{1,5},{2,6},{3,7},{4,0},{5,1},{6,2},{7,3},{8,12},{9,13},{10,... | collective-permute-start | bytes 393224 | tf_op jit(solution)/shard_map/ppermute | solution.py:41
  47.9 4.7 %collective-permute-start.15 = (bf16[1,1,256,256]{3,2,1,0:T(8,128)(2,1)S(1)}, bf16[1,1,256,256]{3,2,1,0:T(8,128)(2,1)S(1)}, u32[]{:S(2)}, u32[]{:S(2)}) collective-permute-start(bf16[1,1,256,256]{3,2,1,0:T(8,128)(2,1)S(1)} %get-tuple-element.79), channel_id=1, source_target_pairs={{0,1},{1,0},{2,3},{3,2},{4,8},{5,9},{6,10},{7,11},{8,4},{9,5},{10,... | collective-permute-start | bytes 393224 | tf_op jit(solution)/shard_map/ppermute | solution.py:41
